TPU v7x, 32 devices: a whole 2x2x4 slice. The times are simulated.
32 devices in a mesh: seq: 4 (over y, x), shard: 8 (over z, core).
Axes of the slice: x: 2, y: 2, z: 4, core: 2. Of those that a mesh axis runs over, the one named last changes fastest.
Arguments:
- tokens: bfloat16 [8, 1024, 768], P('shard', 'seq'), may hold values from -6 to 6
- lengths: int32 [8], P('shard'), may hold values from 128 to 1024, as said below
- w_qkv: bfloat16 [768, 2304], P('shard'), may hold values from -0.21875 to 0.21875
- q_bias: bfloat16 [768], P('shard'), may hold values from -3 to 3
- v_bias: bfloat16 [768], P('shard'), may hold values from -3 to 3
- w_out: bfloat16 [768, 768], P('shard'), may hold values from -1.25 to 1.25
- out_bias: bfloat16 [768], P('shard'), may hold values from -3 to 3
- gain_one: bfloat16 [768], P('shard'), may hold values from 0.5 to 1.5
- shift_one: bfloat16 [768], P('shard'), may hold values from -3 to 3
- w_up: bfloat16 [768, 3072], P('shard'), may hold values from -0.21875 to 0.21875
- up_bias: bfloat16 [3072], P('shard'), may hold values from -3 to 3
- w_down: bfloat16 [3072, 768], P('shard'), may hold values from -0.109375 to 0.109375
- down_bias: bfloat16 [768], P('shard'), may hold values from -3 to 3
- gain_two: bfloat16 [768], P('shard'), may hold values from 0.5 to 1.5
- shift_two: bfloat16 [768], P('shard'), may hold values from -3 to 3
- cotangent: bfloat16 [8, 1024, 768], P('shard', 'seq'), may hold values from -6 to 6
Outputs:
- output: bfloat16 [8, 1024, 768], P('shard', 'seq')
- grad_tokens: bfloat16 [8, 1024, 768], P('shard', 'seq')
- grad_w_qkv: float32 [768, 2304], P('shard')
- grad_q_bias: float32 [768], P('shard')
- grad_v_bias: float32 [768], P('shard')
- grad_w_out: float32 [768, 768], P('shard')
- grad_out_bias: float32 [768], P('shard')
- grad_gain_one: float32 [768], P('shard')
- grad_shift_one: float32 [768], P('shard')
- grad_w_up: float32 [768, 3072], P('shard')
- grad_up_bias: float32 [3072], P('shard')
- grad_w_down: float32 [3072, 768], P('shard')
- grad_down_bias: float32 [768], P('shard')
- grad_gain_two: float32 [768], P('shard')
- grad_shift_two: float32 [768], P('shard')
Inputs may be any that keep to these rules, and one draw needn't show every extreme that they name: `lengths`: each sequence has from 128 to 1024 valid positions; in every draw some sequence has exactly 1024 and another exactly 128.
All inputs are finite; a program needn't handle non-finite values.
Results may differ from a plain program's by a relative error of at most 0.015.
Values may be sent and summed in bfloat16 or wider, within the bound.
No kernel may reach another device: no remote copies, remote signals or barrier semaphores. Data moves between devices by JAX's collectives and lax.ppermute only.
A program may use at most 128 MiB of HBM per device.

v0:
```python
import jax
import jax.numpy as jnp
from jax import lax
from jax.experimental import pallas as pl
from jax.experimental.pallas import tpu as pltpu
from jax.sharding import PartitionSpec as P

HEAD_DIM = 64
LEN = 1024
Q_BLOCK = 512


epsilon = 1e-05
masked_score = -1000000000.0


def layer_norm(values, gain, shift):
    center = values - jnp.mean(values, axis=-1, keepdims=True)
    spread = jnp.mean(center * center, axis=-1, keepdims=True)
    return center * lax.rsqrt(spread + epsilon) * gain + shift


def gelu_exact(values):
    return jax.nn.gelu(values, approximate=False)


def contract_rows(left, right):
    return lax.dot_general(
        left, right, (((0,), (0,)), ((), ())), preferred_element_type=jnp.float32
    )


def contract_cols(left, right):
    return lax.dot_general(
        left, right, (((1,), (1,)), ((), ())), preferred_element_type=jnp.float32
    )


def block_scores(q_block, k_seq, key_valid):
    scores = jnp.einsum(
        "qhd,khd->hqk", q_block, k_seq, preferred_element_type=jnp.float32
    ) * HEAD_DIM ** (-0.5)
    return jnp.where(key_valid[None, None, :], scores, masked_score)


def attend_forward(q_seq, k_seq, v_seq, length):
    local_heads = q_seq.shape[1]
    key_valid = jnp.arange(LEN, dtype=jnp.int32) < length
    q_blocks = q_seq.reshape(LEN // Q_BLOCK, Q_BLOCK, local_heads, HEAD_DIM)

    def one_block(q_block):
        scores = block_scores(q_block, k_seq, key_valid)
        row_peak = jnp.max(scores, axis=-1, keepdims=True)
        shifted = jnp.exp(scores - row_peak)
        row_total = jnp.sum(shifted, axis=-1, keepdims=True)
        attn_probs = (shifted / row_total).astype(jnp.bfloat16)
        context = jnp.einsum("hqk,khd->qhd", attn_probs, v_seq, preferred_element_type=jnp.float32)
        return (context.astype(jnp.bfloat16), (row_peak + jnp.log(row_total))[..., 0])

    context, log_total = lax.map(one_block, q_blocks)
    return (context.reshape(LEN, local_heads, HEAD_DIM), log_total)


def attend_backward(q_seq, k_seq, v_seq, grad_seq, log_total, length):
    local_heads = q_seq.shape[1]
    score_scale = HEAD_DIM ** (-0.5)
    key_valid = jnp.arange(LEN, dtype=jnp.int32) < length
    q_blocks = q_seq.reshape(LEN // Q_BLOCK, Q_BLOCK, local_heads, HEAD_DIM)
    g_blocks = grad_seq.reshape(LEN // Q_BLOCK, Q_BLOCK, local_heads, HEAD_DIM)

    def one_block(accum, block_item):
        q_block, g_block, lse_block = block_item
        scores = block_scores(q_block, k_seq, key_valid)
        attn_probs = jnp.exp(scores - lse_block[..., None])
        grad_probs = jnp.einsum("qhd,khd->hqk", g_block, v_seq, preferred_element_type=jnp.float32)
        row_dot = jnp.sum(attn_probs * grad_probs, axis=-1, keepdims=True)
        grad_scores = (attn_probs * (grad_probs - row_dot)).astype(jnp.bfloat16)
        grad_q = (
            jnp.einsum("hqk,khd->qhd", grad_scores, k_seq, preferred_element_type=jnp.float32)
            * score_scale
        )
        grad_k = (
            accum[0]
            + jnp.einsum("hqk,qhd->khd", grad_scores, q_block, preferred_element_type=jnp.float32)
            * score_scale
        )
        grad_v = accum[1] + jnp.einsum(
            "hqk,qhd->khd",
            attn_probs.astype(jnp.bfloat16),
            g_block,
            preferred_element_type=jnp.float32,
        )
        return ((grad_k, grad_v), grad_q.astype(jnp.bfloat16))

    zero_keys = jnp.zeros((LEN, local_heads, HEAD_DIM), jnp.float32)
    (grad_k, grad_v), grad_q = lax.scan(
        one_block, (zero_keys, zero_keys), (q_blocks, g_blocks, log_total)
    )
    return (
        grad_q.reshape(LEN, local_heads, HEAD_DIM),
        grad_k.astype(jnp.bfloat16),
        grad_v.astype(jnp.bfloat16),
    )


def body(
    tokens,
    lengths,
    w_qkv,
    q_bias,
    v_bias,
    w_out,
    out_bias,
    gain_one,
    shift_one,
    w_up,
    up_bias,
    w_down,
    down_bias,
    gain_two,
    shift_two,
    cotangent,
):
    seq_count, local_len, model_width = tokens.shape
    row_count = seq_count * local_len
    head_count = model_width // HEAD_DIM
    gathered = (
        lax.all_gather(w_qkv, "shard", axis=0, tiled=True),
        lax.all_gather(q_bias, "shard", axis=0, tiled=True),
        lax.all_gather(v_bias, "shard", axis=0, tiled=True),
        lax.all_gather(w_out, "shard", axis=0, tiled=True),
        lax.all_gather(out_bias, "shard", axis=0, tiled=True),
        lax.all_gather(gain_one, "shard", axis=0, tiled=True),
        lax.all_gather(shift_one, "shard", axis=0, tiled=True),
        lax.all_gather(w_up, "shard", axis=0, tiled=True),
        lax.all_gather(up_bias, "shard", axis=0, tiled=True),
        lax.all_gather(w_down, "shard", axis=0, tiled=True),
        lax.all_gather(down_bias, "shard", axis=0, tiled=True),
        lax.all_gather(gain_two, "shard", axis=0, tiled=True),
        lax.all_gather(shift_two, "shard", axis=0, tiled=True),
    )
    (
        full_qkv,
        full_q_bias,
        full_v_bias,
        full_out,
        full_out_bias,
        full_gain_one,
        full_shift_one,
        full_up,
        full_up_bias,
        full_down,
        full_down_bias,
        full_gain_two,
        full_shift_two,
    ) = gathered
    token_rows = tokens.reshape(row_count, model_width)
    joined_bias = jnp.concatenate([full_q_bias, jnp.zeros_like(full_q_bias), full_v_bias]).astype(
        jnp.float32
    )
    qkv_rows = (
        jnp.dot(token_rows, full_qkv, preferred_element_type=jnp.float32) + joined_bias
    ).astype(jnp.bfloat16)
    qkv_tokens = qkv_rows.reshape(seq_count, local_len, 3, head_count, HEAD_DIM)
    qkv_heads = lax.all_to_all(qkv_tokens, "seq", split_axis=3, concat_axis=1, tiled=True)

    def forward_seq(seq_item):
        qkv_seq, length = seq_item
        return attend_forward(qkv_seq[:, 0], qkv_seq[:, 1], qkv_seq[:, 2], length)

    context_heads, log_total = lax.map(forward_seq, (qkv_heads, lengths))
    context_tokens = lax.all_to_all(context_heads, "seq", split_axis=1, concat_axis=2, tiled=True)
    context_rows = context_tokens.reshape(row_count, model_width)
    residual_one = (
        token_rows.astype(jnp.float32)
        + jnp.dot(context_rows, full_out, preferred_element_type=jnp.float32)
        + full_out_bias.astype(jnp.float32)
    )
    normed_one, norm_one_pull = jax.vjp(
        layer_norm,
        residual_one,
        full_gain_one.astype(jnp.float32),
        full_shift_one.astype(jnp.float32),
    )
    normed_low = normed_one.astype(jnp.bfloat16)
    up_rows = jnp.dot(
        normed_low, full_up, preferred_element_type=jnp.float32
    ) + full_up_bias.astype(jnp.float32)
    active, gelu_pull = jax.vjp(gelu_exact, up_rows)
    active_low = active.astype(jnp.bfloat16)
    residual_two = (
        normed_one
        + jnp.dot(active_low, full_down, preferred_element_type=jnp.float32)
        + full_down_bias.astype(jnp.float32)
    )
    final_rows, norm_two_pull = jax.vjp(
        layer_norm,
        residual_two,
        full_gain_two.astype(jnp.float32),
        full_shift_two.astype(jnp.float32),
    )
    output = final_rows.astype(jnp.bfloat16).reshape(tokens.shape)
    back_qkv, back_out, back_up, back_down = (full_qkv, full_out, full_up, full_down)
    grad_rows = cotangent.reshape(row_count, model_width).astype(jnp.float32)
    grad_two, grad_gain_two, grad_shift_two = norm_two_pull(grad_rows)
    grad_down_bias = jnp.sum(grad_two, axis=0)
    grad_two_low = grad_two.astype(jnp.bfloat16)
    grad_w_down = contract_rows(active_low, grad_two_low)
    grad_active = contract_cols(grad_two_low, back_down)
    (grad_up,) = gelu_pull(grad_active)
    grad_up_bias = jnp.sum(grad_up, axis=0)
    grad_up_low = grad_up.astype(jnp.bfloat16)
    grad_w_up = contract_rows(normed_low, grad_up_low)
    grad_normed = grad_two + contract_cols(grad_up_low, back_up)
    grad_one, grad_gain_one, grad_shift_one = norm_one_pull(grad_normed)
    grad_out_bias = jnp.sum(grad_one, axis=0)
    grad_one_low = grad_one.astype(jnp.bfloat16)
    grad_w_out = contract_rows(context_rows, grad_one_low)
    grad_context = contract_cols(grad_one_low, back_out).astype(jnp.bfloat16)
    grad_context = grad_context.reshape(seq_count, local_len, head_count, HEAD_DIM)
    grad_context_heads = lax.all_to_all(
        grad_context, "seq", split_axis=2, concat_axis=1, tiled=True
    )

    def backward_seq(seq_item):
        qkv_seq, grad_seq, lse_seq, length = seq_item
        grad_q, grad_k, grad_v = attend_backward(
            qkv_seq[:, 0], qkv_seq[:, 1], qkv_seq[:, 2], grad_seq, lse_seq, length
        )
        return jnp.stack([grad_q, grad_k, grad_v], axis=1)

    grad_qkv_heads = lax.map(backward_seq, (qkv_heads, grad_context_heads, log_total, lengths))
    grad_qkv_tokens = lax.all_to_all(grad_qkv_heads, "seq", split_axis=1, concat_axis=3, tiled=True)
    grad_qkv_rows = grad_qkv_tokens.reshape(row_count, 3 * model_width)
    grad_q_bias = jnp.sum(grad_qkv_rows[:, :model_width], axis=0, dtype=jnp.float32)
    grad_v_bias = jnp.sum(grad_qkv_rows[:, 2 * model_width :], axis=0, dtype=jnp.float32)
    grad_w_qkv = contract_rows(token_rows, grad_qkv_rows)
    grad_tokens = grad_one + contract_cols(grad_qkv_rows, back_qkv)
    grad_tokens = grad_tokens.astype(jnp.bfloat16).reshape(tokens.shape)
    owned = (
        lax.psum_scatter(grad_w_qkv, "shard", scatter_dimension=0, tiled=True),
        lax.psum_scatter(grad_q_bias, "shard", scatter_dimension=0, tiled=True),
        lax.psum_scatter(grad_v_bias, "shard", scatter_dimension=0, tiled=True),
        lax.psum_scatter(grad_w_out, "shard", scatter_dimension=0, tiled=True),
        lax.psum_scatter(grad_out_bias, "shard", scatter_dimension=0, tiled=True),
        lax.psum_scatter(grad_gain_one, "shard", scatter_dimension=0, tiled=True),
        lax.psum_scatter(grad_shift_one, "shard", scatter_dimension=0, tiled=True),
        lax.psum_scatter(grad_w_up, "shard", scatter_dimension=0, tiled=True),
        lax.psum_scatter(grad_up_bias, "shard", scatter_dimension=0, tiled=True),
        lax.psum_scatter(grad_w_down, "shard", scatter_dimension=0, tiled=True),
        lax.psum_scatter(grad_down_bias, "shard", scatter_dimension=0, tiled=True),
        lax.psum_scatter(grad_gain_two, "shard", scatter_dimension=0, tiled=True),
        lax.psum_scatter(grad_shift_two, "shard", scatter_dimension=0, tiled=True),
    )
    owned_columns = (
        lax.psum_scatter(
            owned[0].astype(jnp.bfloat16), "seq", scatter_dimension=1, tiled=True
        ).astype(jnp.float32),
        lax.psum_scatter(
            owned[3].astype(jnp.bfloat16), "seq", scatter_dimension=1, tiled=True
        ).astype(jnp.float32),
        lax.psum_scatter(
            owned[7].astype(jnp.bfloat16), "seq", scatter_dimension=1, tiled=True
        ).astype(jnp.float32),
        lax.psum_scatter(
            owned[9].astype(jnp.bfloat16), "seq", scatter_dimension=1, tiled=True
        ).astype(jnp.float32),
    )
    matrices = (
        lax.all_gather(owned_columns[0].astype(jnp.bfloat16), "seq", axis=1, tiled=True).astype(
            jnp.float32
        ),
        lax.all_gather(owned_columns[1].astype(jnp.bfloat16), "seq", axis=1, tiled=True).astype(
            jnp.float32
        ),
        lax.all_gather(owned_columns[2].astype(jnp.bfloat16), "seq", axis=1, tiled=True).astype(
            jnp.float32
        ),
        lax.all_gather(owned_columns[3].astype(jnp.bfloat16), "seq", axis=1, tiled=True).astype(
            jnp.float32
        ),
    )
    vectors = lax.psum(
        (
            owned[1],
            owned[2],
            owned[4],
            owned[5],
            owned[6],
            owned[8],
            owned[10],
            owned[11],
            owned[12],
        ),
        "seq",
    )
    result_qkv, result_out, result_up, result_down = (
        matrices[0],
        matrices[1],
        matrices[2],
        matrices[3],
    )
    result_q_bias, result_v_bias, result_out_bias = (vectors[0], vectors[1], vectors[2])
    result_gain_one, result_shift_one, result_up_bias = (vectors[3], vectors[4], vectors[5])
    result_down_bias, result_gain_two, result_shift_two = (vectors[6], vectors[7], vectors[8])
    return (
        output,
        grad_tokens,
        result_qkv,
        result_q_bias,
        result_v_bias,
        result_out,
        result_out_bias,
        result_gain_one,
        result_shift_one,
        result_up,
        result_up_bias,
        result_down,
        result_down_bias,
        result_gain_two,
        result_shift_two,
    )


AXES = ("seq", "z", "core")
NORMAL_SCALE = 0.3989422804014327
HALF_ROOT = 0.7071067811865476


def dot_nn(left, right):
    return lax.dot_general(
        left, right, (((1,), (0,)), ((), ())), preferred_element_type=jnp.float32
    )


def dot_nt(left, right):
    return contract_cols(left, right)


def dot_tn(left, right):
    return contract_rows(left, right)


def vmem_specs(count):
    return [pl.BlockSpec(memory_space=pltpu.VMEM)] * count


def work(micros):
    return pl.CostEstimate(
        flops=int(micros * 9e7), transcendentals=0, bytes_accessed=int(micros * 3e5)
    )


def smem_spec():
    return pl.BlockSpec(memory_space=pltpu.SMEM)


def key_bias(sc, block_rows):
    length, place = sc[0], sc[1]
    columns = []
    for j in range(4):
        position = (place ^ j) * block_rows + lax.broadcasted_iota(
            jnp.int32, (block_rows, 1), 0
        )
        columns.append(jnp.where(position < length, 0.0, masked_score))
    return jnp.concatenate(columns, axis=0)


def attend_forward_kernel(
    sc, t0, t1, t2, t3, own, other, qkv, ctx_t, c0, c1, c2, c3, lse, weight, vectors, held
):
    place, core, level = sc[1], sc[2], sc[3]
    rows = t0.shape[0]
    shard_rows = weight.shape[2]
    width = weight.shape[3]
    head_width = width // 3
    heads = head_width // HEAD_DIM
    for k in range(4):
        for block, side in ((own, core), (other, 1 - core)):
            weight[level ^ k, side] = block[k, :shard_rows, :]
            vectors[level ^ k, side] = block[k, shard_rows + 1 : shard_rows + 3, :].astype(
                jnp.float32
            )
    full = weight[...].reshape(-1, width)
    bias = (
        own[level ^ place, shard_rows : shard_rows + 1, :].astype(jnp.float32)
        + other[level ^ place, shard_rows : shard_rows + 1, :].astype(jnp.float32)
    )
    for j, block in enumerate((t0, t1, t2, t3)):
        qkv[j * rows : (j + 1) * rows, :] = (dot_nn(block[...], full) + bias).astype(jnp.bfloat16)
    mask = key_bias(sc, rows)
    def one_block(j, carry):
        span = pl.ds(pl.multiple_of(j * rows, 128), rows)
        parts = []
        q_all = qkv[span, 0:head_width] * jnp.bfloat16(HEAD_DIM**-0.5)
        for h in range(heads):
            low = h * HEAD_DIM
            q = q_all[:, low : low + HEAD_DIM]
            k = qkv[:, head_width + low : head_width + low + HEAD_DIM]
            v = qkv[:, 2 * head_width + low : 2 * head_width + low + HEAD_DIM]
            scores = dot_nt(k, q) + mask
            peak = jnp.max(scores, axis=0, keepdims=True)
            shifted = jnp.exp(scores - peak)
            total = jnp.sum(shifted, axis=0, keepdims=True)
            part = dot_tn(v, shifted.astype(jnp.bfloat16)) / total
            parts.append(part)
            lse[h : h + 1, span] = peak + jnp.log(total)
        joined = jnp.concatenate(parts, axis=0)
        ctx_t[:, span] = joined
        held[j] = joined.T.astype(jnp.bfloat16)
        return carry

    lax.fori_loop(0, 4, one_block, 0)
    for j, out in enumerate((c0, c1, c2, c3)):
        out[...] = held[j]


def attend_backward_kernel(sc, qkv, ctx_t, lse, g0, g1, g2, g3, dqkv, dk_acc, dv_acc, held):
    rows = g0.shape[0]
    head_width = g0.shape[1]
    heads = head_width // HEAD_DIM
    mask = key_bias(sc, rows)
    scale = jnp.bfloat16(HEAD_DIM**-0.5)
    for j, g_ref in enumerate((g0, g1, g2, g3)):
        held[j] = g_ref[...]
    dk_acc[...] = jnp.zeros_like(dk_acc)
    dv_acc[...] = jnp.zeros_like(dv_acc)

    def one_block(j, carry):
        span = pl.ds(pl.multiple_of(j * rows, 128), rows)
        g_all = held[j]
        product = g_all.astype(jnp.float32).T * ctx_t[:, span]
        q_all = qkv[span, 0:head_width] * scale
        parts = []
        for h in range(heads):
            low = h * HEAD_DIM
            q = q_all[:, low : low + HEAD_DIM]
            g = g_all[:, low : low + HEAD_DIM]
            k = qkv[:, head_width + low : head_width + low + HEAD_DIM]
            v = qkv[:, 2 * head_width + low : 2 * head_width + low + HEAD_DIM]
            probs = jnp.exp(dot_nt(k, q) + mask - lse[h : h + 1, span])
            row_dot = jnp.sum(product[low : low + HEAD_DIM, :], axis=0, keepdims=True)
            grad_scores = (probs * (dot_nt(v, g) - row_dot)).astype(jnp.bfloat16)
            grad_v = dot_nn(probs.astype(jnp.bfloat16), g)
            grad_k = dot_nn(grad_scores, q)
            dv_acc[h] += grad_v
            dk_acc[h] += grad_k
            parts.append(dot_tn(k, grad_scores) * (HEAD_DIM**-0.5))
        dqkv[span, 0:head_width] = jnp.concatenate(parts, axis=0).T.astype(jnp.bfloat16)
        return carry

    lax.fori_loop(0, 4, one_block, 0)
    dk = jnp.concatenate([dk_acc[h] for h in range(heads)], axis=1)
    dv = jnp.concatenate([dv_acc[h] for h in range(heads)], axis=1)
    dqkv[:, head_width:] = jnp.concatenate([dk, dv], axis=1).astype(jnp.bfloat16)


def grad_qkv_weight_kernel(sc, t0, t1, t2, t3, dqkv, keep, send, sums):
    core = sc[2]
    rows = t0.shape[0]
    total = None
    for j, block in enumerate((t0, t1, t2, t3)):
        part = dot_tn(block[...], dqkv[j * rows : (j + 1) * rows, :])
        total = part if total is None else total + part
    sums[...] = jnp.sum(dqkv[...].astype(jnp.float32), axis=0, keepdims=True)
    shard_rows = keep.shape[1]
    low = total.astype(jnp.bfloat16)
    for z in range(keep.shape[0]):
        even = low[(2 * z) * shard_rows : (2 * z + 1) * shard_rows]
        odd = low[(2 * z + 1) * shard_rows : (2 * z + 2) * shard_rows]
        keep[z] = jnp.where(core == 0, even, odd)
        send[z] = jnp.where(core == 0, odd, even)


def grad_tokens_kernel(sc, dqkv, weight, out):
    place = sc[1]
    rows = out.shape[1]
    full = weight[...].reshape(-1, weight.shape[3])
    for j in range(4):
        part = dot_nt(dqkv[j * rows : (j + 1) * rows, :], full)
        out[place ^ j] = part.astype(out.dtype)


def normalize(values):
    center = values - jnp.mean(values, axis=-1, keepdims=True)
    inverse = lax.rsqrt(jnp.mean(center * center, axis=-1, keepdims=True) + epsilon)
    return center * inverse, inverse


def normalize_back(grad, unit, inverse):
    return inverse * (
        grad
        - jnp.mean(grad, axis=-1, keepdims=True)
        - unit * jnp.mean(grad * unit, axis=-1, keepdims=True)
    )


def middle_kernel(
    sc,
    x0,
    x1,
    x2,
    x3,
    token,
    cotangent,
    small,
    up_bias,
    gathered,
    output,
    grad_one,
    y0,
    y1,
    y2,
    y3,
    keep,
    send,
    sums,
    up_sums,
    w_out,
    w_up,
    w_down,
    slope,
    active,
    grad_up,
    context,
    sems,
):
    place, core = sc[1], sc[2]
    blocks = w_up.shape[0]
    shard_rows = w_up.shape[3]
    width = w_up.shape[4]
    third = shard_rows // 3
    copies = []
    for b in range(blocks):
        copies.append(
            pltpu.make_async_copy(gathered.at[:, :, b, 0:shard_rows, :], w_up.at[b], sems.at[b])
        )
    copies.append(
        pltpu.make_async_copy(
            gathered.at[:, :, :, shard_rows : 2 * shard_rows, :], w_down, sems.at[blocks]
        )
    )
    out_copies = [
        pltpu.make_async_copy(
            gathered.at[:, :, b, 2 * shard_rows : 2 * shard_rows + third, :],
            w_out.at[:, :, b * third : (b + 1) * third, :],
            sems.at[blocks + 1 + b],
        )
        for b in range(3)
    ]
    for copy in out_copies + copies:
        copy.start()
    for copy in out_copies:
        copy.wait()
    out_rows = 2 * shard_rows

    def out_block(j):
        return w_out[place ^ j].reshape(out_rows, width)

    residual = token[...].astype(jnp.float32) + small[0:1, :]
    for j, block in enumerate((x0, x1, x2, x3)):
        residual = residual + dot_nn(block[...], out_block(j))
    unit_one, inverse_one = normalize(residual)
    gain_one = small[1:2, :]
    normed = unit_one * gain_one + small[2:3, :]
    normed_low = normed.astype(jnp.bfloat16)
    for b in range(blocks):
        copies[b].wait()
        span = slice(b * width, (b + 1) * width)
        up = dot_nn(normed_low, w_up[b].reshape(width, width)) + up_bias[:, span]
        phi = 0.5 + 0.5 * lax.erf(up * HALF_ROOT)
        slope[:, span] = phi + up * (jnp.exp(-0.5 * up * up) * NORMAL_SCALE)
        active[:, span] = (up * phi).astype(jnp.bfloat16)
    copies[blocks].wait()
    residual = normed + small[3:4, :] + dot_nn(active[...], w_down[...].reshape(-1, width))
    unit_two, inverse_two = normalize(residual)
    gain_two = small[4:5, :]
    output[...] = (unit_two * gain_two + small[5:6, :]).astype(jnp.bfloat16)
    grad = cotangent[...].astype(jnp.float32)
    sums[3:4, :] = jnp.sum(grad * unit_two, axis=0, keepdims=True)
    sums[4:5, :] = jnp.sum(grad, axis=0, keepdims=True)
    grad_two = normalize_back(grad * gain_two, unit_two, inverse_two)
    sums[5:6, :] = jnp.sum(grad_two, axis=0, keepdims=True)
    two_low = grad_two.astype(jnp.bfloat16)
    grad_normed = grad_two
    for b in range(blocks):
        span = slice(b * width, (b + 1) * width)
        rows_down = w_down[b].reshape(width, width)
        part = dot_nt(two_low, rows_down) * slope[:, span]
        up_sums[:, span] = jnp.sum(part, axis=0, keepdims=True)
        part = part.astype(jnp.bfloat16)
        grad_up[:, span] = part
        grad_normed = grad_normed + dot_nt(part, w_up[b].reshape(width, width))
    sums[1:2, :] = jnp.sum(grad_normed * unit_one, axis=0, keepdims=True)
    sums[2:3, :] = jnp.sum(grad_normed, axis=0, keepdims=True)
    first = normalize_back(grad_normed * gain_one, unit_one, inverse_one)
    sums[0:1, :] = jnp.sum(first, axis=0, keepdims=True)
    sums[6:8, :] = jnp.zeros((2, width), jnp.float32)
    grad_one[...] = first
    one_low = first.astype(jnp.bfloat16)
    for j, out in enumerate((y0, y1, y2, y3)):
        out[...] = dot_nt(one_low, out_block(j)).astype(jnp.bfloat16)
    for j, block in enumerate((x0, x1, x2, x3)):
        context[place ^ j] = block[...]
    joined = jnp.concatenate([context[j] for j in range(4)], axis=1)
    half = width // 2
    down_rows = blocks * shard_rows
    for ref, mine in ((keep, core), (send, 1 - core)):
        for z in range(4):
            even = active[:, (2 * z) * down_rows : (2 * z + 1) * down_rows]
            odd = active[:, (2 * z + 1) * down_rows : (2 * z + 2) * down_rows]
            ref[:, z * down_rows : (z + 1) * down_rows] = jnp.where(mine == 0, even, odd)
        at = 4 * down_rows
        ref[:, at : at + width] = two_low
        at += width
        ref[:, at : at + width] = normed_low
        at += width
        ref[:, at : at + 2 * width] = jnp.where(
            mine == 0, grad_up[:, : 2 * width], grad_up[:, 2 * width :]
        )
        at += 2 * width
        ref[:, at : at + width] = joined
        at += width
        ref[:, at : at + half] = jnp.where(mine == 0, one_low[:, :half], one_low[:, half:])


def down_grad_kernel(sc, keep, got, near, far, part):
    place = sc[1]
    _, zs, shard_rows, width = near.shape
    down_rows = 4 * shard_rows
    at_two = zs * down_rows
    right = slice(at_two, at_two + width)
    for z in range(zs):
        left = slice(z * down_rows, (z + 1) * down_rows)
        total = dot_tn(keep[:, left], keep[:, right]) + dot_tn(got[:, left], got[:, right])
        part[...] = total.astype(jnp.bfloat16).reshape(4, shard_rows, width)
        for out, at, j in ((near, 0, 0), (near, 1, 2), (far, 0, 1), (far, 1, 3)):
            out[at, z] = part[place ^ j]


def up_grad_kernel(sc, keep, got, near, far, part):
    place = sc[1]
    _, zs, block_rows, cols = near.shape
    quarter = part.shape[2]
    pair_rows = block_rows - quarter
    width = zs * pair_rows
    at_norm = 2 * width + width
    at_up = at_norm + width
    at_ctx = at_up + 2 * width
    at_one = at_ctx + width
    left = slice(at_ctx, at_ctx + width)
    right = slice(at_one, at_one + cols)
    total = dot_tn(keep[:, left], keep[:, right]) + dot_tn(got[:, left], got[:, right])
    part[...] = total.astype(jnp.bfloat16).reshape(part.shape)
    left = slice(at_norm, at_norm + width)
    for out, at, j in ((near, 0, 0), (near, 1, 1), (far, 0, 2), (far, 1, 3)):
        right = pl.ds(pl.multiple_of(at_up + (place ^ j) * cols, 128), cols)
        total = dot_tn(keep[:, left], keep[:, right]) + dot_tn(got[:, left], got[:, right])
        total = total.astype(jnp.bfloat16)
        for z in range(zs):
            out[at, z, :pair_rows] = total[z * pair_rows : (z + 1) * pair_rows]
            out[at, z, pair_rows:] = part[z, place ^ j]


def fold_kernel(near, got, mine, pass_on):
    for at, out in ((0, mine), (1, pass_on)):
        total = near[at].astype(jnp.float32) + got[at].astype(jnp.float32)
        out[...] = total.astype(jnp.bfloat16)


def level_fold_kernel(sc, mine, got, near, far):
    level = sc[3]
    for out, at, k in ((near, 0, 0), (near, 1, 2), (far, 0, 1), (far, 1, 3)):
        total = mine[level ^ k].astype(jnp.float32) + got[level ^ k].astype(jnp.float32)
        out[at] = total.astype(jnp.bfloat16)


def block_sum(refs):
    total = refs[0][...].astype(jnp.float32)
    for ref in refs[1:]:
        total = total + ref[...].astype(jnp.float32)
    return total


def split_up_kernel(sc, e0, e1, keep, send, held):
    core = sc[2]
    shard_rows = (keep.shape[0] * 2) // 3
    held[...] = block_sum((e0, e1)).astype(jnp.bfloat16)
    for ref, side in ((keep, core), (send, 1 - core)):
        ref[:shard_rows] = held[pl.ds(pl.multiple_of(side * shard_rows, 16), shard_rows), :]
        ref[shard_rows:] = held[2 * shard_rows :, :]


def join_kernel(sc, e0, e1, keep, got, out):
    core = sc[2]
    shard_rows = e0.shape[0]
    cols = keep.shape[1]
    out[:shard_rows] = block_sum((e0, e1)).astype(jnp.bfloat16)
    for ref, side in ((keep, core), (got, 1 - core)):
        out[shard_rows:, pl.ds(pl.multiple_of(side * cols, 128), cols)] = ref[...]


def finish_kernel(sc, b0, b1, b2, b3, down, up, out):
    place, core = sc[1], sc[2]
    shard_rows = up.shape[0]
    quarter = shard_rows // 2
    cols = b0.shape[1] // 2
    for j, ref in enumerate((b0, b1, b2, b3)):
        where = place ^ j
        rows = pl.ds(pl.multiple_of(where * shard_rows, 8), shard_rows)
        down[rows, :] = ref[:shard_rows].astype(jnp.float32)
        for side in range(2):
            at = pl.multiple_of((side * 4 + where) * cols, 128)
            up[:, pl.ds(at, cols)] = ref[
                shard_rows : 2 * shard_rows, side * cols : (side + 1) * cols
            ].astype(jnp.float32)

        @pl.when(where // 2 == core)
        def _(ref=ref, where=where):
            at = pl.multiple_of((where % 2) * quarter, 8)
            out[pl.ds(at, quarter), :] = ref[2 * shard_rows :].astype(jnp.float32)


def sum_kernel(e0, e1, out):
    out[...] = block_sum((e0, e1)).astype(out.dtype)


def finish_qkv_kernel(sc, b0, b1, b2, b3, out, held):
    place = sc[1]
    head_width = b0.shape[1] // 3
    for j, ref in enumerate((b0, b1, b2, b3)):
        held[place ^ j] = ref[...].astype(jnp.float32)
    for part in range(3):
        for s in range(4):
            at = (part * 4 + s) * head_width
            out[:, at : at + head_width] = held[s, :, part * head_width : (part + 1) * head_width]


def fast_body(
    tokens,
    lengths,
    w_qkv,
    q_bias,
    v_bias,
    w_out,
    out_bias,
    gain_one,
    shift_one,
    w_up,
    up_bias,
    w_down,
    down_bias,
    gain_two,
    shift_two,
    cotangent,
):
    bf16, f32 = jnp.bfloat16, jnp.float32
    _, rows, width = tokens.shape
    shard_rows = w_qkv.shape[0]
    hidden = w_up.shape[1]
    head_width = width // 4
    place = lax.axis_index("seq")
    core = lax.axis_index("core")
    zs = 4
    third = shard_rows // 3
    swap = [(0, 1), (1, 0)]

    def struct(shape, dtype=bf16):
        return jax.ShapeDtypeStruct(shape, dtype)

    def across(value, step):
        return lax.ppermute(value, "seq", [(i, i ^ step) for i in range(4)])

    def partner(value):
        return lax.ppermute(value, "core", swap)

    def level_across(value, step):
        return lax.ppermute(value, "z", [(i, i ^ step) for i in range(4)])

    token = tokens[0]
    quarter = jnp.concatenate(
        [
            lax.dynamic_slice_in_dim(w_up, place * width, width, axis=1),
            lax.dynamic_slice_in_dim(w_down, place * shard_rows, shard_rows, axis=0),
            lax.dynamic_slice_in_dim(w_out, jnp.minimum(place, 2) * third, third, axis=0),
        ],
        axis=0,
    )
    gathered = lax.all_gather(quarter, ("z", "core", "seq"), axis=0, tiled=True)
    gathered = gathered.reshape(zs, 2, 4, 2 * shard_rows + third, width)
    columns = lax.dynamic_index_in_dim(
        w_qkv.reshape(shard_rows, 3, 4, head_width), place, axis=2, keepdims=False
    ).reshape(shard_rows, 3 * head_width)
    pair_rows = jnp.zeros((2, 2, shard_rows), bf16)
    placed_q = lax.dynamic_update_slice(pair_rows[0], q_bias[None], (core, 0)).reshape(1, -1)
    placed_v = lax.dynamic_update_slice(pair_rows[0], v_bias[None], (core, 0)).reshape(1, -1)
    bias_row = jnp.concatenate(
        [placed_q, jnp.zeros((1, head_width), bf16), placed_v], axis=1
    )
    vectors = jnp.concatenate(
        [out_bias, gain_one, shift_one, down_bias, gain_two, shift_two, up_bias]
    )
    pad = 15 * 3 * head_width - vectors.shape[0]
    vector_rows = jnp.pad(vectors, (0, pad)).reshape(15, 3 * head_width)
    own_block = jnp.concatenate([columns, bias_row, vector_rows], axis=0)
    t1, t2, t3 = across(token, 1), across(token, 2), across(token, 3)
    own_cols = jnp.stack([own_block] + [level_across(own_block, k) for k in (1, 2, 3)])
    other_cols = partner(own_cols)
    sc = jnp.stack([lengths[0], place, core, lax.axis_index("z")]).astype(jnp.int32)
    all_rows = 4 * rows
    qkv, ctx_t, c0, c1, c2, c3, lse, full_qkv, vector_sets = pl.pallas_call(
        attend_forward_kernel,
        name="attend_forward",
        cost_estimate=work(13),
        out_shape=(
            struct((all_rows, 3 * head_width)),
            struct((head_width, all_rows), f32),
            struct((rows, head_width)),
            struct((rows, head_width)),
            struct((rows, head_width)),
            struct((rows, head_width)),
            struct((head_width // HEAD_DIM, all_rows), f32),
            struct((zs, 2, shard_rows, 3 * head_width)),
            struct((zs, 2, 2, 3 * head_width), f32),
        ),
        in_specs=[smem_spec()] + vmem_specs(6),
        out_specs=tuple(vmem_specs(9)),
        scratch_shapes=[pltpu.VMEM((4, rows, head_width), bf16)],
    )(sc, token, t1, t2, t3, own_cols, other_cols)
    x1, x2, x3 = across(c1, 1), across(c2, 2), across(c3, 3)
    all_vec = vector_sets.reshape(2 * zs, -1)
    six = all_vec[:, : 6 * shard_rows].reshape(2 * zs, 6, shard_rows)
    six = six.transpose(1, 0, 2).reshape(6, width)
    small = jnp.concatenate([six, jnp.zeros((2, width), f32)], axis=0)
    full_up_bias = all_vec[:, 6 * shard_rows : 6 * shard_rows + hidden // 8].reshape(1, hidden)
    packed = hidden // 2 + 5 * width + width // 2
    output, grad_one, y0, y1, y2, y3, keep, send, sums, up_sums = pl.pallas_call(
        middle_kernel,
        name="middle",
        cost_estimate=work(15),
        out_shape=(
            struct((rows, width)),
            struct((rows, width), f32),
            struct((rows, head_width)),
            struct((rows, head_width)),
            struct((rows, head_width)),
            struct((rows, head_width)),
            struct((rows, packed)),
            struct((rows, packed)),
            struct((8, width), f32),
            struct((1, hidden), f32),
        ),
        in_specs=[smem_spec()]
        + vmem_specs(8)
        + [pl.BlockSpec(memory_space=pl.ANY)],
        out_specs=tuple(vmem_specs(10)),
        scratch_shapes=[
            pltpu.VMEM((zs, 2, shard_rows, width), bf16),
            pltpu.VMEM((4, zs, 2, shard_rows, width), bf16),
            pltpu.VMEM((zs, 2, 4, shard_rows, width), bf16),
            pltpu.VMEM((rows, hidden), f32),
            pltpu.VMEM((rows, hidden), bf16),
            pltpu.VMEM((rows, hidden), bf16),
            pltpu.VMEM((4, rows, head_width), bf16),
            pltpu.SemaphoreType.DMA((8,)),
        ],
    )(
        sc,
        c0,
        x1,
        x2,
        x3,
        token,
        cotangent[0],
        small,
        full_up_bias,
        gathered,
    )
    g1, g2, g3 = across(y1, 1), across(y2, 2), across(y3, 3)
    got, g1, g2, g3 = lax.optimization_barrier((partner(send), g1, g2, g3))
    quad = hidden // 8

    def call(kernel, micros, outs, *args, scratch=(), scalars=True):
        return pl.pallas_call(
            kernel,
            name=kernel.__name__.replace("_kernel", ""),
            cost_estimate=work(micros),
            out_shape=tuple(outs),
            in_specs=([smem_spec()] if scalars else []) + vmem_specs(len(args)),
            out_specs=tuple(vmem_specs(len(outs))),
            scratch_shapes=list(scratch),
        )(*(((sc,) if scalars else ()) + args))

    d_near, d_far = call(
        down_grad_kernel,
        4,
        [struct((2, zs, shard_rows, width))] * 2,
        keep,
        got,
        scratch=[pltpu.VMEM((4, shard_rows, width), bf16)],
    )
    block_rows = 2 * shard_rows + shard_rows // 2
    u_near, u_far = call(
        up_grad_kernel,
        4,
        [struct((2, zs, block_rows, quad))] * 2,
        keep,
        got,
        scratch=[pltpu.VMEM((zs, 4, shard_rows // 2, quad), bf16)],
    )
    d_got = across(d_far, 1)
    u_got = across(u_far, 2)
    y0, d_near, u_near = lax.optimization_barrier((y0, d_near, u_near))

    dqkv = pl.pallas_call(
        attend_backward_kernel,
        name="attend_backward",
        cost_estimate=work(11),
        out_shape=struct((all_rows, 3 * head_width)),
        in_specs=[smem_spec()] + vmem_specs(7),
        out_specs=pl.BlockSpec(memory_space=pltpu.VMEM),
        scratch_shapes=[
            pltpu.VMEM((head_width // HEAD_DIM, all_rows, HEAD_DIM), f32),
            pltpu.VMEM((head_width // HEAD_DIM, all_rows, HEAD_DIM), f32),
            pltpu.VMEM((4, rows, head_width), bf16),
        ],
    )(sc, qkv, ctx_t, lse, y0, g1, g2, g3)
    q_keep, q_send, q_sums = pl.pallas_call(
        grad_qkv_weight_kernel,
        name="grad_qkv_weight",
        cost_estimate=work(4),
        out_shape=(
            struct((zs, shard_rows, 3 * head_width)),
            struct((zs, shard_rows, 3 * head_width)),
            struct((1, 3 * head_width), f32),
        ),
        in_specs=[smem_spec()] + vmem_specs(5),
        out_specs=tuple(vmem_specs(3)),
    )(sc, token, t1, t2, t3, dqkv)
    d_mine, d_pass = call(
        fold_kernel, 1, [struct((zs, shard_rows, width))] * 2, d_near, d_got, scalars=False
    )
    u_mine, u_pass = call(
        fold_kernel, 1, [struct((zs, block_rows, quad))] * 2, u_near, u_got, scalars=False
    )
    q_send, d_mine, u_mine = lax.optimization_barrier((q_send, d_mine, u_mine))
    q_got = partner(q_send)
    late_dqkv, q_keep = lax.optimization_barrier((dqkv, q_keep))
    (token_parts,) = call(
        grad_tokens_kernel,
        4,
        [struct((4, rows, width))],
        late_dqkv,
        full_qkv,
    )
    token_sum = lax.psum_scatter(
        token_parts.reshape(4 * rows, width), "seq", scatter_dimension=0, tiled=True
    )
    q_near, q_far = call(
        level_fold_kernel, 1, [struct((2, shard_rows, 3 * head_width))] * 2, q_keep, q_got
    )

    def level_sum(near, far, shape):
        mine, pass_on = call(
            fold_kernel, 1, [struct(shape)] * 2, near, level_across(far, 1), scalars=False
        )
        return mine, level_across(pass_on, 2)

    q_mine, q_last = level_sum(q_near, q_far, (shard_rows, 3 * head_width))
    (q_part,) = call(
        sum_kernel, 1, [struct((shard_rows, 3 * head_width))], q_mine, q_last, scalars=False
    )

    def seq_sum(mine, pass_on, shape, step):
        near, far = call(
            level_fold_kernel,
            1,
            [struct((2,) + shape[1:])] * 2,
            mine,
            across(pass_on, step),
        )
        return level_sum(near, far, shape[1:])

    d_parts = seq_sum(d_mine, d_pass, (zs, shard_rows, width), 2)
    u_parts = seq_sum(u_mine, u_pass, (zs, block_rows, quad), 1)
    half_rows = shard_rows + shard_rows // 2
    u_keep, u_send = call(
        split_up_kernel,
        1,
        [struct((half_rows, quad))] * 2,
        *u_parts,
        scratch=[pltpu.VMEM((block_rows, quad), bf16)],
    )
    (joined,) = call(
        join_kernel,
        1,
        [struct((shard_rows + half_rows, width))],
        *d_parts,
        u_keep,
        partner(u_send),
    )
    result_down, result_up, result_out = call(
        finish_kernel,
        2,
        [
            struct((4 * shard_rows, width), f32),
            struct((shard_rows, hidden), f32),
            struct((shard_rows, width), f32),
        ],
        joined,
        *[across(joined, j) for j in (1, 2, 3)],
    )
    (result_qkv,) = call(
        finish_qkv_kernel,
        1,
        [struct((shard_rows, 3 * width), f32)],
        q_part,
        *[across(q_part, j) for j in (1, 2, 3)],
        scratch=[pltpu.VMEM((4, shard_rows, 3 * head_width), f32)],
    )
    grad_tokens = (grad_one + token_sum.astype(f32)).astype(bf16)

    q_row = lax.dynamic_update_slice(
        jnp.zeros((1, width), f32), q_sums[:, :head_width], (0, place * head_width)
    )
    v_row = lax.dynamic_update_slice(
        jnp.zeros((1, width), f32), q_sums[:, 2 * head_width :], (0, place * head_width)
    )

    def everywhere(value):
        value = value + partner(value)
        value = value + across(value, 1)
        value = value + across(value, 2)
        value = value + level_across(value, 1)
        value = value + level_across(value, 2)
        return value

    vector_sums = jnp.concatenate([sums[:6], up_sums.reshape(4, width), q_row, v_row], axis=0)
    vector_sums, _ = lax.optimization_barrier((vector_sums, q_mine))
    early = everywhere(vector_sums)
    shard = 2 * lax.axis_index("z") + core

    def owned(vector):
        size = vector.shape[0] // (2 * zs)
        return lax.dynamic_slice(vector, (shard * size,), (size,))

    return (
        output[None],
        grad_tokens[None],
        result_qkv,
        owned(early[10]),
        owned(early[11]),
        result_out,
        owned(early[0]),
        owned(early[1]),
        owned(early[2]),
        result_up,
        owned(early[6:10].reshape(-1)),
        result_down,
        owned(early[5]),
        owned(early[3]),
        owned(early[4]),
    )


def solution(mesh):
    seq_count, shard_count = mesh.shape["seq"], mesh.shape["shard"]
    fast = seq_count == 4 and shard_count == 8
    if fast:
        grid = mesh.devices.reshape(seq_count, shard_count // 2, 2)
        mesh = jax.sharding.Mesh(grid, AXES)
    shard = ("z", "core") if fast else "shard"
    vector, matrix, rows = P(shard), P(shard, None), P(shard, "seq", None)
    return jax.shard_map(
        fast_body if fast else body,
        mesh=mesh,
        in_specs=(
            rows,
            vector,
            matrix,
            vector,
            vector,
            matrix,
            vector,
            vector,
            vector,
            matrix,
            vector,
            matrix,
            vector,
            vector,
            vector,
            rows,
        ),
        out_specs=(
            rows,
            rows,
            matrix,
            vector,
            vector,
            matrix,
            vector,
            vector,
            vector,
            matrix,
            vector,
            matrix,
            vector,
            vector,
            vector,
        ),
        check_vma=False,
    )
```

profile of v0, /device:TPU:0, one launch (start us, length us, event | category | flops | bytes accessed | tf_op | source)
XLA Modules:
  0.0 310.2 jit_solution(225941726675758490)
XLA Ops:
  11.9 5.1 %collective-permute-start.5 = (bf16[112,576]{1,0:T(8,128)(2,1)S(1)}, bf16[112,576]{1,0:T(8,128)(2,1)S(1)}, u32[]{:S(2)}, u32[]{:S(2)}) collective-permute-start(bf16[112,576]{1,0:T(8,128)(2,1)S(1)} %pad_maximum_fusion.2), channel_id=1, source_target_pairs={{0,6},{2,4},{4,2},{6,0},{1,7},{3,5},{5,3},{7,1},{8,14},{10,12},{12... | collective-permute-start | bytes 387080 | tf_op jit(solution)/shard_map/ppermute | solution.py:778
  17.7 3.9 %collective-permute-done.5 = bf16[112,576]{1,0:T(8,128)(2,1)S(1)} collective-permute-done((bf16[112,576]{1,0:T(8,128)(2,1)S(1)}, bf16[112,576]{1,0:T(8,128)(2,1)S(1)}, u32[]{:S(2)}, u32[]{:S(2)}) %collective-permute-start.5) | collective-permute-done | bytes 129056 | tf_op jit(solution)/shard_map/ppermute | solution.py:778
  21.6 3.3 %collective-permute-done.3 = bf16[112,576]{1,0:T(8,128)(2,1)S(1)} collective-permute-done((bf16[112,576]{1,0:T(8,128)(2,1)S(1)}, bf16[112,576]{1,0:T(8,128)(2,1)S(1)}, u32[]{:S(2)}, u32[]{:S(2)}) %collective-permute-start.3) | collective-permute-done | bytes 129056 | tf_op jit(solution)/shard_map/ppermute | solution.py:778
  24.9 9.0 %collective-permute-done.4 = bf16[112,576]{1,0:T(8,128)(2,1)S(1)} collective-permute-done((bf16[112,576]{1,0:T(8,128)(2,1)S(1)}, bf16[112,576]{1,0:T(8,128)(2,1)S(1)}, u32[]{:S(2)}, u32[]{:S(2)}) %collective-permute-start.4) | collective-permute-done | bytes 129056 | tf_op jit(solution)/shard_map/ppermute | solution.py:778
  34.1 1.4 collective-permute-start
  35.5 1.5 collective-permute-start.1
  39.0 7.1 %collective-permute-done.t1 = bf16[256,768]{1,0:T(8,128)(2,1)S(1)} collective-permute-done((bf16[256,768]{1,0:T(8,128)(2,1)S(1)}, bf16[256,768]{1,0:T(8,128)(2,1)S(1)}, u32[]{:S(2)}, u32[]{:S(2)}) %collective-permute-start) | collective-permute-done | bytes 393248 | tf_op jit(solution)/shard_map/ppermute | solution.py:772
  46.1 5.1 %collective-permute-done.1.t2 = bf16[256,768]{1,0:T(8,128)(2,1)S(1)} collective-permute-done((bf16[256,768]{1,0:T(8,128)(2,1)S(1)}, bf16[256,768]{1,0:T(8,128)(2,1)S(1)}, u32[]{:S(2)}, u32[]{:S(2)}) %collective-permute-start.1) | collective-permute-done | bytes 393248 | tf_op jit(solution)/shard_map/ppermute | solution.py:772
  51.2 11.5 %collective-permute-done.2.t3 = bf16[256,768]{1,0:T(8,128)(2,1)S(1)} collective-permute-done((bf16[256,768]{1,0:T(8,128)(2,1)S(1)}, bf16[256,768]{1,0:T(8,128)(2,1)S(1)}, u32[]{:S(2)}, u32[]{:S(2)}) %collective-permute-start.2) | collective-permute-done | bytes 393248 | tf_op jit(solution)/shard_map/ppermute | solution.py:772
  64.3 13.0 %attend_forward.1 = (bf16[1024,576]{1,0:T(8,128)(2,1)}, f32[192,1024]{1,0:T(8,128)}, bf16[256,192]{1,0:T(8,128)(2,1)}, bf16[256,192]{1,0:T(8,128)(2,1)}, bf16[25...) custom-call(s32[4]{0:T(128)} %pad_add_fusion.sc, ...), custom_call_target="tpu_custom_call" | custom-call | flops 1170000000 | bytes 3900000 | tf_op jit(solution)/shard_map/attend_forward/pallas_call | solution.py:811
  78.2 2.3 collective-permute-start.7
  83.6 4.3 %collective-permute-done.7.x1 = bf16[256,192]{1,0:T(8,128)(2,1)S(1)} collective-permute-done((bf16[256,192]{1,0:T(8,128)(2,1)}, bf16[256,192]{1,0:T(8,128)(2,1)S(1)}, u32[]{:S(2)}, u32[]{:S(2)}) %collective-permute-start.7) | collective-permute-done | bytes 98336 | tf_op jit(solution)/shard_map/ppermute | solution.py:772
  87.9 3.5 %collective-permute-done.8.x2 = bf16[256,192]{1,0:T(8,128)(2,1)S(1)} collective-permute-done((bf16[256,192]{1,0:T(8,128)(2,1)}, bf16[256,192]{1,0:T(8,128)(2,1)S(1)}, u32[]{:S(2)}, u32[]{:S(2)}) %collective-permute-start.8) | collective-permute-done | bytes 98336 | tf_op jit(solution)/shard_map/ppermute | solution.py:772
  91.4 1.5 collective-permute-done.9.x3
  92.9 24.4 %all-gather.2.cloned.1.call-done = bf16[7168,768]{1,0:T(8,128)(2,1)} async-done(((bf16[224,768]{1,0:T(8,128)(2,1)}), bf16[7168,768]{1,0:T(8,128)(2,1)}) %all-gather.2.cloned.1.call-update) | async-done | bytes 11010064 | tf_op jit(solution)/shard_map/all_gather | solution.py:789
  117.3 15.3 %middle.1 = (bf16[256,768]{1,0:T(8,128)(2,1)}, f32[256,768]{1,0:T(8,128)}, bf16[256,192]{1,0:T(8,128)(2,1)}, bf16[256,192]{1,0:T(8,128)(2,1)}, bf16[256,192]{1,0...) custom-call(s32[4]{0:T(128)} %pad_add_fusion.sc, ...), custom_call_target="tpu_custom_call" | custom-call | flops 1350000000 | bytes 4500000 | tf_op jit(solution)/shard_map/middle/pallas_call | solution.py:837
  133.0 1.4 collective-permute-start.12
  134.5 1.9 collective-permute-start.13
  136.4 3.1 collective-permute-done.11.g1
  139.5 2.4 collective-permute-done.13.g3
  141.8 1.6 copy-done.1
  143.4 6.1 %up_grad.1 = (bf16[2,4,240,384]{3,2,1,0:T(8,128)(2,1)}, bf16[2,4,240,384]{3,2,1,0:T(8,128)(2,1)}) custom-call(s32[4]{0:T(128)} %pad_add_fusion.sc, bf16[256,5760]{1,0:T(8,128)(2,1)} %get-tuple-element.86.keep, bf16[256,5760]{1,0:T(8,128)(2,1)} %copy-done.1), custom_call_target="tpu_custom_call" | custom-call | flops 360000000 | bytes 1200000 | tf_op jit(solution)/shard_map/up_grad/pallas_call | solution.py:884
  149.5 1.2 collective-permute-start.15
  150.7 5.8 %down_grad.1 = (bf16[2,4,96,768]{3,2,1,0:T(8,128)(2,1)}, bf16[2,4,96,768]{3,2,1,0:T(8,128)(2,1)}) custom-call(s32[4]{0:T(128)} %pad_add_fusion.sc, bf16[256,5760]{1,0:T(8,128)(2,1)} %get-tuple-element.86.keep, bf16[256,5760]{1,0:T(8,128)(2,1)} %copy-done.1), custom_call_target="tpu_custom_call" | custom-call | flops 360000000 | bytes 1200000 | tf_op jit(solution)/shard_map/down_grad/pallas_call | solution.py:884
  156.6 1.2 collective-permute-start.14
  157.8 12.5 %attend_backward.1.dqkv = bf16[1024,576]{1,0:T(8,128)(2,1)} custom-call(s32[4]{0:T(128)} %pad_add_fusion.sc, bf16[1024,576]{1,0:T(8,128)(2,1)} %get-tuple-element.82.qkv, f32[192,1024]{1,0:T(8,128)} %get-tuple-element.83.ctx_t, f32[3,1024]{1,0:T(4,128)} %get-tuple-element.84.lse, bf16[256,192]{1,0:T(8,128)(2,1)} %get-tuple-element.94.g0, ...), custom_call_target="tpu_custom_call" | custom-call | flops 990000000 | bytes 3300000 | tf_op jit(solution)/shard_map/attend_backward/pallas_call | solution.py:915
  170.3 4.2 %grad_qkv_weight.1 = (bf16[4,96,576]{2,1,0:T(8,128)(2,1)}, bf16[4,96,576]{2,1,0:T(8,128)(2,1)}, f32[1,576]{1,0:T(1,128)}) custom-call(s32[4]{0:T(128)} %pad_add_fusion.sc, bf16[256,768]{1,0:T(8,128)(2,1)} %bitcast.44, bf16[256,768]{1,0:T(8,128)(2,1)} %copy-done.11, bf16[256,768]{1,0:T(8,128)(2,1)} %copy-done.12, bf16[256,768]{1,0:T(8,128)(2,1)} %copy-done.13, ...), custom_call_target="tpu_custom_call" | custom-call | flops 360000000 | bytes 1200000 | tf_op jit(solution)/shard_map/grad_qkv_weight/pallas_call | solution.py:928
  174.6 4.2 %grad_tokens.1 = bf16[4,256,768]{2,1,0:T(8,128)(2,1)} custom-call(s32[4]{0:T(128)} %pad_add_fusion.sc, bf16[1024,576]{1,0:T(8,128)(2,1)} %attend_backward.1.dqkv, bf16[4,2,96,576]{3,2,1,0:T(8,128)(2,1)} %get-tuple-element.100.weight), custom_call_target="tpu_custom_call" | custom-call | flops 360000000 | bytes 1200000 | tf_op jit(solution)/shard_map/grad_tokens/pallas_call | solution.py:884
  178.8 5.1 %collective-permute-done.14.got = bf16[2,4,96,768]{3,2,1,0:T(8,128)(2,1)S(1)} collective-permute-done((bf16[2,4,96,768]{3,2,1,0:T(8,128)(2,1)}, bf16[2,4,96,768]{3,2,1,0:T(8,128)(2,1)S(1)}, u32[]{:S(2)}, u32[]{:S(2)}) %collective-permute-start.14) | collective-permute-done | bytes 1179680 | tf_op jit(solution)/shard_map/ppermute | solution.py:772
  183.9 1.0 copy-done.4
  184.9 2.8 fold.5
  188.5 1.1 copy-done.3
  189.7 3.1 fold.6
  194.9 14.9 %collective-permute-done.27.got = bf16[4,96,768]{2,1,0:T(8,128)(2,1)S(1)} collective-permute-done((bf16[4,96,768]{2,1,0:T(8,128)(2,1)}, bf16[4,96,768]{2,1,0:T(8,128)(2,1)S(1)}, u32[]{:S(2)}, u32[]{:S(2)}) %collective-permute-start.27) | collective-permute-done | bytes 589856 | tf_op jit(solution)/shard_map/ppermute | solution.py:772
  210.6 2.3 level_fold.4
  212.9 1.4 collective-permute-start.28
  215.1 2.1 level_fold.3
  218.2 8.0 %collective-permute-done.17.got = bf16[2,96,576]{2,1,0:T(8,128)(2,1)S(1)} collective-permute-done((bf16[2,96,576]{2,1,0:T(8,128)(2,1)}, bf16[2,96,576]{2,1,0:T(8,128)(2,1)S(1)}, u32[]{:S(2)}, u32[]{:S(2)}) %collective-permute-start.17) | collective-permute-done | bytes 221216 | tf_op jit(solution)/shard_map/ppermute | solution.py:778
  226.9 1.8 fold.7
  228.7 1.2 collective-permute-done.22
  230.0 1.4 collective-permute-start.23
  231.4 2.6 collective-permute-start.18
  234.6 3.6 %collective-permute-done.24 = f32[12,768]{1,0:T(8,128)S(1)} collective-permute-done((f32[12,768]{1,0:T(8,128)S(1)}, f32[12,768]{1,0:T(8,128)S(1)}, u32[]{:S(2)}, u32[]{:S(2)}) %collective-permute-start.24) | collective-permute-done | bytes 36896 | tf_op jit(solution)/shard_map/ppermute | solution.py:772
  238.3 1.5 collective-permute-start.25
  239.8 2.7 collective-permute-done.25
  242.5 2.9 collective-permute-start.26
  246.0 1.8 fold.8
  248.8 2.3 level_fold.5
  251.1 1.4 collective-permute-start.31
  253.2 1.6 sum.1.b0
  254.9 1.7 collective-permute-start.19
  257.0 1.4 collective-permute-start.21
  261.7 1.9 fold.9
  263.6 1.1 collective-permute-start.32
  266.6 6.0 %collective-permute-done.32.e1 = bf16[240,384]{1,0:T(8,128)(2,1)S(1)} collective-permute-done((bf16[240,384]{1,0:T(8,128)(2,1)}, bf16[240,384]{1,0:T(8,128)(2,1)S(1)}, u32[]{:S(2)}, u32[]{:S(2)}) %collective-permute-start.32) | collective-permute-done | bytes 184352 | tf_op jit(solution)/shard_map/ppermute | solution.py:778
  273.2 1.8 split_up.1
  277.2 1.9 join.1.b0
  279.1 1.2 collective-permute-start.34
  280.8 1.8 collective-permute-start.36
  284.5 2.3 finish_qkv.1
  286.8 1.8 fusion
  288.6 2.2 collective-permute-done.34.b1
  290.8 8.1 %collective-permute-done.35.b2 = bf16[240,768]{1,0:T(8,128)(2,1)S(1)} collective-permute-done((bf16[240,768]{1,0:T(8,128)(2,1)}, bf16[240,768]{1,0:T(8,128)(2,1)S(1)}, u32[]{:S(2)}, u32[]{:S(2)}) %collective-permute-start.35) | collective-permute-done | bytes 368672 | tf_op jit(solution)/shard_map/ppermute | solution.py:772
  300.3 3.0 finish.1
  (186 shorter events, 34.1 us)
Async XLA Ops:
  7.2 2.8 copy-start.10
  7.2 110.1 %all-gather.2.cloned.1.call-start = ((), (), s32[]{:S(2)}) async-start(), calls=%async_computation.1 | async-start | bytes 11354112 | tf_op jit(solution)/shard_map/all_gather | solution.py:789
  9.9 1.7 copy-start.36
  9.9 1.7 copy-start.37
  9.9 1.7 copy-start.38
  9.9 1.7 copy-start.39
  9.9 1.7 copy-start.40
  9.9 1.7 copy-start.41
  9.9 1.7 copy-start.42
  10.0 276.8 %reduce-scatter.2.cloned.1.call-start = ((), (), s32[]{:S(2)}) async-start(), calls=%async_computation.2 | async-start | bytes 1966080 | tf_op jit(solution)/shard_map/reduce_scatter | solution.py:956
  10.6 23.5 %copy-start.2 = (bf16[1,256,768]{2,1,0:T(8,128)(2,1)S(1)}, bf16[1,256,768]{2,1,0:T(8,128)(2,1)}, u32[]{:S(2)}) copy-start(bf16[1,256,768]{2,1,0:T(8,128)(2,1)} %param.16) | copy-start | bytes 1179652
  11.9 9.7 %collective-permute-start.5 = (bf16[112,576]{1,0:T(8,128)(2,1)S(1)}, bf16[112,576]{1,0:T(8,128)(2,1)S(1)}, u32[]{:S(2)}, u32[]{:S(2)}) collective-permute-start(bf16[112,576]{1,0:T(8,128)(2,1)S(1)} %pad_maximum_fusion.2), channel_id=1, source_target_pairs={{0,6},{2,4},{4,2},{6,0},{1,7},{3,5},{5,3},{7,1},{8,14},{10,12},{12... | collective-permute-start | bytes 387080 | tf_op jit(solution)/shard_map/ppermute | solution.py:778
  17.0 7.9 %collective-permute-start.3 = (bf16[112,576]{1,0:T(8,128)(2,1)S(1)}, bf16[112,576]{1,0:T(8,128)(2,1)S(1)}, u32[]{:S(2)}, u32[]{:S(2)}) collective-permute-start(bf16[112,576]{1,0:T(8,128)(2,1)S(1)} %pad_maximum_fusion.2), channel_id=1, source_target_pairs={{0,2},{2,0},{4,6},{6,4},{1,3},{3,1},{5,7},{7,5},{8,10},{10,8},{12,... | collective-permute-start | bytes 387080 | tf_op jit(solution)/shard_map/ppermute | solution.py:778
  17.0 16.9 %collective-permute-start.4 = (bf16[112,576]{1,0:T(8,128)(2,1)S(1)}, bf16[112,576]{1,0:T(8,128)(2,1)S(1)}, u32[]{:S(2)}, u32[]{:S(2)}) collective-permute-start(bf16[112,576]{1,0:T(8,128)(2,1)S(1)} %pad_maximum_fusion.2), channel_id=1, source_target_pairs={{0,4},{2,6},{4,0},{6,2},{1,5},{3,7},{5,1},{7,3},{8,12},{10,14},{12... | collective-permute-start | bytes 387080 | tf_op jit(solution)/shard_map/ppermute | solution.py:778
  34.0 28.7 %copy-start.8 = (bf16[4,112,576]{2,1,0:T(8,128)(2,1)}, bf16[4,112,576]{2,1,0:T(8,128)(2,1)S(1)}, u32[]{:S(2)}) copy-start(bf16[4,112,576]{2,1,0:T(8,128)(2,1)S(1)} %pad_maximum_fusion.own) | copy-start | bytes 1548292
  34.0 28.7 %collective-permute-start.6 = (bf16[4,112,576]{2,1,0:T(8,128)(2,1)S(1)}, bf16[4,112,576]{2,1,0:T(8,128)(2,1)S(1)}, u32[]{:S(2)}, u32[]{:S(2)}) collective-permute-start(bf16[4,112,576]{2,1,0:T(8,128)(2,1)S(1)} %pad_maximum_fusion.own), channel_id=1, source_target_pairs={{0,1},{1,0},{2,3},{3,2},{4,5},{5,4},{6,7},{7,6},{8,9},{9,8},{10,11... | collective-permute-start | bytes 1548296 | tf_op jit(solution)/shard_map/ppermute | solution.py:775
  34.1 12.0 %collective-permute-start = (bf16[256,768]{1,0:T(8,128)(2,1)S(1)}, bf16[256,768]{1,0:T(8,128)(2,1)S(1)}, u32[]{:S(2)}, u32[]{:S(2)}) collective-permute-start(bf16[256,768]{1,0:T(8,128)(2,1)S(1)} %bitcast.45), channel_id=1, source_target_pairs={{0,8},{8,0},{16,24},{24,16},{1,9},{9,1},{17,25},{25,17},{2,10},{10... | collective-permute-start | bytes 1179656 | tf_op jit(solution)/shard_map/ppermute | solution.py:772
  35.5 15.7 %collective-permute-start.1 = (bf16[256,768]{1,0:T(8,128)(2,1)S(1)}, bf16[256,768]{1,0:T(8,128)(2,1)S(1)}, u32[]{:S(2)}, u32[]{:S(2)}) collective-permute-start(bf16[256,768]{1,0:T(8,128)(2,1)S(1)} %bitcast.46), channel_id=1, source_target_pairs={{0,16},{8,24},{16,0},{24,8},{1,17},{9,25},{17,1},{25,9},{2,18},{10... | collective-permute-start | bytes 1179656 | tf_op jit(solution)/shard_map/ppermute | solution.py:772
  37.0 25.7 %collective-permute-start.2 = (bf16[256,768]{1,0:T(8,128)(2,1)S(1)}, bf16[256,768]{1,0:T(8,128)(2,1)S(1)}, u32[]{:S(2)}, u32[]{:S(2)}) collective-permute-start(bf16[256,768]{1,0:T(8,128)(2,1)S(1)} %bitcast.47), channel_id=1, source_target_pairs={{0,24},{8,16},{16,8},{24,0},{1,25},{9,17},{17,9},{25,1},{2,26},{10... | collective-permute-start | bytes 1179656 | tf_op jit(solution)/shard_map/ppermute | solution.py:772
  46.1 16.6 %copy-start.11 = (bf16[256,768]{1,0:T(8,128)(2,1)}, bf16[256,768]{1,0:T(8,128)(2,1)S(1)}, u32[]{:S(2)}) copy-start(bf16[256,768]{1,0:T(8,128)(2,1)S(1)} %collective-permute-done.t1) | copy-start | bytes 1179652
  51.2 11.5 %copy-start.12 = (bf16[256,768]{1,0:T(8,128)(2,1)}, bf16[256,768]{1,0:T(8,128)(2,1)S(1)}, u32[]{:S(2)}) copy-start(bf16[256,768]{1,0:T(8,128)(2,1)S(1)} %collective-permute-done.1.t2) | copy-start | bytes 1179652
  78.2 9.7 %collective-permute-start.7 = (bf16[256,192]{1,0:T(8,128)(2,1)}, bf16[256,192]{1,0:T(8,128)(2,1)S(1)}, u32[]{:S(2)}, u32[]{:S(2)}) collective-permute-start(bf16[256,192]{1,0:T(8,128)(2,1)} %get-tuple-element.76), channel_id=1, source_target_pairs={{0,8},{8,0},{16,24},{24,16},{1,9},{9,1},{17,25},{25,17},{2,10},{10... | collective-permute-start | bytes 294920 | tf_op jit(solution)/shard_map/ppermute | solution.py:772
  80.5 10.8 %collective-permute-start.8 = (bf16[256,192]{1,0:T(8,128)(2,1)}, bf16[256,192]{1,0:T(8,128)(2,1)S(1)}, u32[]{:S(2)}, u32[]{:S(2)}) collective-permute-start(bf16[256,192]{1,0:T(8,128)(2,1)} %get-tuple-element.77), channel_id=1, source_target_pairs={{0,16},{8,24},{16,0},{24,8},{1,17},{9,25},{17,1},{25,9},{2,18},{10... | collective-permute-start | bytes 294920 | tf_op jit(solution)/shard_map/ppermute | solution.py:772
  81.3 11.6 %collective-permute-start.9 = (bf16[256,192]{1,0:T(8,128)(2,1)}, bf16[256,192]{1,0:T(8,128)(2,1)S(1)}, u32[]{:S(2)}, u32[]{:S(2)}) collective-permute-start(bf16[256,192]{1,0:T(8,128)(2,1)} %get-tuple-element.78), channel_id=1, source_target_pairs={{0,24},{8,16},{16,8},{24,0},{1,25},{9,17},{17,9},{25,1},{2,26},{10... | collective-permute-start | bytes 294920 | tf_op jit(solution)/shard_map/ppermute | solution.py:772
  87.9 29.4 %copy-start.22 = (bf16[256,192]{1,0:T(8,128)(2,1)}, bf16[256,192]{1,0:T(8,128)(2,1)S(1)}, u32[]{:S(2)}) copy-start(bf16[256,192]{1,0:T(8,128)(2,1)S(1)} %collective-permute-done.7.x1) | copy-start | bytes 294916
  91.4 25.9 %copy-start.23 = (bf16[256,192]{1,0:T(8,128)(2,1)}, bf16[256,192]{1,0:T(8,128)(2,1)S(1)}, u32[]{:S(2)}) copy-start(bf16[256,192]{1,0:T(8,128)(2,1)S(1)} %collective-permute-done.8.x2) | copy-start | bytes 294916
  92.9 24.4 %copy-start.24 = (bf16[256,192]{1,0:T(8,128)(2,1)}, bf16[256,192]{1,0:T(8,128)(2,1)S(1)}, u32[]{:S(2)}) copy-start(bf16[256,192]{1,0:T(8,128)(2,1)S(1)} %collective-permute-done.9.x3) | copy-start | bytes 294916
  132.6 9.3 %collective-permute-start.10 = (bf16[256,5760]{1,0:T(8,128)(2,1)}, bf16[256,5760]{1,0:T(8,128)(2,1)S(1)}, u32[]{:S(2)}, u32[]{:S(2)}) collective-permute-start(bf16[256,5760]{1,0:T(8,128)(2,1)} %get-tuple-element.87), channel_id=1, source_target_pairs={{0,1},{1,0},{2,3},{3,2},{4,5},{5,4},{6,7},{7,6},{8,9},{9,8},{10,11... | collective-permute-start | bytes 8847368 | tf_op jit(solution)/shard_map/ppermute | solution.py:775
  132.9 6.5 %collective-permute-start.11 = (bf16[256,192]{1,0:T(8,128)(2,1)}, bf16[256,192]{1,0:T(8,128)(2,1)S(1)}, u32[]{:S(2)}, u32[]{:S(2)}) collective-permute-start(bf16[256,192]{1,0:T(8,128)(2,1)} %get-tuple-element.88), channel_id=1, source_target_pairs={{0,8},{8,0},{16,24},{24,16},{1,9},{9,1},{17,25},{25,17},{2,10},{10... | collective-permute-start | bytes 294920 | tf_op jit(solution)/shard_map/ppermute | solution.py:772
  133.0 6.4 %collective-permute-start.12 = (bf16[256,192]{1,0:T(8,128)(2,1)}, bf16[256,192]{1,0:T(8,128)(2,1)S(1)}, u32[]{:S(2)}, u32[]{:S(2)}) collective-permute-start(bf16[256,192]{1,0:T(8,128)(2,1)} %get-tuple-element.89), channel_id=1, source_target_pairs={{0,16},{8,24},{16,0},{24,8},{1,17},{9,25},{17,1},{25,9},{2,18},{10... | collective-permute-start | bytes 294920 | tf_op jit(solution)/shard_map/ppermute | solution.py:772
  134.5 7.4 %collective-permute-start.13 = (bf16[256,192]{1,0:T(8,128)(2,1)}, bf16[256,192]{1,0:T(8,128)(2,1)S(1)}, u32[]{:S(2)}, u32[]{:S(2)}) collective-permute-start(bf16[256,192]{1,0:T(8,128)(2,1)} %get-tuple-element.90), channel_id=1, source_target_pairs={{0,24},{8,16},{16,8},{24,0},{1,25},{9,17},{17,9},{25,1},{2,26},{10... | collective-permute-start | bytes 294920 | tf_op jit(solution)/shard_map/ppermute | solution.py:772
  139.4 17.1 %copy-start.25 = (bf16[256,192]{1,0:T(8,128)(2,1)}, bf16[256,192]{1,0:T(8,128)(2,1)S(1)}, u32[]{:S(2)}) copy-start(bf16[256,192]{1,0:T(8,128)(2,1)S(1)} %collective-permute-done.11.g1) | copy-start | bytes 294916
  139.4 17.1 %copy-start.26 = (bf16[256,192]{1,0:T(8,128)(2,1)}, bf16[256,192]{1,0:T(8,128)(2,1)S(1)}, u32[]{:S(2)}) copy-start(bf16[256,192]{1,0:T(8,128)(2,1)S(1)} %collective-permute-done.12.g2) | copy-start | bytes 294916
  141.8 14.7 %copy-start.27 = (bf16[256,192]{1,0:T(8,128)(2,1)}, bf16[256,192]{1,0:T(8,128)(2,1)S(1)}, u32[]{:S(2)}) copy-start(bf16[256,192]{1,0:T(8,128)(2,1)S(1)} %collective-permute-done.13.g3) | copy-start | bytes 294916
  149.5 39.0 %collective-permute-start.15 = (bf16[2,4,240,384]{3,2,1,0:T(8,128)(2,1)}, bf16[2,4,240,384]{3,2,1,0:T(8,128)(2,1)S(1)}, u32[]{:S(2)}, u32[]{:S(2)}) collective-permute-start(bf16[2,4,240,384]{3,2,1,0:T(8,128)(2,1)} %get-tuple-element.107), channel_id=1, source_target_pairs={{0,16},{8,24},{16,0},{24,8},{1,17},{9,25},{17,1},{25,9},{2,18},{10... | collective-permute-start | bytes 4423688 | tf_op jit(solution)/shard_map/ppermute | solution.py:772
  156.6 27.3 %collective-permute-start.14 = (bf16[2,4,96,768]{3,2,1,0:T(8,128)(2,1)}, bf16[2,4,96,768]{3,2,1,0:T(8,128)(2,1)S(1)}, u32[]{:S(2)}, u32[]{:S(2)}) collective-permute-start(bf16[2,4,96,768]{3,2,1,0:T(8,128)(2,1)} %get-tuple-element.104), channel_id=1, source_target_pairs={{0,8},{8,0},{16,24},{24,16},{1,9},{9,1},{17,25},{25,17},{2,10},{10... | collective-permute-start | bytes 3538952 | tf_op jit(solution)/shard_map/ppermute | solution.py:772
  187.7 5.1 %copy-start.46 = (bf16[4,96,576]{2,1,0:T(8,128)(2,1)S(1)}, bf16[4,96,576]{2,1,0:T(8,128)(2,1)}, u32[]{:S(2)}) copy-start(bf16[4,96,576]{2,1,0:T(8,128)(2,1)} %get-tuple-element.109) | copy-start | bytes 1327108
  187.7 6.5 %copy-start.34 = (f32[1,3072]{1,0:T(1,128)S(1)}, f32[1,3072]{1,0:T(1,128)}, u32[]{:S(2)}) copy-start(f32[1,3072]{1,0:T(1,128)} %get-tuple-element.115) | copy-start | bytes 36868
  187.7 22.1 %collective-permute-start.27 = (bf16[4,96,768]{2,1,0:T(8,128)(2,1)}, bf16[4,96,768]{2,1,0:T(8,128)(2,1)S(1)}, u32[]{:S(2)}, u32[]{:S(2)}) collective-permute-start(bf16[4,96,768]{2,1,0:T(8,128)(2,1)} %get-tuple-element.119), channel_id=1, source_target_pairs={{0,16},{8,24},{16,0},{24,8},{1,17},{9,25},{17,1},{25,9},{2,18},{10... | collective-permute-start | bytes 1769480 | tf_op jit(solution)/shard_map/ppermute | solution.py:772
  192.8 25.1 %copy-start.35 = (f32[1,576]{1,0:T(1,128)S(1)}, f32[1,576]{1,0:T(1,128)}, u32[]{:S(2)}) copy-start(f32[1,576]{1,0:T(1,128)} %get-tuple-element.116) | copy-start | bytes 6916
  192.8 25.4 %copy-start.33 = (f32[8,768]{1,0:T(8,128)S(1)}, f32[8,768]{1,0:T(8,128)}, u32[]{:S(2)}) copy-start(f32[8,768]{1,0:T(8,128)} %get-tuple-element.114) | copy-start | bytes 73732
  192.8 21.6 %collective-permute-start.16 = (bf16[4,96,576]{2,1,0:T(8,128)(2,1)S(1)}, bf16[4,96,576]{2,1,0:T(8,128)(2,1)S(1)}, u32[]{:S(2)}, u32[]{:S(2)}) collective-permute-start(bf16[4,96,576]{2,1,0:T(8,128)(2,1)S(1)} %copy-done.46), channel_id=1, source_target_pairs={{0,1},{1,0},{2,3},{3,2},{4,5},{5,4},{6,7},{7,6},{8,9},{9,8},{10,11... | collective-permute-start | bytes 1327112 | tf_op jit(solution)/shard_map/ppermute | solution.py:775
  192.9 55.1 %collective-permute-start.30 = (bf16[4,240,384]{2,1,0:T(8,128)(2,1)}, bf16[4,240,384]{2,1,0:T(8,128)(2,1)S(1)}, u32[]{:S(2)}, u32[]{:S(2)}) collective-permute-start(bf16[4,240,384]{2,1,0:T(8,128)(2,1)} %get-tuple-element.125), channel_id=1, source_target_pairs={{0,8},{8,0},{16,24},{24,16},{1,9},{9,1},{17,25},{25,17},{2,10},{10... | collective-permute-start | bytes 2211848 | tf_op jit(solution)/shard_map/ppermute | solution.py:772
  212.9 32.4 %collective-permute-start.28 = (bf16[2,96,768]{2,1,0:T(8,128)(2,1)}, bf16[2,96,768]{2,1,0:T(8,128)(2,1)S(1)}, u32[]{:S(2)}, u32[]{:S(2)}) collective-permute-start(bf16[2,96,768]{2,1,0:T(8,128)(2,1)} %get-tuple-element.121), channel_id=1, source_target_pairs={{0,2},{2,0},{4,6},{6,4},{1,3},{3,1},{5,7},{7,5},{8,10},{10,8},{12,... | collective-permute-start | bytes 884744 | tf_op jit(solution)/shard_map/ppermute | solution.py:778
  217.2 9.0 %collective-permute-start.17 = (bf16[2,96,576]{2,1,0:T(8,128)(2,1)}, bf16[2,96,576]{2,1,0:T(8,128)(2,1)S(1)}, u32[]{:S(2)}, u32[]{:S(2)}) collective-permute-start(bf16[2,96,576]{2,1,0:T(8,128)(2,1)} %get-tuple-element.111), channel_id=1, source_target_pairs={{0,2},{2,0},{4,6},{6,4},{1,3},{3,1},{5,7},{7,5},{8,10},{10,8},{12,... | collective-permute-start | bytes 663560 | tf_op jit(solution)/shard_map/ppermute | solution.py:778
  228.7 1.2 collective-permute-start.22
  230.0 4.2 %collective-permute-start.23 = (f32[12,768]{1,0:T(8,128)S(1)}, f32[12,768]{1,0:T(8,128)S(1)}, u32[]{:S(2)}, u32[]{:S(2)}) collective-permute-start(f32[12,768]{1,0:T(8,128)S(1)} %add.68), channel_id=1, source_target_pairs={{0,8},{8,0},{16,24},{24,16},{1,9},{9,1},{17,25},{25,17},{2,10},{10... | collective-permute-start | bytes 110600 | tf_op jit(solution)/shard_map/ppermute | solution.py:772
  231.4 21.1 %collective-permute-start.18 = (bf16[96,576]{1,0:T(8,128)(2,1)}, bf16[96,576]{1,0:T(8,128)(2,1)S(1)}, u32[]{:S(2)}, u32[]{:S(2)}) collective-permute-start(bf16[96,576]{1,0:T(8,128)(2,1)} %get-tuple-element.113), channel_id=1, source_target_pairs={{0,4},{2,6},{4,0},{6,2},{1,5},{3,7},{5,1},{7,3},{8,12},{10,14},{12... | collective-permute-start | bytes 331784 | tf_op jit(solution)/shard_map/ppermute | solution.py:778
  234.1 4.2 %collective-permute-start.24 = (f32[12,768]{1,0:T(8,128)S(1)}, f32[12,768]{1,0:T(8,128)S(1)}, u32[]{:S(2)}, u32[]{:S(2)}) collective-permute-start(f32[12,768]{1,0:T(8,128)S(1)} %add.69), channel_id=1, source_target_pairs={{0,16},{8,24},{16,0},{24,8},{1,17},{9,25},{17,1},{25,9},{2,18},{10... | collective-permute-start | bytes 110600 | tf_op jit(solution)/shard_map/ppermute | solution.py:772
  238.3 4.2 %collective-permute-start.25 = (f32[12,768]{1,0:T(8,128)S(1)}, f32[12,768]{1,0:T(8,128)S(1)}, u32[]{:S(2)}, u32[]{:S(2)}) collective-permute-start(f32[12,768]{1,0:T(8,128)S(1)} %add.70), channel_id=1, source_target_pairs={{0,2},{2,0},{4,6},{6,4},{1,3},{3,1},{5,7},{7,5},{8,10},{10,8},{12,... | collective-permute-start | bytes 110600 | tf_op jit(solution)/shard_map/ppermute | solution.py:778
  242.5 14.5 %collective-permute-start.26 = (f32[12,768]{1,0:T(8,128)S(1)}, f32[12,768]{1,0:T(8,128)S(1)}, u32[]{:S(2)}, u32[]{:S(2)}) collective-permute-start(f32[12,768]{1,0:T(8,128)S(1)} %add.71), channel_id=1, source_target_pairs={{0,4},{2,6},{4,0},{6,2},{1,5},{3,7},{5,1},{7,3},{8,12},{10,14},{12... | collective-permute-start | bytes 110600 | tf_op jit(solution)/shard_map/ppermute | solution.py:778
  247.9 27.8 %collective-permute-start.29 = (bf16[96,768]{1,0:T(8,128)(2,1)}, bf16[96,768]{1,0:T(8,128)(2,1)S(1)}, u32[]{:S(2)}, u32[]{:S(2)}) collective-permute-start(bf16[96,768]{1,0:T(8,128)(2,1)} %get-tuple-element.123), channel_id=1, source_target_pairs={{0,4},{2,6},{4,0},{6,2},{1,5},{3,7},{5,1},{7,3},{8,12},{10,14},{12... | collective-permute-start | bytes 442376 | tf_op jit(solution)/shard_map/ppermute | solution.py:778
  251.1 9.8 %collective-permute-start.31 = (bf16[2,240,384]{2,1,0:T(8,128)(2,1)}, bf16[2,240,384]{2,1,0:T(8,128)(2,1)S(1)}, u32[]{:S(2)}, u32[]{:S(2)}) collective-permute-start(bf16[2,240,384]{2,1,0:T(8,128)(2,1)} %get-tuple-element.127), channel_id=1, source_target_pairs={{0,2},{2,0},{4,6},{6,4},{1,3},{3,1},{5,7},{7,5},{8,10},{10,8},{12,... | collective-permute-start | bytes 1105928 | tf_op jit(solution)/shard_map/ppermute | solution.py:778
  254.9 25.9 %collective-permute-start.19 = (bf16[96,576]{1,0:T(8,128)(2,1)}, bf16[96,576]{1,0:T(8,128)(2,1)S(1)}, u32[]{:S(2)}, u32[]{:S(2)}) collective-permute-start(bf16[96,576]{1,0:T(8,128)(2,1)} %sum.1.b0), channel_id=1, source_target_pairs={{0,8},{8,0},{16,24},{24,16},{1,9},{9,1},{17,25},{25,17},{2,10},{10... | collective-permute-start | bytes 331784 | tf_op jit(solution)/shard_map/ppermute | solution.py:772
  256.6 26.6 %collective-permute-start.20 = (bf16[96,576]{1,0:T(8,128)(2,1)}, bf16[96,576]{1,0:T(8,128)(2,1)S(1)}, u32[]{:S(2)}, u32[]{:S(2)}) collective-permute-start(bf16[96,576]{1,0:T(8,128)(2,1)} %sum.1.b0), channel_id=1, source_target_pairs={{0,16},{8,24},{16,0},{24,8},{1,17},{9,25},{17,1},{25,9},{2,18},{10... | collective-permute-start | bytes 331784 | tf_op jit(solution)/shard_map/ppermute | solution.py:772
  257.0 26.2 %collective-permute-start.21 = (bf16[96,576]{1,0:T(8,128)(2,1)}, bf16[96,576]{1,0:T(8,128)(2,1)S(1)}, u32[]{:S(2)}, u32[]{:S(2)}) collective-permute-start(bf16[96,576]{1,0:T(8,128)(2,1)} %sum.1.b0), channel_id=1, source_target_pairs={{0,24},{8,16},{16,8},{24,0},{1,25},{9,17},{17,9},{25,1},{2,26},{10... | collective-permute-start | bytes 331784 | tf_op jit(solution)/shard_map/ppermute | solution.py:772
  263.6 23.2 %copy-start.5 = (f32[256,768]{1,0:T(8,128)S(1)}, f32[256,768]{1,0:T(8,128)}, u32[]{:S(2)}) copy-start(f32[256,768]{1,0:T(8,128)} %get-tuple-element.81) | copy-start | bytes 2359300
  263.6 9.0 %collective-permute-start.32 = (bf16[240,384]{1,0:T(8,128)(2,1)}, bf16[240,384]{1,0:T(8,128)(2,1)S(1)}, u32[]{:S(2)}, u32[]{:S(2)}) collective-permute-start(bf16[240,384]{1,0:T(8,128)(2,1)} %get-tuple-element.129), channel_id=1, source_target_pairs={{0,4},{2,6},{4,0},{6,2},{1,5},{3,7},{5,1},{7,3},{8,12},{10,14},{12... | collective-permute-start | bytes 552968 | tf_op jit(solution)/shard_map/ppermute | solution.py:778
  275.0 1.5 collective-permute-start.33
  279.1 11.6 %collective-permute-start.34 = (bf16[240,768]{1,0:T(8,128)(2,1)}, bf16[240,768]{1,0:T(8,128)(2,1)S(1)}, u32[]{:S(2)}, u32[]{:S(2)}) collective-permute-start(bf16[240,768]{1,0:T(8,128)(2,1)} %join.1.b0), channel_id=1, source_target_pairs={{0,8},{8,0},{16,24},{24,16},{1,9},{9,1},{17,25},{25,17},{2,10},{10... | collective-permute-start | bytes 1105928 | tf_op jit(solution)/shard_map/ppermute | solution.py:772
  280.3 18.5 %collective-permute-start.35 = (bf16[240,768]{1,0:T(8,128)(2,1)}, bf16[240,768]{1,0:T(8,128)(2,1)S(1)}, u32[]{:S(2)}, u32[]{:S(2)}) collective-permute-start(bf16[240,768]{1,0:T(8,128)(2,1)} %join.1.b0), channel_id=1, source_target_pairs={{0,16},{8,24},{16,0},{24,8},{1,17},{9,25},{17,1},{25,9},{2,18},{10... | collective-permute-start | bytes 1105928 | tf_op jit(solution)/shard_map/ppermute | solution.py:772
  280.8 2.4 copy-start.28
  280.8 18.0 %collective-permute-start.36 = (bf16[240,768]{1,0:T(8,128)(2,1)}, bf16[240,768]{1,0:T(8,128)(2,1)S(1)}, u32[]{:S(2)}, u32[]{:S(2)}) collective-permute-start(bf16[240,768]{1,0:T(8,128)(2,1)} %join.1.b0), channel_id=1, source_target_pairs={{0,24},{8,16},{16,8},{24,0},{1,25},{9,17},{17,9},{25,1},{2,26},{10... | collective-permute-start | bytes 1105928 | tf_op jit(solution)/shard_map/ppermute | solution.py:772
  290.8 8.1 %copy-start.15 = (bf16[240,768]{1,0:T(8,128)(2,1)}, bf16[240,768]{1,0:T(8,128)(2,1)S(1)}, u32[]{:S(2)}) copy-start(bf16[240,768]{1,0:T(8,128)(2,1)S(1)} %collective-permute-done.34.b1) | copy-start | bytes 1105924
  (22 other events, 19.6 us)
Sparse Core Ops, SparseCore 0:
  11.5 105.7 all-gather.1
  178.9 41.0 reduce-scatter.1
where the time goes:
time: 311 us; the launch traced here: 310 us
  waiting for transfers between devices  132 us (42%)
  Pallas kernels  90 us (29%)
  starting transfers between devices  41.8 us (13%)
  local copies, waits for them, and re-layouts  26.9 us (9%)
  between operations  15.1 us (5%)
  other arithmetic  4.21 us (1%)
    ppermute x21, waiting for transfers between devices, across(): return lax.ppermute(value, 'seq', [(i, i ^ step) for i in range(4)])  72.5 us
    pallas_call x16, Pallas kernels, call(): pl.pallas_call(kernel, name=kernel.__name__.replace('_kernel', ''), cost_...  44.9 us
    ppermute x11, waiting for transfers between devices, level_across(): return lax.ppermute(value, 'z', [(i, i ^ step) for i in range(4)])  33.1 us
    all_gather x1, waiting for transfers between devices, fast_body(): gathered = lax.all_gather(quarter, ('z', 'core', 'seq'), axis=0, tiled=True)  24.4 us
    ppermute x21, starting transfers between devices, across(): return lax.ppermute(value, 'seq', [(i, i ^ step) for i in range(4)])  23.9 us
    ppermute x11, starting transfers between devices, level_across(): return lax.ppermute(value, 'z', [(i, i ^ step) for i in range(4)])  17.4 us
    unnamed x97, local copies, waits for them, and re-layouts  16.5 us
    pallas_call x1, Pallas kernels, fast_body(): pl.pallas_call(middle_kernel, name='middle', cost_estimate=work(15), out_...  15.3 us
  transfers between devices with their start and end apart: 39, of which 24 were waited for; matrix products, arithmetic and copies ran while one was open for 4% of the time, Pallas kernels for 21%

commit v1 on v0

--- a/solution.py
+++ b/solution.py
@@ -506,6 +506,8 @@
     small,
     up_bias,
     gathered,
+    own_down,
+    other_down,
     output,
     grad_one,
     y0,
@@ -525,7 +527,7 @@
     context,
     sems,
 ):
-    place, core = sc[1], sc[2]
+    place, core, level = sc[1], sc[2], sc[3]
     blocks = w_up.shape[0]
     shard_rows = w_up.shape[3]
     width = w_up.shape[4]
@@ -535,20 +537,26 @@
         copies.append(
             pltpu.make_async_copy(gathered.at[:, :, b, 0:shard_rows, :], w_up.at[b], sems.at[b])
         )
-    copies.append(
-        pltpu.make_async_copy(
-            gathered.at[:, :, :, shard_rows : 2 * shard_rows, :], w_down, sems.at[blocks]
-        )
-    )
+    down_copies = []
+    for j in range(4):
+        for k in range(4):
+            for side, block in ((core, own_down), (1 - core, other_down)):
+                down_copies.append(
+                    pltpu.make_async_copy(
+                        block.at[j, k],
+                        w_down.at[level ^ k, side, place ^ j],
+                        sems.at[7 + len(down_copies)],
+                    )
+                )
     out_copies = [
         pltpu.make_async_copy(
-            gathered.at[:, :, b, 2 * shard_rows : 2 * shard_rows + third, :],
+            gathered.at[:, :, b, shard_rows : shard_rows + third, :],
             w_out.at[:, :, b * third : (b + 1) * third, :],
-            sems.at[blocks + 1 + b],
+            sems.at[blocks + b],
         )
         for b in range(3)
     ]
-    for copy in out_copies + copies:
+    for copy in out_copies + copies + down_copies:
         copy.start()
     for copy in out_copies:
         copy.wait()
@@ -571,7 +579,8 @@
         phi = 0.5 + 0.5 * lax.erf(up * HALF_ROOT)
         slope[:, span] = phi + up * (jnp.exp(-0.5 * up * up) * NORMAL_SCALE)
         active[:, span] = (up * phi).astype(jnp.bfloat16)
-    copies[blocks].wait()
+    for copy in down_copies:
+        copy.wait()
     residual = normed + small[3:4, :] + dot_nn(active[...], w_down[...].reshape(-1, width))
     unit_two, inverse_two = normalize(residual)
     gain_two = small[4:5, :]
@@ -781,13 +790,12 @@
     quarter = jnp.concatenate(
         [
             lax.dynamic_slice_in_dim(w_up, place * width, width, axis=1),
-            lax.dynamic_slice_in_dim(w_down, place * shard_rows, shard_rows, axis=0),
             lax.dynamic_slice_in_dim(w_out, jnp.minimum(place, 2) * third, third, axis=0),
         ],
         axis=0,
     )
     gathered = lax.all_gather(quarter, ("z", "core", "seq"), axis=0, tiled=True)
-    gathered = gathered.reshape(zs, 2, 4, 2 * shard_rows + third, width)
+    gathered = gathered.reshape(zs, 2, 4, shard_rows + third, width)
     columns = lax.dynamic_index_in_dim(
         w_qkv.reshape(shard_rows, 3, 4, head_width), place, axis=2, keepdims=False
     ).reshape(shard_rows, 3 * head_width)
@@ -804,8 +812,14 @@
     vector_rows = jnp.pad(vectors, (0, pad)).reshape(15, 3 * head_width)
     own_block = jnp.concatenate([columns, bias_row, vector_rows], axis=0)
     t1, t2, t3 = across(token, 1), across(token, 2), across(token, 3)
-    own_cols = jnp.stack([own_block] + [level_across(own_block, k) for k in (1, 2, 3)])
+    two_cols = jnp.stack([own_block, level_across(own_block, 1)])
+    own_cols = jnp.concatenate([two_cols, level_across(two_cols, 2)])
+    down_quarter = lax.dynamic_slice_in_dim(w_down, place * shard_rows, shard_rows, axis=0)
+    two_down = jnp.stack([down_quarter, level_across(down_quarter, 1)])
+    own_down = jnp.concatenate([two_down, level_across(two_down, 2)])
+    own_down, own_cols, t1, t2, t3 = lax.optimization_barrier((own_down, own_cols, t1, t2, t3))
     other_cols = partner(own_cols)
+    down_sets = [own_down] + [across(own_down, j) for j in (1, 2, 3)]
     sc = jnp.stack([lengths[0], place, core, lax.axis_index("z")]).astype(jnp.int32)
     all_rows = 4 * rows
     qkv, ctx_t, c0, c1, c2, c3, lse, full_qkv, vector_sets = pl.pallas_call(
@@ -828,6 +842,9 @@
         scratch_shapes=[pltpu.VMEM((4, rows, head_width), bf16)],
     )(sc, token, t1, t2, t3, own_cols, other_cols)
     x1, x2, x3 = across(c1, 1), across(c2, 2), across(c3, 3)
+    down_sets[0], _ = lax.optimization_barrier((down_sets[0], c0))
+    own_down = jnp.stack(down_sets)
+    other_down = partner(own_down)
     all_vec = vector_sets.reshape(2 * zs, -1)
     six = all_vec[:, : 6 * shard_rows].reshape(2 * zs, 6, shard_rows)
     six = six.transpose(1, 0, 2).reshape(6, width)
@@ -852,7 +869,7 @@
         ),
         in_specs=[smem_spec()]
         + vmem_specs(8)
-        + [pl.BlockSpec(memory_space=pl.ANY)],
+        + [pl.BlockSpec(memory_space=pl.ANY)] * 3,
         out_specs=tuple(vmem_specs(10)),
         scratch_shapes=[
             pltpu.VMEM((zs, 2, shard_rows, width), bf16),
@@ -862,7 +879,7 @@
             pltpu.VMEM((rows, hidden), bf16),
             pltpu.VMEM((rows, hidden), bf16),
             pltpu.VMEM((4, rows, head_width), bf16),
-            pltpu.SemaphoreType.DMA((8,)),
+            pltpu.SemaphoreType.DMA((7 + 32,)),
         ],
     )(
         sc,
@@ -875,6 +892,8 @@
         small,
         full_up_bias,
         gathered,
+        own_down,
+        other_down,
     )
     g1, g2, g3 = across(y1, 1), across(y2, 2), across(y3, 3)
     got, g1, g2, g3 = lax.optimization_barrier((partner(send), g1, g2, g3))
@@ -937,13 +956,13 @@
         in_specs=[smem_spec()] + vmem_specs(5),
         out_specs=tuple(vmem_specs(3)),
     )(sc, token, t1, t2, t3, dqkv)
+    d_near, u_near, q_keep = lax.optimization_barrier((d_near, u_near, q_keep))
     d_mine, d_pass = call(
         fold_kernel, 1, [struct((zs, shard_rows, width))] * 2, d_near, d_got, scalars=False
     )
     u_mine, u_pass = call(
         fold_kernel, 1, [struct((zs, block_rows, quad))] * 2, u_near, u_got, scalars=False
     )
-    q_send, d_mine, u_mine = lax.optimization_barrier((q_send, d_mine, u_mine))
     q_got = partner(q_send)
     late_dqkv, q_keep = lax.optimization_barrier((dqkv, q_keep))
     (token_parts,) = call(
@@ -953,9 +972,6 @@
         late_dqkv,
         full_qkv,
     )
-    token_sum = lax.psum_scatter(
-        token_parts.reshape(4 * rows, width), "seq", scatter_dimension=0, tiled=True
-    )
     q_near, q_far = call(
         level_fold_kernel, 1, [struct((2, shard_rows, 3 * head_width))] * 2, q_keep, q_got
     )
@@ -972,17 +988,23 @@
     )
 
     def seq_sum(mine, pass_on, shape, step):
-        near, far = call(
+        return call(
             level_fold_kernel,
             1,
             [struct((2,) + shape[1:])] * 2,
             mine,
             across(pass_on, step),
         )
-        return level_sum(near, far, shape[1:])
-
-    d_parts = seq_sum(d_mine, d_pass, (zs, shard_rows, width), 2)
-    u_parts = seq_sum(u_mine, u_pass, (zs, block_rows, quad), 1)
+
+    d_mine, u_mine, _ = lax.optimization_barrier((d_mine, u_mine, q_mine))
+    d_near, d_far = seq_sum(d_mine, d_pass, (zs, shard_rows, width), 2)
+    u_near, u_far = seq_sum(u_mine, u_pass, (zs, block_rows, quad), 1)
+    token_parts, _, _ = lax.optimization_barrier((token_parts, u_near, d_near))
+    token_sum = lax.psum_scatter(
+        token_parts.reshape(4 * rows, width), "seq", scatter_dimension=0, tiled=True
+    )
+    d_parts = level_sum(d_near, d_far, (shard_rows, width))
+    u_parts = level_sum(u_near, u_far, (block_rows, quad))
     half_rows = shard_rows + shard_rows // 2
     u_keep, u_send = call(
         split_up_kernel,

time: 311 us -> 298 us (0.958)
  waiting for transfers between devices: 132 us -> 114 us
  starting transfers between devices: 41.8 us -> 47.4 us
    all_gather x1, waiting for transfers between devices: 24.4 us -> 9.46 us  [fast_body(): gathered = lax.all_gather(quarter, ('z', 'core', 'seq'), axis=0, tiled=True)]
    ppermute x21 -> x24, waiting for transfers between devices: 72.5 us -> 59.2 us  [across(): return lax.ppermute(value, 'seq', [(i, i ^ step) for i in range(4)])]
    ppermute x11 -> x12, waiting for transfers between devices: 33.1 us -> 45.7 us  [level_across(): return lax.ppermute(value, 'z', [(i, i ^ step) for i in range(4)])]
    ppermute x21 -> x24, starting transfers between devices: 23.9 us -> 27.4 us  [across(): return lax.ppermute(value, 'seq', [(i, i ^ step) for i in range(4)])]
    ppermute x11 -> x12, starting transfers between devices: 17.4 us -> 19.3 us  [level_across(): return lax.ppermute(value, 'z', [(i, i ^ step) for i in range(4)])]
  transfers between devices with their start and end apart: 39 -> 44, of which waited for: 24 -> 22; matrix products, arithmetic and copies ran while one was open for 4% -> 4% of each run, Pallas kernels for 21% -> 22%
where the time goes in v1:
time: 298 us; the launch traced here: 297 us
  waiting for transfers between devices  114 us (38%)
  Pallas kernels  90.1 us (30%)
  starting transfers between devices  47.4 us (16%)
  local copies, waits for them, and re-layouts  24.3 us (8%)
  between operations  15.3 us (5%)
  other arithmetic  5.95 us (2%)
    ppermute x24, waiting for transfers between devices, across(): return lax.ppermute(value, 'seq', [(i, i ^ step) for i in range(4)])  59.2 us
    ppermute x12, waiting for transfers between devices, level_across(): return lax.ppermute(value, 'z', [(i, i ^ step) for i in range(4)])  45.7 us
    pallas_call x16, Pallas kernels, call(): pl.pallas_call(kernel, name=kernel.__name__.replace('_kernel', ''), cost_...  44.6 us
    ppermute x24, starting transfers between devices, across(): return lax.ppermute(value, 'seq', [(i, i ^ step) for i in range(4)])  27.4 us
    ppermute x12, starting transfers between devices, level_across(): return lax.ppermute(value, 'z', [(i, i ^ step) for i in range(4)])  19.3 us
    pallas_call x1, Pallas kernels, fast_body(): pl.pallas_call(middle_kernel, name='middle', cost_estimate=work(15), out_...  15.5 us
    unnamed x97, local copies, waits for them, and re-layouts  14.3 us
    pallas_call x1, Pallas kernels, fast_body(): pl.pallas_call(attend_forward_kernel, name='attend_forward', cost_estimat...  13.1 us
  transfers between devices with their start and end apart: 44, of which 22 were waited for; matrix products, arithmetic and copies ran while one was open for 4% of the time, Pallas kernels for 22%

profile of v1, /device:TPU:0, one launch (start us, length us, event | category | flops | bytes accessed | tf_op | source)
XLA Modules:
  0.0 297.5 jit_solution(8816201895570421444)
XLA Ops:
  9.9 1.7 reshape.78
  12.9 3.0 %collective-permute-start.2 = (bf16[112,576]{1,0:T(8,128)(2,1)S(1)}, bf16[112,576]{1,0:T(8,128)(2,1)S(1)}, u32[]{:S(2)}, u32[]{:S(2)}) collective-permute-start(bf16[112,576]{1,0:T(8,128)(2,1)S(1)} %pad_maximum_fusion.6), channel_id=1, source_target_pairs={{0,2},{2,0},{4,6},{6,4},{1,3},{3,1},{5,7},{7,5},{8,10},{10,8},{12,... | collective-permute-start | bytes 387080 | tf_op jit(solution)/shard_map/ppermute | solution.py:787
  16.1 4.4 %collective-permute-done.2 = bf16[112,576]{1,0:T(8,128)(2,1)S(1)} collective-permute-done((bf16[112,576]{1,0:T(8,128)(2,1)S(1)}, bf16[112,576]{1,0:T(8,128)(2,1)S(1)}, u32[]{:S(2)}, u32[]{:S(2)}) %collective-permute-start.2) | collective-permute-done | bytes 129056 | tf_op jit(solution)/shard_map/ppermute | solution.py:787
  20.6 3.1 %collective-permute-start.3 = (bf16[2,112,576]{2,1,0:T(8,128)(2,1)S(1)}, bf16[2,112,576]{2,1,0:T(8,128)(2,1)S(1)}, u32[]{:S(2)}, u32[]{:S(2)}) collective-permute-start(bf16[2,112,576]{2,1,0:T(8,128)(2,1)S(1)} %pad_maximum_fusion.4), channel_id=1, source_target_pairs={{0,4},{2,6},{4,0},{6,2},{1,5},{3,7},{5,1},{7,3},{8,12},{10,14},{12... | collective-permute-start | bytes 774152 | tf_op jit(solution)/shard_map/ppermute | solution.py:787
  24.4 2.5 collective-permute-start.1
  26.9 1.5 collective-permute-start.4
  28.4 1.5 collective-permute-start.5
  30.3 17.2 %collective-permute-done.3 = bf16[2,112,576]{2,1,0:T(8,128)(2,1)S(1)} collective-permute-done((bf16[2,112,576]{2,1,0:T(8,128)(2,1)S(1)}, bf16[2,112,576]{2,1,0:T(8,128)(2,1)S(1)}, u32[]{:S(2)}, u32[]{:S(2)}) %collective-permute-start.3) | collective-permute-done | bytes 258080 | tf_op jit(solution)/shard_map/ppermute | solution.py:787
  47.6 4.2 %collective-permute-done.1 = bf16[2,96,768]{2,1,0:T(8,128)(2,1)S(1)} collective-permute-done((bf16[2,96,768]{2,1,0:T(8,128)(2,1)S(1)}, bf16[2,96,768]{2,1,0:T(8,128)(2,1)S(1)}, u32[]{:S(2)}, u32[]{:S(2)}) %collective-permute-start.1) | collective-permute-done | bytes 294944 | tf_op jit(solution)/shard_map/ppermute | solution.py:787
  52.0 1.4 collective-permute-start.11
  53.4 1.5 collective-permute-start.12
  57.7 13.1 %attend_forward.1 = (bf16[1024,576]{1,0:T(8,128)(2,1)}, f32[192,1024]{1,0:T(8,128)}, bf16[256,192]{1,0:T(8,128)(2,1)}, bf16[256,192]{1,0:T(8,128)(2,1)}, bf16[25...) custom-call(s32[4]{0:T(128)} %pad_add_fusion.sc, ...), custom_call_target="tpu_custom_call" | custom-call | flops 1170000000 | bytes 3900000 | tf_op jit(solution)/shard_map/attend_forward/pallas_call | solution.py:825
  70.8 3.1 %collective-permute-done.11 = bf16[4,96,768]{2,1,0:T(8,128)(2,1)} collective-permute-done((bf16[4,96,768]{2,1,0:T(8,128)(2,1)S(1)}, bf16[4,96,768]{2,1,0:T(8,128)(2,1)}, u32[]{:S(2)}, u32[]{:S(2)}) %collective-permute-start.11) | collective-permute-done | bytes 589856 | tf_op jit(solution)/shard_map/ppermute | solution.py:781
  74.0 14.2 %collective-permute-done.13 = bf16[4,96,768]{2,1,0:T(8,128)(2,1)} collective-permute-done((bf16[4,96,768]{2,1,0:T(8,128)(2,1)S(1)}, bf16[4,96,768]{2,1,0:T(8,128)(2,1)}, u32[]{:S(2)}, u32[]{:S(2)}) %collective-permute-start.13) | collective-permute-done | bytes 589856 | tf_op jit(solution)/shard_map/ppermute | solution.py:781
  88.1 1.7 pad_maximum_fusion.own_down
  90.9 2.6 collective-permute-start.10
  93.5 1.3 collective-permute-start.9
  96.3 4.8 %collective-permute-done.10.x3 = bf16[256,192]{1,0:T(8,128)(2,1)S(1)} collective-permute-done((bf16[256,192]{1,0:T(8,128)(2,1)}, bf16[256,192]{1,0:T(8,128)(2,1)S(1)}, u32[]{:S(2)}, u32[]{:S(2)}) %collective-permute-start.10) | collective-permute-done | bytes 98336 | tf_op jit(solution)/shard_map/ppermute | solution.py:781
  101.1 1.8 collective-permute-done.8.x1
  103.7 9.5 %all-gather.2.cloned.1.call-done = bf16[4096,768]{1,0:T(8,128)(2,1)} async-done(((bf16[128,768]{1,0:T(8,128)(2,1)}), bf16[4096,768]{1,0:T(8,128)(2,1)}) %all-gather.2.cloned.1.call-update) | async-done | bytes 6291472 | tf_op jit(solution)/shard_map/all_gather | solution.py:797
  113.2 15.5 %middle.1 = (bf16[256,768]{1,0:T(8,128)(2,1)}, f32[256,768]{1,0:T(8,128)}, bf16[256,192]{1,0:T(8,128)(2,1)}, bf16[256,192]{1,0:T(8,128)(2,1)}, bf16[256,192]{1,0...) custom-call(s32[4]{0:T(128)} %pad_add_fusion.sc, ...), custom_call_target="tpu_custom_call" | custom-call | flops 1350000000 | bytes 4500000 | tf_op jit(solution)/shard_map/middle/pallas_call | solution.py:854
  129.0 1.3 collective-permute-start.16
  130.4 2.1 collective-permute-start.18
  132.5 2.9 collective-permute-done.16.g1
  135.4 3.4 %collective-permute-done.17.g2 = bf16[256,192]{1,0:T(8,128)(2,1)S(1)} collective-permute-done((bf16[256,192]{1,0:T(8,128)(2,1)}, bf16[256,192]{1,0:T(8,128)(2,1)S(1)}, u32[]{:S(2)}, u32[]{:S(2)}) %collective-permute-start.17) | collective-permute-done | bytes 98336 | tf_op jit(solution)/shard_map/ppermute | solution.py:781
  139.4 1.6 copy-done.1
  141.0 6.1 %up_grad.1 = (bf16[2,4,240,384]{3,2,1,0:T(8,128)(2,1)}, bf16[2,4,240,384]{3,2,1,0:T(8,128)(2,1)}) custom-call(s32[4]{0:T(128)} %pad_add_fusion.sc, bf16[256,5760]{1,0:T(8,128)(2,1)} %get-tuple-element.101.keep, bf16[256,5760]{1,0:T(8,128)(2,1)} %copy-done.1), custom_call_target="tpu_custom_call" | custom-call | flops 360000000 | bytes 1200000 | tf_op jit(solution)/shard_map/up_grad/pallas_call | solution.py:903
  147.5 5.8 %down_grad.1 = (bf16[2,4,96,768]{3,2,1,0:T(8,128)(2,1)}, bf16[2,4,96,768]{3,2,1,0:T(8,128)(2,1)}) custom-call(s32[4]{0:T(128)} %pad_add_fusion.sc, bf16[256,5760]{1,0:T(8,128)(2,1)} %get-tuple-element.101.keep, bf16[256,5760]{1,0:T(8,128)(2,1)} %copy-done.1), custom_call_target="tpu_custom_call" | custom-call | flops 360000000 | bytes 1200000 | tf_op jit(solution)/shard_map/down_grad/pallas_call | solution.py:903
  153.3 1.6 collective-permute-start.19
  155.0 12.5 %attend_backward.1.dqkv = bf16[1024,576]{1,0:T(8,128)(2,1)} custom-call(s32[4]{0:T(128)} %pad_add_fusion.sc, bf16[1024,576]{1,0:T(8,128)(2,1)} %get-tuple-element.97.qkv, f32[192,1024]{1,0:T(8,128)} %get-tuple-element.98.ctx_t, f32[3,1024]{1,0:T(4,128)} %get-tuple-element.99.lse, bf16[256,192]{1,0:T(8,128)(2,1)} %get-tuple-element.109.g0, ...), custom_call_target="tpu_custom_call" | custom-call | flops 990000000 | bytes 3300000 | tf_op jit(solution)/shard_map/attend_backward/pallas_call | solution.py:934
  167.5 4.3 %grad_qkv_weight.1 = (bf16[4,96,576]{2,1,0:T(8,128)(2,1)}, bf16[4,96,576]{2,1,0:T(8,128)(2,1)}, f32[1,576]{1,0:T(1,128)}) custom-call(s32[4]{0:T(128)} %pad_add_fusion.sc, bf16[256,768]{1,0:T(8,128)(2,1)} %bitcast.50, bf16[256,768]{1,0:T(8,128)(2,1)} %copy-done.10, bf16[256,768]{1,0:T(8,128)(2,1)} %copy-done.11, bf16[256,768]{1,0:T(8,128)(2,1)} %copy-done.12, ...), custom_call_target="tpu_custom_call" | custom-call | flops 360000000 | bytes 1200000 | tf_op jit(solution)/shard_map/grad_qkv_weight/pallas_call | solution.py:947
  171.8 8.9 %collective-permute-done.20.got = bf16[2,4,240,384]{3,2,1,0:T(8,128)(2,1)S(1)} collective-permute-done((bf16[2,4,240,384]{3,2,1,0:T(8,128)(2,1)}, bf16[2,4,240,384]{3,2,1,0:T(8,128)(2,1)S(1)}, u32[]{:S(2)}, u32[]{:S(2)}) %collective-permute-start.20) | collective-permute-done | bytes 1474592 | tf_op jit(solution)/shard_map/ppermute | solution.py:781
  180.6 1.1 copy-done.4
  181.8 3.1 %fold.6 = (bf16[4,240,384]{2,1,0:T(8,128)(2,1)}, bf16[4,240,384]{2,1,0:T(8,128)(2,1)}) custom-call(bf16[2,4,240,384]{3,2,1,0:T(8,128)(2,1)} %get-tuple-element.122.near, bf16[2,4,240,384]{3,2,1,0:T(8,128)(2,1)} %copy-done.4), custom_call_target="tpu_custom_call" | custom-call | flops 90000000 | bytes 300000 | tf_op jit(solution)/shard_map/fold/pallas_call | solution.py:903
  186.2 2.8 fold.5
  189.0 1.7 collective-permute-start.24
  190.8 2.0 level_fold.3
  192.8 2.0 collective-permute-start.22
  194.8 4.2 %grad_tokens.1 = bf16[4,256,768]{2,1,0:T(8,128)(2,1)} custom-call(s32[4]{0:T(128)} %pad_add_fusion.sc, bf16[1024,576]{1,0:T(8,128)(2,1)} %attend_backward.1.dqkv, bf16[4,2,96,576]{3,2,1,0:T(8,128)(2,1)} %get-tuple-element.118.weight), custom_call_target="tpu_custom_call" | custom-call | flops 360000000 | bytes 1200000 | tf_op jit(solution)/shard_map/grad_tokens/pallas_call | solution.py:903
  199.0 2.4 collective-permute-done.22.got
  202.1 1.8 fold.7
  203.9 1.1 collective-permute-done.24.got
  205.8 2.1 level_fold.5
  208.8 2.3 level_fold.4
  211.1 2.9 collective-permute-start.36
  215.9 7.8 %collective-permute-done.36.got = bf16[2,240,384]{2,1,0:T(8,128)(2,1)S(1)} collective-permute-done((bf16[2,240,384]{2,1,0:T(8,128)(2,1)}, bf16[2,240,384]{2,1,0:T(8,128)(2,1)S(1)}, u32[]{:S(2)}, u32[]{:S(2)}) %collective-permute-start.36) | collective-permute-done | bytes 368672 | tf_op jit(solution)/shard_map/ppermute | solution.py:787
  224.4 1.9 fold.9
  226.3 2.4 collective-permute-start.37
  230.3 2.6 collective-permute-done.30
  233.9 3.1 %collective-permute-done.31 = f32[12,768]{1,0:T(8,128)S(1)} collective-permute-done((f32[12,768]{1,0:T(8,128)S(1)}, f32[12,768]{1,0:T(8,128)S(1)}, u32[]{:S(2)}, u32[]{:S(2)}) %collective-permute-start.31) | collective-permute-done | bytes 36896 | tf_op jit(solution)/shard_map/ppermute | solution.py:781
  237.4 5.3 %collective-permute-done.32 = f32[12,768]{1,0:T(8,128)S(1)} collective-permute-done((f32[12,768]{1,0:T(8,128)S(1)}, f32[12,768]{1,0:T(8,128)S(1)}, u32[]{:S(2)}, u32[]{:S(2)}) %collective-permute-start.32) | collective-permute-done | bytes 36896 | tf_op jit(solution)/shard_map/ppermute | solution.py:787
  243.5 1.6 sum.1.b0
  245.1 1.2 collective-permute-start.26
  248.5 1.8 fold.8
  250.3 2.2 collective-permute-start.35
  253.2 1.8 split_up.1
  255.0 3.1 %collective-permute-done.35.e1 = bf16[96,768]{1,0:T(8,128)(2,1)S(1)} collective-permute-done((bf16[96,768]{1,0:T(8,128)(2,1)}, bf16[96,768]{1,0:T(8,128)(2,1)S(1)}, u32[]{:S(2)}, u32[]{:S(2)}) %collective-permute-start.35) | collective-permute-done | bytes 147488 | tf_op jit(solution)/shard_map/ppermute | solution.py:787
  258.8 1.9 join.1.b0
  262.7 1.5 collective-permute-start.41
  266.7 1.4 collective-permute-start.28
  268.7 12.5 %collective-permute-done.28.b3 = bf16[96,576]{1,0:T(8,128)(2,1)S(1)} collective-permute-done((bf16[96,576]{1,0:T(8,128)(2,1)}, bf16[96,576]{1,0:T(8,128)(2,1)S(1)}, u32[]{:S(2)}, u32[]{:S(2)}) %collective-permute-start.28) | collective-permute-done | bytes 110624 | tf_op jit(solution)/shard_map/ppermute | solution.py:781
  281.9 2.3 finish_qkv.1
  285.8 3.0 %finish.1 = (f32[384,768]{1,0:T(8,128)}, f32[96,3072]{1,0:T(8,128)}, f32[96,768]{1,0:T(8,128)}) custom-call(s32[4]{0:T(128)} %pad_add_fusion.sc, bf16[240,768]{1,0:T(8,128)(2,1)} %join.1.b0, bf16[240,768]{1,0:T(8,128)(2,1)} %copy-done.13, bf16[240,768]{1,0:T(8,128)(2,1)} %copy-done.14, bf16[240,768]{1,0:T(8,128)(2,1)} %copy-done.15), custom_call_target="tpu_custom_call" | custom-call | flops 180000000 | bytes 600000 | tf_op jit(solution)/shard_map/finish/pallas_call | solution.py:903
  288.8 1.8 fusion
  (198 shorter events, 33.0 us)
Async XLA Ops:
  7.2 8.8 %copy-start = (bf16[384,768]{1,0:T(8,128)(2,1)S(1)}, bf16[384,768]{1,0:T(8,128)(2,1)}, u32[]{:S(2)}) copy-start(bf16[384,768]{1,0:T(8,128)(2,1)} %param.27) | copy-start | bytes 1769476
  7.2 5.3 %copy-start.36 = (bf16[96]{0:T(256)(128)(2,1)S(1)}, bf16[96]{0:T(256)(128)(2,1)}, u32[]{:S(2)}) copy-start(bf16[96]{0:T(256)(128)(2,1)} %param.22) | copy-start | bytes 580
  7.2 5.3 %copy-start.37 = (bf16[96]{0:T(256)(128)(2,1)S(1)}, bf16[96]{0:T(256)(128)(2,1)}, u32[]{:S(2)}) copy-start(bf16[96]{0:T(256)(128)(2,1)} %param.23) | copy-start | bytes 580
  7.2 5.3 %copy-start.38 = (bf16[96]{0:T(256)(128)(2,1)S(1)}, bf16[96]{0:T(256)(128)(2,1)}, u32[]{:S(2)}) copy-start(bf16[96]{0:T(256)(128)(2,1)} %param.24) | copy-start | bytes 580
  7.2 5.3 %copy-start.35 = (bf16[384]{0:T(512)(128)(2,1)S(1)}, bf16[384]{0:T(512)(128)(2,1)}, u32[]{:S(2)}) copy-start(bf16[384]{0:T(512)(128)(2,1)} %param.26) | copy-start | bytes 2308
  7.3 5.3 %copy-start.39 = (bf16[96]{0:T(256)(128)(2,1)S(1)}, bf16[96]{0:T(256)(128)(2,1)}, u32[]{:S(2)}) copy-start(bf16[96]{0:T(256)(128)(2,1)} %param.28) | copy-start | bytes 580
  7.3 105.9 %all-gather.2.cloned.1.call-start = ((), (), s32[]{:S(2)}) async-start(), calls=%async_computation.1 | async-start | bytes 6488064 | tf_op jit(solution)/shard_map/all_gather | solution.py:797
  9.8 279.0 %reduce-scatter.2.cloned.1.call-start = ((), (), s32[]{:S(2)}) async-start(), calls=%async_computation.2 | async-start | bytes 1966080 | tf_op jit(solution)/shard_map/reduce_scatter | solution.py:1003
  9.9 17.0 %copy-start.3 = (bf16[1,256,768]{2,1,0:T(8,128)(2,1)S(1)}, bf16[1,256,768]{2,1,0:T(8,128)(2,1)}, u32[]{:S(2)}) copy-start(bf16[1,256,768]{2,1,0:T(8,128)(2,1)} %param.16) | copy-start | bytes 1179652
  12.9 7.6 %collective-permute-start.2 = (bf16[112,576]{1,0:T(8,128)(2,1)S(1)}, bf16[112,576]{1,0:T(8,128)(2,1)S(1)}, u32[]{:S(2)}, u32[]{:S(2)}) collective-permute-start(bf16[112,576]{1,0:T(8,128)(2,1)S(1)} %pad_maximum_fusion.6), channel_id=1, source_target_pairs={{0,2},{2,0},{4,6},{6,4},{1,3},{3,1},{5,7},{7,5},{8,10},{10,8},{12,... | collective-permute-start | bytes 387080 | tf_op jit(solution)/shard_map/ppermute | solution.py:787
  16.0 8.4 %collective-permute-start = (bf16[96,768]{1,0:T(8,128)(2,1)S(1)}, bf16[96,768]{1,0:T(8,128)(2,1)S(1)}, u32[]{:S(2)}, u32[]{:S(2)}) collective-permute-start(bf16[96,768]{1,0:T(8,128)(2,1)S(1)} %constant_dynamic-slice_fusion.11), channel_id=1, source_target_pairs={{0,2},{2,0},{4,6},{6,4},{1,3},{3,1},{5,7},{7,5},{8,10},{10,8},{12,... | collective-permute-start | bytes 442376 | tf_op jit(solution)/shard_map/ppermute | solution.py:787
  20.6 26.9 %collective-permute-start.3 = (bf16[2,112,576]{2,1,0:T(8,128)(2,1)S(1)}, bf16[2,112,576]{2,1,0:T(8,128)(2,1)S(1)}, u32[]{:S(2)}, u32[]{:S(2)}) collective-permute-start(bf16[2,112,576]{2,1,0:T(8,128)(2,1)S(1)} %pad_maximum_fusion.4), channel_id=1, source_target_pairs={{0,4},{2,6},{4,0},{6,2},{1,5},{3,7},{5,1},{7,3},{8,12},{10,14},{12... | collective-permute-start | bytes 774152 | tf_op jit(solution)/shard_map/ppermute | solution.py:787
  24.4 27.5 %collective-permute-start.1 = (bf16[2,96,768]{2,1,0:T(8,128)(2,1)S(1)}, bf16[2,96,768]{2,1,0:T(8,128)(2,1)S(1)}, u32[]{:S(2)}, u32[]{:S(2)}) collective-permute-start(bf16[2,96,768]{2,1,0:T(8,128)(2,1)S(1)} %pad_maximum_fusion.3), channel_id=1, source_target_pairs={{0,4},{2,6},{4,0},{6,2},{1,5},{3,7},{5,1},{7,3},{8,12},{10,14},{12... | collective-permute-start | bytes 884744 | tf_op jit(solution)/shard_map/ppermute | solution.py:787
  26.9 25.0 %collective-permute-start.4 = (bf16[256,768]{1,0:T(8,128)(2,1)S(1)}, bf16[256,768]{1,0:T(8,128)(2,1)S(1)}, u32[]{:S(2)}, u32[]{:S(2)}) collective-permute-start(bf16[256,768]{1,0:T(8,128)(2,1)S(1)} %bitcast.51), channel_id=1, source_target_pairs={{0,8},{8,0},{16,24},{24,16},{1,9},{9,1},{17,25},{25,17},{2,10},{10... | collective-permute-start | bytes 1179656 | tf_op jit(solution)/shard_map/ppermute | solution.py:781
  28.4 23.6 %collective-permute-start.5 = (bf16[256,768]{1,0:T(8,128)(2,1)S(1)}, bf16[256,768]{1,0:T(8,128)(2,1)S(1)}, u32[]{:S(2)}, u32[]{:S(2)}) collective-permute-start(bf16[256,768]{1,0:T(8,128)(2,1)S(1)} %bitcast.52), channel_id=1, source_target_pairs={{0,16},{8,24},{16,0},{24,8},{1,17},{9,25},{17,1},{25,9},{2,18},{10... | collective-permute-start | bytes 1179656 | tf_op jit(solution)/shard_map/ppermute | solution.py:781
  29.9 22.1 %collective-permute-start.6 = (bf16[256,768]{1,0:T(8,128)(2,1)S(1)}, bf16[256,768]{1,0:T(8,128)(2,1)S(1)}, u32[]{:S(2)}, u32[]{:S(2)}) collective-permute-start(bf16[256,768]{1,0:T(8,128)(2,1)S(1)} %bitcast.53), channel_id=1, source_target_pairs={{0,24},{8,16},{16,8},{24,0},{1,25},{9,17},{17,9},{25,1},{2,26},{10... | collective-permute-start | bytes 1179656 | tf_op jit(solution)/shard_map/ppermute | solution.py:781
  47.6 9.3 %copy-start.9 = (bf16[4,112,576]{2,1,0:T(8,128)(2,1)}, bf16[4,112,576]{2,1,0:T(8,128)(2,1)S(1)}, u32[]{:S(2)}) copy-start(bf16[4,112,576]{2,1,0:T(8,128)(2,1)S(1)} %pad_maximum_fusion.2.own) | copy-start | bytes 1548292
  52.0 4.9 %collective-permute-start.7 = (bf16[4,112,576]{2,1,0:T(8,128)(2,1)S(1)}, bf16[4,112,576]{2,1,0:T(8,128)(2,1)S(1)}, u32[]{:S(2)}, u32[]{:S(2)}) collective-permute-start(bf16[4,112,576]{2,1,0:T(8,128)(2,1)S(1)} %pad_maximum_fusion.2.own), channel_id=1, source_target_pairs={{0,1},{1,0},{2,3},{3,2},{4,5},{5,4},{6,7},{7,6},{8,9},{9,8},{10,11... | collective-permute-start | bytes 1548296 | tf_op jit(solution)/shard_map/ppermute | solution.py:784
  52.0 21.9 %collective-permute-start.11 = (bf16[4,96,768]{2,1,0:T(8,128)(2,1)S(1)}, bf16[4,96,768]{2,1,0:T(8,128)(2,1)}, u32[]{:S(2)}, u32[]{:S(2)}) collective-permute-start(bf16[4,96,768]{2,1,0:T(8,128)(2,1)S(1)} %pad_maximum_fusion.1), channel_id=1, source_target_pairs={{0,8},{8,0},{16,24},{24,16},{1,9},{9,1},{17,25},{25,17},{2,10},{10... | collective-permute-start | bytes 1769480 | tf_op jit(solution)/shard_map/ppermute | solution.py:781
  53.4 20.5 %collective-permute-start.12 = (bf16[4,96,768]{2,1,0:T(8,128)(2,1)S(1)}, bf16[4,96,768]{2,1,0:T(8,128)(2,1)}, u32[]{:S(2)}, u32[]{:S(2)}) collective-permute-start(bf16[4,96,768]{2,1,0:T(8,128)(2,1)S(1)} %pad_maximum_fusion.1), channel_id=1, source_target_pairs={{0,16},{8,24},{16,0},{24,8},{1,17},{9,25},{17,1},{25,9},{2,18},{10... | collective-permute-start | bytes 1769480 | tf_op jit(solution)/shard_map/ppermute | solution.py:781
  55.0 33.2 %collective-permute-start.13 = (bf16[4,96,768]{2,1,0:T(8,128)(2,1)S(1)}, bf16[4,96,768]{2,1,0:T(8,128)(2,1)}, u32[]{:S(2)}, u32[]{:S(2)}) collective-permute-start(bf16[4,96,768]{2,1,0:T(8,128)(2,1)S(1)} %pad_maximum_fusion.1), channel_id=1, source_target_pairs={{0,24},{8,16},{16,8},{24,0},{1,25},{9,17},{17,9},{25,1},{2,26},{10... | collective-permute-start | bytes 1769480 | tf_op jit(solution)/shard_map/ppermute | solution.py:781
  89.9 23.3 %copy-start.2 = (bf16[4,4,96,768]{3,2,1,0:T(8,128)(2,1)}, bf16[4,4,96,768]{3,2,1,0:T(8,128)(2,1)S(1)}, u32[]{:S(2)}) copy-start(bf16[4,4,96,768]{3,2,1,0:T(8,128)(2,1)S(1)} %pad_maximum_fusion.own_down) | copy-start | bytes 7077892
  89.9 13.8 %collective-permute-start.14 = (bf16[4,4,96,768]{3,2,1,0:T(8,128)(2,1)S(1)}, bf16[4,4,96,768]{3,2,1,0:T(8,128)(2,1)}, u32[]{:S(2)}, u32[]{:S(2)}) collective-permute-start(bf16[4,4,96,768]{3,2,1,0:T(8,128)(2,1)S(1)} %pad_maximum_fusion.own_down), channel_id=1, source_target_pairs={{0,1},{1,0},{2,3},{3,2},{4,5},{5,4},{6,7},{7,6},{8,9},{9,8},{10,11... | collective-permute-start | bytes 7077896 | tf_op jit(solution)/shard_map/ppermute | solution.py:784
  90.9 10.2 %collective-permute-start.10 = (bf16[256,192]{1,0:T(8,128)(2,1)}, bf16[256,192]{1,0:T(8,128)(2,1)S(1)}, u32[]{:S(2)}, u32[]{:S(2)}) collective-permute-start(bf16[256,192]{1,0:T(8,128)(2,1)} %get-tuple-element.91), channel_id=1, source_target_pairs={{0,24},{8,16},{16,8},{24,0},{1,25},{9,17},{17,9},{25,1},{2,26},{10... | collective-permute-start | bytes 294920 | tf_op jit(solution)/shard_map/ppermute | solution.py:781
  93.5 9.4 %collective-permute-start.8 = (bf16[256,192]{1,0:T(8,128)(2,1)}, bf16[256,192]{1,0:T(8,128)(2,1)S(1)}, u32[]{:S(2)}, u32[]{:S(2)}) collective-permute-start(bf16[256,192]{1,0:T(8,128)(2,1)} %get-tuple-element.89), channel_id=1, source_target_pairs={{0,8},{8,0},{16,24},{24,16},{1,9},{9,1},{17,25},{25,17},{2,10},{10... | collective-permute-start | bytes 294920 | tf_op jit(solution)/shard_map/ppermute | solution.py:781
  93.5 10.2 %collective-permute-start.9 = (bf16[256,192]{1,0:T(8,128)(2,1)}, bf16[256,192]{1,0:T(8,128)(2,1)S(1)}, u32[]{:S(2)}, u32[]{:S(2)}) collective-permute-start(bf16[256,192]{1,0:T(8,128)(2,1)} %get-tuple-element.90), channel_id=1, source_target_pairs={{0,16},{8,24},{16,0},{24,8},{1,17},{9,25},{17,1},{25,9},{2,18},{10... | collective-permute-start | bytes 294920 | tf_op jit(solution)/shard_map/ppermute | solution.py:781
  101.1 12.1 %copy-start.21 = (bf16[256,192]{1,0:T(8,128)(2,1)}, bf16[256,192]{1,0:T(8,128)(2,1)S(1)}, u32[]{:S(2)}) copy-start(bf16[256,192]{1,0:T(8,128)(2,1)S(1)} %collective-permute-done.10.x3) | copy-start | bytes 294916
  102.9 10.3 %copy-start.22 = (bf16[256,192]{1,0:T(8,128)(2,1)}, bf16[256,192]{1,0:T(8,128)(2,1)S(1)}, u32[]{:S(2)}) copy-start(bf16[256,192]{1,0:T(8,128)(2,1)S(1)} %collective-permute-done.8.x1) | copy-start | bytes 294916
  103.7 9.5 %copy-start.23 = (bf16[256,192]{1,0:T(8,128)(2,1)}, bf16[256,192]{1,0:T(8,128)(2,1)S(1)}, u32[]{:S(2)}) copy-start(bf16[256,192]{1,0:T(8,128)(2,1)S(1)} %collective-permute-done.9.x2) | copy-start | bytes 294916
  128.7 10.1 %collective-permute-start.15 = (bf16[256,5760]{1,0:T(8,128)(2,1)}, bf16[256,5760]{1,0:T(8,128)(2,1)S(1)}, u32[]{:S(2)}, u32[]{:S(2)}) collective-permute-start(bf16[256,5760]{1,0:T(8,128)(2,1)} %get-tuple-element.102), channel_id=1, source_target_pairs={{0,1},{1,0},{2,3},{3,2},{4,5},{5,4},{6,7},{7,6},{8,9},{9,8},{10,11... | collective-permute-start | bytes 8847368 | tf_op jit(solution)/shard_map/ppermute | solution.py:784
  129.0 6.4 %collective-permute-start.16 = (bf16[256,192]{1,0:T(8,128)(2,1)}, bf16[256,192]{1,0:T(8,128)(2,1)S(1)}, u32[]{:S(2)}, u32[]{:S(2)}) collective-permute-start(bf16[256,192]{1,0:T(8,128)(2,1)} %get-tuple-element.103), channel_id=1, source_target_pairs={{0,8},{8,0},{16,24},{24,16},{1,9},{9,1},{17,25},{25,17},{2,10},{10... | collective-permute-start | bytes 294920 | tf_op jit(solution)/shard_map/ppermute | solution.py:781
  130.4 8.4 %collective-permute-start.17 = (bf16[256,192]{1,0:T(8,128)(2,1)}, bf16[256,192]{1,0:T(8,128)(2,1)S(1)}, u32[]{:S(2)}, u32[]{:S(2)}) collective-permute-start(bf16[256,192]{1,0:T(8,128)(2,1)} %get-tuple-element.104), channel_id=1, source_target_pairs={{0,16},{8,24},{16,0},{24,8},{1,17},{9,25},{17,1},{25,9},{2,18},{10... | collective-permute-start | bytes 294920 | tf_op jit(solution)/shard_map/ppermute | solution.py:781
  130.4 8.4 %collective-permute-start.18 = (bf16[256,192]{1,0:T(8,128)(2,1)}, bf16[256,192]{1,0:T(8,128)(2,1)S(1)}, u32[]{:S(2)}, u32[]{:S(2)}) collective-permute-start(bf16[256,192]{1,0:T(8,128)(2,1)} %get-tuple-element.105), channel_id=1, source_target_pairs={{0,24},{8,16},{16,8},{24,0},{1,25},{9,17},{17,9},{25,1},{2,26},{10... | collective-permute-start | bytes 294920 | tf_op jit(solution)/shard_map/ppermute | solution.py:781
  147.1 33.5 %collective-permute-start.20 = (bf16[2,4,240,384]{3,2,1,0:T(8,128)(2,1)}, bf16[2,4,240,384]{3,2,1,0:T(8,128)(2,1)S(1)}, u32[]{:S(2)}, u32[]{:S(2)}) collective-permute-start(bf16[2,4,240,384]{3,2,1,0:T(8,128)(2,1)} %get-tuple-element.123), channel_id=1, source_target_pairs={{0,16},{8,24},{16,0},{24,8},{1,17},{9,25},{17,1},{25,9},{2,18},{10... | collective-permute-start | bytes 4423688 | tf_op jit(solution)/shard_map/ppermute | solution.py:781
  153.3 31.9 %collective-permute-start.19 = (bf16[2,4,96,768]{3,2,1,0:T(8,128)(2,1)}, bf16[2,4,96,768]{3,2,1,0:T(8,128)(2,1)S(1)}, u32[]{:S(2)}, u32[]{:S(2)}) collective-permute-start(bf16[2,4,96,768]{3,2,1,0:T(8,128)(2,1)} %get-tuple-element.120), channel_id=1, source_target_pairs={{0,8},{8,0},{16,24},{24,16},{1,9},{9,1},{17,25},{25,17},{2,10},{10... | collective-permute-start | bytes 3538952 | tf_op jit(solution)/shard_map/ppermute | solution.py:781
  184.9 23.1 %collective-permute-start.23 = (bf16[4,240,384]{2,1,0:T(8,128)(2,1)}, bf16[4,240,384]{2,1,0:T(8,128)(2,1)S(1)}, u32[]{:S(2)}, u32[]{:S(2)}) collective-permute-start(bf16[4,240,384]{2,1,0:T(8,128)(2,1)} %get-tuple-element.131), channel_id=1, source_target_pairs={{0,8},{8,0},{16,24},{24,16},{1,9},{9,1},{17,25},{25,17},{2,10},{10... | collective-permute-start | bytes 2211848 | tf_op jit(solution)/shard_map/ppermute | solution.py:781
  185.2 5.6 %collective-permute-start.21 = (bf16[4,96,576]{2,1,0:T(8,128)(2,1)}, bf16[4,96,576]{2,1,0:T(8,128)(2,1)}, u32[]{:S(2)}, u32[]{:S(2)}) collective-permute-start(bf16[4,96,576]{2,1,0:T(8,128)(2,1)} %get-tuple-element.126), channel_id=1, source_target_pairs={{0,1},{1,0},{2,3},{3,2},{4,5},{5,4},{6,7},{7,6},{8,9},{9,8},{10,11... | collective-permute-start | bytes 1327112 | tf_op jit(solution)/shard_map/ppermute | solution.py:784
  189.0 16.0 %collective-permute-start.24 = (bf16[4,96,768]{2,1,0:T(8,128)(2,1)}, bf16[4,96,768]{2,1,0:T(8,128)(2,1)S(1)}, u32[]{:S(2)}, u32[]{:S(2)}) collective-permute-start(bf16[4,96,768]{2,1,0:T(8,128)(2,1)} %get-tuple-element.134), channel_id=1, source_target_pairs={{0,16},{8,24},{16,0},{24,8},{1,17},{9,25},{17,1},{25,9},{2,18},{10... | collective-permute-start | bytes 1769480 | tf_op jit(solution)/shard_map/ppermute | solution.py:781
  192.8 8.6 %collective-permute-start.22 = (bf16[2,96,576]{2,1,0:T(8,128)(2,1)}, bf16[2,96,576]{2,1,0:T(8,128)(2,1)S(1)}, u32[]{:S(2)}, u32[]{:S(2)}) collective-permute-start(bf16[2,96,576]{2,1,0:T(8,128)(2,1)} %get-tuple-element.128), channel_id=1, source_target_pairs={{0,2},{2,0},{4,6},{6,4},{1,3},{3,1},{5,7},{7,5},{8,10},{10,8},{12,... | collective-permute-start | bytes 663560 | tf_op jit(solution)/shard_map/ppermute | solution.py:787
  202.1 12.5 %copy-start.33 = (f32[1,3072]{1,0:T(1,128)S(1)}, f32[1,3072]{1,0:T(1,128)}, u32[]{:S(2)}) copy-start(f32[1,3072]{1,0:T(1,128)} %get-tuple-element.139) | copy-start | bytes 36868
  202.1 13.2 %copy-start.34 = (f32[1,576]{1,0:T(1,128)S(1)}, f32[1,576]{1,0:T(1,128)}, u32[]{:S(2)}) copy-start(f32[1,576]{1,0:T(1,128)} %get-tuple-element.140) | copy-start | bytes 6916
  202.1 13.7 %copy-start.32 = (f32[8,768]{1,0:T(8,128)S(1)}, f32[8,768]{1,0:T(8,128)}, u32[]{:S(2)}) copy-start(f32[8,768]{1,0:T(8,128)} %get-tuple-element.138) | copy-start | bytes 73732
  207.9 7.7 %copy-start.45 = (bf16[2,96,768]{2,1,0:T(8,128)(2,1)S(1)}, bf16[2,96,768]{2,1,0:T(8,128)(2,1)}, u32[]{:S(2)}) copy-start(bf16[2,96,768]{2,1,0:T(8,128)(2,1)} %get-tuple-element.142) | copy-start | bytes 884740
  207.9 21.8 %copy-start.46 = (bf16[96,576]{1,0:T(8,128)(2,1)S(1)}, bf16[96,576]{1,0:T(8,128)(2,1)}, u32[]{:S(2)}) copy-start(bf16[96,576]{1,0:T(8,128)(2,1)} %get-tuple-element.137) | copy-start | bytes 331780
  211.1 12.6 %collective-permute-start.36 = (bf16[2,240,384]{2,1,0:T(8,128)(2,1)}, bf16[2,240,384]{2,1,0:T(8,128)(2,1)S(1)}, u32[]{:S(2)}, u32[]{:S(2)}) collective-permute-start(bf16[2,240,384]{2,1,0:T(8,128)(2,1)} %get-tuple-element.145), channel_id=1, source_target_pairs={{0,2},{2,0},{4,6},{6,4},{1,3},{3,1},{5,7},{7,5},{8,10},{10,8},{12,... | collective-permute-start | bytes 1105928 | tf_op jit(solution)/shard_map/ppermute | solution.py:787
  215.7 32.1 %collective-permute-start.34 = (bf16[2,96,768]{2,1,0:T(8,128)(2,1)S(1)}, bf16[2,96,768]{2,1,0:T(8,128)(2,1)S(1)}, u32[]{:S(2)}, u32[]{:S(2)}) collective-permute-start(bf16[2,96,768]{2,1,0:T(8,128)(2,1)S(1)} %copy-done.45), channel_id=1, source_target_pairs={{0,2},{2,0},{4,6},{6,4},{1,3},{3,1},{5,7},{7,5},{8,10},{10,8},{12,... | collective-permute-start | bytes 884744 | tf_op jit(solution)/shard_map/ppermute | solution.py:787
  215.8 12.9 %collective-permute-start.29 = (f32[12,768]{1,0:T(8,128)S(1)}, f32[12,768]{1,0:T(8,128)S(1)}, u32[]{:S(2)}, u32[]{:S(2)}) collective-permute-start(f32[12,768]{1,0:T(8,128)S(1)} %pad_maximum_fusion.7), channel_id=1, source_target_pairs={{0,1},{1,0},{2,3},{3,2},{4,5},{5,4},{6,7},{7,6},{8,9},{9,8},{10,11... | collective-permute-start | bytes 110600 | tf_op jit(solution)/shard_map/ppermute | solution.py:784
  226.3 26.2 %collective-permute-start.37 = (bf16[240,384]{1,0:T(8,128)(2,1)}, bf16[240,384]{1,0:T(8,128)(2,1)S(1)}, u32[]{:S(2)}, u32[]{:S(2)}) collective-permute-start(bf16[240,384]{1,0:T(8,128)(2,1)} %get-tuple-element.147), channel_id=1, source_target_pairs={{0,4},{2,6},{4,0},{6,2},{1,5},{3,7},{5,1},{7,3},{8,12},{10,14},{12... | collective-permute-start | bytes 552968 | tf_op jit(solution)/shard_map/ppermute | solution.py:787
  228.7 4.2 %collective-permute-start.30 = (f32[12,768]{1,0:T(8,128)S(1)}, f32[12,768]{1,0:T(8,128)S(1)}, u32[]{:S(2)}, u32[]{:S(2)}) collective-permute-start(f32[12,768]{1,0:T(8,128)S(1)} %add.68), channel_id=1, source_target_pairs={{0,8},{8,0},{16,24},{24,16},{1,9},{9,1},{17,25},{25,17},{2,10},{10... | collective-permute-start | bytes 110600 | tf_op jit(solution)/shard_map/ppermute | solution.py:781
  229.7 13.1 %collective-permute-start.25 = (bf16[96,576]{1,0:T(8,128)(2,1)S(1)}, bf16[96,576]{1,0:T(8,128)(2,1)S(1)}, u32[]{:S(2)}, u32[]{:S(2)}) collective-permute-start(bf16[96,576]{1,0:T(8,128)(2,1)S(1)} %copy-done.46), channel_id=1, source_target_pairs={{0,4},{2,6},{4,0},{6,2},{1,5},{3,7},{5,1},{7,3},{8,12},{10,14},{12... | collective-permute-start | bytes 331784 | tf_op jit(solution)/shard_map/ppermute | solution.py:787
  232.9 4.2 %collective-permute-start.31 = (f32[12,768]{1,0:T(8,128)S(1)}, f32[12,768]{1,0:T(8,128)S(1)}, u32[]{:S(2)}, u32[]{:S(2)}) collective-permute-start(f32[12,768]{1,0:T(8,128)S(1)} %add.69), channel_id=1, source_target_pairs={{0,16},{8,24},{16,0},{24,8},{1,17},{9,25},{17,1},{25,9},{2,18},{10... | collective-permute-start | bytes 110600 | tf_op jit(solution)/shard_map/ppermute | solution.py:781
  237.0 5.7 %collective-permute-start.32 = (f32[12,768]{1,0:T(8,128)S(1)}, f32[12,768]{1,0:T(8,128)S(1)}, u32[]{:S(2)}, u32[]{:S(2)}) collective-permute-start(f32[12,768]{1,0:T(8,128)S(1)} %add.70), channel_id=1, source_target_pairs={{0,2},{2,0},{4,6},{6,4},{1,3},{3,1},{5,7},{7,5},{8,10},{10,8},{12,... | collective-permute-start | bytes 110600 | tf_op jit(solution)/shard_map/ppermute | solution.py:787
  242.7 5.0 %collective-permute-start.33 = (f32[12,768]{1,0:T(8,128)S(1)}, f32[12,768]{1,0:T(8,128)S(1)}, u32[]{:S(2)}, u32[]{:S(2)}) collective-permute-start(f32[12,768]{1,0:T(8,128)S(1)} %add.71), channel_id=1, source_target_pairs={{0,4},{2,6},{4,0},{6,2},{1,5},{3,7},{5,1},{7,3},{8,12},{10,14},{12... | collective-permute-start | bytes 110600 | tf_op jit(solution)/shard_map/ppermute | solution.py:787
  245.1 21.6 %collective-permute-start.26 = (bf16[96,576]{1,0:T(8,128)(2,1)}, bf16[96,576]{1,0:T(8,128)(2,1)S(1)}, u32[]{:S(2)}, u32[]{:S(2)}) collective-permute-start(bf16[96,576]{1,0:T(8,128)(2,1)} %sum.1.b0), channel_id=1, source_target_pairs={{0,8},{8,0},{16,24},{24,16},{1,9},{9,1},{17,25},{25,17},{2,10},{10... | collective-permute-start | bytes 331784 | tf_op jit(solution)/shard_map/ppermute | solution.py:781
  246.3 22.4 %collective-permute-start.27 = (bf16[96,576]{1,0:T(8,128)(2,1)}, bf16[96,576]{1,0:T(8,128)(2,1)S(1)}, u32[]{:S(2)}, u32[]{:S(2)}) collective-permute-start(bf16[96,576]{1,0:T(8,128)(2,1)} %sum.1.b0), channel_id=1, source_target_pairs={{0,16},{8,24},{16,0},{24,8},{1,17},{9,25},{17,1},{25,9},{2,18},{10... | collective-permute-start | bytes 331784 | tf_op jit(solution)/shard_map/ppermute | solution.py:781
  247.8 41.0 %copy-start.6 = (f32[256,768]{1,0:T(8,128)S(1)}, f32[256,768]{1,0:T(8,128)}, u32[]{:S(2)}) copy-start(f32[256,768]{1,0:T(8,128)} %get-tuple-element.96) | copy-start | bytes 2359300
  250.3 7.8 %collective-permute-start.35 = (bf16[96,768]{1,0:T(8,128)(2,1)}, bf16[96,768]{1,0:T(8,128)(2,1)S(1)}, u32[]{:S(2)}, u32[]{:S(2)}) collective-permute-start(bf16[96,768]{1,0:T(8,128)(2,1)} %get-tuple-element.144), channel_id=1, source_target_pairs={{0,4},{2,6},{4,0},{6,2},{1,5},{3,7},{5,1},{7,3},{8,12},{10,14},{12... | collective-permute-start | bytes 442376 | tf_op jit(solution)/shard_map/ppermute | solution.py:787
  255.0 3.2 %collective-permute-start.38 = (bf16[144,384]{1,0:T(8,128)(2,1)}, bf16[144,384]{1,0:T(8,128)(2,1)S(1)}, u32[]{:S(2)}, u32[]{:S(2)}) collective-permute-start(bf16[144,384]{1,0:T(8,128)(2,1)} %get-tuple-element.149), channel_id=1, source_target_pairs={{0,1},{1,0},{2,3},{3,2},{4,5},{5,4},{6,7},{7,6},{8,9},{9,8},{10,11... | collective-permute-start | bytes 331784 | tf_op jit(solution)/shard_map/ppermute | solution.py:784
  260.8 23.4 %collective-permute-start.39 = (bf16[240,768]{1,0:T(8,128)(2,1)}, bf16[240,768]{1,0:T(8,128)(2,1)S(1)}, u32[]{:S(2)}, u32[]{:S(2)}) collective-permute-start(bf16[240,768]{1,0:T(8,128)(2,1)} %join.1.b0), channel_id=1, source_target_pairs={{0,8},{8,0},{16,24},{24,16},{1,9},{9,1},{17,25},{25,17},{2,10},{10... | collective-permute-start | bytes 1105928 | tf_op jit(solution)/shard_map/ppermute | solution.py:781
  261.8 22.4 %collective-permute-start.40 = (bf16[240,768]{1,0:T(8,128)(2,1)}, bf16[240,768]{1,0:T(8,128)(2,1)S(1)}, u32[]{:S(2)}, u32[]{:S(2)}) collective-permute-start(bf16[240,768]{1,0:T(8,128)(2,1)} %join.1.b0), channel_id=1, source_target_pairs={{0,16},{8,24},{16,0},{24,8},{1,17},{9,25},{17,1},{25,9},{2,18},{10... | collective-permute-start | bytes 1105928 | tf_op jit(solution)/shard_map/ppermute | solution.py:781
  262.7 21.5 %collective-permute-start.41 = (bf16[240,768]{1,0:T(8,128)(2,1)}, bf16[240,768]{1,0:T(8,128)(2,1)S(1)}, u32[]{:S(2)}, u32[]{:S(2)}) collective-permute-start(bf16[240,768]{1,0:T(8,128)(2,1)} %join.1.b0), channel_id=1, source_target_pairs={{0,24},{8,16},{16,8},{24,0},{1,25},{9,17},{17,9},{25,1},{2,26},{10... | collective-permute-start | bytes 1105928 | tf_op jit(solution)/shard_map/ppermute | solution.py:781
  266.7 14.6 %copy-start.27 = (bf16[96,576]{1,0:T(8,128)(2,1)}, bf16[96,576]{1,0:T(8,128)(2,1)S(1)}, u32[]{:S(2)}) copy-start(bf16[96,576]{1,0:T(8,128)(2,1)S(1)} %collective-permute-done.26.b1) | copy-start | bytes 331780
  266.7 14.6 %collective-permute-start.28 = (bf16[96,576]{1,0:T(8,128)(2,1)}, bf16[96,576]{1,0:T(8,128)(2,1)S(1)}, u32[]{:S(2)}, u32[]{:S(2)}) collective-permute-start(bf16[96,576]{1,0:T(8,128)(2,1)} %sum.1.b0), channel_id=1, source_target_pairs={{0,24},{8,16},{16,8},{24,0},{1,25},{9,17},{17,9},{25,1},{2,26},{10... | collective-permute-start | bytes 331784 | tf_op jit(solution)/shard_map/ppermute | solution.py:781
  268.7 12.5 %copy-start.28 = (bf16[96,576]{1,0:T(8,128)(2,1)}, bf16[96,576]{1,0:T(8,128)(2,1)S(1)}, u32[]{:S(2)}) copy-start(bf16[96,576]{1,0:T(8,128)(2,1)S(1)} %collective-permute-done.27.b2) | copy-start | bytes 331780
  (27 other events, 51.1 us)
Sparse Core Ops, SparseCore 0:
  11.6 101.5 all-gather.1
  211.3 31.1 reduce-scatter.1

commit v2 on v1

--- a/solution.py
+++ b/solution.py
@@ -455,21 +455,24 @@
     dqkv[:, head_width:] = jnp.concatenate([dk, dv], axis=1).astype(jnp.bfloat16)
 
 
-def grad_qkv_weight_kernel(sc, t0, t1, t2, t3, dqkv, keep, send, sums):
+def grad_qkv_weight_kernel(sc, t0, t1, t2, t3, dqkv, keep, send):
     core = sc[2]
     rows = t0.shape[0]
     total = None
     for j, block in enumerate((t0, t1, t2, t3)):
         part = dot_tn(block[...], dqkv[j * rows : (j + 1) * rows, :])
         total = part if total is None else total + part
-    sums[...] = jnp.sum(dqkv[...].astype(jnp.float32), axis=0, keepdims=True)
-    shard_rows = keep.shape[1]
+    sums = jnp.sum(dqkv[...].astype(jnp.float32), axis=0, keepdims=True)
+    sums = jnp.broadcast_to(sums, (16, sums.shape[1])).astype(jnp.bfloat16)
+    shard_rows = keep.shape[1] - 16
     low = total.astype(jnp.bfloat16)
     for z in range(keep.shape[0]):
         even = low[(2 * z) * shard_rows : (2 * z + 1) * shard_rows]
         odd = low[(2 * z + 1) * shard_rows : (2 * z + 2) * shard_rows]
-        keep[z] = jnp.where(core == 0, even, odd)
-        send[z] = jnp.where(core == 0, odd, even)
+        keep[z, :shard_rows] = jnp.where(core == 0, even, odd)
+        send[z, :shard_rows] = jnp.where(core == 0, odd, even)
+        keep[z, shard_rows:] = sums
+        send[z, shard_rows:] = sums
 
 
 def grad_tokens_kernel(sc, dqkv, weight, out):
@@ -647,11 +650,11 @@
             out[at, z] = part[place ^ j]
 
 
-def up_grad_kernel(sc, keep, got, near, far, part):
+def up_grad_kernel(sc, keep, got, vectors, near, far, part):
     place = sc[1]
     _, zs, block_rows, cols = near.shape
     quarter = part.shape[2]
-    pair_rows = block_rows - quarter
+    pair_rows = block_rows - quarter - 16
     width = zs * pair_rows
     at_norm = 2 * width + width
     at_up = at_norm + width
@@ -668,7 +671,8 @@
         total = total.astype(jnp.bfloat16)
         for z in range(zs):
             out[at, z, :pair_rows] = total[z * pair_rows : (z + 1) * pair_rows]
-            out[at, z, pair_rows:] = part[z, place ^ j]
+            out[at, z, pair_rows : pair_rows + quarter] = part[z, place ^ j]
+            out[at, z, pair_rows + quarter :] = vectors[z]
 
 
 def fold_kernel(near, got, mine, pass_on):
@@ -693,20 +697,21 @@
 
 def split_up_kernel(sc, e0, e1, keep, send, held):
     core = sc[2]
-    shard_rows = (keep.shape[0] * 2) // 3
+    shard_rows = ((keep.shape[0] - 16) * 2) // 3
     held[...] = block_sum((e0, e1)).astype(jnp.bfloat16)
     for ref, side in ((keep, core), (send, 1 - core)):
         ref[:shard_rows] = held[pl.ds(pl.multiple_of(side * shard_rows, 16), shard_rows), :]
         ref[shard_rows:] = held[2 * shard_rows :, :]
 
 
-def join_kernel(sc, e0, e1, keep, got, out):
+def join_kernel(sc, e0, e1, keep, got, out, vectors):
     core = sc[2]
     shard_rows = e0.shape[0]
     cols = keep.shape[1]
     out[:shard_rows] = block_sum((e0, e1)).astype(jnp.bfloat16)
     for ref, side in ((keep, core), (got, 1 - core)):
-        out[shard_rows:, pl.ds(pl.multiple_of(side * cols, 128), cols)] = ref[...]
+        out[shard_rows:, pl.ds(pl.multiple_of(side * cols, 128), cols)] = ref[:-16]
+    vectors[...] = keep[-16:].astype(jnp.float32) + got[-16:].astype(jnp.float32)
 
 
 def finish_kernel(sc, b0, b1, b2, b3, down, up, out):
@@ -734,15 +739,23 @@
     out[...] = block_sum((e0, e1)).astype(out.dtype)
 
 
-def finish_qkv_kernel(sc, b0, b1, b2, b3, out, held):
-    place = sc[1]
+def finish_qkv_kernel(sc, b0, b1, b2, b3, out, q_out, v_out, held):
+    place, core, level = sc[1], sc[2], sc[3]
+    shard_rows = out.shape[0]
     head_width = b0.shape[1] // 3
     for j, ref in enumerate((b0, b1, b2, b3)):
         held[place ^ j] = ref[...].astype(jnp.float32)
     for part in range(3):
         for s in range(4):
             at = (part * 4 + s) * head_width
-            out[:, at : at + head_width] = held[s, :, part * head_width : (part + 1) * head_width]
+            out[:, at : at + head_width] = held[
+                s, :shard_rows, part * head_width : (part + 1) * head_width
+            ]
+    row = held[level, shard_rows : shard_rows + 1, :]
+    for ref, at in ((q_out, 0), (v_out, 2 * head_width)):
+        ref[...] = jnp.where(
+            core == 0, row[:, at : at + shard_rows], row[:, at + shard_rows : at + 2 * shard_rows]
+        )
 
 
 def fast_body(
@@ -918,13 +931,18 @@
         got,
         scratch=[pltpu.VMEM((4, shard_rows, width), bf16)],
     )
-    block_rows = 2 * shard_rows + shard_rows // 2
+    block_rows = 2 * shard_rows + shard_rows // 2 + 16
+    six_sets = sums[:6].reshape(6, zs, 2 * shard_rows).transpose(1, 0, 2)
+    up_sets = up_sums.reshape(zs, 4, 2 * shard_rows)
+    vector_rows = jnp.concatenate([six_sets, up_sets], axis=1).reshape(zs, 5, quad)
+    vector_rows = jnp.pad(vector_rows.astype(bf16), ((0, 0), (0, 11), (0, 0)))
     u_near, u_far = call(
         up_grad_kernel,
         4,
         [struct((2, zs, block_rows, quad))] * 2,
         keep,
         got,
+        vector_rows,
         scratch=[pltpu.VMEM((zs, 4, shard_rows // 2, quad), bf16)],
     )
     d_got = across(d_far, 1)
@@ -944,17 +962,17 @@
             pltpu.VMEM((4, rows, head_width), bf16),
         ],
     )(sc, qkv, ctx_t, lse, y0, g1, g2, g3)
-    q_keep, q_send, q_sums = pl.pallas_call(
+    q_rows = shard_rows + 16
+    q_keep, q_send = pl.pallas_call(
         grad_qkv_weight_kernel,
         name="grad_qkv_weight",
         cost_estimate=work(4),
         out_shape=(
-            struct((zs, shard_rows, 3 * head_width)),
-            struct((zs, shard_rows, 3 * head_width)),
-            struct((1, 3 * head_width), f32),
+            struct((zs, q_rows, 3 * head_width)),
+            struct((zs, q_rows, 3 * head_width)),
         ),
         in_specs=[smem_spec()] + vmem_specs(5),
-        out_specs=tuple(vmem_specs(3)),
+        out_specs=tuple(vmem_specs(2)),
     )(sc, token, t1, t2, t3, dqkv)
     d_near, u_near, q_keep = lax.optimization_barrier((d_near, u_near, q_keep))
     d_mine, d_pass = call(
@@ -973,7 +991,7 @@
         full_qkv,
     )
     q_near, q_far = call(
-        level_fold_kernel, 1, [struct((2, shard_rows, 3 * head_width))] * 2, q_keep, q_got
+        level_fold_kernel, 1, [struct((2, q_rows, 3 * head_width))] * 2, q_keep, q_got
     )
 
     def level_sum(near, far, shape):
@@ -982,9 +1000,9 @@
         )
         return mine, level_across(pass_on, 2)
 
-    q_mine, q_last = level_sum(q_near, q_far, (shard_rows, 3 * head_width))
+    q_mine, q_last = level_sum(q_near, q_far, (q_rows, 3 * head_width))
     (q_part,) = call(
-        sum_kernel, 1, [struct((shard_rows, 3 * head_width))], q_mine, q_last, scalars=False
+        sum_kernel, 1, [struct((q_rows, 3 * head_width))], q_mine, q_last, scalars=False
     )
 
     def seq_sum(mine, pass_on, shape, step):
@@ -1005,7 +1023,7 @@
     )
     d_parts = level_sum(d_near, d_far, (shard_rows, width))
     u_parts = level_sum(u_near, u_far, (block_rows, quad))
-    half_rows = shard_rows + shard_rows // 2
+    half_rows = shard_rows + shard_rows // 2 + 16
     u_keep, u_send = call(
         split_up_kernel,
         1,
@@ -1013,14 +1031,20 @@
         *u_parts,
         scratch=[pltpu.VMEM((block_rows, quad), bf16)],
     )
-    (joined,) = call(
+    joined, vector_totals = call(
         join_kernel,
         1,
-        [struct((shard_rows + half_rows, width))],
+        [struct((shard_rows + half_rows - 16, width)), struct((16, quad), f32)],
         *d_parts,
         u_keep,
         partner(u_send),
     )
+    q_others = [across(q_part, j) for j in (1, 2, 3)]
+    joined, q_others = lax.optimization_barrier((joined, q_others))
+    six = lax.dynamic_index_in_dim(
+        vector_totals[:3].reshape(6, 2, shard_rows), core, axis=1, keepdims=False
+    )
+    result_up_bias = lax.dynamic_index_in_dim(vector_totals[3:5], core, axis=0, keepdims=False)
     result_down, result_up, result_out = call(
         finish_kernel,
         2,
@@ -1032,56 +1056,32 @@
         joined,
         *[across(joined, j) for j in (1, 2, 3)],
     )
-    (result_qkv,) = call(
+    result_qkv, result_q_bias, result_v_bias = call(
         finish_qkv_kernel,
         1,
-        [struct((shard_rows, 3 * width), f32)],
+        [struct((shard_rows, 3 * width), f32)] + [struct((1, shard_rows), f32)] * 2,
         q_part,
-        *[across(q_part, j) for j in (1, 2, 3)],
-        scratch=[pltpu.VMEM((4, shard_rows, 3 * head_width), f32)],
+        *q_others,
+        scratch=[pltpu.VMEM((4, q_rows, 3 * head_width), f32)],
     )
     grad_tokens = (grad_one + token_sum.astype(f32)).astype(bf16)
-
-    q_row = lax.dynamic_update_slice(
-        jnp.zeros((1, width), f32), q_sums[:, :head_width], (0, place * head_width)
-    )
-    v_row = lax.dynamic_update_slice(
-        jnp.zeros((1, width), f32), q_sums[:, 2 * head_width :], (0, place * head_width)
-    )
-
-    def everywhere(value):
-        value = value + partner(value)
-        value = value + across(value, 1)
-        value = value + across(value, 2)
-        value = value + level_across(value, 1)
-        value = value + level_across(value, 2)
-        return value
-
-    vector_sums = jnp.concatenate([sums[:6], up_sums.reshape(4, width), q_row, v_row], axis=0)
-    vector_sums, _ = lax.optimization_barrier((vector_sums, q_mine))
-    early = everywhere(vector_sums)
-    shard = 2 * lax.axis_index("z") + core
-
-    def owned(vector):
-        size = vector.shape[0] // (2 * zs)
-        return lax.dynamic_slice(vector, (shard * size,), (size,))
 
     return (
         output[None],
         grad_tokens[None],
         result_qkv,
-        owned(early[10]),
-        owned(early[11]),
+        result_q_bias[0],
+        result_v_bias[0],
         result_out,
-        owned(early[0]),
-        owned(early[1]),
-        owned(early[2]),
+        six[0],
+        six[1],
+        six[2],
         result_up,
-        owned(early[6:10].reshape(-1)),
+        result_up_bias,
         result_down,
-        owned(early[5]),
-        owned(early[3]),
-        owned(early[4]),
+        six[5],
+        six[3],
+        six[4],
     )
 
 

time: 298 us -> 295 us (0.990)
  waiting for transfers between devices: 114 us -> 107 us
  local copies, waits for them, and re-layouts: 24.3 us -> 28 us
  starting transfers between devices: 47.4 us -> 44.1 us
    ppermute x24 -> x22, waiting for transfers between devices: 59.2 us -> 53.3 us  [across(): return lax.ppermute(value, 'seq', [(i, i ^ step) for i in range(4)])]
    ppermute x24 -> x22, starting transfers between devices: 27.4 us -> 25.5 us  [across(): return lax.ppermute(value, 'seq', [(i, i ^ step) for i in range(4)])]
    unnamed x97 -> x85, local copies, waits for them, and re-layouts: 14.3 us -> 12.9 us
    ppermute x12 -> x10, starting transfers between devices: 19.3 us -> 18.1 us  [level_across(): return lax.ppermute(value, 'z', [(i, i ^ step) for i in range(4)])]
    ppermute x12 -> x10, waiting for transfers between devices: 45.7 us -> 44.6 us  [level_across(): return lax.ppermute(value, 'z', [(i, i ^ step) for i in range(4)])]
  transfers between devices with their start and end apart: 44 -> 39, of which waited for: 22 -> 21; matrix products, arithmetic and copies ran while one was open for 4% -> 7% of each run, Pallas kernels for 22% -> 23%
where the time goes in v2:
time: 295 us; the launch traced here: 294 us
  waiting for transfers between devices  107 us (36%)
  Pallas kernels  91 us (31%)
  starting transfers between devices  44.1 us (15%)
  local copies, waits for them, and re-layouts  28 us (9%)
  between operations  15.1 us (5%)
  other arithmetic  7.86 us (3%)
    ppermute x22, waiting for transfers between devices, across(): return lax.ppermute(value, 'seq', [(i, i ^ step) for i in range(4)])  53.3 us
    pallas_call x16, Pallas kernels, call(): pl.pallas_call(kernel, name=kernel.__name__.replace('_kernel', ''), cost_...  45.5 us
    ppermute x10, waiting for transfers between devices, level_across(): return lax.ppermute(value, 'z', [(i, i ^ step) for i in range(4)])  44.6 us
    ppermute x22, starting transfers between devices, across(): return lax.ppermute(value, 'seq', [(i, i ^ step) for i in range(4)])  25.5 us
    ppermute x10, starting transfers between devices, level_across(): return lax.ppermute(value, 'z', [(i, i ^ step) for i in range(4)])  18.1 us
    pallas_call x1, Pallas kernels, fast_body(): pl.pallas_call(middle_kernel, name='middle', cost_estimate=work(15), out_...  15.5 us
    pallas_call x1, Pallas kernels, fast_body(): pl.pallas_call(attend_forward_kernel, name='attend_forward', cost_estimat...  13.1 us
    unnamed x85, local copies, waits for them, and re-layouts  12.9 us
  transfers between devices with their start and end apart: 39, of which 21 were waited for; matrix products, arithmetic and copies ran while one was open for 7% of the time, Pallas kernels for 23%

profile of v2, /device:TPU:0, one launch (start us, length us, event | category | flops | bytes accessed | tf_op | source)
XLA Modules:
  0.0 293.5 jit_solution(11329457356834765112)
XLA Ops:
  9.9 1.7 reshape.89
  12.9 3.0 %collective-permute-start.2 = (bf16[112,576]{1,0:T(8,128)(2,1)S(1)}, bf16[112,576]{1,0:T(8,128)(2,1)S(1)}, u32[]{:S(2)}, u32[]{:S(2)}) collective-permute-start(bf16[112,576]{1,0:T(8,128)(2,1)S(1)} %pad_maximum_fusion.6), channel_id=1, source_target_pairs={{0,2},{2,0},{4,6},{6,4},{1,3},{3,1},{5,7},{7,5},{8,10},{10,8},{12,... | collective-permute-start | bytes 387080 | tf_op jit(solution)/shard_map/ppermute | solution.py:800
  16.1 4.4 %collective-permute-done.2 = bf16[112,576]{1,0:T(8,128)(2,1)S(1)} collective-permute-done((bf16[112,576]{1,0:T(8,128)(2,1)S(1)}, bf16[112,576]{1,0:T(8,128)(2,1)S(1)}, u32[]{:S(2)}, u32[]{:S(2)}) %collective-permute-start.2) | collective-permute-done | bytes 129056 | tf_op jit(solution)/shard_map/ppermute | solution.py:800
  20.6 3.1 %collective-permute-start.3 = (bf16[2,112,576]{2,1,0:T(8,128)(2,1)S(1)}, bf16[2,112,576]{2,1,0:T(8,128)(2,1)S(1)}, u32[]{:S(2)}, u32[]{:S(2)}) collective-permute-start(bf16[2,112,576]{2,1,0:T(8,128)(2,1)S(1)} %pad_maximum_fusion.4), channel_id=1, source_target_pairs={{0,4},{2,6},{4,0},{6,2},{1,5},{3,7},{5,1},{7,3},{8,12},{10,14},{12... | collective-permute-start | bytes 774152 | tf_op jit(solution)/shard_map/ppermute | solution.py:800
  24.4 2.5 collective-permute-start.1
  26.9 1.5 collective-permute-start.4
  28.4 1.5 collective-permute-start.5
  30.3 17.2 %collective-permute-done.3 = bf16[2,112,576]{2,1,0:T(8,128)(2,1)S(1)} collective-permute-done((bf16[2,112,576]{2,1,0:T(8,128)(2,1)S(1)}, bf16[2,112,576]{2,1,0:T(8,128)(2,1)S(1)}, u32[]{:S(2)}, u32[]{:S(2)}) %collective-permute-start.3) | collective-permute-done | bytes 258080 | tf_op jit(solution)/shard_map/ppermute | solution.py:800
  47.6 4.2 %collective-permute-done.1 = bf16[2,96,768]{2,1,0:T(8,128)(2,1)S(1)} collective-permute-done((bf16[2,96,768]{2,1,0:T(8,128)(2,1)S(1)}, bf16[2,96,768]{2,1,0:T(8,128)(2,1)S(1)}, u32[]{:S(2)}, u32[]{:S(2)}) %collective-permute-start.1) | collective-permute-done | bytes 294944 | tf_op jit(solution)/shard_map/ppermute | solution.py:800
  52.0 1.4 collective-permute-start.11
  53.4 1.5 collective-permute-start.12
  57.7 13.1 %attend_forward.1 = (bf16[1024,576]{1,0:T(8,128)(2,1)}, f32[192,1024]{1,0:T(8,128)}, bf16[256,192]{1,0:T(8,128)(2,1)}, bf16[256,192]{1,0:T(8,128)(2,1)}, bf16[25...) custom-call(s32[4]{0:T(128)} %pad_add_fusion.sc, ...), custom_call_target="tpu_custom_call" | custom-call | flops 1170000000 | bytes 3900000 | tf_op jit(solution)/shard_map/attend_forward/pallas_call | solution.py:838
  70.8 3.2 %collective-permute-done.11 = bf16[4,96,768]{2,1,0:T(8,128)(2,1)} collective-permute-done((bf16[4,96,768]{2,1,0:T(8,128)(2,1)S(1)}, bf16[4,96,768]{2,1,0:T(8,128)(2,1)}, u32[]{:S(2)}, u32[]{:S(2)}) %collective-permute-start.11) | collective-permute-done | bytes 589856 | tf_op jit(solution)/shard_map/ppermute | solution.py:794
  74.0 14.2 %collective-permute-done.13 = bf16[4,96,768]{2,1,0:T(8,128)(2,1)} collective-permute-done((bf16[4,96,768]{2,1,0:T(8,128)(2,1)S(1)}, bf16[4,96,768]{2,1,0:T(8,128)(2,1)}, u32[]{:S(2)}, u32[]{:S(2)}) %collective-permute-start.13) | collective-permute-done | bytes 589856 | tf_op jit(solution)/shard_map/ppermute | solution.py:794
  88.1 1.7 pad_maximum_fusion.own_down
  90.9 2.6 collective-permute-start.10
  93.5 1.3 collective-permute-start.9
  96.3 4.8 %collective-permute-done.10.x3 = bf16[256,192]{1,0:T(8,128)(2,1)S(1)} collective-permute-done((bf16[256,192]{1,0:T(8,128)(2,1)}, bf16[256,192]{1,0:T(8,128)(2,1)S(1)}, u32[]{:S(2)}, u32[]{:S(2)}) %collective-permute-start.10) | collective-permute-done | bytes 98336 | tf_op jit(solution)/shard_map/ppermute | solution.py:794
  101.1 1.8 collective-permute-done.8.x1
  103.7 9.5 %all-gather.2.cloned.1.call-done = bf16[4096,768]{1,0:T(8,128)(2,1)} async-done(((bf16[128,768]{1,0:T(8,128)(2,1)}), bf16[4096,768]{1,0:T(8,128)(2,1)}) %all-gather.2.cloned.1.call-update) | async-done | bytes 6291472 | tf_op jit(solution)/shard_map/all_gather | solution.py:810
  113.2 15.5 %middle.1 = (bf16[256,768]{1,0:T(8,128)(2,1)}, f32[256,768]{1,0:T(8,128)}, bf16[256,192]{1,0:T(8,128)(2,1)}, bf16[256,192]{1,0:T(8,128)(2,1)}, bf16[256,192]{1,0...) custom-call(s32[4]{0:T(128)} %pad_add_fusion.sc, ...), custom_call_target="tpu_custom_call" | custom-call | flops 1350000000 | bytes 4500000 | tf_op jit(solution)/shard_map/middle/pallas_call | solution.py:867
  131.1 1.3 convert_reduce_fusion
  132.5 1.4 reshape.100
  133.8 1.3 collective-permute-start.16
  135.2 2.1 collective-permute-start.18
  137.3 1.3 pad_maximum_fusion.7
  138.7 1.5 convert_element_type.14
  140.1 1.4 pad.10.vectors
  141.5 2.2 collective-permute-done.17.g2
  143.7 1.6 copy-done.1
  145.3 6.6 %up_grad.1 = (bf16[2,4,256,384]{3,2,1,0:T(8,128)(2,1)}, bf16[2,4,256,384]{3,2,1,0:T(8,128)(2,1)}) custom-call(s32[4]{0:T(128)} %pad_add_fusion.sc, bf16[256,5760]{1,0:T(8,128)(2,1)} %get-tuple-element.108.keep, bf16[256,5760]{1,0:T(8,128)(2,1)} %copy-done.1, bf16[4,16,384]{2,1,0:T(8,128)(2,1)} %pad.10.vectors), custom_call_target="tpu_custom_call" | custom-call | flops 360000000 | bytes 1200000 | tf_op jit(solution)/shard_map/up_grad/pallas_call | solution.py:916
  152.3 5.8 %down_grad.1 = (bf16[2,4,96,768]{3,2,1,0:T(8,128)(2,1)}, bf16[2,4,96,768]{3,2,1,0:T(8,128)(2,1)}) custom-call(s32[4]{0:T(128)} %pad_add_fusion.sc, bf16[256,5760]{1,0:T(8,128)(2,1)} %get-tuple-element.108.keep, bf16[256,5760]{1,0:T(8,128)(2,1)} %copy-done.1), custom_call_target="tpu_custom_call" | custom-call | flops 360000000 | bytes 1200000 | tf_op jit(solution)/shard_map/down_grad/pallas_call | solution.py:916
  158.1 1.6 collective-permute-start.19
  159.7 12.6 %attend_backward.1.dqkv = bf16[1024,576]{1,0:T(8,128)(2,1)} custom-call(s32[4]{0:T(128)} %pad_add_fusion.sc, bf16[1024,576]{1,0:T(8,128)(2,1)} %get-tuple-element.104.qkv, f32[192,1024]{1,0:T(8,128)} %get-tuple-element.105.ctx_t, f32[3,1024]{1,0:T(4,128)} %get-tuple-element.106.lse, bf16[256,192]{1,0:T(8,128)(2,1)} %get-tuple-element.118.g0, ...), custom_call_target="tpu_custom_call" | custom-call | flops 990000000 | bytes 3300000 | tf_op jit(solution)/shard_map/attend_backward/pallas_call | solution.py:952
  172.3 4.3 %grad_qkv_weight.1 = (bf16[4,112,576]{2,1,0:T(8,128)(2,1)}, bf16[4,112,576]{2,1,0:T(8,128)(2,1)}) custom-call(s32[4]{0:T(128)} %pad_add_fusion.sc, bf16[256,768]{1,0:T(8,128)(2,1)} %bitcast.50, bf16[256,768]{1,0:T(8,128)(2,1)} %copy-done.10, bf16[256,768]{1,0:T(8,128)(2,1)} %copy-done.11, bf16[256,768]{1,0:T(8,128)(2,1)} %copy-done.12, ...), custom_call_target="tpu_custom_call" | custom-call | flops 360000000 | bytes 1200000 | tf_op jit(solution)/shard_map/grad_qkv_weight/pallas_call | solution.py:966
  176.6 10.9 %collective-permute-done.20.got = bf16[2,4,256,384]{3,2,1,0:T(8,128)(2,1)S(1)} collective-permute-done((bf16[2,4,256,384]{3,2,1,0:T(8,128)(2,1)}, bf16[2,4,256,384]{3,2,1,0:T(8,128)(2,1)S(1)}, u32[]{:S(2)}, u32[]{:S(2)}) %collective-permute-start.20) | collective-permute-done | bytes 1572896 | tf_op jit(solution)/shard_map/ppermute | solution.py:794
  188.7 3.2 %fold.6 = (bf16[4,256,384]{2,1,0:T(8,128)(2,1)}, bf16[4,256,384]{2,1,0:T(8,128)(2,1)}) custom-call(bf16[2,4,256,384]{3,2,1,0:T(8,128)(2,1)} %get-tuple-element.131.near, bf16[2,4,256,384]{3,2,1,0:T(8,128)(2,1)} %copy-done.4), custom_call_target="tpu_custom_call" | custom-call | flops 90000000 | bytes 300000 | tf_op jit(solution)/shard_map/fold/pallas_call | solution.py:916
  193.3 2.8 fold.5
  196.0 1.7 collective-permute-start.24
  197.8 2.1 level_fold.3
  199.9 2.0 collective-permute-start.22
  202.0 4.2 %grad_tokens.1 = bf16[4,256,768]{2,1,0:T(8,128)(2,1)} custom-call(s32[4]{0:T(128)} %pad_add_fusion.sc, bf16[1024,576]{1,0:T(8,128)(2,1)} %attend_backward.1.dqkv, bf16[4,2,96,576]{3,2,1,0:T(8,128)(2,1)} %get-tuple-element.127.weight), custom_call_target="tpu_custom_call" | custom-call | flops 360000000 | bytes 1200000 | tf_op jit(solution)/shard_map/grad_tokens/pallas_call | solution.py:916
  207.8 1.8 fold.7
  210.4 2.1 level_fold.5
  213.5 2.4 level_fold.4
  215.8 2.6 collective-permute-start.28
  218.6 10.8 %collective-permute-done.28.got = bf16[2,256,384]{2,1,0:T(8,128)(2,1)S(1)} collective-permute-done((bf16[2,256,384]{2,1,0:T(8,128)(2,1)}, bf16[2,256,384]{2,1,0:T(8,128)(2,1)S(1)}, u32[]{:S(2)}, u32[]{:S(2)}) %collective-permute-start.28) | collective-permute-done | bytes 393248 | tf_op jit(solution)/shard_map/ppermute | solution.py:800
  230.1 1.9 fold.9
  232.0 1.7 collective-permute-start.29
  233.8 1.2 collective-permute-start.25
  236.4 1.8 fold.8
  238.2 1.7 collective-permute-start.27
  239.9 5.7 %collective-permute-done.29.e1 = bf16[256,384]{1,0:T(8,128)(2,1)S(1)} collective-permute-done((bf16[256,384]{1,0:T(8,128)(2,1)}, bf16[256,384]{1,0:T(8,128)(2,1)S(1)}, u32[]{:S(2)}, u32[]{:S(2)}) %collective-permute-start.29) | collective-permute-done | bytes 196640 | tf_op jit(solution)/shard_map/ppermute | solution.py:800
  246.3 1.8 split_up.1
  248.8 1.7 sum.1.b0
  251.4 2.1 collective-permute-start.32
  254.6 1.9 join.1
  257.2 3.0 %collective-permute-done.32.b2 = bf16[112,576]{1,0:T(8,128)(2,1)S(1)} collective-permute-done((bf16[112,576]{1,0:T(8,128)(2,1)}, bf16[112,576]{1,0:T(8,128)(2,1)S(1)}, u32[]{:S(2)}, u32[]{:S(2)}) %collective-permute-start.32) | collective-permute-done | bytes 129056 | tf_op jit(solution)/shard_map/ppermute | solution.py:794
  262.3 1.2 collective-permute-start.35
  266.8 2.3 finish_qkv.1
  269.7 3.2 %collective-permute-done.34.b1 = bf16[240,768]{1,0:T(8,128)(2,1)S(1)} collective-permute-done((bf16[240,768]{1,0:T(8,128)(2,1)}, bf16[240,768]{1,0:T(8,128)(2,1)S(1)}, u32[]{:S(2)}, u32[]{:S(2)}) %collective-permute-start.34) | collective-permute-done | bytes 368672 | tf_op jit(solution)/shard_map/ppermute | solution.py:794
  272.9 7.5 %collective-permute-done.35.b2 = bf16[240,768]{1,0:T(8,128)(2,1)S(1)} collective-permute-done((bf16[240,768]{1,0:T(8,128)(2,1)}, bf16[240,768]{1,0:T(8,128)(2,1)S(1)}, u32[]{:S(2)}, u32[]{:S(2)}) %collective-permute-start.35) | collective-permute-done | bytes 368672 | tf_op jit(solution)/shard_map/ppermute | solution.py:794
  281.9 3.0 %finish.1 = (f32[384,768]{1,0:T(8,128)}, f32[96,3072]{1,0:T(8,128)}, f32[96,768]{1,0:T(8,128)}) custom-call(s32[4]{0:T(128)} %pad_add_fusion.sc, bf16[240,768]{1,0:T(8,128)(2,1)} %get-tuple-element.162.b0, bf16[240,768]{1,0:T(8,128)(2,1)} %copy-done.14, bf16[240,768]{1,0:T(8,128)(2,1)} %copy-done.15, bf16[240,768]{1,0:T(8,128)(2,1)} %copy-done.16), custom_call_target="tpu_custom_call" | custom-call | flops 180000000 | bytes 600000 | tf_op jit(solution)/shard_map/finish/pallas_call | solution.py:916
  284.9 1.8 fusion
  (167 shorter events, 33.3 us)
Async XLA Ops:
  7.2 8.8 %copy-start = (bf16[384,768]{1,0:T(8,128)(2,1)S(1)}, bf16[384,768]{1,0:T(8,128)(2,1)}, u32[]{:S(2)}) copy-start(bf16[384,768]{1,0:T(8,128)(2,1)} %param.27) | copy-start | bytes 1769476
  7.2 5.1 %copy-start.36 = (bf16[96]{0:T(256)(128)(2,1)S(1)}, bf16[96]{0:T(256)(128)(2,1)}, u32[]{:S(2)}) copy-start(bf16[96]{0:T(256)(128)(2,1)} %param.19) | copy-start | bytes 580
  7.2 5.2 %copy-start.37 = (bf16[96]{0:T(256)(128)(2,1)S(1)}, bf16[96]{0:T(256)(128)(2,1)}, u32[]{:S(2)}) copy-start(bf16[96]{0:T(256)(128)(2,1)} %param.20) | copy-start | bytes 580
  7.2 5.3 %copy-start.30 = (bf16[96]{0:T(256)(128)(2,1)S(1)}, bf16[96]{0:T(256)(128)(2,1)}, u32[]{:S(2)}) copy-start(bf16[96]{0:T(256)(128)(2,1)} %param.22) | copy-start | bytes 580
  7.2 5.3 %copy-start.31 = (bf16[96]{0:T(256)(128)(2,1)S(1)}, bf16[96]{0:T(256)(128)(2,1)}, u32[]{:S(2)}) copy-start(bf16[96]{0:T(256)(128)(2,1)} %param.23) | copy-start | bytes 580
  7.2 5.3 %copy-start.32 = (bf16[96]{0:T(256)(128)(2,1)S(1)}, bf16[96]{0:T(256)(128)(2,1)}, u32[]{:S(2)}) copy-start(bf16[96]{0:T(256)(128)(2,1)} %param.24) | copy-start | bytes 580
  7.2 5.3 %copy-start.29 = (bf16[384]{0:T(512)(128)(2,1)S(1)}, bf16[384]{0:T(512)(128)(2,1)}, u32[]{:S(2)}) copy-start(bf16[384]{0:T(512)(128)(2,1)} %param.26) | copy-start | bytes 2308
  7.3 5.3 %copy-start.33 = (bf16[96]{0:T(256)(128)(2,1)S(1)}, bf16[96]{0:T(256)(128)(2,1)}, u32[]{:S(2)}) copy-start(bf16[96]{0:T(256)(128)(2,1)} %param.28) | copy-start | bytes 580
  7.3 5.3 %copy-start.34 = (bf16[96]{0:T(256)(128)(2,1)S(1)}, bf16[96]{0:T(256)(128)(2,1)}, u32[]{:S(2)}) copy-start(bf16[96]{0:T(256)(128)(2,1)} %param.29) | copy-start | bytes 580
  7.3 5.3 %copy-start.35 = (bf16[96]{0:T(256)(128)(2,1)S(1)}, bf16[96]{0:T(256)(128)(2,1)}, u32[]{:S(2)}) copy-start(bf16[96]{0:T(256)(128)(2,1)} %param.30) | copy-start | bytes 580
  7.3 105.9 %all-gather.2.cloned.1.call-start = ((), (), s32[]{:S(2)}) async-start(), calls=%async_computation.1 | async-start | bytes 6488064 | tf_op jit(solution)/shard_map/all_gather | solution.py:810
  9.8 275.0 %reduce-scatter.2.cloned.1.call-start = ((), (), s32[]{:S(2)}) async-start(), calls=%async_computation.2 | async-start | bytes 1966080 | tf_op jit(solution)/shard_map/reduce_scatter | solution.py:1021
  9.9 17.0 %copy-start.3 = (bf16[1,256,768]{2,1,0:T(8,128)(2,1)S(1)}, bf16[1,256,768]{2,1,0:T(8,128)(2,1)}, u32[]{:S(2)}) copy-start(bf16[1,256,768]{2,1,0:T(8,128)(2,1)} %param.16) | copy-start | bytes 1179652
  12.9 7.6 %collective-permute-start.2 = (bf16[112,576]{1,0:T(8,128)(2,1)S(1)}, bf16[112,576]{1,0:T(8,128)(2,1)S(1)}, u32[]{:S(2)}, u32[]{:S(2)}) collective-permute-start(bf16[112,576]{1,0:T(8,128)(2,1)S(1)} %pad_maximum_fusion.6), channel_id=1, source_target_pairs={{0,2},{2,0},{4,6},{6,4},{1,3},{3,1},{5,7},{7,5},{8,10},{10,8},{12,... | collective-permute-start | bytes 387080 | tf_op jit(solution)/shard_map/ppermute | solution.py:800
  16.0 8.4 %collective-permute-start = (bf16[96,768]{1,0:T(8,128)(2,1)S(1)}, bf16[96,768]{1,0:T(8,128)(2,1)S(1)}, u32[]{:S(2)}, u32[]{:S(2)}) collective-permute-start(bf16[96,768]{1,0:T(8,128)(2,1)S(1)} %constant_dynamic-slice_fusion.10), channel_id=1, source_target_pairs={{0,2},{2,0},{4,6},{6,4},{1,3},{3,1},{5,7},{7,5},{8,10},{10,8},{12,... | collective-permute-start | bytes 442376 | tf_op jit(solution)/shard_map/ppermute | solution.py:800
  20.6 26.9 %collective-permute-start.3 = (bf16[2,112,576]{2,1,0:T(8,128)(2,1)S(1)}, bf16[2,112,576]{2,1,0:T(8,128)(2,1)S(1)}, u32[]{:S(2)}, u32[]{:S(2)}) collective-permute-start(bf16[2,112,576]{2,1,0:T(8,128)(2,1)S(1)} %pad_maximum_fusion.4), channel_id=1, source_target_pairs={{0,4},{2,6},{4,0},{6,2},{1,5},{3,7},{5,1},{7,3},{8,12},{10,14},{12... | collective-permute-start | bytes 774152 | tf_op jit(solution)/shard_map/ppermute | solution.py:800
  24.4 27.5 %collective-permute-start.1 = (bf16[2,96,768]{2,1,0:T(8,128)(2,1)S(1)}, bf16[2,96,768]{2,1,0:T(8,128)(2,1)S(1)}, u32[]{:S(2)}, u32[]{:S(2)}) collective-permute-start(bf16[2,96,768]{2,1,0:T(8,128)(2,1)S(1)} %pad_maximum_fusion.3), channel_id=1, source_target_pairs={{0,4},{2,6},{4,0},{6,2},{1,5},{3,7},{5,1},{7,3},{8,12},{10,14},{12... | collective-permute-start | bytes 884744 | tf_op jit(solution)/shard_map/ppermute | solution.py:800
  26.9 25.0 %collective-permute-start.4 = (bf16[256,768]{1,0:T(8,128)(2,1)S(1)}, bf16[256,768]{1,0:T(8,128)(2,1)S(1)}, u32[]{:S(2)}, u32[]{:S(2)}) collective-permute-start(bf16[256,768]{1,0:T(8,128)(2,1)S(1)} %bitcast.51), channel_id=1, source_target_pairs={{0,8},{8,0},{16,24},{24,16},{1,9},{9,1},{17,25},{25,17},{2,10},{10... | collective-permute-start | bytes 1179656 | tf_op jit(solution)/shard_map/ppermute | solution.py:794
  28.4 23.6 %collective-permute-start.5 = (bf16[256,768]{1,0:T(8,128)(2,1)S(1)}, bf16[256,768]{1,0:T(8,128)(2,1)S(1)}, u32[]{:S(2)}, u32[]{:S(2)}) collective-permute-start(bf16[256,768]{1,0:T(8,128)(2,1)S(1)} %bitcast.52), channel_id=1, source_target_pairs={{0,16},{8,24},{16,0},{24,8},{1,17},{9,25},{17,1},{25,9},{2,18},{10... | collective-permute-start | bytes 1179656 | tf_op jit(solution)/shard_map/ppermute | solution.py:794
  29.9 22.1 %collective-permute-start.6 = (bf16[256,768]{1,0:T(8,128)(2,1)S(1)}, bf16[256,768]{1,0:T(8,128)(2,1)S(1)}, u32[]{:S(2)}, u32[]{:S(2)}) collective-permute-start(bf16[256,768]{1,0:T(8,128)(2,1)S(1)} %bitcast.53), channel_id=1, source_target_pairs={{0,24},{8,16},{16,8},{24,0},{1,25},{9,17},{17,9},{25,1},{2,26},{10... | collective-permute-start | bytes 1179656 | tf_op jit(solution)/shard_map/ppermute | solution.py:794
  47.6 9.2 %copy-start.9 = (bf16[4,112,576]{2,1,0:T(8,128)(2,1)}, bf16[4,112,576]{2,1,0:T(8,128)(2,1)S(1)}, u32[]{:S(2)}) copy-start(bf16[4,112,576]{2,1,0:T(8,128)(2,1)S(1)} %pad_maximum_fusion.2.own) | copy-start | bytes 1548292
  51.9 4.9 %copy-start.10 = (bf16[256,768]{1,0:T(8,128)(2,1)}, bf16[256,768]{1,0:T(8,128)(2,1)S(1)}, u32[]{:S(2)}) copy-start(bf16[256,768]{1,0:T(8,128)(2,1)S(1)} %collective-permute-done.4.t1) | copy-start | bytes 1179652
  51.9 4.9 %copy-start.11 = (bf16[256,768]{1,0:T(8,128)(2,1)}, bf16[256,768]{1,0:T(8,128)(2,1)S(1)}, u32[]{:S(2)}) copy-start(bf16[256,768]{1,0:T(8,128)(2,1)S(1)} %collective-permute-done.5.t2) | copy-start | bytes 1179652
  52.0 4.9 %collective-permute-start.7 = (bf16[4,112,576]{2,1,0:T(8,128)(2,1)S(1)}, bf16[4,112,576]{2,1,0:T(8,128)(2,1)S(1)}, u32[]{:S(2)}, u32[]{:S(2)}) collective-permute-start(bf16[4,112,576]{2,1,0:T(8,128)(2,1)S(1)} %pad_maximum_fusion.2.own), channel_id=1, source_target_pairs={{0,1},{1,0},{2,3},{3,2},{4,5},{5,4},{6,7},{7,6},{8,9},{9,8},{10,11... | collective-permute-start | bytes 1548296 | tf_op jit(solution)/shard_map/ppermute | solution.py:797
  52.0 21.9 %collective-permute-start.11 = (bf16[4,96,768]{2,1,0:T(8,128)(2,1)S(1)}, bf16[4,96,768]{2,1,0:T(8,128)(2,1)}, u32[]{:S(2)}, u32[]{:S(2)}) collective-permute-start(bf16[4,96,768]{2,1,0:T(8,128)(2,1)S(1)} %pad_maximum_fusion.1), channel_id=1, source_target_pairs={{0,8},{8,0},{16,24},{24,16},{1,9},{9,1},{17,25},{25,17},{2,10},{10... | collective-permute-start | bytes 1769480 | tf_op jit(solution)/shard_map/ppermute | solution.py:794
  53.4 20.5 %collective-permute-start.12 = (bf16[4,96,768]{2,1,0:T(8,128)(2,1)S(1)}, bf16[4,96,768]{2,1,0:T(8,128)(2,1)}, u32[]{:S(2)}, u32[]{:S(2)}) collective-permute-start(bf16[4,96,768]{2,1,0:T(8,128)(2,1)S(1)} %pad_maximum_fusion.1), channel_id=1, source_target_pairs={{0,16},{8,24},{16,0},{24,8},{1,17},{9,25},{17,1},{25,9},{2,18},{10... | collective-permute-start | bytes 1769480 | tf_op jit(solution)/shard_map/ppermute | solution.py:794
  55.0 33.2 %collective-permute-start.13 = (bf16[4,96,768]{2,1,0:T(8,128)(2,1)S(1)}, bf16[4,96,768]{2,1,0:T(8,128)(2,1)}, u32[]{:S(2)}, u32[]{:S(2)}) collective-permute-start(bf16[4,96,768]{2,1,0:T(8,128)(2,1)S(1)} %pad_maximum_fusion.1), channel_id=1, source_target_pairs={{0,24},{8,16},{16,8},{24,0},{1,25},{9,17},{17,9},{25,1},{2,26},{10... | collective-permute-start | bytes 1769480 | tf_op jit(solution)/shard_map/ppermute | solution.py:794
  89.9 23.3 %copy-start.2 = (bf16[4,4,96,768]{3,2,1,0:T(8,128)(2,1)}, bf16[4,4,96,768]{3,2,1,0:T(8,128)(2,1)S(1)}, u32[]{:S(2)}) copy-start(bf16[4,4,96,768]{3,2,1,0:T(8,128)(2,1)S(1)} %pad_maximum_fusion.own_down) | copy-start | bytes 7077892
  89.9 13.8 %collective-permute-start.14 = (bf16[4,4,96,768]{3,2,1,0:T(8,128)(2,1)S(1)}, bf16[4,4,96,768]{3,2,1,0:T(8,128)(2,1)}, u32[]{:S(2)}, u32[]{:S(2)}) collective-permute-start(bf16[4,4,96,768]{3,2,1,0:T(8,128)(2,1)S(1)} %pad_maximum_fusion.own_down), channel_id=1, source_target_pairs={{0,1},{1,0},{2,3},{3,2},{4,5},{5,4},{6,7},{7,6},{8,9},{9,8},{10,11... | collective-permute-start | bytes 7077896 | tf_op jit(solution)/shard_map/ppermute | solution.py:797
  90.9 10.2 %collective-permute-start.10 = (bf16[256,192]{1,0:T(8,128)(2,1)}, bf16[256,192]{1,0:T(8,128)(2,1)S(1)}, u32[]{:S(2)}, u32[]{:S(2)}) collective-permute-start(bf16[256,192]{1,0:T(8,128)(2,1)} %get-tuple-element.98), channel_id=1, source_target_pairs={{0,24},{8,16},{16,8},{24,0},{1,25},{9,17},{17,9},{25,1},{2,26},{10... | collective-permute-start | bytes 294920 | tf_op jit(solution)/shard_map/ppermute | solution.py:794
  93.5 9.4 %collective-permute-start.8 = (bf16[256,192]{1,0:T(8,128)(2,1)}, bf16[256,192]{1,0:T(8,128)(2,1)S(1)}, u32[]{:S(2)}, u32[]{:S(2)}) collective-permute-start(bf16[256,192]{1,0:T(8,128)(2,1)} %get-tuple-element.96), channel_id=1, source_target_pairs={{0,8},{8,0},{16,24},{24,16},{1,9},{9,1},{17,25},{25,17},{2,10},{10... | collective-permute-start | bytes 294920 | tf_op jit(solution)/shard_map/ppermute | solution.py:794
  93.5 10.2 %collective-permute-start.9 = (bf16[256,192]{1,0:T(8,128)(2,1)}, bf16[256,192]{1,0:T(8,128)(2,1)S(1)}, u32[]{:S(2)}, u32[]{:S(2)}) collective-permute-start(bf16[256,192]{1,0:T(8,128)(2,1)} %get-tuple-element.97), channel_id=1, source_target_pairs={{0,16},{8,24},{16,0},{24,8},{1,17},{9,25},{17,1},{25,9},{2,18},{10... | collective-permute-start | bytes 294920 | tf_op jit(solution)/shard_map/ppermute | solution.py:794
  101.1 12.1 %copy-start.25 = (bf16[256,192]{1,0:T(8,128)(2,1)}, bf16[256,192]{1,0:T(8,128)(2,1)S(1)}, u32[]{:S(2)}) copy-start(bf16[256,192]{1,0:T(8,128)(2,1)S(1)} %collective-permute-done.10.x3) | copy-start | bytes 294916
  102.9 10.3 %copy-start.26 = (bf16[256,192]{1,0:T(8,128)(2,1)}, bf16[256,192]{1,0:T(8,128)(2,1)S(1)}, u32[]{:S(2)}) copy-start(bf16[256,192]{1,0:T(8,128)(2,1)S(1)} %collective-permute-done.8.x1) | copy-start | bytes 294916
  103.7 9.5 %copy-start.27 = (bf16[256,192]{1,0:T(8,128)(2,1)}, bf16[256,192]{1,0:T(8,128)(2,1)S(1)}, u32[]{:S(2)}) copy-start(bf16[256,192]{1,0:T(8,128)(2,1)S(1)} %collective-permute-done.9.x2) | copy-start | bytes 294916
  128.7 15.0 %collective-permute-start.15 = (bf16[256,5760]{1,0:T(8,128)(2,1)}, bf16[256,5760]{1,0:T(8,128)(2,1)S(1)}, u32[]{:S(2)}, u32[]{:S(2)}) collective-permute-start(bf16[256,5760]{1,0:T(8,128)(2,1)} %get-tuple-element.109), channel_id=1, source_target_pairs={{0,1},{1,0},{2,3},{3,2},{4,5},{5,4},{6,7},{7,6},{8,9},{9,8},{10,11... | collective-permute-start | bytes 8847368 | tf_op jit(solution)/shard_map/ppermute | solution.py:797
  133.8 7.6 %collective-permute-start.16 = (bf16[256,192]{1,0:T(8,128)(2,1)}, bf16[256,192]{1,0:T(8,128)(2,1)}, u32[]{:S(2)}, u32[]{:S(2)}) collective-permute-start(bf16[256,192]{1,0:T(8,128)(2,1)} %get-tuple-element.110), channel_id=1, source_target_pairs={{0,8},{8,0},{16,24},{24,16},{1,9},{9,1},{17,25},{25,17},{2,10},{10... | collective-permute-start | bytes 294920 | tf_op jit(solution)/shard_map/ppermute | solution.py:794
  135.2 8.5 %collective-permute-start.17 = (bf16[256,192]{1,0:T(8,128)(2,1)}, bf16[256,192]{1,0:T(8,128)(2,1)}, u32[]{:S(2)}, u32[]{:S(2)}) collective-permute-start(bf16[256,192]{1,0:T(8,128)(2,1)} %get-tuple-element.111), channel_id=1, source_target_pairs={{0,16},{8,24},{16,0},{24,8},{1,17},{9,25},{17,1},{25,9},{2,18},{10... | collective-permute-start | bytes 294920 | tf_op jit(solution)/shard_map/ppermute | solution.py:794
  135.2 8.5 %collective-permute-start.18 = (bf16[256,192]{1,0:T(8,128)(2,1)}, bf16[256,192]{1,0:T(8,128)(2,1)}, u32[]{:S(2)}, u32[]{:S(2)}) collective-permute-start(bf16[256,192]{1,0:T(8,128)(2,1)} %get-tuple-element.112), channel_id=1, source_target_pairs={{0,24},{8,16},{16,8},{24,0},{1,25},{9,17},{17,9},{25,1},{2,26},{10... | collective-permute-start | bytes 294920 | tf_op jit(solution)/shard_map/ppermute | solution.py:794
  151.9 35.7 %collective-permute-start.20 = (bf16[2,4,256,384]{3,2,1,0:T(8,128)(2,1)}, bf16[2,4,256,384]{3,2,1,0:T(8,128)(2,1)S(1)}, u32[]{:S(2)}, u32[]{:S(2)}) collective-permute-start(bf16[2,4,256,384]{3,2,1,0:T(8,128)(2,1)} %get-tuple-element.132), channel_id=1, source_target_pairs={{0,16},{8,24},{16,0},{24,8},{1,17},{9,25},{17,1},{25,9},{2,18},{10... | collective-permute-start | bytes 4718600 | tf_op jit(solution)/shard_map/ppermute | solution.py:794
  158.1 34.1 %collective-permute-start.19 = (bf16[2,4,96,768]{3,2,1,0:T(8,128)(2,1)}, bf16[2,4,96,768]{3,2,1,0:T(8,128)(2,1)S(1)}, u32[]{:S(2)}, u32[]{:S(2)}) collective-permute-start(bf16[2,4,96,768]{3,2,1,0:T(8,128)(2,1)} %get-tuple-element.129), channel_id=1, source_target_pairs={{0,8},{8,0},{16,24},{24,16},{1,9},{9,1},{17,25},{25,17},{2,10},{10... | collective-permute-start | bytes 3538952 | tf_op jit(solution)/shard_map/ppermute | solution.py:794
  176.6 21.2 %collective-permute-start.21 = (bf16[4,112,576]{2,1,0:T(8,128)(2,1)}, bf16[4,112,576]{2,1,0:T(8,128)(2,1)}, u32[]{:S(2)}, u32[]{:S(2)}) collective-permute-start(bf16[4,112,576]{2,1,0:T(8,128)(2,1)} %get-tuple-element.135), channel_id=1, source_target_pairs={{0,1},{1,0},{2,3},{3,2},{4,5},{5,4},{6,7},{7,6},{8,9},{9,8},{10,11... | collective-permute-start | bytes 1548296 | tf_op jit(solution)/shard_map/ppermute | solution.py:797
  191.9 20.6 %collective-permute-start.23 = (bf16[4,256,384]{2,1,0:T(8,128)(2,1)}, bf16[4,256,384]{2,1,0:T(8,128)(2,1)S(1)}, u32[]{:S(2)}, u32[]{:S(2)}) collective-permute-start(bf16[4,256,384]{2,1,0:T(8,128)(2,1)} %get-tuple-element.140), channel_id=1, source_target_pairs={{0,8},{8,0},{16,24},{24,16},{1,9},{9,1},{17,25},{25,17},{2,10},{10... | collective-permute-start | bytes 2359304 | tf_op jit(solution)/shard_map/ppermute | solution.py:794
  196.0 13.6 %collective-permute-start.24 = (bf16[4,96,768]{2,1,0:T(8,128)(2,1)}, bf16[4,96,768]{2,1,0:T(8,128)(2,1)S(1)}, u32[]{:S(2)}, u32[]{:S(2)}) collective-permute-start(bf16[4,96,768]{2,1,0:T(8,128)(2,1)} %get-tuple-element.143), channel_id=1, source_target_pairs={{0,16},{8,24},{16,0},{24,8},{1,17},{9,25},{17,1},{25,9},{2,18},{10... | collective-permute-start | bytes 1769480 | tf_op jit(solution)/shard_map/ppermute | solution.py:794
  199.9 7.2 %collective-permute-start.22 = (bf16[2,112,576]{2,1,0:T(8,128)(2,1)}, bf16[2,112,576]{2,1,0:T(8,128)(2,1)S(1)}, u32[]{:S(2)}, u32[]{:S(2)}) collective-permute-start(bf16[2,112,576]{2,1,0:T(8,128)(2,1)} %get-tuple-element.137), channel_id=1, source_target_pairs={{0,2},{2,0},{4,6},{6,4},{1,3},{3,1},{5,7},{7,5},{8,10},{10,8},{12,... | collective-permute-start | bytes 774152 | tf_op jit(solution)/shard_map/ppermute | solution.py:800
  209.6 24.1 %copy-start.40 = (bf16[112,576]{1,0:T(8,128)(2,1)S(1)}, bf16[112,576]{1,0:T(8,128)(2,1)}, u32[]{:S(2)}) copy-start(bf16[112,576]{1,0:T(8,128)(2,1)} %get-tuple-element.146) | copy-start | bytes 387076
  212.6 5.9 %copy-start.39 = (bf16[2,96,768]{2,1,0:T(8,128)(2,1)S(1)}, bf16[2,96,768]{2,1,0:T(8,128)(2,1)}, u32[]{:S(2)}) copy-start(bf16[2,96,768]{2,1,0:T(8,128)(2,1)} %get-tuple-element.147) | copy-start | bytes 884740
  215.8 13.5 %collective-permute-start.28 = (bf16[2,256,384]{2,1,0:T(8,128)(2,1)}, bf16[2,256,384]{2,1,0:T(8,128)(2,1)S(1)}, u32[]{:S(2)}, u32[]{:S(2)}) collective-permute-start(bf16[2,256,384]{2,1,0:T(8,128)(2,1)} %get-tuple-element.150), channel_id=1, source_target_pairs={{0,2},{2,0},{4,6},{6,4},{1,3},{3,1},{5,7},{7,5},{8,10},{10,8},{12,... | collective-permute-start | bytes 1179656 | tf_op jit(solution)/shard_map/ppermute | solution.py:800
  218.5 66.4 %copy-start.6 = (f32[256,768]{1,0:T(8,128)S(1)}, f32[256,768]{1,0:T(8,128)}, u32[]{:S(2)}) copy-start(f32[256,768]{1,0:T(8,128)} %get-tuple-element.103) | copy-start | bytes 2359300
  218.5 17.2 %collective-permute-start.26 = (bf16[2,96,768]{2,1,0:T(8,128)(2,1)S(1)}, bf16[2,96,768]{2,1,0:T(8,128)(2,1)S(1)}, u32[]{:S(2)}, u32[]{:S(2)}) collective-permute-start(bf16[2,96,768]{2,1,0:T(8,128)(2,1)S(1)} %copy-done.39), channel_id=1, source_target_pairs={{0,2},{2,0},{4,6},{6,4},{1,3},{3,1},{5,7},{7,5},{8,10},{10,8},{12,... | collective-permute-start | bytes 884744 | tf_op jit(solution)/shard_map/ppermute | solution.py:800
  232.0 13.6 %collective-permute-start.29 = (bf16[256,384]{1,0:T(8,128)(2,1)}, bf16[256,384]{1,0:T(8,128)(2,1)S(1)}, u32[]{:S(2)}, u32[]{:S(2)}) collective-permute-start(bf16[256,384]{1,0:T(8,128)(2,1)} %get-tuple-element.152), channel_id=1, source_target_pairs={{0,4},{2,6},{4,0},{6,2},{1,5},{3,7},{5,1},{7,3},{8,12},{10,14},{12... | collective-permute-start | bytes 589832 | tf_op jit(solution)/shard_map/ppermute | solution.py:800
  233.8 14.3 %collective-permute-start.25 = (bf16[112,576]{1,0:T(8,128)(2,1)S(1)}, bf16[112,576]{1,0:T(8,128)(2,1)S(1)}, u32[]{:S(2)}, u32[]{:S(2)}) collective-permute-start(bf16[112,576]{1,0:T(8,128)(2,1)S(1)} %copy-done.40), channel_id=1, source_target_pairs={{0,4},{2,6},{4,0},{6,2},{1,5},{3,7},{5,1},{7,3},{8,12},{10,14},{12... | collective-permute-start | bytes 387080 | tf_op jit(solution)/shard_map/ppermute | solution.py:800
  238.2 15.7 %collective-permute-start.27 = (bf16[96,768]{1,0:T(8,128)(2,1)}, bf16[96,768]{1,0:T(8,128)(2,1)S(1)}, u32[]{:S(2)}, u32[]{:S(2)}) collective-permute-start(bf16[96,768]{1,0:T(8,128)(2,1)} %get-tuple-element.149), channel_id=1, source_target_pairs={{0,4},{2,6},{4,0},{6,2},{1,5},{3,7},{5,1},{7,3},{8,12},{10,14},{12... | collective-permute-start | bytes 442376 | tf_op jit(solution)/shard_map/ppermute | solution.py:800
  248.1 5.8 %collective-permute-start.30 = (bf16[160,384]{1,0:T(8,128)(2,1)}, bf16[160,384]{1,0:T(8,128)(2,1)S(1)}, u32[]{:S(2)}, u32[]{:S(2)}) collective-permute-start(bf16[160,384]{1,0:T(8,128)(2,1)} %get-tuple-element.154), channel_id=1, source_target_pairs={{0,1},{1,0},{2,3},{3,2},{4,5},{5,4},{6,7},{7,6},{8,9},{9,8},{10,11... | collective-permute-start | bytes 368648 | tf_op jit(solution)/shard_map/ppermute | solution.py:797
  250.4 6.8 %collective-permute-start.31 = (bf16[112,576]{1,0:T(8,128)(2,1)}, bf16[112,576]{1,0:T(8,128)(2,1)S(1)}, u32[]{:S(2)}, u32[]{:S(2)}) collective-permute-start(bf16[112,576]{1,0:T(8,128)(2,1)} %sum.1.b0), channel_id=1, source_target_pairs={{0,8},{8,0},{16,24},{24,16},{1,9},{9,1},{17,25},{25,17},{2,10},{10... | collective-permute-start | bytes 387080 | tf_op jit(solution)/shard_map/ppermute | solution.py:794
  251.4 8.9 %collective-permute-start.32 = (bf16[112,576]{1,0:T(8,128)(2,1)}, bf16[112,576]{1,0:T(8,128)(2,1)S(1)}, u32[]{:S(2)}, u32[]{:S(2)}) collective-permute-start(bf16[112,576]{1,0:T(8,128)(2,1)} %sum.1.b0), channel_id=1, source_target_pairs={{0,16},{8,24},{16,0},{24,8},{1,17},{9,25},{17,1},{25,9},{2,18},{10... | collective-permute-start | bytes 387080 | tf_op jit(solution)/shard_map/ppermute | solution.py:794
  253.4 7.8 %collective-permute-start.33 = (bf16[112,576]{1,0:T(8,128)(2,1)}, bf16[112,576]{1,0:T(8,128)(2,1)S(1)}, u32[]{:S(2)}, u32[]{:S(2)}) collective-permute-start(bf16[112,576]{1,0:T(8,128)(2,1)} %sum.1.b0), channel_id=1, source_target_pairs={{0,24},{8,16},{16,8},{24,0},{1,25},{9,17},{17,9},{25,1},{2,26},{10... | collective-permute-start | bytes 387080 | tf_op jit(solution)/shard_map/ppermute | solution.py:794
  257.2 9.6 %copy-start.21 = (bf16[112,576]{1,0:T(8,128)(2,1)}, bf16[112,576]{1,0:T(8,128)(2,1)S(1)}, u32[]{:S(2)}) copy-start(bf16[112,576]{1,0:T(8,128)(2,1)S(1)} %collective-permute-done.31.b1) | copy-start | bytes 387076
  260.2 6.6 %copy-start.22 = (bf16[112,576]{1,0:T(8,128)(2,1)}, bf16[112,576]{1,0:T(8,128)(2,1)S(1)}, u32[]{:S(2)}) copy-start(bf16[112,576]{1,0:T(8,128)(2,1)S(1)} %collective-permute-done.32.b2) | copy-start | bytes 387076
  261.2 5.6 %copy-start.23 = (bf16[112,576]{1,0:T(8,128)(2,1)}, bf16[112,576]{1,0:T(8,128)(2,1)S(1)}, u32[]{:S(2)}) copy-start(bf16[112,576]{1,0:T(8,128)(2,1)S(1)} %collective-permute-done.33.b3) | copy-start | bytes 387076
  261.2 11.7 %collective-permute-start.34 = (bf16[240,768]{1,0:T(8,128)(2,1)}, bf16[240,768]{1,0:T(8,128)(2,1)S(1)}, u32[]{:S(2)}, u32[]{:S(2)}) collective-permute-start(bf16[240,768]{1,0:T(8,128)(2,1)} %get-tuple-element.162.b0), channel_id=1, source_target_pairs={{0,8},{8,0},{16,24},{24,16},{1,9},{9,1},{17,25},{25,17},{2,10},{10... | collective-permute-start | bytes 1105928 | tf_op jit(solution)/shard_map/ppermute | solution.py:794
  262.3 18.0 %collective-permute-start.35 = (bf16[240,768]{1,0:T(8,128)(2,1)}, bf16[240,768]{1,0:T(8,128)(2,1)S(1)}, u32[]{:S(2)}, u32[]{:S(2)}) collective-permute-start(bf16[240,768]{1,0:T(8,128)(2,1)} %get-tuple-element.162.b0), channel_id=1, source_target_pairs={{0,16},{8,24},{16,0},{24,8},{1,17},{9,25},{17,1},{25,9},{2,18},{10... | collective-permute-start | bytes 1105928 | tf_op jit(solution)/shard_map/ppermute | solution.py:794
  263.6 16.8 %collective-permute-start.36 = (bf16[240,768]{1,0:T(8,128)(2,1)}, bf16[240,768]{1,0:T(8,128)(2,1)S(1)}, u32[]{:S(2)}, u32[]{:S(2)}) collective-permute-start(bf16[240,768]{1,0:T(8,128)(2,1)} %get-tuple-element.162.b0), channel_id=1, source_target_pairs={{0,24},{8,16},{16,8},{24,0},{1,25},{9,17},{17,9},{25,1},{2,26},{10... | collective-permute-start | bytes 1105928 | tf_op jit(solution)/shard_map/ppermute | solution.py:794
  272.9 7.5 %copy-start.14 = (bf16[240,768]{1,0:T(8,128)(2,1)}, bf16[240,768]{1,0:T(8,128)(2,1)S(1)}, u32[]{:S(2)}) copy-start(bf16[240,768]{1,0:T(8,128)(2,1)S(1)} %collective-permute-done.34.b1) | copy-start | bytes 1105924
  (16 other events, 14.1 us)
Sparse Core Ops, SparseCore 0:
  11.6 101.5 all-gather.1
  216.0 30.8 reduce-scatter.1

commit v3 on v2

--- a/solution.py
+++ b/solution.py
@@ -519,8 +519,7 @@
     y3,
     keep,
     send,
-    sums,
-    up_sums,
+    vectors,
     w_out,
     w_up,
     w_down,
@@ -589,25 +588,35 @@
     gain_two = small[4:5, :]
     output[...] = (unit_two * gain_two + small[5:6, :]).astype(jnp.bfloat16)
     grad = cotangent[...].astype(jnp.float32)
-    sums[3:4, :] = jnp.sum(grad * unit_two, axis=0, keepdims=True)
-    sums[4:5, :] = jnp.sum(grad, axis=0, keepdims=True)
+    sum_rows = {
+        3: jnp.sum(grad * unit_two, axis=0, keepdims=True),
+        4: jnp.sum(grad, axis=0, keepdims=True),
+    }
     grad_two = normalize_back(grad * gain_two, unit_two, inverse_two)
-    sums[5:6, :] = jnp.sum(grad_two, axis=0, keepdims=True)
+    sum_rows[5] = jnp.sum(grad_two, axis=0, keepdims=True)
+    vectors[...] = jnp.zeros_like(vectors)
+    half = width // 2
     two_low = grad_two.astype(jnp.bfloat16)
     grad_normed = grad_two
     for b in range(blocks):
         span = slice(b * width, (b + 1) * width)
         rows_down = w_down[b].reshape(width, width)
         part = dot_nt(two_low, rows_down) * slope[:, span]
-        up_sums[:, span] = jnp.sum(part, axis=0, keepdims=True)
+        up_row = jnp.sum(part, axis=0, keepdims=True).astype(jnp.bfloat16)
+        vectors[b, 3:4, :] = up_row[:, :half]
+        vectors[b, 4:5, :] = up_row[:, half:]
         part = part.astype(jnp.bfloat16)
         grad_up[:, span] = part
         grad_normed = grad_normed + dot_nt(part, w_up[b].reshape(width, width))
-    sums[1:2, :] = jnp.sum(grad_normed * unit_one, axis=0, keepdims=True)
-    sums[2:3, :] = jnp.sum(grad_normed, axis=0, keepdims=True)
+    sum_rows[1] = jnp.sum(grad_normed * unit_one, axis=0, keepdims=True)
+    sum_rows[2] = jnp.sum(grad_normed, axis=0, keepdims=True)
     first = normalize_back(grad_normed * gain_one, unit_one, inverse_one)
-    sums[0:1, :] = jnp.sum(first, axis=0, keepdims=True)
-    sums[6:8, :] = jnp.zeros((2, width), jnp.float32)
+    sum_rows[0] = jnp.sum(first, axis=0, keepdims=True)
+    for z in range(4):
+        at = slice(z * out_rows, (z + 1) * out_rows)
+        for row in range(3):
+            pair = [sum_rows[2 * row][:, at], sum_rows[2 * row + 1][:, at]]
+            vectors[z, row : row + 1, :] = jnp.concatenate(pair, axis=1).astype(jnp.bfloat16)
     grad_one[...] = first
     one_low = first.astype(jnp.bfloat16)
     for j, out in enumerate((y0, y1, y2, y3)):
@@ -615,7 +624,6 @@
     for j, block in enumerate((x0, x1, x2, x3)):
         context[place ^ j] = block[...]
     joined = jnp.concatenate([context[j] for j in range(4)], axis=1)
-    half = width // 2
     down_rows = blocks * shard_rows
     for ref, mine in ((keep, core), (send, 1 - core)):
         for z in range(4):
@@ -641,10 +649,12 @@
     _, zs, shard_rows, width = near.shape
     down_rows = 4 * shard_rows
     at_two = zs * down_rows
-    right = slice(at_two, at_two + width)
+    def both(where):
+        return jnp.concatenate([keep[:, where], got[:, where]], axis=0)
+
+    right = both(slice(at_two, at_two + width))
     for z in range(zs):
-        left = slice(z * down_rows, (z + 1) * down_rows)
-        total = dot_tn(keep[:, left], keep[:, right]) + dot_tn(got[:, left], got[:, right])
+        total = dot_tn(both(slice(z * down_rows, (z + 1) * down_rows)), right)
         part[...] = total.astype(jnp.bfloat16).reshape(4, shard_rows, width)
         for out, at, j in ((near, 0, 0), (near, 1, 2), (far, 0, 1), (far, 1, 3)):
             out[at, z] = part[place ^ j]
@@ -660,15 +670,15 @@
     at_up = at_norm + width
     at_ctx = at_up + 2 * width
     at_one = at_ctx + width
-    left = slice(at_ctx, at_ctx + width)
-    right = slice(at_one, at_one + cols)
-    total = dot_tn(keep[:, left], keep[:, right]) + dot_tn(got[:, left], got[:, right])
+    def both(where):
+        return jnp.concatenate([keep[:, where], got[:, where]], axis=0)
+
+    total = dot_tn(both(slice(at_ctx, at_ctx + width)), both(slice(at_one, at_one + cols)))
     part[...] = total.astype(jnp.bfloat16).reshape(part.shape)
-    left = slice(at_norm, at_norm + width)
+    left = both(slice(at_norm, at_norm + width)).T
     for out, at, j in ((near, 0, 0), (near, 1, 1), (far, 0, 2), (far, 1, 3)):
         right = pl.ds(pl.multiple_of(at_up + (place ^ j) * cols, 128), cols)
-        total = dot_tn(keep[:, left], keep[:, right]) + dot_tn(got[:, left], got[:, right])
-        total = total.astype(jnp.bfloat16)
+        total = dot_nn(left, both(right)).astype(jnp.bfloat16)
         for z in range(zs):
             out[at, z, :pair_rows] = total[z * pair_rows : (z + 1) * pair_rows]
             out[at, z, pair_rows : pair_rows + quarter] = part[z, place ^ j]
@@ -688,6 +698,19 @@
         out[at] = total.astype(jnp.bfloat16)
 
 
+def level_merge_kernel(sc, d_mine, d_got, u_mine, u_got, near, far):
+    level = sc[3]
+    up_rows, cols = u_mine.shape[1:]
+    rows = d_mine.shape[1]
+    for out, at, k in ((near, 0, 0), (near, 1, 2), (far, 0, 1), (far, 1, 3)):
+        total = u_mine[level ^ k].astype(jnp.float32) + u_got[level ^ k].astype(jnp.float32)
+        out[at, :up_rows] = total.astype(jnp.bfloat16)
+        total = d_mine[level ^ k].astype(jnp.float32) + d_got[level ^ k].astype(jnp.float32)
+        total = total.astype(jnp.bfloat16)
+        out[at, up_rows : up_rows + rows] = total[:, :cols]
+        out[at, up_rows + rows :] = total[:, cols:]
+
+
 def block_sum(refs):
     total = refs[0][...].astype(jnp.float32)
     for ref in refs[1:]:
@@ -695,20 +718,25 @@
     return total
 
 
-def split_up_kernel(sc, e0, e1, keep, send, held):
+def split_up_kernel(sc, e0, e1, keep, send, down, held):
     core = sc[2]
-    shard_rows = ((keep.shape[0] - 16) * 2) // 3
+    shard_rows, width = down.shape
+    cols = width // 2
+    half_rows = keep.shape[0] - shard_rows
     held[...] = block_sum((e0, e1)).astype(jnp.bfloat16)
     for ref, side in ((keep, core), (send, 1 - core)):
         ref[:shard_rows] = held[pl.ds(pl.multiple_of(side * shard_rows, 16), shard_rows), :]
-        ref[shard_rows:] = held[2 * shard_rows :, :]
-
-
-def join_kernel(sc, e0, e1, keep, got, out, vectors):
+        ref[shard_rows:] = held[2 * shard_rows : 2 * shard_rows + half_rows, :]
+    at = 2 * shard_rows + half_rows
+    down[:, :cols] = held[at : at + shard_rows, :]
+    down[:, cols:] = held[at + shard_rows :, :]
+
+
+def join_kernel(sc, down, keep, got, out, vectors):
     core = sc[2]
-    shard_rows = e0.shape[0]
+    shard_rows = down.shape[0]
     cols = keep.shape[1]
-    out[:shard_rows] = block_sum((e0, e1)).astype(jnp.bfloat16)
+    out[:shard_rows] = down[...]
     for ref, side in ((keep, core), (got, 1 - core)):
         out[shard_rows:, pl.ds(pl.multiple_of(side * cols, 128), cols)] = ref[:-16]
     vectors[...] = keep[-16:].astype(jnp.float32) + got[-16:].astype(jnp.float32)
@@ -864,7 +892,7 @@
     small = jnp.concatenate([six, jnp.zeros((2, width), f32)], axis=0)
     full_up_bias = all_vec[:, 6 * shard_rows : 6 * shard_rows + hidden // 8].reshape(1, hidden)
     packed = hidden // 2 + 5 * width + width // 2
-    output, grad_one, y0, y1, y2, y3, keep, send, sums, up_sums = pl.pallas_call(
+    output, grad_one, y0, y1, y2, y3, keep, send, vector_rows = pl.pallas_call(
         middle_kernel,
         name="middle",
         cost_estimate=work(15),
@@ -877,13 +905,12 @@
             struct((rows, head_width)),
             struct((rows, packed)),
             struct((rows, packed)),
-            struct((8, width), f32),
-            struct((1, hidden), f32),
+            struct((zs, 16, hidden // 8)),
         ),
         in_specs=[smem_spec()]
         + vmem_specs(8)
         + [pl.BlockSpec(memory_space=pl.ANY)] * 3,
-        out_specs=tuple(vmem_specs(10)),
+        out_specs=tuple(vmem_specs(9)),
         scratch_shapes=[
             pltpu.VMEM((zs, 2, shard_rows, width), bf16),
             pltpu.VMEM((4, zs, 2, shard_rows, width), bf16),
@@ -932,10 +959,6 @@
         scratch=[pltpu.VMEM((4, shard_rows, width), bf16)],
     )
     block_rows = 2 * shard_rows + shard_rows // 2 + 16
-    six_sets = sums[:6].reshape(6, zs, 2 * shard_rows).transpose(1, 0, 2)
-    up_sets = up_sums.reshape(zs, 4, 2 * shard_rows)
-    vector_rows = jnp.concatenate([six_sets, up_sets], axis=1).reshape(zs, 5, quad)
-    vector_rows = jnp.pad(vector_rows.astype(bf16), ((0, 0), (0, 11), (0, 0)))
     u_near, u_far = call(
         up_grad_kernel,
         4,
@@ -1005,42 +1028,40 @@
         sum_kernel, 1, [struct((q_rows, 3 * head_width))], q_mine, q_last, scalars=False
     )
 
-    def seq_sum(mine, pass_on, shape, step):
-        return call(
-            level_fold_kernel,
-            1,
-            [struct((2,) + shape[1:])] * 2,
-            mine,
-            across(pass_on, step),
-        )
-
     d_mine, u_mine, _ = lax.optimization_barrier((d_mine, u_mine, q_mine))
-    d_near, d_far = seq_sum(d_mine, d_pass, (zs, shard_rows, width), 2)
-    u_near, u_far = seq_sum(u_mine, u_pass, (zs, block_rows, quad), 1)
-    token_parts, _, _ = lax.optimization_barrier((token_parts, u_near, d_near))
+    merged_rows = block_rows + 2 * shard_rows
+    near, far = call(
+        level_merge_kernel,
+        2,
+        [struct((2, merged_rows, quad))] * 2,
+        d_mine,
+        across(d_pass, 2),
+        u_mine,
+        across(u_pass, 1),
+    )
+    token_parts, _ = lax.optimization_barrier((token_parts, near))
     token_sum = lax.psum_scatter(
         token_parts.reshape(4 * rows, width), "seq", scatter_dimension=0, tiled=True
     )
-    d_parts = level_sum(d_near, d_far, (shard_rows, width))
-    u_parts = level_sum(u_near, u_far, (block_rows, quad))
+    merged = level_sum(near, far, (merged_rows, quad))
     half_rows = shard_rows + shard_rows // 2 + 16
-    u_keep, u_send = call(
+    u_keep, u_send, d_part = call(
         split_up_kernel,
         1,
-        [struct((half_rows, quad))] * 2,
-        *u_parts,
-        scratch=[pltpu.VMEM((block_rows, quad), bf16)],
+        [struct((half_rows, quad))] * 2 + [struct((shard_rows, width))],
+        *merged,
+        scratch=[pltpu.VMEM((merged_rows, quad), bf16)],
     )
     joined, vector_totals = call(
         join_kernel,
         1,
         [struct((shard_rows + half_rows - 16, width)), struct((16, quad), f32)],
-        *d_parts,
+        d_part,
         u_keep,
         partner(u_send),
     )
     q_others = [across(q_part, j) for j in (1, 2, 3)]
-    joined, q_others = lax.optimization_barrier((joined, q_others))
+    joined, q_others, token_sum = lax.optimization_barrier((joined, q_others, token_sum))
     six = lax.dynamic_index_in_dim(
         vector_totals[:3].reshape(6, 2, shard_rows), core, axis=1, keepdims=False
     )

time: 295 us -> 294 us (level)
  waiting for transfers between devices: 107 us -> 121 us
  local copies, waits for them, and re-layouts: 28 us -> 21 us
    ppermute x10 -> x8, waiting for transfers between devices: 44.6 us -> 56.3 us  [level_across(): return lax.ppermute(value, 'z', [(i, i ^ step) for i in range(4)])]
    pallas_call x16 -> x14, Pallas kernels: 45.5 us -> 42.7 us  [call(): pl.pallas_call(kernel, name=kernel.__name__.replace('_kernel', ''), cost_...]
    ppermute x10 -> x8, starting transfers between devices: 18.1 us -> 16.4 us  [level_across(): return lax.ppermute(value, 'z', [(i, i ^ step) for i in range(4)])]
  transfers between devices with their start and end apart: 39 -> 37, of which waited for: 21 -> 21; matrix products, arithmetic and copies ran while one was open for 7% -> 4% of each run, Pallas kernels for 23% -> 20%
where the time goes in v3:
time: 294 us; the launch traced here: 293 us
  waiting for transfers between devices  121 us (41%)
  Pallas kernels  88.1 us (30%)
  starting transfers between devices  42.4 us (14%)
  local copies, waits for them, and re-layouts  21 us (7%)
  between operations  15.1 us (5%)
  other arithmetic  5.23 us (2%)
    ppermute x8, waiting for transfers between devices, level_across(): return lax.ppermute(value, 'z', [(i, i ^ step) for i in range(4)])  56.3 us
    ppermute x22, waiting for transfers between devices, across(): return lax.ppermute(value, 'seq', [(i, i ^ step) for i in range(4)])  55.6 us
    pallas_call x14, Pallas kernels, call(): pl.pallas_call(kernel, name=kernel.__name__.replace('_kernel', ''), cost_...  42.7 us
    ppermute x22, starting transfers between devices, across(): return lax.ppermute(value, 'seq', [(i, i ^ step) for i in range(4)])  25.5 us
    ppermute x8, starting transfers between devices, level_across(): return lax.ppermute(value, 'z', [(i, i ^ step) for i in range(4)])  16.4 us
    pallas_call x1, Pallas kernels, fast_body(): pl.pallas_call(middle_kernel, name='middle', cost_estimate=work(15), out_...  15.4 us
    pallas_call x1, Pallas kernels, fast_body(): pl.pallas_call(attend_forward_kernel, name='attend_forward', cost_estimat...  13.1 us
    pallas_call x1, Pallas kernels, fast_body(): pl.pallas_call(attend_backward_kernel, name='attend_backward', cost_estim...  12.6 us
  transfers between devices with their start and end apart: 37, of which 21 were waited for; matrix products, arithmetic and copies ran while one was open for 4% of the time, Pallas kernels for 20%

profile of v3, /device:TPU:0, one launch (start us, length us, event | category | flops | bytes accessed | tf_op | source)
XLA Modules:
  0.0 293.4 jit_solution(8620562667735589552)
XLA Ops:
  7.3 1.0 constant_dynamic-slice_fusion.8
  9.9 1.7 reshape.79
  12.9 3.0 %collective-permute-start.2 = (bf16[112,576]{1,0:T(8,128)(2,1)S(1)}, bf16[112,576]{1,0:T(8,128)(2,1)S(1)}, u32[]{:S(2)}, u32[]{:S(2)}) collective-permute-start(bf16[112,576]{1,0:T(8,128)(2,1)S(1)} %pad_maximum_fusion.6), channel_id=1, source_target_pairs={{0,2},{2,0},{4,6},{6,4},{1,3},{3,1},{5,7},{7,5},{8,10},{10,8},{12,... | collective-permute-start | bytes 387080 | tf_op jit(solution)/shard_map/ppermute | solution.py:828
  16.1 4.4 %collective-permute-done.2 = bf16[112,576]{1,0:T(8,128)(2,1)S(1)} collective-permute-done((bf16[112,576]{1,0:T(8,128)(2,1)S(1)}, bf16[112,576]{1,0:T(8,128)(2,1)S(1)}, u32[]{:S(2)}, u32[]{:S(2)}) %collective-permute-start.2) | collective-permute-done | bytes 129056 | tf_op jit(solution)/shard_map/ppermute | solution.py:828
  20.6 3.1 %collective-permute-start.3 = (bf16[2,112,576]{2,1,0:T(8,128)(2,1)S(1)}, bf16[2,112,576]{2,1,0:T(8,128)(2,1)S(1)}, u32[]{:S(2)}, u32[]{:S(2)}) collective-permute-start(bf16[2,112,576]{2,1,0:T(8,128)(2,1)S(1)} %pad_maximum_fusion.4), channel_id=1, source_target_pairs={{0,4},{2,6},{4,0},{6,2},{1,5},{3,7},{5,1},{7,3},{8,12},{10,14},{12... | collective-permute-start | bytes 774152 | tf_op jit(solution)/shard_map/ppermute | solution.py:828
  24.4 2.5 collective-permute-start.1
  26.9 1.5 collective-permute-start.4
  28.4 1.5 collective-permute-start.5
  30.3 17.2 %collective-permute-done.3 = bf16[2,112,576]{2,1,0:T(8,128)(2,1)S(1)} collective-permute-done((bf16[2,112,576]{2,1,0:T(8,128)(2,1)S(1)}, bf16[2,112,576]{2,1,0:T(8,128)(2,1)S(1)}, u32[]{:S(2)}, u32[]{:S(2)}) %collective-permute-start.3) | collective-permute-done | bytes 258080 | tf_op jit(solution)/shard_map/ppermute | solution.py:828
  47.6 4.2 %collective-permute-done.1 = bf16[2,96,768]{2,1,0:T(8,128)(2,1)S(1)} collective-permute-done((bf16[2,96,768]{2,1,0:T(8,128)(2,1)S(1)}, bf16[2,96,768]{2,1,0:T(8,128)(2,1)S(1)}, u32[]{:S(2)}, u32[]{:S(2)}) %collective-permute-start.1) | collective-permute-done | bytes 294944 | tf_op jit(solution)/shard_map/ppermute | solution.py:828
  52.0 1.4 collective-permute-start.11
  53.4 1.5 collective-permute-start.12
  57.7 13.1 %attend_forward.1 = (bf16[1024,576]{1,0:T(8,128)(2,1)}, f32[192,1024]{1,0:T(8,128)}, bf16[256,192]{1,0:T(8,128)(2,1)}, bf16[256,192]{1,0:T(8,128)(2,1)}, bf16[25...) custom-call(s32[4]{0:T(128)} %pad_add_fusion.sc, ...), custom_call_target="tpu_custom_call" | custom-call | flops 1170000000 | bytes 3900000 | tf_op jit(solution)/shard_map/attend_forward/pallas_call | solution.py:866
  70.8 3.1 %collective-permute-done.11 = bf16[4,96,768]{2,1,0:T(8,128)(2,1)} collective-permute-done((bf16[4,96,768]{2,1,0:T(8,128)(2,1)S(1)}, bf16[4,96,768]{2,1,0:T(8,128)(2,1)}, u32[]{:S(2)}, u32[]{:S(2)}) %collective-permute-start.11) | collective-permute-done | bytes 589856 | tf_op jit(solution)/shard_map/ppermute | solution.py:822
  74.0 14.2 %collective-permute-done.13 = bf16[4,96,768]{2,1,0:T(8,128)(2,1)} collective-permute-done((bf16[4,96,768]{2,1,0:T(8,128)(2,1)S(1)}, bf16[4,96,768]{2,1,0:T(8,128)(2,1)}, u32[]{:S(2)}, u32[]{:S(2)}) %collective-permute-start.13) | collective-permute-done | bytes 589856 | tf_op jit(solution)/shard_map/ppermute | solution.py:822
  88.1 1.7 pad_maximum_fusion.own_down
  90.9 2.6 collective-permute-start.10
  93.5 1.3 collective-permute-start.9
  96.2 4.8 %collective-permute-done.10.x3 = bf16[256,192]{1,0:T(8,128)(2,1)S(1)} collective-permute-done((bf16[256,192]{1,0:T(8,128)(2,1)}, bf16[256,192]{1,0:T(8,128)(2,1)S(1)}, u32[]{:S(2)}, u32[]{:S(2)}) %collective-permute-start.10) | collective-permute-done | bytes 98336 | tf_op jit(solution)/shard_map/ppermute | solution.py:822
  101.1 1.8 collective-permute-done.8.x1
  103.7 9.5 %all-gather.2.cloned.1.call-done = bf16[4096,768]{1,0:T(8,128)(2,1)} async-done(((bf16[128,768]{1,0:T(8,128)(2,1)}), bf16[4096,768]{1,0:T(8,128)(2,1)}) %all-gather.2.cloned.1.call-update) | async-done | bytes 6291472 | tf_op jit(solution)/shard_map/all_gather | solution.py:838
  113.2 15.4 %middle.1 = (bf16[256,768]{1,0:T(8,128)(2,1)}, f32[256,768]{1,0:T(8,128)}, bf16[256,192]{1,0:T(8,128)(2,1)}, bf16[256,192]{1,0:T(8,128)(2,1)}, bf16[256,192]{1,0...) custom-call(s32[4]{0:T(128)} %pad_add_fusion.sc, ...), custom_call_target="tpu_custom_call" | custom-call | flops 1350000000 | bytes 4500000 | tf_op jit(solution)/shard_map/middle/pallas_call | solution.py:895
  128.9 1.3 collective-permute-start.16
  130.3 2.2 collective-permute-start.18
  132.4 2.9 collective-permute-done.16.g1
  135.3 3.4 %collective-permute-done.17.g2 = bf16[256,192]{1,0:T(8,128)(2,1)S(1)} collective-permute-done((bf16[256,192]{1,0:T(8,128)(2,1)}, bf16[256,192]{1,0:T(8,128)(2,1)S(1)}, u32[]{:S(2)}, u32[]{:S(2)}) %collective-permute-start.17) | collective-permute-done | bytes 98336 | tf_op jit(solution)/shard_map/ppermute | solution.py:822
  139.4 1.0 copy-done.1
  140.4 6.6 %up_grad.1 = (bf16[2,4,256,384]{3,2,1,0:T(8,128)(2,1)}, bf16[2,4,256,384]{3,2,1,0:T(8,128)(2,1)}) custom-call(s32[4]{0:T(128)} %pad_add_fusion.sc, bf16[256,5760]{1,0:T(8,128)(2,1)} %get-tuple-element.102.keep, bf16[256,5760]{1,0:T(8,128)(2,1)} %copy-done.1, bf16[4,16,384]{2,1,0:T(8,128)(2,1)} %get-tuple-element.109.vectors), custom_call_target="tpu_custom_call" | custom-call | flops 360000000 | bytes 1200000 | tf_op jit(solution)/shard_map/up_grad/pallas_call | solution.py:943
  147.3 5.9 %down_grad.1 = (bf16[2,4,96,768]{3,2,1,0:T(8,128)(2,1)}, bf16[2,4,96,768]{3,2,1,0:T(8,128)(2,1)}) custom-call(s32[4]{0:T(128)} %pad_add_fusion.sc, bf16[256,5760]{1,0:T(8,128)(2,1)} %get-tuple-element.102.keep, bf16[256,5760]{1,0:T(8,128)(2,1)} %copy-done.1), custom_call_target="tpu_custom_call" | custom-call | flops 360000000 | bytes 1200000 | tf_op jit(solution)/shard_map/down_grad/pallas_call | solution.py:943
  153.2 1.6 collective-permute-start.19
  154.9 12.6 %attend_backward.1.dqkv = bf16[1024,576]{1,0:T(8,128)(2,1)} custom-call(s32[4]{0:T(128)} %pad_add_fusion.sc, bf16[1024,576]{1,0:T(8,128)(2,1)} %get-tuple-element.113.qkv, f32[192,1024]{1,0:T(8,128)} %get-tuple-element.114.ctx_t, f32[3,1024]{1,0:T(4,128)} %get-tuple-element.115.lse, bf16[256,192]{1,0:T(8,128)(2,1)} %get-tuple-element.116.g0, ...), custom_call_target="tpu_custom_call" | custom-call | flops 990000000 | bytes 3300000 | tf_op jit(solution)/shard_map/attend_backward/pallas_call | solution.py:975
  167.4 4.3 %grad_qkv_weight.1 = (bf16[4,112,576]{2,1,0:T(8,128)(2,1)}, bf16[4,112,576]{2,1,0:T(8,128)(2,1)}) custom-call(s32[4]{0:T(128)} %pad_add_fusion.sc, bf16[256,768]{1,0:T(8,128)(2,1)} %bitcast.47, bf16[256,768]{1,0:T(8,128)(2,1)} %copy-done.11, bf16[256,768]{1,0:T(8,128)(2,1)} %copy-done.12, bf16[256,768]{1,0:T(8,128)(2,1)} %copy-done.13, ...), custom_call_target="tpu_custom_call" | custom-call | flops 360000000 | bytes 1200000 | tf_op jit(solution)/shard_map/grad_qkv_weight/pallas_call | solution.py:989
  171.8 10.8 %collective-permute-done.20.got = bf16[2,4,256,384]{3,2,1,0:T(8,128)(2,1)S(1)} collective-permute-done((bf16[2,4,256,384]{3,2,1,0:T(8,128)(2,1)}, bf16[2,4,256,384]{3,2,1,0:T(8,128)(2,1)S(1)}, u32[]{:S(2)}, u32[]{:S(2)}) %collective-permute-start.20) | collective-permute-done | bytes 1572896 | tf_op jit(solution)/shard_map/ppermute | solution.py:822
  182.6 1.1 copy-done.4
  183.7 3.2 %fold.5 = (bf16[4,256,384]{2,1,0:T(8,128)(2,1)}, bf16[4,256,384]{2,1,0:T(8,128)(2,1)}) custom-call(bf16[2,4,256,384]{3,2,1,0:T(8,128)(2,1)} %get-tuple-element.124.near, bf16[2,4,256,384]{3,2,1,0:T(8,128)(2,1)} %copy-done.4), custom_call_target="tpu_custom_call" | custom-call | flops 90000000 | bytes 300000 | tf_op jit(solution)/shard_map/fold/pallas_call | solution.py:943
  187.3 1.0 copy-done.5
  188.3 2.8 fold.4
  191.1 1.7 collective-permute-start.23
  192.8 2.1 level_fold.1
  194.9 2.0 collective-permute-start.22
  196.9 4.2 %grad_tokens.1 = bf16[4,256,768]{2,1,0:T(8,128)(2,1)} custom-call(s32[4]{0:T(128)} %pad_add_fusion.sc, bf16[1024,576]{1,0:T(8,128)(2,1)} %attend_backward.1.dqkv, bf16[4,2,96,576]{3,2,1,0:T(8,128)(2,1)} %get-tuple-element.147.weight), custom_call_target="tpu_custom_call" | custom-call | flops 360000000 | bytes 1200000 | tf_op jit(solution)/shard_map/grad_tokens/pallas_call | solution.py:943
  201.1 1.0 collective-permute-done.22.got
  202.8 1.8 fold.6
  206.3 3.0 %level_merge.1 = (bf16[2,448,384]{2,1,0:T(8,128)(2,1)}, bf16[2,448,384]{2,1,0:T(8,128)(2,1)}) custom-call(s32[4]{0:T(128)} %pad_add_fusion.sc, bf16[4,96,768]{2,1,0:T(8,128)(2,1)} %get-tuple-element.133.d_mine, bf16[4,96,768]{2,1,0:T(8,128)(2,1)} %copy-done.9, bf16[4,256,384]{2,1,0:T(8,128)(2,1)} %get-tuple-element.135.u_mine, bf16[4,256,384]{2,1,0:T(8,128)(2,1)} %copy-done.7), custom_call_target="tpu_custom_call" | custom-call | flops 180000000 | bytes 600000 | tf_op jit(solution)/shard_map/level_merge/pallas_call | solution.py:943
  209.3 2.7 collective-permute-start.25
  212.1 12.8 %collective-permute-done.25.got = bf16[2,448,384]{2,1,0:T(8,128)(2,1)S(1)} collective-permute-done((bf16[2,448,384]{2,1,0:T(8,128)(2,1)}, bf16[2,448,384]{2,1,0:T(8,128)(2,1)S(1)}, u32[]{:S(2)}, u32[]{:S(2)}) %collective-permute-start.25) | collective-permute-done | bytes 688160 | tf_op jit(solution)/shard_map/ppermute | solution.py:828
  225.7 2.2 fold.7
  228.0 2.1 collective-permute-start.26
  230.9 16.1 %collective-permute-done.26.e1 = bf16[448,384]{1,0:T(8,128)(2,1)S(1)} collective-permute-done((bf16[448,384]{1,0:T(8,128)(2,1)}, bf16[448,384]{1,0:T(8,128)(2,1)S(1)}, u32[]{:S(2)}, u32[]{:S(2)}) %collective-permute-start.26) | collective-permute-done | bytes 344096 | tf_op jit(solution)/shard_map/ppermute | solution.py:828
  247.8 2.0 split_up.1
  250.4 1.7 sum.1.b0
  252.1 1.0 collective-permute-start.29
  253.1 2.0 collective-permute-start.30
  256.2 1.8 join.1
  260.2 1.7 collective-permute-done.30.b2
  261.9 1.0 collective-permute-done.31.b3
  262.8 1.1 collective-permute-start.32
  264.0 1.3 collective-permute-start.33
  265.2 1.1 collective-permute-start.34
  266.9 2.3 finish_qkv.1
  269.2 1.8 fusion
  271.0 3.5 %collective-permute-done.32.b1 = bf16[240,768]{1,0:T(8,128)(2,1)S(1)} collective-permute-done((bf16[240,768]{1,0:T(8,128)(2,1)}, bf16[240,768]{1,0:T(8,128)(2,1)S(1)}, u32[]{:S(2)}, u32[]{:S(2)}) %collective-permute-start.32) | collective-permute-done | bytes 368672 | tf_op jit(solution)/shard_map/ppermute | solution.py:822
  274.6 7.5 %collective-permute-done.33.b2 = bf16[240,768]{1,0:T(8,128)(2,1)S(1)} collective-permute-done((bf16[240,768]{1,0:T(8,128)(2,1)}, bf16[240,768]{1,0:T(8,128)(2,1)S(1)}, u32[]{:S(2)}, u32[]{:S(2)}) %collective-permute-start.33) | collective-permute-done | bytes 368672 | tf_op jit(solution)/shard_map/ppermute | solution.py:822
  283.5 3.0 %finish.1 = (f32[384,768]{1,0:T(8,128)}, f32[96,3072]{1,0:T(8,128)}, f32[96,768]{1,0:T(8,128)}) custom-call(s32[4]{0:T(128)} %pad_add_fusion.sc, bf16[240,768]{1,0:T(8,128)(2,1)} %get-tuple-element.156.b0, bf16[240,768]{1,0:T(8,128)(2,1)} %copy-done.14, bf16[240,768]{1,0:T(8,128)(2,1)} %copy-done.15, bf16[240,768]{1,0:T(8,128)(2,1)} %copy-done.16), custom_call_target="tpu_custom_call" | custom-call | flops 180000000 | bytes 600000 | tf_op jit(solution)/shard_map/finish/pallas_call | solution.py:943
  (153 shorter events, 22.5 us)
Async XLA Ops:
  7.2 8.8 %copy-start = (bf16[384,768]{1,0:T(8,128)(2,1)S(1)}, bf16[384,768]{1,0:T(8,128)(2,1)}, u32[]{:S(2)}) copy-start(bf16[384,768]{1,0:T(8,128)(2,1)} %param.27) | copy-start | bytes 1769476
  7.2 5.1 %copy-start.37 = (bf16[96]{0:T(256)(128)(2,1)S(1)}, bf16[96]{0:T(256)(128)(2,1)}, u32[]{:S(2)}) copy-start(bf16[96]{0:T(256)(128)(2,1)} %param.19) | copy-start | bytes 580
  7.2 5.2 %copy-start.38 = (bf16[96]{0:T(256)(128)(2,1)S(1)}, bf16[96]{0:T(256)(128)(2,1)}, u32[]{:S(2)}) copy-start(bf16[96]{0:T(256)(128)(2,1)} %param.20) | copy-start | bytes 580
  7.2 5.3 %copy-start.31 = (bf16[96]{0:T(256)(128)(2,1)S(1)}, bf16[96]{0:T(256)(128)(2,1)}, u32[]{:S(2)}) copy-start(bf16[96]{0:T(256)(128)(2,1)} %param.22) | copy-start | bytes 580
  7.2 5.3 %copy-start.32 = (bf16[96]{0:T(256)(128)(2,1)S(1)}, bf16[96]{0:T(256)(128)(2,1)}, u32[]{:S(2)}) copy-start(bf16[96]{0:T(256)(128)(2,1)} %param.23) | copy-start | bytes 580
  7.2 5.3 %copy-start.33 = (bf16[96]{0:T(256)(128)(2,1)S(1)}, bf16[96]{0:T(256)(128)(2,1)}, u32[]{:S(2)}) copy-start(bf16[96]{0:T(256)(128)(2,1)} %param.24) | copy-start | bytes 580
  7.2 5.3 %copy-start.30 = (bf16[384]{0:T(512)(128)(2,1)S(1)}, bf16[384]{0:T(512)(128)(2,1)}, u32[]{:S(2)}) copy-start(bf16[384]{0:T(512)(128)(2,1)} %param.26) | copy-start | bytes 2308
  7.3 5.3 %copy-start.34 = (bf16[96]{0:T(256)(128)(2,1)S(1)}, bf16[96]{0:T(256)(128)(2,1)}, u32[]{:S(2)}) copy-start(bf16[96]{0:T(256)(128)(2,1)} %param.28) | copy-start | bytes 580
  7.3 5.3 %copy-start.35 = (bf16[96]{0:T(256)(128)(2,1)S(1)}, bf16[96]{0:T(256)(128)(2,1)}, u32[]{:S(2)}) copy-start(bf16[96]{0:T(256)(128)(2,1)} %param.29) | copy-start | bytes 580
  7.3 5.3 %copy-start.36 = (bf16[96]{0:T(256)(128)(2,1)S(1)}, bf16[96]{0:T(256)(128)(2,1)}, u32[]{:S(2)}) copy-start(bf16[96]{0:T(256)(128)(2,1)} %param.30) | copy-start | bytes 580
  7.3 105.9 %all-gather.2.cloned.1.call-start = ((), (), s32[]{:S(2)}) async-start(), calls=%async_computation.1 | async-start | bytes 6488064 | tf_op jit(solution)/shard_map/all_gather | solution.py:838
  9.8 253.0 %reduce-scatter.2.cloned.1.call-start = ((), (), s32[]{:S(2)}) async-start(), calls=%async_computation.2 | async-start | bytes 1966080 | tf_op jit(solution)/shard_map/reduce_scatter | solution.py:1043
  9.9 17.0 %copy-start.3 = (bf16[1,256,768]{2,1,0:T(8,128)(2,1)S(1)}, bf16[1,256,768]{2,1,0:T(8,128)(2,1)}, u32[]{:S(2)}) copy-start(bf16[1,256,768]{2,1,0:T(8,128)(2,1)} %param.16) | copy-start | bytes 1179652
  12.9 7.6 %collective-permute-start.2 = (bf16[112,576]{1,0:T(8,128)(2,1)S(1)}, bf16[112,576]{1,0:T(8,128)(2,1)S(1)}, u32[]{:S(2)}, u32[]{:S(2)}) collective-permute-start(bf16[112,576]{1,0:T(8,128)(2,1)S(1)} %pad_maximum_fusion.6), channel_id=1, source_target_pairs={{0,2},{2,0},{4,6},{6,4},{1,3},{3,1},{5,7},{7,5},{8,10},{10,8},{12,... | collective-permute-start | bytes 387080 | tf_op jit(solution)/shard_map/ppermute | solution.py:828
  16.0 8.4 %collective-permute-start = (bf16[96,768]{1,0:T(8,128)(2,1)S(1)}, bf16[96,768]{1,0:T(8,128)(2,1)S(1)}, u32[]{:S(2)}, u32[]{:S(2)}) collective-permute-start(bf16[96,768]{1,0:T(8,128)(2,1)S(1)} %constant_dynamic-slice_fusion.10), channel_id=1, source_target_pairs={{0,2},{2,0},{4,6},{6,4},{1,3},{3,1},{5,7},{7,5},{8,10},{10,8},{12,... | collective-permute-start | bytes 442376 | tf_op jit(solution)/shard_map/ppermute | solution.py:828
  20.6 26.9 %collective-permute-start.3 = (bf16[2,112,576]{2,1,0:T(8,128)(2,1)S(1)}, bf16[2,112,576]{2,1,0:T(8,128)(2,1)S(1)}, u32[]{:S(2)}, u32[]{:S(2)}) collective-permute-start(bf16[2,112,576]{2,1,0:T(8,128)(2,1)S(1)} %pad_maximum_fusion.4), channel_id=1, source_target_pairs={{0,4},{2,6},{4,0},{6,2},{1,5},{3,7},{5,1},{7,3},{8,12},{10,14},{12... | collective-permute-start | bytes 774152 | tf_op jit(solution)/shard_map/ppermute | solution.py:828
  24.4 27.5 %collective-permute-start.1 = (bf16[2,96,768]{2,1,0:T(8,128)(2,1)S(1)}, bf16[2,96,768]{2,1,0:T(8,128)(2,1)S(1)}, u32[]{:S(2)}, u32[]{:S(2)}) collective-permute-start(bf16[2,96,768]{2,1,0:T(8,128)(2,1)S(1)} %pad_maximum_fusion.3), channel_id=1, source_target_pairs={{0,4},{2,6},{4,0},{6,2},{1,5},{3,7},{5,1},{7,3},{8,12},{10,14},{12... | collective-permute-start | bytes 884744 | tf_op jit(solution)/shard_map/ppermute | solution.py:828
  26.9 25.0 %collective-permute-start.4 = (bf16[256,768]{1,0:T(8,128)(2,1)S(1)}, bf16[256,768]{1,0:T(8,128)(2,1)S(1)}, u32[]{:S(2)}, u32[]{:S(2)}) collective-permute-start(bf16[256,768]{1,0:T(8,128)(2,1)S(1)} %bitcast.48), channel_id=1, source_target_pairs={{0,8},{8,0},{16,24},{24,16},{1,9},{9,1},{17,25},{25,17},{2,10},{10... | collective-permute-start | bytes 1179656 | tf_op jit(solution)/shard_map/ppermute | solution.py:822
  28.4 23.6 %collective-permute-start.5 = (bf16[256,768]{1,0:T(8,128)(2,1)S(1)}, bf16[256,768]{1,0:T(8,128)(2,1)S(1)}, u32[]{:S(2)}, u32[]{:S(2)}) collective-permute-start(bf16[256,768]{1,0:T(8,128)(2,1)S(1)} %bitcast.49), channel_id=1, source_target_pairs={{0,16},{8,24},{16,0},{24,8},{1,17},{9,25},{17,1},{25,9},{2,18},{10... | collective-permute-start | bytes 1179656 | tf_op jit(solution)/shard_map/ppermute | solution.py:822
  29.9 22.1 %collective-permute-start.6 = (bf16[256,768]{1,0:T(8,128)(2,1)S(1)}, bf16[256,768]{1,0:T(8,128)(2,1)S(1)}, u32[]{:S(2)}, u32[]{:S(2)}) collective-permute-start(bf16[256,768]{1,0:T(8,128)(2,1)S(1)} %bitcast.50), channel_id=1, source_target_pairs={{0,24},{8,16},{16,8},{24,0},{1,25},{9,17},{17,9},{25,1},{2,26},{10... | collective-permute-start | bytes 1179656 | tf_op jit(solution)/shard_map/ppermute | solution.py:822
  47.6 9.3 %copy-start.10 = (bf16[4,112,576]{2,1,0:T(8,128)(2,1)}, bf16[4,112,576]{2,1,0:T(8,128)(2,1)S(1)}, u32[]{:S(2)}) copy-start(bf16[4,112,576]{2,1,0:T(8,128)(2,1)S(1)} %pad_maximum_fusion.2.own) | copy-start | bytes 1548292
  51.9 5.0 %copy-start.11 = (bf16[256,768]{1,0:T(8,128)(2,1)}, bf16[256,768]{1,0:T(8,128)(2,1)S(1)}, u32[]{:S(2)}) copy-start(bf16[256,768]{1,0:T(8,128)(2,1)S(1)} %collective-permute-done.4.t1) | copy-start | bytes 1179652
  51.9 4.9 %copy-start.12 = (bf16[256,768]{1,0:T(8,128)(2,1)}, bf16[256,768]{1,0:T(8,128)(2,1)S(1)}, u32[]{:S(2)}) copy-start(bf16[256,768]{1,0:T(8,128)(2,1)S(1)} %collective-permute-done.5.t2) | copy-start | bytes 1179652
  52.0 1.5 copy-start.13
  52.0 4.9 %collective-permute-start.7 = (bf16[4,112,576]{2,1,0:T(8,128)(2,1)S(1)}, bf16[4,112,576]{2,1,0:T(8,128)(2,1)S(1)}, u32[]{:S(2)}, u32[]{:S(2)}) collective-permute-start(bf16[4,112,576]{2,1,0:T(8,128)(2,1)S(1)} %pad_maximum_fusion.2.own), channel_id=1, source_target_pairs={{0,1},{1,0},{2,3},{3,2},{4,5},{5,4},{6,7},{7,6},{8,9},{9,8},{10,11... | collective-permute-start | bytes 1548296 | tf_op jit(solution)/shard_map/ppermute | solution.py:825
  52.0 21.9 %collective-permute-start.11 = (bf16[4,96,768]{2,1,0:T(8,128)(2,1)S(1)}, bf16[4,96,768]{2,1,0:T(8,128)(2,1)}, u32[]{:S(2)}, u32[]{:S(2)}) collective-permute-start(bf16[4,96,768]{2,1,0:T(8,128)(2,1)S(1)} %pad_maximum_fusion.1), channel_id=1, source_target_pairs={{0,8},{8,0},{16,24},{24,16},{1,9},{9,1},{17,25},{25,17},{2,10},{10... | collective-permute-start | bytes 1769480 | tf_op jit(solution)/shard_map/ppermute | solution.py:822
  53.4 20.5 %collective-permute-start.12 = (bf16[4,96,768]{2,1,0:T(8,128)(2,1)S(1)}, bf16[4,96,768]{2,1,0:T(8,128)(2,1)}, u32[]{:S(2)}, u32[]{:S(2)}) collective-permute-start(bf16[4,96,768]{2,1,0:T(8,128)(2,1)S(1)} %pad_maximum_fusion.1), channel_id=1, source_target_pairs={{0,16},{8,24},{16,0},{24,8},{1,17},{9,25},{17,1},{25,9},{2,18},{10... | collective-permute-start | bytes 1769480 | tf_op jit(solution)/shard_map/ppermute | solution.py:822
  55.0 33.2 %collective-permute-start.13 = (bf16[4,96,768]{2,1,0:T(8,128)(2,1)S(1)}, bf16[4,96,768]{2,1,0:T(8,128)(2,1)}, u32[]{:S(2)}, u32[]{:S(2)}) collective-permute-start(bf16[4,96,768]{2,1,0:T(8,128)(2,1)S(1)} %pad_maximum_fusion.1), channel_id=1, source_target_pairs={{0,24},{8,16},{16,8},{24,0},{1,25},{9,17},{17,9},{25,1},{2,26},{10... | collective-permute-start | bytes 1769480 | tf_op jit(solution)/shard_map/ppermute | solution.py:822
  89.9 23.3 %copy-start.2 = (bf16[4,4,96,768]{3,2,1,0:T(8,128)(2,1)}, bf16[4,4,96,768]{3,2,1,0:T(8,128)(2,1)S(1)}, u32[]{:S(2)}) copy-start(bf16[4,4,96,768]{3,2,1,0:T(8,128)(2,1)S(1)} %pad_maximum_fusion.own_down) | copy-start | bytes 7077892
  89.9 13.8 %collective-permute-start.14 = (bf16[4,4,96,768]{3,2,1,0:T(8,128)(2,1)S(1)}, bf16[4,4,96,768]{3,2,1,0:T(8,128)(2,1)}, u32[]{:S(2)}, u32[]{:S(2)}) collective-permute-start(bf16[4,4,96,768]{3,2,1,0:T(8,128)(2,1)S(1)} %pad_maximum_fusion.own_down), channel_id=1, source_target_pairs={{0,1},{1,0},{2,3},{3,2},{4,5},{5,4},{6,7},{7,6},{8,9},{9,8},{10,11... | collective-permute-start | bytes 7077896 | tf_op jit(solution)/shard_map/ppermute | solution.py:825
  90.9 10.2 %collective-permute-start.10 = (bf16[256,192]{1,0:T(8,128)(2,1)}, bf16[256,192]{1,0:T(8,128)(2,1)S(1)}, u32[]{:S(2)}, u32[]{:S(2)}) collective-permute-start(bf16[256,192]{1,0:T(8,128)(2,1)} %get-tuple-element.95), channel_id=1, source_target_pairs={{0,24},{8,16},{16,8},{24,0},{1,25},{9,17},{17,9},{25,1},{2,26},{10... | collective-permute-start | bytes 294920 | tf_op jit(solution)/shard_map/ppermute | solution.py:822
  93.5 9.4 %collective-permute-start.8 = (bf16[256,192]{1,0:T(8,128)(2,1)}, bf16[256,192]{1,0:T(8,128)(2,1)S(1)}, u32[]{:S(2)}, u32[]{:S(2)}) collective-permute-start(bf16[256,192]{1,0:T(8,128)(2,1)} %get-tuple-element.93), channel_id=1, source_target_pairs={{0,8},{8,0},{16,24},{24,16},{1,9},{9,1},{17,25},{25,17},{2,10},{10... | collective-permute-start | bytes 294920 | tf_op jit(solution)/shard_map/ppermute | solution.py:822
  93.5 10.2 %collective-permute-start.9 = (bf16[256,192]{1,0:T(8,128)(2,1)}, bf16[256,192]{1,0:T(8,128)(2,1)S(1)}, u32[]{:S(2)}, u32[]{:S(2)}) collective-permute-start(bf16[256,192]{1,0:T(8,128)(2,1)} %get-tuple-element.94), channel_id=1, source_target_pairs={{0,16},{8,24},{16,0},{24,8},{1,17},{9,25},{17,1},{25,9},{2,18},{10... | collective-permute-start | bytes 294920 | tf_op jit(solution)/shard_map/ppermute | solution.py:822
  101.1 12.1 %copy-start.23 = (bf16[256,192]{1,0:T(8,128)(2,1)}, bf16[256,192]{1,0:T(8,128)(2,1)S(1)}, u32[]{:S(2)}) copy-start(bf16[256,192]{1,0:T(8,128)(2,1)S(1)} %collective-permute-done.10.x3) | copy-start | bytes 294916
  102.9 10.3 %copy-start.24 = (bf16[256,192]{1,0:T(8,128)(2,1)}, bf16[256,192]{1,0:T(8,128)(2,1)S(1)}, u32[]{:S(2)}) copy-start(bf16[256,192]{1,0:T(8,128)(2,1)S(1)} %collective-permute-done.8.x1) | copy-start | bytes 294916
  103.7 9.5 %copy-start.25 = (bf16[256,192]{1,0:T(8,128)(2,1)}, bf16[256,192]{1,0:T(8,128)(2,1)S(1)}, u32[]{:S(2)}) copy-start(bf16[256,192]{1,0:T(8,128)(2,1)S(1)} %collective-permute-done.9.x2) | copy-start | bytes 294916
  128.6 10.1 %collective-permute-start.15 = (bf16[256,5760]{1,0:T(8,128)(2,1)}, bf16[256,5760]{1,0:T(8,128)(2,1)S(1)}, u32[]{:S(2)}, u32[]{:S(2)}) collective-permute-start(bf16[256,5760]{1,0:T(8,128)(2,1)} %get-tuple-element.103), channel_id=1, source_target_pairs={{0,1},{1,0},{2,3},{3,2},{4,5},{5,4},{6,7},{7,6},{8,9},{9,8},{10,11... | collective-permute-start | bytes 8847368 | tf_op jit(solution)/shard_map/ppermute | solution.py:825
  128.9 6.3 %collective-permute-start.16 = (bf16[256,192]{1,0:T(8,128)(2,1)}, bf16[256,192]{1,0:T(8,128)(2,1)S(1)}, u32[]{:S(2)}, u32[]{:S(2)}) collective-permute-start(bf16[256,192]{1,0:T(8,128)(2,1)} %get-tuple-element.104), channel_id=1, source_target_pairs={{0,8},{8,0},{16,24},{24,16},{1,9},{9,1},{17,25},{25,17},{2,10},{10... | collective-permute-start | bytes 294920 | tf_op jit(solution)/shard_map/ppermute | solution.py:822
  130.3 8.4 %collective-permute-start.17 = (bf16[256,192]{1,0:T(8,128)(2,1)}, bf16[256,192]{1,0:T(8,128)(2,1)S(1)}, u32[]{:S(2)}, u32[]{:S(2)}) collective-permute-start(bf16[256,192]{1,0:T(8,128)(2,1)} %get-tuple-element.105), channel_id=1, source_target_pairs={{0,16},{8,24},{16,0},{24,8},{1,17},{9,25},{17,1},{25,9},{2,18},{10... | collective-permute-start | bytes 294920 | tf_op jit(solution)/shard_map/ppermute | solution.py:822
  130.3 8.4 %collective-permute-start.18 = (bf16[256,192]{1,0:T(8,128)(2,1)}, bf16[256,192]{1,0:T(8,128)(2,1)S(1)}, u32[]{:S(2)}, u32[]{:S(2)}) collective-permute-start(bf16[256,192]{1,0:T(8,128)(2,1)} %get-tuple-element.106), channel_id=1, source_target_pairs={{0,24},{8,16},{16,8},{24,0},{1,25},{9,17},{17,9},{25,1},{2,26},{10... | collective-permute-start | bytes 294920 | tf_op jit(solution)/shard_map/ppermute | solution.py:822
  135.3 3.4 %copy-start.26 = (bf16[256,192]{1,0:T(8,128)(2,1)}, bf16[256,192]{1,0:T(8,128)(2,1)S(1)}, u32[]{:S(2)}) copy-start(bf16[256,192]{1,0:T(8,128)(2,1)S(1)} %collective-permute-done.16.g1) | copy-start | bytes 294916
  138.7 1.7 copy-start.1
  147.0 35.6 %collective-permute-start.20 = (bf16[2,4,256,384]{3,2,1,0:T(8,128)(2,1)}, bf16[2,4,256,384]{3,2,1,0:T(8,128)(2,1)S(1)}, u32[]{:S(2)}, u32[]{:S(2)}) collective-permute-start(bf16[2,4,256,384]{3,2,1,0:T(8,128)(2,1)} %get-tuple-element.125), channel_id=1, source_target_pairs={{0,16},{8,24},{16,0},{24,8},{1,17},{9,25},{17,1},{25,9},{2,18},{10... | collective-permute-start | bytes 4718600 | tf_op jit(solution)/shard_map/ppermute | solution.py:822
  153.2 34.0 %collective-permute-start.19 = (bf16[2,4,96,768]{3,2,1,0:T(8,128)(2,1)}, bf16[2,4,96,768]{3,2,1,0:T(8,128)(2,1)S(1)}, u32[]{:S(2)}, u32[]{:S(2)}) collective-permute-start(bf16[2,4,96,768]{3,2,1,0:T(8,128)(2,1)} %get-tuple-element.122), channel_id=1, source_target_pairs={{0,8},{8,0},{16,24},{24,16},{1,9},{9,1},{17,25},{25,17},{2,10},{10... | collective-permute-start | bytes 3538952 | tf_op jit(solution)/shard_map/ppermute | solution.py:822
  171.8 21.1 %collective-permute-start.21 = (bf16[4,112,576]{2,1,0:T(8,128)(2,1)}, bf16[4,112,576]{2,1,0:T(8,128)(2,1)}, u32[]{:S(2)}, u32[]{:S(2)}) collective-permute-start(bf16[4,112,576]{2,1,0:T(8,128)(2,1)} %get-tuple-element.129), channel_id=1, source_target_pairs={{0,1},{1,0},{2,3},{3,2},{4,5},{5,4},{6,7},{7,6},{8,9},{9,8},{10,11... | collective-permute-start | bytes 1548296 | tf_op jit(solution)/shard_map/ppermute | solution.py:825
  186.9 17.8 %collective-permute-start.24 = (bf16[4,256,384]{2,1,0:T(8,128)(2,1)}, bf16[4,256,384]{2,1,0:T(8,128)(2,1)S(1)}, u32[]{:S(2)}, u32[]{:S(2)}) collective-permute-start(bf16[4,256,384]{2,1,0:T(8,128)(2,1)} %get-tuple-element.136), channel_id=1, source_target_pairs={{0,8},{8,0},{16,24},{24,16},{1,9},{9,1},{17,25},{25,17},{2,10},{10... | collective-permute-start | bytes 2359304 | tf_op jit(solution)/shard_map/ppermute | solution.py:822
  191.1 13.5 %collective-permute-start.23 = (bf16[4,96,768]{2,1,0:T(8,128)(2,1)}, bf16[4,96,768]{2,1,0:T(8,128)(2,1)S(1)}, u32[]{:S(2)}, u32[]{:S(2)}) collective-permute-start(bf16[4,96,768]{2,1,0:T(8,128)(2,1)} %get-tuple-element.134), channel_id=1, source_target_pairs={{0,16},{8,24},{16,0},{24,8},{1,17},{9,25},{17,1},{25,9},{2,18},{10... | collective-permute-start | bytes 1769480 | tf_op jit(solution)/shard_map/ppermute | solution.py:822
  194.9 7.1 %collective-permute-start.22 = (bf16[2,112,576]{2,1,0:T(8,128)(2,1)}, bf16[2,112,576]{2,1,0:T(8,128)(2,1)S(1)}, u32[]{:S(2)}, u32[]{:S(2)}) collective-permute-start(bf16[2,112,576]{2,1,0:T(8,128)(2,1)} %get-tuple-element.131), channel_id=1, source_target_pairs={{0,2},{2,0},{4,6},{6,4},{1,3},{3,1},{5,7},{7,5},{8,10},{10,8},{12,... | collective-permute-start | bytes 774152 | tf_op jit(solution)/shard_map/ppermute | solution.py:828
  204.6 25.4 %copy-start.40 = (bf16[112,576]{1,0:T(8,128)(2,1)S(1)}, bf16[112,576]{1,0:T(8,128)(2,1)}, u32[]{:S(2)}) copy-start(bf16[112,576]{1,0:T(8,128)(2,1)} %get-tuple-element.145) | copy-start | bytes 387076
  209.3 59.9 %copy-start.6 = (f32[256,768]{1,0:T(8,128)S(1)}, f32[256,768]{1,0:T(8,128)}, u32[]{:S(2)}) copy-start(f32[256,768]{1,0:T(8,128)} %get-tuple-element.100) | copy-start | bytes 2359300
  209.3 15.6 %collective-permute-start.25 = (bf16[2,448,384]{2,1,0:T(8,128)(2,1)}, bf16[2,448,384]{2,1,0:T(8,128)(2,1)S(1)}, u32[]{:S(2)}, u32[]{:S(2)}) collective-permute-start(bf16[2,448,384]{2,1,0:T(8,128)(2,1)} %get-tuple-element.138), channel_id=1, source_target_pairs={{0,2},{2,0},{4,6},{6,4},{1,3},{3,1},{5,7},{7,5},{8,10},{10,8},{12,... | collective-permute-start | bytes 2064392 | tf_op jit(solution)/shard_map/ppermute | solution.py:828
  228.0 19.1 %collective-permute-start.26 = (bf16[448,384]{1,0:T(8,128)(2,1)}, bf16[448,384]{1,0:T(8,128)(2,1)S(1)}, u32[]{:S(2)}, u32[]{:S(2)}) collective-permute-start(bf16[448,384]{1,0:T(8,128)(2,1)} %get-tuple-element.140), channel_id=1, source_target_pairs={{0,4},{2,6},{4,0},{6,2},{1,5},{3,7},{5,1},{7,3},{8,12},{10,14},{12... | collective-permute-start | bytes 1032200 | tf_op jit(solution)/shard_map/ppermute | solution.py:828
  230.0 19.7 %collective-permute-start.28 = (bf16[112,576]{1,0:T(8,128)(2,1)S(1)}, bf16[112,576]{1,0:T(8,128)(2,1)S(1)}, u32[]{:S(2)}, u32[]{:S(2)}) collective-permute-start(bf16[112,576]{1,0:T(8,128)(2,1)S(1)} %copy-done.40), channel_id=1, source_target_pairs={{0,4},{2,6},{4,0},{6,2},{1,5},{3,7},{5,1},{7,3},{8,12},{10,14},{12... | collective-permute-start | bytes 387080 | tf_op jit(solution)/shard_map/ppermute | solution.py:828
  249.8 5.8 %collective-permute-start.27 = (bf16[160,384]{1,0:T(8,128)(2,1)}, bf16[160,384]{1,0:T(8,128)(2,1)S(1)}, u32[]{:S(2)}, u32[]{:S(2)}) collective-permute-start(bf16[160,384]{1,0:T(8,128)(2,1)} %get-tuple-element.143), channel_id=1, source_target_pairs={{0,1},{1,0},{2,3},{3,2},{4,5},{5,4},{6,7},{7,6},{8,9},{9,8},{10,11... | collective-permute-start | bytes 368648 | tf_op jit(solution)/shard_map/ppermute | solution.py:825
  252.1 8.1 %collective-permute-start.29 = (bf16[112,576]{1,0:T(8,128)(2,1)}, bf16[112,576]{1,0:T(8,128)(2,1)S(1)}, u32[]{:S(2)}, u32[]{:S(2)}) collective-permute-start(bf16[112,576]{1,0:T(8,128)(2,1)} %sum.1.b0), channel_id=1, source_target_pairs={{0,8},{8,0},{16,24},{24,16},{1,9},{9,1},{17,25},{25,17},{2,10},{10... | collective-permute-start | bytes 387080 | tf_op jit(solution)/shard_map/ppermute | solution.py:822
  253.1 8.8 %collective-permute-start.30 = (bf16[112,576]{1,0:T(8,128)(2,1)}, bf16[112,576]{1,0:T(8,128)(2,1)S(1)}, u32[]{:S(2)}, u32[]{:S(2)}) collective-permute-start(bf16[112,576]{1,0:T(8,128)(2,1)} %sum.1.b0), channel_id=1, source_target_pairs={{0,16},{8,24},{16,0},{24,8},{1,17},{9,25},{17,1},{25,9},{2,18},{10... | collective-permute-start | bytes 387080 | tf_op jit(solution)/shard_map/ppermute | solution.py:822
  255.1 7.8 %collective-permute-start.31 = (bf16[112,576]{1,0:T(8,128)(2,1)}, bf16[112,576]{1,0:T(8,128)(2,1)S(1)}, u32[]{:S(2)}, u32[]{:S(2)}) collective-permute-start(bf16[112,576]{1,0:T(8,128)(2,1)} %sum.1.b0), channel_id=1, source_target_pairs={{0,24},{8,16},{16,8},{24,0},{1,25},{9,17},{17,9},{25,1},{2,26},{10... | collective-permute-start | bytes 387080 | tf_op jit(solution)/shard_map/ppermute | solution.py:822
  260.2 6.7 %copy-start.19 = (bf16[112,576]{1,0:T(8,128)(2,1)}, bf16[112,576]{1,0:T(8,128)(2,1)S(1)}, u32[]{:S(2)}) copy-start(bf16[112,576]{1,0:T(8,128)(2,1)S(1)} %collective-permute-done.29.b1) | copy-start | bytes 387076
  261.9 5.0 %copy-start.20 = (bf16[112,576]{1,0:T(8,128)(2,1)}, bf16[112,576]{1,0:T(8,128)(2,1)S(1)}, u32[]{:S(2)}) copy-start(bf16[112,576]{1,0:T(8,128)(2,1)S(1)} %collective-permute-done.30.b2) | copy-start | bytes 387076
  262.8 4.0 %copy-start.21 = (bf16[112,576]{1,0:T(8,128)(2,1)}, bf16[112,576]{1,0:T(8,128)(2,1)S(1)}, u32[]{:S(2)}) copy-start(bf16[112,576]{1,0:T(8,128)(2,1)S(1)} %collective-permute-done.31.b3) | copy-start | bytes 387076
  262.8 11.7 %collective-permute-start.32 = (bf16[240,768]{1,0:T(8,128)(2,1)}, bf16[240,768]{1,0:T(8,128)(2,1)S(1)}, u32[]{:S(2)}, u32[]{:S(2)}) collective-permute-start(bf16[240,768]{1,0:T(8,128)(2,1)} %get-tuple-element.156.b0), channel_id=1, source_target_pairs={{0,8},{8,0},{16,24},{24,16},{1,9},{9,1},{17,25},{25,17},{2,10},{10... | collective-permute-start | bytes 1105928 | tf_op jit(solution)/shard_map/ppermute | solution.py:822
  264.0 18.0 %collective-permute-start.33 = (bf16[240,768]{1,0:T(8,128)(2,1)}, bf16[240,768]{1,0:T(8,128)(2,1)S(1)}, u32[]{:S(2)}, u32[]{:S(2)}) collective-permute-start(bf16[240,768]{1,0:T(8,128)(2,1)} %get-tuple-element.156.b0), channel_id=1, source_target_pairs={{0,16},{8,24},{16,0},{24,8},{1,17},{9,25},{17,1},{25,9},{2,18},{10... | collective-permute-start | bytes 1105928 | tf_op jit(solution)/shard_map/ppermute | solution.py:822
  265.2 16.8 %collective-permute-start.34 = (bf16[240,768]{1,0:T(8,128)(2,1)}, bf16[240,768]{1,0:T(8,128)(2,1)S(1)}, u32[]{:S(2)}, u32[]{:S(2)}) collective-permute-start(bf16[240,768]{1,0:T(8,128)(2,1)} %get-tuple-element.156.b0), channel_id=1, source_target_pairs={{0,24},{8,16},{16,8},{24,0},{1,25},{9,17},{17,9},{25,1},{2,26},{10... | collective-permute-start | bytes 1105928 | tf_op jit(solution)/shard_map/ppermute | solution.py:822
  274.5 7.5 %copy-start.14 = (bf16[240,768]{1,0:T(8,128)(2,1)}, bf16[240,768]{1,0:T(8,128)(2,1)S(1)}, u32[]{:S(2)}) copy-start(bf16[240,768]{1,0:T(8,128)(2,1)S(1)} %collective-permute-done.32.b1) | copy-start | bytes 1105924
  (14 other events, 11.1 us)
Sparse Core Ops, SparseCore 0:
  11.6 101.5 all-gather.1
  209.4 30.8 reduce-scatter.1

commit v4 on v3

--- a/solution.py
+++ b/solution.py
@@ -511,6 +511,8 @@
     gathered,
     own_down,
     other_down,
+    own_out,
+    other_out,
     output,
     grad_one,
     y0,
@@ -533,7 +535,6 @@
     blocks = w_up.shape[0]
     shard_rows = w_up.shape[3]
     width = w_up.shape[4]
-    third = shard_rows // 3
     copies = []
     for b in range(blocks):
         copies.append(
@@ -550,14 +551,14 @@
                         sems.at[7 + len(down_copies)],
                     )
                 )
-    out_copies = [
-        pltpu.make_async_copy(
-            gathered.at[:, :, b, shard_rows : shard_rows + third, :],
-            w_out.at[:, :, b * third : (b + 1) * third, :],
-            sems.at[blocks + b],
-        )
-        for b in range(3)
-    ]
+    out_copies = []
+    for k in range(4):
+        for side, block in ((core, own_out), (1 - core, other_out)):
+            out_copies.append(
+                pltpu.make_async_copy(
+                    block.at[k], w_out.at[level ^ k, side], sems.at[40 + len(out_copies)]
+                )
+            )
     for copy in out_copies + copies + down_copies:
         copy.start()
     for copy in out_copies:
@@ -732,14 +733,21 @@
     down[:, cols:] = held[at + shard_rows :, :]
 
 
-def join_kernel(sc, down, keep, got, out, vectors):
+def join_kernel(sc, down, keep, got, out, six, up_row):
     core = sc[2]
     shard_rows = down.shape[0]
     cols = keep.shape[1]
     out[:shard_rows] = down[...]
     for ref, side in ((keep, core), (got, 1 - core)):
         out[shard_rows:, pl.ds(pl.multiple_of(side * cols, 128), cols)] = ref[:-16]
-    vectors[...] = keep[-16:].astype(jnp.float32) + got[-16:].astype(jnp.float32)
+    vectors = keep[-16:].astype(jnp.float32) + got[-16:].astype(jnp.float32)
+    for row in range(3):
+        for side in range(2):
+            pair = vectors[row : row + 1, side * 2 * shard_rows : (side + 1) * 2 * shard_rows]
+            six[2 * row + side : 2 * row + side + 1, :] = jnp.where(
+                core == 0, pair[:, :shard_rows], pair[:, shard_rows:]
+            )
+    up_row[...] = jnp.where(core == 0, vectors[3:4], vectors[4:5])
 
 
 def finish_kernel(sc, b0, b1, b2, b3, down, up, out):
@@ -812,7 +820,6 @@
     place = lax.axis_index("seq")
     core = lax.axis_index("core")
     zs = 4
-    third = shard_rows // 3
     swap = [(0, 1), (1, 0)]
 
     def struct(shape, dtype=bf16):
@@ -831,12 +838,11 @@
     quarter = jnp.concatenate(
         [
             lax.dynamic_slice_in_dim(w_up, place * width, width, axis=1),
-            lax.dynamic_slice_in_dim(w_out, jnp.minimum(place, 2) * third, third, axis=0),
         ],
         axis=0,
     )
     gathered = lax.all_gather(quarter, ("z", "core", "seq"), axis=0, tiled=True)
-    gathered = gathered.reshape(zs, 2, 4, shard_rows + third, width)
+    gathered = gathered.reshape(zs, 2, 4, shard_rows, width)
     columns = lax.dynamic_index_in_dim(
         w_qkv.reshape(shard_rows, 3, 4, head_width), place, axis=2, keepdims=False
     ).reshape(shard_rows, 3 * head_width)
@@ -860,6 +866,11 @@
     own_down = jnp.concatenate([two_down, level_across(two_down, 2)])
     own_down, own_cols, t1, t2, t3 = lax.optimization_barrier((own_down, own_cols, t1, t2, t3))
     other_cols = partner(own_cols)
+    late_out, _ = lax.optimization_barrier((w_out, own_cols))
+    two_out = jnp.stack([late_out, level_across(late_out, 1)])
+    own_out = jnp.concatenate([two_out, level_across(two_out, 2)])
+    other_out = partner(own_out)
+    t1, own_out = lax.optimization_barrier((t1, own_out))
     down_sets = [own_down] + [across(own_down, j) for j in (1, 2, 3)]
     sc = jnp.stack([lengths[0], place, core, lax.axis_index("z")]).astype(jnp.int32)
     all_rows = 4 * rows
@@ -909,7 +920,7 @@
         ),
         in_specs=[smem_spec()]
         + vmem_specs(8)
-        + [pl.BlockSpec(memory_space=pl.ANY)] * 3,
+        + [pl.BlockSpec(memory_space=pl.ANY)] * 5,
         out_specs=tuple(vmem_specs(9)),
         scratch_shapes=[
             pltpu.VMEM((zs, 2, shard_rows, width), bf16),
@@ -919,7 +930,7 @@
             pltpu.VMEM((rows, hidden), bf16),
             pltpu.VMEM((rows, hidden), bf16),
             pltpu.VMEM((4, rows, head_width), bf16),
-            pltpu.SemaphoreType.DMA((7 + 32,)),
+            pltpu.SemaphoreType.DMA((48,)),
         ],
     )(
         sc,
@@ -934,6 +945,8 @@
         gathered,
         own_down,
         other_down,
+        own_out,
+        other_out,
     )
     g1, g2, g3 = across(y1, 1), across(y2, 2), across(y3, 3)
     got, g1, g2, g3 = lax.optimization_barrier((partner(send), g1, g2, g3))
@@ -1043,7 +1056,10 @@
     token_sum = lax.psum_scatter(
         token_parts.reshape(4 * rows, width), "seq", scatter_dimension=0, tiled=True
     )
+    near, q_part = lax.optimization_barrier((near, q_part))
+    q_others = [across(q_part, j) for j in (1, 2, 3)]
     merged = level_sum(near, far, (merged_rows, quad))
+    merged, q_others = lax.optimization_barrier((merged, q_others))
     half_rows = shard_rows + shard_rows // 2 + 16
     u_keep, u_send, d_part = call(
         split_up_kernel,
@@ -1052,20 +1068,15 @@
         *merged,
         scratch=[pltpu.VMEM((merged_rows, quad), bf16)],
     )
-    joined, vector_totals = call(
+    joined, six, up_row = call(
         join_kernel,
         1,
-        [struct((shard_rows + half_rows - 16, width)), struct((16, quad), f32)],
+        [struct((shard_rows + half_rows - 16, width)), struct((8, shard_rows), f32), struct((1, quad), f32)],
         d_part,
         u_keep,
         partner(u_send),
     )
-    q_others = [across(q_part, j) for j in (1, 2, 3)]
-    joined, q_others, token_sum = lax.optimization_barrier((joined, q_others, token_sum))
-    six = lax.dynamic_index_in_dim(
-        vector_totals[:3].reshape(6, 2, shard_rows), core, axis=1, keepdims=False
-    )
-    result_up_bias = lax.dynamic_index_in_dim(vector_totals[3:5], core, axis=0, keepdims=False)
+    joined, token_sum, q_others = lax.optimization_barrier((joined, token_sum, q_others))
     result_down, result_up, result_out = call(
         finish_kernel,
         2,
@@ -1098,7 +1109,7 @@
         six[1],
         six[2],
         result_up,
-        result_up_bias,
+        up_row[0],
         result_down,
         six[5],
         six[3],

time: 294 us -> 286 us (0.973)
  waiting for transfers between devices: 121 us -> 97.3 us
  local copies, waits for them, and re-layouts: 21 us -> 32.3 us
    ppermute x22, waiting for transfers between devices: 55.6 us -> 36.9 us  [across(): return lax.ppermute(value, 'seq', [(i, i ^ step) for i in range(4)])]
    all_gather x1, waiting for transfers between devices: 9.46 us -> 0.02 us  [fast_body(): gathered = lax.all_gather(quarter, ('z', 'core', 'seq'), axis=0, tiled=True)]
    concatenate x1, local copies, waits for them, and re-layouts: 0.09 us -> 4.78 us  [fast_body(): jnp.concatenate([out_bias, gain_one, shift_one, down_bias, gain_two, shif...]
    ppermute x8 -> x10, waiting for transfers between devices: 56.3 us -> 58.8 us  [level_across(): return lax.ppermute(value, 'z', [(i, i ^ step) for i in range(4)])]
    ppermute x8 -> x10, starting transfers between devices: 16.4 us -> 18.3 us  [level_across(): return lax.ppermute(value, 'z', [(i, i ^ step) for i in range(4)])]
    unnamed x85 -> x65, local copies, waits for them, and re-layouts: 12.2 us -> 12.2 us
  transfers between devices with their start and end apart: 37 -> 40, of which waited for: 21 -> 19; matrix products, arithmetic and copies ran while one was open for 4% -> 10% of each run, Pallas kernels for 20% -> 21%
where the time goes in v4:
time: 286 us; the launch traced here: 284 us
  waiting for transfers between devices  97.3 us (34%)
  Pallas kernels  88.4 us (31%)
  starting transfers between devices  44.1 us (15%)
  local copies, waits for them, and re-layouts  32.3 us (11%)
  between operations  15.1 us (5%)
  other arithmetic  7.1 us (2%)
    ppermute x10, waiting for transfers between devices, level_across(): return lax.ppermute(value, 'z', [(i, i ^ step) for i in range(4)])  58.8 us
    pallas_call x14, Pallas kernels, call(): pl.pallas_call(kernel, name=kernel.__name__.replace('_kernel', ''), cost_...  42.7 us
    ppermute x22, waiting for transfers between devices, across(): return lax.ppermute(value, 'seq', [(i, i ^ step) for i in range(4)])  36.9 us
    ppermute x22, starting transfers between devices, across(): return lax.ppermute(value, 'seq', [(i, i ^ step) for i in range(4)])  25.1 us
    ppermute x10, starting transfers between devices, level_across(): return lax.ppermute(value, 'z', [(i, i ^ step) for i in range(4)])  18.3 us
    pallas_call x1, Pallas kernels, fast_body(): pl.pallas_call(middle_kernel, name='middle', cost_estimate=work(15), out_...  15.7 us
    pallas_call x1, Pallas kernels, fast_body(): pl.pallas_call(attend_forward_kernel, name='attend_forward', cost_estimat...  13.2 us
    pallas_call x1, Pallas kernels, fast_body(): pl.pallas_call(attend_backward_kernel, name='attend_backward', cost_estim...  12.5 us
  transfers between devices with their start and end apart: 40, of which 19 were waited for; matrix products, arithmetic and copies ran while one was open for 10% of the time, Pallas kernels for 21%

profile of v4, /device:TPU:0, one launch (start us, length us, event | category | flops | bytes accessed | tf_op | source)
XLA Modules:
  0.0 284.3 jit_solution(12720443758781612339)
XLA Ops:
  7.2 1.6 constant_dynamic-slice_fusion
  9.0 3.1 %collective-permute-start = (bf16[96,768]{1,0:T(8,128)(2,1)S(1)}, bf16[96,768]{1,0:T(8,128)(2,1)S(1)}, u32[]{:S(2)}, u32[]{:S(2)}) collective-permute-start(bf16[96,768]{1,0:T(8,128)(2,1)S(1)} %constant_dynamic-slice_fusion.2), channel_id=1, source_target_pairs={{0,2},{2,0},{4,6},{6,4},{1,3},{3,1},{5,7},{7,5},{8,10},{10,8},{12,... | collective-permute-start | bytes 442376 | tf_op jit(solution)/shard_map/ppermute | solution.py:835
  13.6 4.8 %concatenate.26 = bf16[960]{0:T(1024)(128)(2,1)S(1)} concatenate(bf16[96]{0:T(256)(128)(2,1)} %param.22, bf16[96]{0:T(256)(128)(2,1)} %param.23, bf16[96]{0:T(256)(128)(2,1)} %param.24, bf16[96]{0:T(256)(128)(2,1)} %param.28, bf16[96]{0:T(256)(128)(2,1)} %param.29, bf16[96]{0:T(256)(128)(2,1)} %param.30, bf16[384]{0:T(512)(128)(2,1)} %param.26), dimensions={0} | concatenate | bytes 3840 | tf_op jit(solution)/shard_map/concatenate | solution.py:855
  18.5 1.6 reshape.64
  21.1 5.6 %collective-permute-done.2 = bf16[112,576]{1,0:T(8,128)(2,1)S(1)} collective-permute-done((bf16[112,576]{1,0:T(8,128)(2,1)S(1)}, bf16[112,576]{1,0:T(8,128)(2,1)S(1)}, u32[]{:S(2)}, u32[]{:S(2)}) %collective-permute-start.2) | collective-permute-done | bytes 129056 | tf_op jit(solution)/shard_map/ppermute | solution.py:835
  26.7 3.8 %collective-permute-start.3 = (bf16[2,112,576]{2,1,0:T(8,128)(2,1)S(1)}, bf16[2,112,576]{2,1,0:T(8,128)(2,1)S(1)}, u32[]{:S(2)}, u32[]{:S(2)}) collective-permute-start(bf16[2,112,576]{2,1,0:T(8,128)(2,1)S(1)} %pad_maximum_fusion.6), channel_id=1, source_target_pairs={{0,4},{2,6},{4,0},{6,2},{1,5},{3,7},{5,1},{7,3},{8,12},{10,14},{12... | collective-permute-start | bytes 774152 | tf_op jit(solution)/shard_map/ppermute | solution.py:835
  30.6 2.8 collective-permute-start.6
  34.2 15.9 %collective-permute-done.3 = bf16[2,112,576]{2,1,0:T(8,128)(2,1)S(1)} collective-permute-done((bf16[2,112,576]{2,1,0:T(8,128)(2,1)S(1)}, bf16[2,112,576]{2,1,0:T(8,128)(2,1)S(1)}, u32[]{:S(2)}, u32[]{:S(2)}) %collective-permute-start.3) | collective-permute-done | bytes 258080 | tf_op jit(solution)/shard_map/ppermute | solution.py:835
  50.1 5.7 %collective-permute-done.1 = bf16[2,96,768]{2,1,0:T(8,128)(2,1)S(1)} collective-permute-done((bf16[2,96,768]{2,1,0:T(8,128)(2,1)S(1)}, bf16[2,96,768]{2,1,0:T(8,128)(2,1)S(1)}, u32[]{:S(2)}, u32[]{:S(2)}) %collective-permute-start.1) | collective-permute-done | bytes 294944 | tf_op jit(solution)/shard_map/ppermute | solution.py:835
  56.0 1.4 collective-permute-start.7
  57.4 2.4 collective-permute-start.15
  60.9 3.3 %collective-permute-done.7 = bf16[96,768]{1,0:T(8,128)(2,1)S(1)} collective-permute-done((bf16[96,768]{1,0:T(8,128)(2,1)S(1)}, bf16[96,768]{1,0:T(8,128)(2,1)S(1)}, u32[]{:S(2)}, u32[]{:S(2)}) %collective-permute-start.7) | collective-permute-done | bytes 147488 | tf_op jit(solution)/shard_map/ppermute | solution.py:835
  64.2 2.3 collective-permute-start.8
  67.8 10.8 %collective-permute-done.8 = bf16[2,96,768]{2,1,0:T(8,128)(2,1)} collective-permute-done((bf16[2,96,768]{2,1,0:T(8,128)(2,1)S(1)}, bf16[2,96,768]{2,1,0:T(8,128)(2,1)}, u32[]{:S(2)}, u32[]{:S(2)}) %collective-permute-start.8) | collective-permute-done | bytes 294944 | tf_op jit(solution)/shard_map/ppermute | solution.py:835
  79.6 13.2 %attend_forward.1 = (bf16[1024,576]{1,0:T(8,128)(2,1)}, f32[192,1024]{1,0:T(8,128)}, bf16[256,192]{1,0:T(8,128)(2,1)}, bf16[256,192]{1,0:T(8,128)(2,1)}, bf16[25...) custom-call(s32[4]{0:T(128)} %pad_add_fusion.sc, ...), custom_call_target="tpu_custom_call" | custom-call | flops 1170000000 | bytes 3900000 | tf_op jit(solution)/shard_map/attend_forward/pallas_call | solution.py:877
  92.8 2.1 collective-permute-done.14
  95.3 2.0 pad_maximum_fusion.own_down
  97.8 1.5 reshape.69
  99.4 1.5 collective-permute-start.10
  101.6 1.2 collective-permute-start.12
  103.7 1.3 slice.32
  105.6 1.4 reshape.70
  107.0 1.4 copy.35
  108.4 1.4 reshape.71
  109.8 1.4 concatenate.30.small
  111.2 15.7 %middle.1 = (bf16[256,768]{1,0:T(8,128)(2,1)}, f32[256,768]{1,0:T(8,128)}, bf16[256,192]{1,0:T(8,128)(2,1)}, bf16[256,192]{1,0:T(8,128)(2,1)}, bf16[256,192]{1,0...) custom-call(s32[4]{0:T(128)} %pad_add_fusion.sc, ...), custom_call_target="tpu_custom_call" | custom-call | flops 1350000000 | bytes 4500000 | tf_op jit(solution)/shard_map/middle/pallas_call | solution.py:906
  127.0 1.6 collective-permute-start.19
  129.4 1.2 collective-permute-start.21
  130.6 2.9 %collective-permute-done.19.g1 = bf16[256,192]{1,0:T(8,128)(2,1)S(1)} collective-permute-done((bf16[256,192]{1,0:T(8,128)(2,1)}, bf16[256,192]{1,0:T(8,128)(2,1)S(1)}, u32[]{:S(2)}, u32[]{:S(2)}) %collective-permute-start.19) | collective-permute-done | bytes 98336 | tf_op jit(solution)/shard_map/ppermute | solution.py:829
  133.5 3.7 %collective-permute-done.20.g2 = bf16[256,192]{1,0:T(8,128)(2,1)S(1)} collective-permute-done((bf16[256,192]{1,0:T(8,128)(2,1)}, bf16[256,192]{1,0:T(8,128)(2,1)S(1)}, u32[]{:S(2)}, u32[]{:S(2)}) %collective-permute-start.20) | collective-permute-done | bytes 98336 | tf_op jit(solution)/shard_map/ppermute | solution.py:829
  138.9 6.6 %up_grad.1 = (bf16[2,4,256,384]{3,2,1,0:T(8,128)(2,1)}, bf16[2,4,256,384]{3,2,1,0:T(8,128)(2,1)}) custom-call(s32[4]{0:T(128)} %pad_add_fusion.sc, bf16[256,5760]{1,0:T(8,128)(2,1)} %get-tuple-element.116.keep, bf16[256,5760]{1,0:T(8,128)(2,1)} %copy-done.1, bf16[4,16,384]{2,1,0:T(8,128)(2,1)} %get-tuple-element.123.vectors), custom_call_target="tpu_custom_call" | custom-call | flops 360000000 | bytes 1200000 | tf_op jit(solution)/shard_map/up_grad/pallas_call | solution.py:956
  146.2 5.9 %down_grad.1 = (bf16[2,4,96,768]{3,2,1,0:T(8,128)(2,1)}, bf16[2,4,96,768]{3,2,1,0:T(8,128)(2,1)}) custom-call(s32[4]{0:T(128)} %pad_add_fusion.sc, bf16[256,5760]{1,0:T(8,128)(2,1)} %get-tuple-element.116.keep, bf16[256,5760]{1,0:T(8,128)(2,1)} %copy-done.1), custom_call_target="tpu_custom_call" | custom-call | flops 360000000 | bytes 1200000 | tf_op jit(solution)/shard_map/down_grad/pallas_call | solution.py:956
  153.3 12.5 %attend_backward.1.dqkv = bf16[1024,576]{1,0:T(8,128)(2,1)} custom-call(s32[4]{0:T(128)} %pad_add_fusion.sc, bf16[1024,576]{1,0:T(8,128)(2,1)} %get-tuple-element.127.qkv, f32[192,1024]{1,0:T(8,128)} %get-tuple-element.128.ctx_t, f32[3,1024]{1,0:T(4,128)} %get-tuple-element.129.lse, bf16[256,192]{1,0:T(8,128)(2,1)} %get-tuple-element.130.g0, ...), custom_call_target="tpu_custom_call" | custom-call | flops 990000000 | bytes 3300000 | tf_op jit(solution)/shard_map/attend_backward/pallas_call | solution.py:988
  165.9 4.2 %grad_qkv_weight.1 = (bf16[4,112,576]{2,1,0:T(8,128)(2,1)}, bf16[4,112,576]{2,1,0:T(8,128)(2,1)}) custom-call(s32[4]{0:T(128)} %pad_add_fusion.sc, bf16[256,768]{1,0:T(8,128)(2,1)} %bitcast.49, bf16[256,768]{1,0:T(8,128)(2,1)} %copy-done.16, bf16[256,768]{1,0:T(8,128)(2,1)} %copy-done.15, bf16[256,768]{1,0:T(8,128)(2,1)} %copy-done.14, ...), custom_call_target="tpu_custom_call" | custom-call | flops 360000000 | bytes 1200000 | tf_op jit(solution)/shard_map/grad_qkv_weight/pallas_call | solution.py:1002
  170.1 11.2 %collective-permute-done.23.got = bf16[2,4,256,384]{3,2,1,0:T(8,128)(2,1)S(1)} collective-permute-done((bf16[2,4,256,384]{3,2,1,0:T(8,128)(2,1)}, bf16[2,4,256,384]{3,2,1,0:T(8,128)(2,1)S(1)}, u32[]{:S(2)}, u32[]{:S(2)}) %collective-permute-start.23) | collective-permute-done | bytes 1572896 | tf_op jit(solution)/shard_map/ppermute | solution.py:829
  182.4 3.2 %fold.5 = (bf16[4,256,384]{2,1,0:T(8,128)(2,1)}, bf16[4,256,384]{2,1,0:T(8,128)(2,1)}) custom-call(bf16[2,4,256,384]{3,2,1,0:T(8,128)(2,1)} %get-tuple-element.138.near, bf16[2,4,256,384]{3,2,1,0:T(8,128)(2,1)} %copy-done.6), custom_call_target="tpu_custom_call" | custom-call | flops 90000000 | bytes 300000 | tf_op jit(solution)/shard_map/fold/pallas_call | solution.py:956
  187.4 2.8 fold.4
  190.2 1.3 collective-permute-start.26
  191.5 2.1 level_fold.1
  194.2 4.2 %grad_tokens.1 = bf16[4,256,768]{2,1,0:T(8,128)(2,1)} custom-call(s32[4]{0:T(128)} %pad_add_fusion.sc, bf16[1024,576]{1,0:T(8,128)(2,1)} %attend_backward.1.dqkv, bf16[4,2,96,576]{3,2,1,0:T(8,128)(2,1)} %get-tuple-element.165.weight), custom_call_target="tpu_custom_call" | custom-call | flops 360000000 | bytes 1200000 | tf_op jit(solution)/shard_map/grad_tokens/pallas_call | solution.py:956
  198.3 2.3 collective-permute-done.25.got
  201.3 1.8 fold.6
  205.7 3.0 %level_merge.1 = (bf16[2,448,384]{2,1,0:T(8,128)(2,1)}, bf16[2,448,384]{2,1,0:T(8,128)(2,1)}) custom-call(s32[4]{0:T(128)} %pad_add_fusion.sc, bf16[4,96,768]{2,1,0:T(8,128)(2,1)} %get-tuple-element.147.d_mine, bf16[4,96,768]{2,1,0:T(8,128)(2,1)} %copy-done.12, bf16[4,256,384]{2,1,0:T(8,128)(2,1)} %get-tuple-element.149.u_mine, bf16[4,256,384]{2,1,0:T(8,128)(2,1)} %copy-done.9), custom_call_target="tpu_custom_call" | custom-call | flops 180000000 | bytes 600000 | tf_op jit(solution)/shard_map/level_merge/pallas_call | solution.py:956
  209.3 3.1 %collective-permute-start.28 = (bf16[112,576]{1,0:T(8,128)(2,1)S(1)}, bf16[112,576]{1,0:T(8,128)(2,1)S(1)}, u32[]{:S(2)}, u32[]{:S(2)}) collective-permute-start(bf16[112,576]{1,0:T(8,128)(2,1)S(1)} %copy-done.30), channel_id=1, source_target_pairs={{0,4},{2,6},{4,0},{6,2},{1,5},{3,7},{5,1},{7,3},{8,12},{10,14},{12... | collective-permute-start | bytes 387080 | tf_op jit(solution)/shard_map/ppermute | solution.py:835
  212.4 12.6 %collective-permute-done.28.e1 = bf16[112,576]{1,0:T(8,128)(2,1)S(1)} collective-permute-done((bf16[112,576]{1,0:T(8,128)(2,1)S(1)}, bf16[112,576]{1,0:T(8,128)(2,1)S(1)}, u32[]{:S(2)}, u32[]{:S(2)}) %collective-permute-start.28) | collective-permute-done | bytes 129056 | tf_op jit(solution)/shard_map/ppermute | solution.py:835
  225.7 1.7 sum.1.b0
  228.2 2.2 fold.7
  230.4 3.4 %collective-permute-start.30 = (bf16[448,384]{1,0:T(8,128)(2,1)}, bf16[448,384]{1,0:T(8,128)(2,1)S(1)}, u32[]{:S(2)}, u32[]{:S(2)}) collective-permute-start(bf16[448,384]{1,0:T(8,128)(2,1)} %get-tuple-element.156), channel_id=1, source_target_pairs={{0,4},{2,6},{4,0},{6,2},{1,5},{3,7},{5,1},{7,3},{8,12},{10,14},{12... | collective-permute-start | bytes 1032200 | tf_op jit(solution)/shard_map/ppermute | solution.py:835
  233.8 1.4 collective-permute-start.33
  235.6 1.7 collective-permute-start.31
  237.3 5.2 %collective-permute-done.33.b3 = bf16[112,576]{1,0:T(8,128)(2,1)S(1)} collective-permute-done((bf16[112,576]{1,0:T(8,128)(2,1)}, bf16[112,576]{1,0:T(8,128)(2,1)S(1)}, u32[]{:S(2)}, u32[]{:S(2)}) %collective-permute-start.33) | collective-permute-done | bytes 129056 | tf_op jit(solution)/shard_map/ppermute | solution.py:829
  242.5 1.4 collective-permute-done.32.b2
  244.0 2.7 collective-permute-done.30.e1
  247.4 2.0 split_up.1
  249.4 1.5 collective-permute-done.34.got
  251.6 1.9 join.1
  255.2 1.8 collective-permute-start.35
  257.0 1.4 slice_bitcast_fusion.1
  258.4 1.3 reduce
  259.7 2.3 finish_qkv.1
  262.1 1.8 fusion
  263.9 2.2 collective-permute-done.37.b3
  266.1 6.8 %collective-permute-done.36.b2 = bf16[240,768]{1,0:T(8,128)(2,1)S(1)} collective-permute-done((bf16[240,768]{1,0:T(8,128)(2,1)}, bf16[240,768]{1,0:T(8,128)(2,1)S(1)}, u32[]{:S(2)}, u32[]{:S(2)}) %collective-permute-start.36) | collective-permute-done | bytes 368672 | tf_op jit(solution)/shard_map/ppermute | solution.py:829
  274.4 3.0 %finish.1 = (f32[384,768]{1,0:T(8,128)}, f32[96,3072]{1,0:T(8,128)}, f32[96,768]{1,0:T(8,128)}) custom-call(s32[4]{0:T(128)} %pad_add_fusion.sc, bf16[240,768]{1,0:T(8,128)(2,1)} %get-tuple-element.177.b0, bf16[240,768]{1,0:T(8,128)(2,1)} %copy-done.19, bf16[240,768]{1,0:T(8,128)(2,1)} %copy-done.18, bf16[240,768]{1,0:T(8,128)(2,1)} %copy-done.17), custom_call_target="tpu_custom_call" | custom-call | flops 180000000 | bytes 600000 | tf_op jit(solution)/shard_map/finish/pallas_call | solution.py:956
  (136 shorter events, 27.8 us)
Async XLA Ops:
  7.2 1.8 copy-start
  7.2 104.0 %all-gather.2.cloned.1.call-start = ((), (), s32[]{:S(2)}) async-start(), calls=%async_computation.1 | async-start | bytes 4866048 | tf_op jit(solution)/shard_map/all_gather | solution.py:844
  8.9 244.6 %reduce-scatter.2.cloned.1.call-start = ((), (), s32[]{:S(2)}) async-start(), calls=%async_computation.2 | async-start | bytes 1966080 | tf_op jit(solution)/shard_map/reduce_scatter | solution.py:1056
  9.0 21.7 %copy-start.5 = (bf16[1,256,768]{2,1,0:T(8,128)(2,1)S(1)}, bf16[1,256,768]{2,1,0:T(8,128)(2,1)}, u32[]{:S(2)}) copy-start(bf16[1,256,768]{2,1,0:T(8,128)(2,1)} %param.16) | copy-start | bytes 1179652
  9.0 21.5 %collective-permute-start = (bf16[96,768]{1,0:T(8,128)(2,1)S(1)}, bf16[96,768]{1,0:T(8,128)(2,1)S(1)}, u32[]{:S(2)}, u32[]{:S(2)}) collective-permute-start(bf16[96,768]{1,0:T(8,128)(2,1)S(1)} %constant_dynamic-slice_fusion.2), channel_id=1, source_target_pairs={{0,2},{2,0},{4,6},{6,4},{1,3},{3,1},{5,7},{7,5},{8,10},{10,8},{12,... | collective-permute-start | bytes 442376 | tf_op jit(solution)/shard_map/ppermute | solution.py:835
  20.7 35.3 %copy-start.11 = (bf16[96,768]{1,0:T(8,128)(2,1)S(1)}, bf16[96,768]{1,0:T(8,128)(2,1)}, u32[]{:S(2)}) copy-start(bf16[96,768]{1,0:T(8,128)(2,1)} %param.21) | copy-start | bytes 442372
  20.9 5.7 %collective-permute-start.2 = (bf16[112,576]{1,0:T(8,128)(2,1)S(1)}, bf16[112,576]{1,0:T(8,128)(2,1)S(1)}, u32[]{:S(2)}, u32[]{:S(2)}) collective-permute-start(bf16[112,576]{1,0:T(8,128)(2,1)S(1)} %pad_maximum_fusion.7), channel_id=1, source_target_pairs={{0,2},{2,0},{4,6},{6,4},{1,3},{3,1},{5,7},{7,5},{8,10},{10,8},{12,... | collective-permute-start | bytes 387080 | tf_op jit(solution)/shard_map/ppermute | solution.py:835
  26.7 23.4 %collective-permute-start.3 = (bf16[2,112,576]{2,1,0:T(8,128)(2,1)S(1)}, bf16[2,112,576]{2,1,0:T(8,128)(2,1)S(1)}, u32[]{:S(2)}, u32[]{:S(2)}) collective-permute-start(bf16[2,112,576]{2,1,0:T(8,128)(2,1)S(1)} %pad_maximum_fusion.6), channel_id=1, source_target_pairs={{0,4},{2,6},{4,0},{6,2},{1,5},{3,7},{5,1},{7,3},{8,12},{10,14},{12... | collective-permute-start | bytes 774152 | tf_op jit(solution)/shard_map/ppermute | solution.py:835
  30.5 25.3 %collective-permute-start.1 = (bf16[2,96,768]{2,1,0:T(8,128)(2,1)S(1)}, bf16[2,96,768]{2,1,0:T(8,128)(2,1)S(1)}, u32[]{:S(2)}, u32[]{:S(2)}) collective-permute-start(bf16[2,96,768]{2,1,0:T(8,128)(2,1)S(1)} %pad_maximum_fusion.4), channel_id=1, source_target_pairs={{0,4},{2,6},{4,0},{6,2},{1,5},{3,7},{5,1},{7,3},{8,12},{10,14},{12... | collective-permute-start | bytes 884744 | tf_op jit(solution)/shard_map/ppermute | solution.py:835
  30.6 25.3 %collective-permute-start.6 = (bf16[256,768]{1,0:T(8,128)(2,1)S(1)}, bf16[256,768]{1,0:T(8,128)(2,1)S(1)}, u32[]{:S(2)}, u32[]{:S(2)}) collective-permute-start(bf16[256,768]{1,0:T(8,128)(2,1)S(1)} %bitcast.50), channel_id=1, source_target_pairs={{0,24},{8,16},{16,8},{24,0},{1,25},{9,17},{17,9},{25,1},{2,26},{10... | collective-permute-start | bytes 1179656 | tf_op jit(solution)/shard_map/ppermute | solution.py:829
  33.4 22.5 %collective-permute-start.5 = (bf16[256,768]{1,0:T(8,128)(2,1)S(1)}, bf16[256,768]{1,0:T(8,128)(2,1)S(1)}, u32[]{:S(2)}, u32[]{:S(2)}) collective-permute-start(bf16[256,768]{1,0:T(8,128)(2,1)S(1)} %bitcast.51), channel_id=1, source_target_pairs={{0,16},{8,24},{16,0},{24,8},{1,17},{9,25},{17,1},{25,9},{2,18},{10... | collective-permute-start | bytes 1179656 | tf_op jit(solution)/shard_map/ppermute | solution.py:829
  33.7 22.2 %collective-permute-start.4 = (bf16[256,768]{1,0:T(8,128)(2,1)S(1)}, bf16[256,768]{1,0:T(8,128)(2,1)S(1)}, u32[]{:S(2)}, u32[]{:S(2)}) collective-permute-start(bf16[256,768]{1,0:T(8,128)(2,1)S(1)} %bitcast.52), channel_id=1, source_target_pairs={{0,8},{8,0},{16,24},{24,16},{1,9},{9,1},{17,25},{25,17},{2,10},{10... | collective-permute-start | bytes 1179656 | tf_op jit(solution)/shard_map/ppermute | solution.py:829
  50.1 29.5 %copy-start.13 = (bf16[4,112,576]{2,1,0:T(8,128)(2,1)}, bf16[4,112,576]{2,1,0:T(8,128)(2,1)S(1)}, u32[]{:S(2)}) copy-start(bf16[4,112,576]{2,1,0:T(8,128)(2,1)S(1)} %pad_maximum_fusion.3.own) | copy-start | bytes 1548292
  55.9 36.9 %copy-start.4 = (bf16[4,96,768]{2,1,0:T(8,128)(2,1)}, bf16[4,96,768]{2,1,0:T(8,128)(2,1)S(1)}, u32[]{:S(2)}) copy-start(bf16[4,96,768]{2,1,0:T(8,128)(2,1)S(1)} %pad_maximum_fusion.1) | copy-start | bytes 1769476
  55.9 23.7 %copy-start.14 = (bf16[256,768]{1,0:T(8,128)(2,1)}, bf16[256,768]{1,0:T(8,128)(2,1)S(1)}, u32[]{:S(2)}) copy-start(bf16[256,768]{1,0:T(8,128)(2,1)S(1)} %collective-permute-done.6.t3) | copy-start | bytes 1179652
  56.0 8.2 %copy-start.15 = (bf16[256,768]{1,0:T(8,128)(2,1)}, bf16[256,768]{1,0:T(8,128)(2,1)S(1)}, u32[]{:S(2)}) copy-start(bf16[256,768]{1,0:T(8,128)(2,1)S(1)} %collective-permute-done.5.t2) | copy-start | bytes 1179652
  56.0 8.2 %copy-start.16 = (bf16[256,768]{1,0:T(8,128)(2,1)}, bf16[256,768]{1,0:T(8,128)(2,1)S(1)}, u32[]{:S(2)}) copy-start(bf16[256,768]{1,0:T(8,128)(2,1)S(1)} %collective-permute-done.4.t1) | copy-start | bytes 1179652
  56.0 8.2 %collective-permute-start.7 = (bf16[96,768]{1,0:T(8,128)(2,1)S(1)}, bf16[96,768]{1,0:T(8,128)(2,1)S(1)}, u32[]{:S(2)}, u32[]{:S(2)}) collective-permute-start(bf16[96,768]{1,0:T(8,128)(2,1)S(1)} %copy-done.11), channel_id=1, source_target_pairs={{0,2},{2,0},{4,6},{6,4},{1,3},{3,1},{5,7},{7,5},{8,10},{10,8},{12,... | collective-permute-start | bytes 442376 | tf_op jit(solution)/shard_map/ppermute | solution.py:835
  57.4 22.2 %collective-permute-start.9 = (bf16[4,112,576]{2,1,0:T(8,128)(2,1)S(1)}, bf16[4,112,576]{2,1,0:T(8,128)(2,1)}, u32[]{:S(2)}, u32[]{:S(2)}) collective-permute-start(bf16[4,112,576]{2,1,0:T(8,128)(2,1)S(1)} %pad_maximum_fusion.3.own), channel_id=1, source_target_pairs={{0,1},{1,0},{2,3},{3,2},{4,5},{5,4},{6,7},{7,6},{8,9},{9,8},{10,11... | collective-permute-start | bytes 1548296 | tf_op jit(solution)/shard_map/ppermute | solution.py:832
  57.4 35.4 %collective-permute-start.15 = (bf16[4,96,768]{2,1,0:T(8,128)(2,1)S(1)}, bf16[4,96,768]{2,1,0:T(8,128)(2,1)}, u32[]{:S(2)}, u32[]{:S(2)}) collective-permute-start(bf16[4,96,768]{2,1,0:T(8,128)(2,1)S(1)} %pad_maximum_fusion.1), channel_id=1, source_target_pairs={{0,24},{8,16},{16,8},{24,0},{1,25},{9,17},{17,9},{25,1},{2,26},{10... | collective-permute-start | bytes 1769480 | tf_op jit(solution)/shard_map/ppermute | solution.py:829
  59.8 35.0 %collective-permute-start.14 = (bf16[4,96,768]{2,1,0:T(8,128)(2,1)S(1)}, bf16[4,96,768]{2,1,0:T(8,128)(2,1)}, u32[]{:S(2)}, u32[]{:S(2)}) collective-permute-start(bf16[4,96,768]{2,1,0:T(8,128)(2,1)S(1)} %pad_maximum_fusion.1), channel_id=1, source_target_pairs={{0,16},{8,24},{16,0},{24,8},{1,17},{9,25},{17,1},{25,9},{2,18},{10... | collective-permute-start | bytes 1769480 | tf_op jit(solution)/shard_map/ppermute | solution.py:829
  60.3 35.0 %collective-permute-start.13 = (bf16[4,96,768]{2,1,0:T(8,128)(2,1)S(1)}, bf16[4,96,768]{2,1,0:T(8,128)(2,1)}, u32[]{:S(2)}, u32[]{:S(2)}) collective-permute-start(bf16[4,96,768]{2,1,0:T(8,128)(2,1)S(1)} %pad_maximum_fusion.1), channel_id=1, source_target_pairs={{0,8},{8,0},{16,24},{24,16},{1,9},{9,1},{17,25},{25,17},{2,10},{10... | collective-permute-start | bytes 1769480 | tf_op jit(solution)/shard_map/ppermute | solution.py:829
  64.2 14.4 %collective-permute-start.8 = (bf16[2,96,768]{2,1,0:T(8,128)(2,1)S(1)}, bf16[2,96,768]{2,1,0:T(8,128)(2,1)}, u32[]{:S(2)}, u32[]{:S(2)}) collective-permute-start(bf16[2,96,768]{2,1,0:T(8,128)(2,1)S(1)} %pad_maximum_fusion.5), channel_id=1, source_target_pairs={{0,4},{2,6},{4,0},{6,2},{1,5},{3,7},{5,1},{7,3},{8,12},{10,14},{12... | collective-permute-start | bytes 884744 | tf_op jit(solution)/shard_map/ppermute | solution.py:835
  79.6 17.7 %copy-start.3 = (bf16[4,96,768]{2,1,0:T(8,128)(2,1)}, bf16[4,96,768]{2,1,0:T(8,128)(2,1)S(1)}, u32[]{:S(2)}) copy-start(bf16[4,96,768]{2,1,0:T(8,128)(2,1)S(1)} %pad_maximum_fusion.2.own_out) | copy-start | bytes 1769476
  97.2 14.0 %copy-start.2 = (bf16[4,4,96,768]{3,2,1,0:T(8,128)(2,1)}, bf16[4,4,96,768]{3,2,1,0:T(8,128)(2,1)S(1)}, u32[]{:S(2)}) copy-start(bf16[4,4,96,768]{3,2,1,0:T(8,128)(2,1)S(1)} %pad_maximum_fusion.own_down) | copy-start | bytes 7077892
  97.2 13.9 %collective-permute-start.16 = (bf16[4,4,96,768]{3,2,1,0:T(8,128)(2,1)S(1)}, bf16[4,4,96,768]{3,2,1,0:T(8,128)(2,1)}, u32[]{:S(2)}, u32[]{:S(2)}) collective-permute-start(bf16[4,4,96,768]{3,2,1,0:T(8,128)(2,1)S(1)} %pad_maximum_fusion.own_down), channel_id=1, source_target_pairs={{0,1},{1,0},{2,3},{3,2},{4,5},{5,4},{6,7},{7,6},{8,9},{9,8},{10,11... | collective-permute-start | bytes 7077896 | tf_op jit(solution)/shard_map/ppermute | solution.py:832
  97.3 13.8 %collective-permute-start.17 = (bf16[4,96,768]{2,1,0:T(8,128)(2,1)S(1)}, bf16[4,96,768]{2,1,0:T(8,128)(2,1)}, u32[]{:S(2)}, u32[]{:S(2)}) collective-permute-start(bf16[4,96,768]{2,1,0:T(8,128)(2,1)S(1)} %pad_maximum_fusion.2.own_out), channel_id=1, source_target_pairs={{0,1},{1,0},{2,3},{3,2},{4,5},{5,4},{6,7},{7,6},{8,9},{9,8},{10,11... | collective-permute-start | bytes 1769480 | tf_op jit(solution)/shard_map/ppermute | solution.py:832
  99.4 11.8 %collective-permute-start.10 = (bf16[256,192]{1,0:T(8,128)(2,1)}, bf16[256,192]{1,0:T(8,128)(2,1)}, u32[]{:S(2)}, u32[]{:S(2)}) collective-permute-start(bf16[256,192]{1,0:T(8,128)(2,1)} %get-tuple-element.106), channel_id=1, source_target_pairs={{0,8},{8,0},{16,24},{24,16},{1,9},{9,1},{17,25},{25,17},{2,10},{10... | collective-permute-start | bytes 294920 | tf_op jit(solution)/shard_map/ppermute | solution.py:829
  100.9 10.3 %collective-permute-start.11 = (bf16[256,192]{1,0:T(8,128)(2,1)}, bf16[256,192]{1,0:T(8,128)(2,1)}, u32[]{:S(2)}, u32[]{:S(2)}) collective-permute-start(bf16[256,192]{1,0:T(8,128)(2,1)} %get-tuple-element.107), channel_id=1, source_target_pairs={{0,16},{8,24},{16,0},{24,8},{1,17},{9,25},{17,1},{25,9},{2,18},{10... | collective-permute-start | bytes 294920 | tf_op jit(solution)/shard_map/ppermute | solution.py:829
  101.6 9.5 %collective-permute-start.12 = (bf16[256,192]{1,0:T(8,128)(2,1)}, bf16[256,192]{1,0:T(8,128)(2,1)}, u32[]{:S(2)}, u32[]{:S(2)}) collective-permute-start(bf16[256,192]{1,0:T(8,128)(2,1)} %get-tuple-element.108), channel_id=1, source_target_pairs={{0,24},{8,16},{16,8},{24,0},{1,25},{9,17},{17,9},{25,1},{2,26},{10... | collective-permute-start | bytes 294920 | tf_op jit(solution)/shard_map/ppermute | solution.py:829
  127.0 10.3 %collective-permute-start.18 = (bf16[256,5760]{1,0:T(8,128)(2,1)}, bf16[256,5760]{1,0:T(8,128)(2,1)S(1)}, u32[]{:S(2)}, u32[]{:S(2)}) collective-permute-start(bf16[256,5760]{1,0:T(8,128)(2,1)} %get-tuple-element.117), channel_id=1, source_target_pairs={{0,1},{1,0},{2,3},{3,2},{4,5},{5,4},{6,7},{7,6},{8,9},{9,8},{10,11... | collective-permute-start | bytes 8847368 | tf_op jit(solution)/shard_map/ppermute | solution.py:832
  127.0 6.4 %collective-permute-start.19 = (bf16[256,192]{1,0:T(8,128)(2,1)}, bf16[256,192]{1,0:T(8,128)(2,1)S(1)}, u32[]{:S(2)}, u32[]{:S(2)}) collective-permute-start(bf16[256,192]{1,0:T(8,128)(2,1)} %get-tuple-element.118), channel_id=1, source_target_pairs={{0,8},{8,0},{16,24},{24,16},{1,9},{9,1},{17,25},{25,17},{2,10},{10... | collective-permute-start | bytes 294920 | tf_op jit(solution)/shard_map/ppermute | solution.py:829
  128.6 8.6 %collective-permute-start.20 = (bf16[256,192]{1,0:T(8,128)(2,1)}, bf16[256,192]{1,0:T(8,128)(2,1)S(1)}, u32[]{:S(2)}, u32[]{:S(2)}) collective-permute-start(bf16[256,192]{1,0:T(8,128)(2,1)} %get-tuple-element.119), channel_id=1, source_target_pairs={{0,16},{8,24},{16,0},{24,8},{1,17},{9,25},{17,1},{25,9},{2,18},{10... | collective-permute-start | bytes 294920 | tf_op jit(solution)/shard_map/ppermute | solution.py:829
  129.4 7.9 %collective-permute-start.21 = (bf16[256,192]{1,0:T(8,128)(2,1)}, bf16[256,192]{1,0:T(8,128)(2,1)S(1)}, u32[]{:S(2)}, u32[]{:S(2)}) collective-permute-start(bf16[256,192]{1,0:T(8,128)(2,1)} %get-tuple-element.120), channel_id=1, source_target_pairs={{0,24},{8,16},{16,8},{24,0},{1,25},{9,17},{17,9},{25,1},{2,26},{10... | collective-permute-start | bytes 294920 | tf_op jit(solution)/shard_map/ppermute | solution.py:829
  133.5 3.7 %copy-start.26 = (bf16[256,192]{1,0:T(8,128)(2,1)}, bf16[256,192]{1,0:T(8,128)(2,1)S(1)}, u32[]{:S(2)}) copy-start(bf16[256,192]{1,0:T(8,128)(2,1)S(1)} %collective-permute-done.19.g1) | copy-start | bytes 294916
  137.2 1.6 copy-start.1
  145.5 35.8 %collective-permute-start.23 = (bf16[2,4,256,384]{3,2,1,0:T(8,128)(2,1)}, bf16[2,4,256,384]{3,2,1,0:T(8,128)(2,1)S(1)}, u32[]{:S(2)}, u32[]{:S(2)}) collective-permute-start(bf16[2,4,256,384]{3,2,1,0:T(8,128)(2,1)} %get-tuple-element.139), channel_id=1, source_target_pairs={{0,16},{8,24},{16,0},{24,8},{1,17},{9,25},{17,1},{25,9},{2,18},{10... | collective-permute-start | bytes 4718600 | tf_op jit(solution)/shard_map/ppermute | solution.py:829
  152.1 34.3 %collective-permute-start.22 = (bf16[2,4,96,768]{3,2,1,0:T(8,128)(2,1)}, bf16[2,4,96,768]{3,2,1,0:T(8,128)(2,1)S(1)}, u32[]{:S(2)}, u32[]{:S(2)}) collective-permute-start(bf16[2,4,96,768]{3,2,1,0:T(8,128)(2,1)} %get-tuple-element.136), channel_id=1, source_target_pairs={{0,8},{8,0},{16,24},{24,16},{1,9},{9,1},{17,25},{25,17},{2,10},{10... | collective-permute-start | bytes 3538952 | tf_op jit(solution)/shard_map/ppermute | solution.py:829
  170.1 21.4 %collective-permute-start.24 = (bf16[4,112,576]{2,1,0:T(8,128)(2,1)}, bf16[4,112,576]{2,1,0:T(8,128)(2,1)}, u32[]{:S(2)}, u32[]{:S(2)}) collective-permute-start(bf16[4,112,576]{2,1,0:T(8,128)(2,1)} %get-tuple-element.143), channel_id=1, source_target_pairs={{0,1},{1,0},{2,3},{3,2},{4,5},{5,4},{6,7},{7,6},{8,9},{9,8},{10,11... | collective-permute-start | bytes 1548296 | tf_op jit(solution)/shard_map/ppermute | solution.py:832
  181.3 1.1 copy-start.6
  185.6 18.4 %collective-permute-start.27 = (bf16[4,256,384]{2,1,0:T(8,128)(2,1)}, bf16[4,256,384]{2,1,0:T(8,128)(2,1)S(1)}, u32[]{:S(2)}, u32[]{:S(2)}) collective-permute-start(bf16[4,256,384]{2,1,0:T(8,128)(2,1)} %get-tuple-element.150), channel_id=1, source_target_pairs={{0,8},{8,0},{16,24},{24,16},{1,9},{9,1},{17,25},{25,17},{2,10},{10... | collective-permute-start | bytes 2359304 | tf_op jit(solution)/shard_map/ppermute | solution.py:829
  186.4 1.0 copy-start.7
  190.2 13.9 %collective-permute-start.26 = (bf16[4,96,768]{2,1,0:T(8,128)(2,1)}, bf16[4,96,768]{2,1,0:T(8,128)(2,1)S(1)}, u32[]{:S(2)}, u32[]{:S(2)}) collective-permute-start(bf16[4,96,768]{2,1,0:T(8,128)(2,1)} %get-tuple-element.148), channel_id=1, source_target_pairs={{0,16},{8,24},{16,0},{24,8},{1,17},{9,25},{17,1},{25,9},{2,18},{10... | collective-permute-start | bytes 1769480 | tf_op jit(solution)/shard_map/ppermute | solution.py:829
  193.6 7.0 %collective-permute-start.25 = (bf16[2,112,576]{2,1,0:T(8,128)(2,1)}, bf16[2,112,576]{2,1,0:T(8,128)(2,1)S(1)}, u32[]{:S(2)}, u32[]{:S(2)}) collective-permute-start(bf16[2,112,576]{2,1,0:T(8,128)(2,1)} %get-tuple-element.145), channel_id=1, source_target_pairs={{0,2},{2,0},{4,6},{6,4},{1,3},{3,1},{5,7},{7,5},{8,10},{10,8},{12,... | collective-permute-start | bytes 774152 | tf_op jit(solution)/shard_map/ppermute | solution.py:835
  203.1 6.2 %copy-start.30 = (bf16[112,576]{1,0:T(8,128)(2,1)S(1)}, bf16[112,576]{1,0:T(8,128)(2,1)}, u32[]{:S(2)}) copy-start(bf16[112,576]{1,0:T(8,128)(2,1)} %get-tuple-element.152) | copy-start | bytes 387076
  204.0 0.8 copy-start.12
  204.9 0.9 copy-start.9
  208.7 53.3 %copy-start.8 = (f32[256,768]{1,0:T(8,128)S(1)}, f32[256,768]{1,0:T(8,128)}, u32[]{:S(2)}) copy-start(f32[256,768]{1,0:T(8,128)} %get-tuple-element.114) | copy-start | bytes 2359300
  208.8 18.6 %collective-permute-start.29 = (bf16[2,448,384]{2,1,0:T(8,128)(2,1)}, bf16[2,448,384]{2,1,0:T(8,128)(2,1)S(1)}, u32[]{:S(2)}, u32[]{:S(2)}) collective-permute-start(bf16[2,448,384]{2,1,0:T(8,128)(2,1)} %get-tuple-element.154), channel_id=1, source_target_pairs={{0,2},{2,0},{4,6},{6,4},{1,3},{3,1},{5,7},{7,5},{8,10},{10,8},{12,... | collective-permute-start | bytes 2064392 | tf_op jit(solution)/shard_map/ppermute | solution.py:835
  209.3 15.7 %collective-permute-start.28 = (bf16[112,576]{1,0:T(8,128)(2,1)S(1)}, bf16[112,576]{1,0:T(8,128)(2,1)S(1)}, u32[]{:S(2)}, u32[]{:S(2)}) collective-permute-start(bf16[112,576]{1,0:T(8,128)(2,1)S(1)} %copy-done.30), channel_id=1, source_target_pairs={{0,4},{2,6},{4,0},{6,2},{1,5},{3,7},{5,1},{7,3},{8,12},{10,14},{12... | collective-permute-start | bytes 387080 | tf_op jit(solution)/shard_map/ppermute | solution.py:835
  227.3 0.8 copy-start.10
  230.4 16.3 %collective-permute-start.30 = (bf16[448,384]{1,0:T(8,128)(2,1)}, bf16[448,384]{1,0:T(8,128)(2,1)S(1)}, u32[]{:S(2)}, u32[]{:S(2)}) collective-permute-start(bf16[448,384]{1,0:T(8,128)(2,1)} %get-tuple-element.156), channel_id=1, source_target_pairs={{0,4},{2,6},{4,0},{6,2},{1,5},{3,7},{5,1},{7,3},{8,12},{10,14},{12... | collective-permute-start | bytes 1032200 | tf_op jit(solution)/shard_map/ppermute | solution.py:835
  233.8 8.7 %collective-permute-start.33 = (bf16[112,576]{1,0:T(8,128)(2,1)}, bf16[112,576]{1,0:T(8,128)(2,1)S(1)}, u32[]{:S(2)}, u32[]{:S(2)}) collective-permute-start(bf16[112,576]{1,0:T(8,128)(2,1)} %sum.1.b0), channel_id=1, source_target_pairs={{0,24},{8,16},{16,8},{24,0},{1,25},{9,17},{17,9},{25,1},{2,26},{10... | collective-permute-start | bytes 387080 | tf_op jit(solution)/shard_map/ppermute | solution.py:829
  235.2 8.8 %collective-permute-start.32 = (bf16[112,576]{1,0:T(8,128)(2,1)}, bf16[112,576]{1,0:T(8,128)(2,1)S(1)}, u32[]{:S(2)}, u32[]{:S(2)}) collective-permute-start(bf16[112,576]{1,0:T(8,128)(2,1)} %sum.1.b0), channel_id=1, source_target_pairs={{0,16},{8,24},{16,0},{24,8},{1,17},{9,25},{17,1},{25,9},{2,18},{10... | collective-permute-start | bytes 387080 | tf_op jit(solution)/shard_map/ppermute | solution.py:829
  235.6 8.4 %collective-permute-start.31 = (bf16[112,576]{1,0:T(8,128)(2,1)}, bf16[112,576]{1,0:T(8,128)(2,1)S(1)}, u32[]{:S(2)}, u32[]{:S(2)}) collective-permute-start(bf16[112,576]{1,0:T(8,128)(2,1)} %sum.1.b0), channel_id=1, source_target_pairs={{0,8},{8,0},{16,24},{24,16},{1,9},{9,1},{17,25},{25,17},{2,10},{10... | collective-permute-start | bytes 387080 | tf_op jit(solution)/shard_map/ppermute | solution.py:829
  242.5 17.2 %copy-start.22 = (bf16[112,576]{1,0:T(8,128)(2,1)}, bf16[112,576]{1,0:T(8,128)(2,1)S(1)}, u32[]{:S(2)}) copy-start(bf16[112,576]{1,0:T(8,128)(2,1)S(1)} %collective-permute-done.33.b3) | copy-start | bytes 387076
  244.0 15.7 %copy-start.23 = (bf16[112,576]{1,0:T(8,128)(2,1)}, bf16[112,576]{1,0:T(8,128)(2,1)S(1)}, u32[]{:S(2)}) copy-start(bf16[112,576]{1,0:T(8,128)(2,1)S(1)} %collective-permute-done.32.b2) | copy-start | bytes 387076
  244.0 15.7 %copy-start.24 = (bf16[112,576]{1,0:T(8,128)(2,1)}, bf16[112,576]{1,0:T(8,128)(2,1)S(1)}, u32[]{:S(2)}) copy-start(bf16[112,576]{1,0:T(8,128)(2,1)S(1)} %collective-permute-done.31.b1) | copy-start | bytes 387076
  249.4 1.5 collective-permute-start.34
  253.5 12.6 %collective-permute-start.37 = (bf16[240,768]{1,0:T(8,128)(2,1)}, bf16[240,768]{1,0:T(8,128)(2,1)S(1)}, u32[]{:S(2)}, u32[]{:S(2)}) collective-permute-start(bf16[240,768]{1,0:T(8,128)(2,1)} %get-tuple-element.177.b0), channel_id=1, source_target_pairs={{0,24},{8,16},{16,8},{24,0},{1,25},{9,17},{17,9},{25,1},{2,26},{10... | collective-permute-start | bytes 1105928 | tf_op jit(solution)/shard_map/ppermute | solution.py:829
  254.4 18.5 %collective-permute-start.36 = (bf16[240,768]{1,0:T(8,128)(2,1)}, bf16[240,768]{1,0:T(8,128)(2,1)S(1)}, u32[]{:S(2)}, u32[]{:S(2)}) collective-permute-start(bf16[240,768]{1,0:T(8,128)(2,1)} %get-tuple-element.177.b0), channel_id=1, source_target_pairs={{0,16},{8,24},{16,0},{24,8},{1,17},{9,25},{17,1},{25,9},{2,18},{10... | collective-permute-start | bytes 1105928 | tf_op jit(solution)/shard_map/ppermute | solution.py:829
  255.2 17.7 %collective-permute-start.35 = (bf16[240,768]{1,0:T(8,128)(2,1)}, bf16[240,768]{1,0:T(8,128)(2,1)S(1)}, u32[]{:S(2)}, u32[]{:S(2)}) collective-permute-start(bf16[240,768]{1,0:T(8,128)(2,1)} %get-tuple-element.177.b0), channel_id=1, source_target_pairs={{0,8},{8,0},{16,24},{24,16},{1,9},{9,1},{17,25},{25,17},{2,10},{10... | collective-permute-start | bytes 1105928 | tf_op jit(solution)/shard_map/ppermute | solution.py:829
  266.1 6.8 %copy-start.17 = (bf16[240,768]{1,0:T(8,128)(2,1)}, bf16[240,768]{1,0:T(8,128)(2,1)S(1)}, u32[]{:S(2)}) copy-start(bf16[240,768]{1,0:T(8,128)(2,1)S(1)} %collective-permute-done.37.b3) | copy-start | bytes 1105924
  273.6 0.7 copy-start.19
  (7 other events, 4.8 us)
Sparse Core Ops, SparseCore 0:
  11.5 93.7 all-gather.1
  208.9 35.5 reduce-scatter.1

commit v5 on v4

--- a/solution.py
+++ b/solution.py
@@ -366,8 +366,24 @@
     return jnp.concatenate(columns, axis=0)
 
 
+def pack_kernel(place_ref, weight, *refs):
+    vectors, out = refs[:-1], refs[-1]
+    place = place_ref[0]
+    rows = weight.shape[0]
+    head_width = out.shape[1] // 3
+    for part in range(3):
+        chosen = weight[:, part * 4 * head_width : (part * 4 + 1) * head_width]
+        for s in range(1, 4):
+            at = (part * 4 + s) * head_width
+            chosen = jnp.where(place == s, weight[:, at : at + head_width], chosen)
+        out[:rows, part * head_width : (part + 1) * head_width] = chosen
+    out[rows:, :] = jnp.zeros((out.shape[0] - rows, out.shape[1]), out.dtype)
+    for row, vector in enumerate(vectors):
+        out[rows + row : rows + row + 1, : vector.shape[1]] = vector[...]
+
+
 def attend_forward_kernel(
-    sc, t0, t1, t2, t3, own, other, qkv, ctx_t, c0, c1, c2, c3, lse, weight, vectors, held
+    sc, t0, t1, t2, t3, own, other, qkv, ctx_t, c0, c1, c2, c3, lse, weight, small, up_bias, held, vectors
 ):
     place, core, level = sc[1], sc[2], sc[3]
     rows = t0.shape[0]
@@ -378,14 +394,21 @@
     for k in range(4):
         for block, side in ((own, core), (other, 1 - core)):
             weight[level ^ k, side] = block[k, :shard_rows, :]
-            vectors[level ^ k, side] = block[k, shard_rows + 1 : shard_rows + 3, :].astype(
-                jnp.float32
-            )
+            vectors[level ^ k, side] = block[k, shard_rows:, :].astype(jnp.float32)
     full = weight[...].reshape(-1, width)
-    bias = (
-        own[level ^ place, shard_rows : shard_rows + 1, :].astype(jnp.float32)
-        + other[level ^ place, shard_rows : shard_rows + 1, :].astype(jnp.float32)
-    )
+    pairs = [
+        vectors[place, side, row : row + 1, :shard_rows] for row in (0, 1) for side in (0, 1)
+    ]
+    gap = jnp.zeros((1, head_width), jnp.float32)
+    bias = jnp.concatenate(pairs[:2] + [gap] + pairs[2:], axis=1)
+    up_cols = up_bias.shape[1] // 8
+    small[...] = jnp.zeros_like(small)
+    for r in range(8):
+        z, side = r // 2, r % 2
+        at = slice(r * shard_rows, (r + 1) * shard_rows)
+        for row in range(6):
+            small[row : row + 1, at] = vectors[z, side, 2 + row : 3 + row, :shard_rows]
+        up_bias[:, r * up_cols : (r + 1) * up_cols] = vectors[z, side, 8:9, :up_cols]
     for j, block in enumerate((t0, t1, t2, t3)):
         qkv[j * rows : (j + 1) * rows, :] = (dot_nn(block[...], full) + bias).astype(jnp.bfloat16)
     mask = key_bias(sc, rows)
@@ -843,21 +866,16 @@
     )
     gathered = lax.all_gather(quarter, ("z", "core", "seq"), axis=0, tiled=True)
     gathered = gathered.reshape(zs, 2, 4, shard_rows, width)
-    columns = lax.dynamic_index_in_dim(
-        w_qkv.reshape(shard_rows, 3, 4, head_width), place, axis=2, keepdims=False
-    ).reshape(shard_rows, 3 * head_width)
-    pair_rows = jnp.zeros((2, 2, shard_rows), bf16)
-    placed_q = lax.dynamic_update_slice(pair_rows[0], q_bias[None], (core, 0)).reshape(1, -1)
-    placed_v = lax.dynamic_update_slice(pair_rows[0], v_bias[None], (core, 0)).reshape(1, -1)
-    bias_row = jnp.concatenate(
-        [placed_q, jnp.zeros((1, head_width), bf16), placed_v], axis=1
-    )
-    vectors = jnp.concatenate(
-        [out_bias, gain_one, shift_one, down_bias, gain_two, shift_two, up_bias]
-    )
-    pad = 15 * 3 * head_width - vectors.shape[0]
-    vector_rows = jnp.pad(vectors, (0, pad)).reshape(15, 3 * head_width)
-    own_block = jnp.concatenate([columns, bias_row, vector_rows], axis=0)
+    vectors = (q_bias, v_bias, out_bias, gain_one, shift_one)
+    vectors += (down_bias, gain_two, shift_two, up_bias)
+    own_block = pl.pallas_call(
+        pack_kernel,
+        name="pack",
+        cost_estimate=work(2),
+        out_shape=struct((shard_rows + 16, 3 * head_width)),
+        in_specs=[smem_spec()] + vmem_specs(1 + len(vectors)),
+        out_specs=pl.BlockSpec(memory_space=pltpu.VMEM),
+    )(place[None].astype(jnp.int32), w_qkv, *[vector[None] for vector in vectors])
     t1, t2, t3 = across(token, 1), across(token, 2), across(token, 3)
     two_cols = jnp.stack([own_block, level_across(own_block, 1)])
     own_cols = jnp.concatenate([two_cols, level_across(two_cols, 2)])
@@ -874,7 +892,7 @@
     down_sets = [own_down] + [across(own_down, j) for j in (1, 2, 3)]
     sc = jnp.stack([lengths[0], place, core, lax.axis_index("z")]).astype(jnp.int32)
     all_rows = 4 * rows
-    qkv, ctx_t, c0, c1, c2, c3, lse, full_qkv, vector_sets = pl.pallas_call(
+    qkv, ctx_t, c0, c1, c2, c3, lse, full_qkv, small, full_up_bias = pl.pallas_call(
         attend_forward_kernel,
         name="attend_forward",
         cost_estimate=work(13),
@@ -887,21 +905,20 @@
             struct((rows, head_width)),
             struct((head_width // HEAD_DIM, all_rows), f32),
             struct((zs, 2, shard_rows, 3 * head_width)),
-            struct((zs, 2, 2, 3 * head_width), f32),
+            struct((8, width), f32),
+            struct((1, hidden), f32),
         ),
         in_specs=[smem_spec()] + vmem_specs(6),
-        out_specs=tuple(vmem_specs(9)),
-        scratch_shapes=[pltpu.VMEM((4, rows, head_width), bf16)],
+        out_specs=tuple(vmem_specs(10)),
+        scratch_shapes=[
+            pltpu.VMEM((4, rows, head_width), bf16),
+            pltpu.VMEM((zs, 2, 16, 3 * head_width), f32),
+        ],
     )(sc, token, t1, t2, t3, own_cols, other_cols)
     x1, x2, x3 = across(c1, 1), across(c2, 2), across(c3, 3)
     down_sets[0], _ = lax.optimization_barrier((down_sets[0], c0))
     own_down = jnp.stack(down_sets)
     other_down = partner(own_down)
-    all_vec = vector_sets.reshape(2 * zs, -1)
-    six = all_vec[:, : 6 * shard_rows].reshape(2 * zs, 6, shard_rows)
-    six = six.transpose(1, 0, 2).reshape(6, width)
-    small = jnp.concatenate([six, jnp.zeros((2, width), f32)], axis=0)
-    full_up_bias = all_vec[:, 6 * shard_rows : 6 * shard_rows + hidden // 8].reshape(1, hidden)
     packed = hidden // 2 + 5 * width + width // 2
     output, grad_one, y0, y1, y2, y3, keep, send, vector_rows = pl.pallas_call(
         middle_kernel,
@@ -1056,8 +1073,8 @@
     token_sum = lax.psum_scatter(
         token_parts.reshape(4 * rows, width), "seq", scatter_dimension=0, tiled=True
     )
-    near, q_part = lax.optimization_barrier((near, q_part))
     q_others = [across(q_part, j) for j in (1, 2, 3)]
+    near, _ = lax.optimization_barrier((near, q_last))
     merged = level_sum(near, far, (merged_rows, quad))
     merged, q_others = lax.optimization_barrier((merged, q_others))
     half_rows = shard_rows + shard_rows // 2 + 16

time: 286 us -> 281 us (0.983)
  local copies, waits for them, and re-layouts: 32.3 us -> 15.3 us
  waiting for transfers between devices: 97.3 us -> 108 us
    reshape x8 -> x0, local copies, waits for them, and re-layouts: 6.42 us -> none  [the longest x1 1.61 us: fast_body(): w_qkv.reshape(shard_rows, 3, 4, head_width)]
    concatenate x2 -> x0, local copies, waits for them, and re-layouts: 6.14 us -> none  [the longest x1 4.78 us: fast_body(): jnp.concatenate([out_bias, gain_one, shift_one, down_bias, gain_two, shif...]
    ppermute x22, waiting for transfers between devices: 36.9 us -> 42.2 us  [across(): return lax.ppermute(value, 'seq', [(i, i ^ step) for i in range(4)])]
    ppermute x10, waiting for transfers between devices: 58.8 us -> 63.8 us  [level_across(): return lax.ppermute(value, 'z', [(i, i ^ step) for i in range(4)])]
    unnamed x65 -> x74, local copies, waits for them, and re-layouts: 12.2 us -> 11 us
  transfers between devices with their start and end apart: 40 -> 40, of which waited for: 19 -> 23; matrix products, arithmetic and copies ran while one was open for 10% -> 4% of each run, Pallas kernels for 21% -> 22%
where the time goes in v5:
time: 281 us; the launch traced here: 280 us
  waiting for transfers between devices  108 us (38%)
  Pallas kernels  90.4 us (32%)
  starting transfers between devices  42.2 us (15%)
  local copies, waits for them, and re-layouts  15.3 us (5%)
  between operations  15 us (5%)
  other arithmetic  9.39 us (3%)
    ppermute x10, waiting for transfers between devices, level_across(): return lax.ppermute(value, 'z', [(i, i ^ step) for i in range(4)])  63.8 us
    pallas_call x14, Pallas kernels, call(): pl.pallas_call(kernel, name=kernel.__name__.replace('_kernel', ''), cost_...  42.8 us
    ppermute x22, waiting for transfers between devices, across(): return lax.ppermute(value, 'seq', [(i, i ^ step) for i in range(4)])  42.2 us
    ppermute x22, starting transfers between devices, across(): return lax.ppermute(value, 'seq', [(i, i ^ step) for i in range(4)])  25.1 us
    ppermute x10, starting transfers between devices, level_across(): return lax.ppermute(value, 'z', [(i, i ^ step) for i in range(4)])  16.4 us
    pallas_call x1, Pallas kernels, fast_body(): pl.pallas_call(middle_kernel, name='middle', cost_estimate=work(15), out_...  15.7 us
    pallas_call x1, Pallas kernels, fast_body(): pl.pallas_call(attend_forward_kernel, name='attend_forward', cost_estimat...  13 us
    pallas_call x1, Pallas kernels, fast_body(): pl.pallas_call(attend_backward_kernel, name='attend_backward', cost_estim...  12.6 us
  transfers between devices with their start and end apart: 40, of which 23 were waited for; matrix products, arithmetic and copies ran while one was open for 4% of the time, Pallas kernels for 22%

profile of v5, /device:TPU:0, one launch (start us, length us, event | category | flops | bytes accessed | tf_op | source)
XLA Modules:
  0.0 279.8 jit_solution(16425290975080413214)
XLA Ops:
  7.3 1.7 constant_dynamic-slice_fusion
  9.0 1.2 broadcast_in_dim.42.refs_8_
  10.2 2.1 pack.1
  12.3 3.0 %collective-permute-start.2 = (bf16[112,576]{1,0:T(8,128)(2,1)}, bf16[112,576]{1,0:T(8,128)(2,1)S(1)}, u32[]{:S(2)}, u32[]{:S(2)}) collective-permute-start(bf16[112,576]{1,0:T(8,128)(2,1)} %pack.1), channel_id=1, source_target_pairs={{0,2},{2,0},{4,6},{6,4},{1,3},{3,1},{5,7},{7,5},{8,10},{10,8},{12,... | collective-permute-start | bytes 387080 | tf_op jit(solution)/shard_map/ppermute | solution.py:858
  15.5 4.7 %collective-permute-done.2 = bf16[112,576]{1,0:T(8,128)(2,1)S(1)} collective-permute-done((bf16[112,576]{1,0:T(8,128)(2,1)}, bf16[112,576]{1,0:T(8,128)(2,1)S(1)}, u32[]{:S(2)}, u32[]{:S(2)}) %collective-permute-start.2) | collective-permute-done | bytes 129056 | tf_op jit(solution)/shard_map/ppermute | solution.py:858
  21.1 3.1 %collective-permute-start.3 = (bf16[2,112,576]{2,1,0:T(8,128)(2,1)S(1)}, bf16[2,112,576]{2,1,0:T(8,128)(2,1)S(1)}, u32[]{:S(2)}, u32[]{:S(2)}) collective-permute-start(bf16[2,112,576]{2,1,0:T(8,128)(2,1)S(1)} %pad_maximum_fusion.6), channel_id=1, source_target_pairs={{0,4},{2,6},{4,0},{6,2},{1,5},{3,7},{5,1},{7,3},{8,12},{10,14},{12... | collective-permute-start | bytes 774152 | tf_op jit(solution)/shard_map/ppermute | solution.py:858
  24.3 1.7 collective-permute-start.1
  26.0 2.4 collective-permute-start.6
  29.5 17.2 %collective-permute-done.3 = bf16[2,112,576]{2,1,0:T(8,128)(2,1)S(1)} collective-permute-done((bf16[2,112,576]{2,1,0:T(8,128)(2,1)S(1)}, bf16[2,112,576]{2,1,0:T(8,128)(2,1)S(1)}, u32[]{:S(2)}, u32[]{:S(2)}) %collective-permute-start.3) | collective-permute-done | bytes 258080 | tf_op jit(solution)/shard_map/ppermute | solution.py:858
  47.7 3.6 %collective-permute-done.1 = bf16[2,96,768]{2,1,0:T(8,128)(2,1)S(1)} collective-permute-done((bf16[2,96,768]{2,1,0:T(8,128)(2,1)S(1)}, bf16[2,96,768]{2,1,0:T(8,128)(2,1)S(1)}, u32[]{:S(2)}, u32[]{:S(2)}) %collective-permute-start.1) | collective-permute-done | bytes 294944 | tf_op jit(solution)/shard_map/ppermute | solution.py:858
  52.0 2.4 collective-permute-start.15
  55.5 1.1 collective-permute-done.7
  56.6 2.8 %collective-permute-start.8 = (bf16[2,96,768]{2,1,0:T(8,128)(2,1)S(1)}, bf16[2,96,768]{2,1,0:T(8,128)(2,1)}, u32[]{:S(2)}, u32[]{:S(2)}) collective-permute-start(bf16[2,96,768]{2,1,0:T(8,128)(2,1)S(1)} %pad_maximum_fusion.5), channel_id=1, source_target_pairs={{0,4},{2,6},{4,0},{6,2},{1,5},{3,7},{5,1},{7,3},{8,12},{10,14},{12... | collective-permute-start | bytes 884744 | tf_op jit(solution)/shard_map/ppermute | solution.py:858
  60.7 18.1 %collective-permute-done.8 = bf16[2,96,768]{2,1,0:T(8,128)(2,1)} collective-permute-done((bf16[2,96,768]{2,1,0:T(8,128)(2,1)S(1)}, bf16[2,96,768]{2,1,0:T(8,128)(2,1)}, u32[]{:S(2)}, u32[]{:S(2)}) %collective-permute-start.8) | collective-permute-done | bytes 294944 | tf_op jit(solution)/shard_map/ppermute | solution.py:858
  78.8 1.8 pad_maximum_fusion.2.own_out
  80.7 13.0 %attend_forward.1 = (bf16[1024,576]{1,0:T(8,128)(2,1)}, f32[192,1024]{1,0:T(8,128)}, bf16[256,192]{1,0:T(8,128)(2,1)}, bf16[256,192]{1,0:T(8,128)(2,1)}, bf16[25...) custom-call(s32[4]{0:T(128)} %pad_add_fusion.sc, ...), custom_call_target="tpu_custom_call" | custom-call | flops 1170000000 | bytes 3900000 | tf_op jit(solution)/shard_map/attend_forward/pallas_call | solution.py:895
  93.7 1.8 pad_maximum_fusion.own_down
  96.9 2.0 collective-permute-start.11
  99.6 2.8 collective-permute-done.10.x1
  102.4 2.0 collective-permute-done.11.x2
  106.6 15.7 %middle.1 = (bf16[256,768]{1,0:T(8,128)(2,1)}, f32[256,768]{1,0:T(8,128)}, bf16[256,192]{1,0:T(8,128)(2,1)}, bf16[256,192]{1,0:T(8,128)(2,1)}, bf16[256,192]{1,0...) custom-call(s32[4]{0:T(128)} %pad_add_fusion.sc, ...), custom_call_target="tpu_custom_call" | custom-call | flops 1350000000 | bytes 4500000 | tf_op jit(solution)/shard_map/middle/pallas_call | solution.py:923
  122.4 1.5 collective-permute-start.19
  124.8 1.1 collective-permute-start.21
  126.0 3.0 %collective-permute-done.19.g1 = bf16[256,192]{1,0:T(8,128)(2,1)S(1)} collective-permute-done((bf16[256,192]{1,0:T(8,128)(2,1)}, bf16[256,192]{1,0:T(8,128)(2,1)S(1)}, u32[]{:S(2)}, u32[]{:S(2)}) %collective-permute-start.19) | collective-permute-done | bytes 98336 | tf_op jit(solution)/shard_map/ppermute | solution.py:852
  129.0 2.1 collective-permute-done.20.g2
  131.1 1.5 collective-permute-done.21.g3
  134.2 6.7 %up_grad.1 = (bf16[2,4,256,384]{3,2,1,0:T(8,128)(2,1)}, bf16[2,4,256,384]{3,2,1,0:T(8,128)(2,1)}) custom-call(s32[4]{0:T(128)} %pad_add_fusion.sc, bf16[256,5760]{1,0:T(8,128)(2,1)} %get-tuple-element.117.keep, bf16[256,5760]{1,0:T(8,128)(2,1)} %copy-done.1, bf16[4,16,384]{2,1,0:T(8,128)(2,1)} %get-tuple-element.124.vectors), custom_call_target="tpu_custom_call" | custom-call | flops 360000000 | bytes 1200000 | tf_op jit(solution)/shard_map/up_grad/pallas_call | solution.py:973
  141.7 5.9 %down_grad.1 = (bf16[2,4,96,768]{3,2,1,0:T(8,128)(2,1)}, bf16[2,4,96,768]{3,2,1,0:T(8,128)(2,1)}) custom-call(s32[4]{0:T(128)} %pad_add_fusion.sc, bf16[256,5760]{1,0:T(8,128)(2,1)} %get-tuple-element.117.keep, bf16[256,5760]{1,0:T(8,128)(2,1)} %copy-done.1), custom_call_target="tpu_custom_call" | custom-call | flops 360000000 | bytes 1200000 | tf_op jit(solution)/shard_map/down_grad/pallas_call | solution.py:973
  147.6 1.4 collective-permute-start.22
  149.1 12.6 %attend_backward.1.dqkv = bf16[1024,576]{1,0:T(8,128)(2,1)} custom-call(s32[4]{0:T(128)} %pad_add_fusion.sc, bf16[1024,576]{1,0:T(8,128)(2,1)} %get-tuple-element.128.qkv, f32[192,1024]{1,0:T(8,128)} %get-tuple-element.129.ctx_t, f32[3,1024]{1,0:T(4,128)} %get-tuple-element.130.lse, bf16[256,192]{1,0:T(8,128)(2,1)} %get-tuple-element.131.g0, ...), custom_call_target="tpu_custom_call" | custom-call | flops 990000000 | bytes 3300000 | tf_op jit(solution)/shard_map/attend_backward/pallas_call | solution.py:1005
  161.7 4.2 %grad_qkv_weight.1 = (bf16[4,112,576]{2,1,0:T(8,128)(2,1)}, bf16[4,112,576]{2,1,0:T(8,128)(2,1)}) custom-call(s32[4]{0:T(128)} %pad_add_fusion.sc, bf16[256,768]{1,0:T(8,128)(2,1)} %bitcast.48, bf16[256,768]{1,0:T(8,128)(2,1)} %copy-done.16, bf16[256,768]{1,0:T(8,128)(2,1)} %copy-done.15, bf16[256,768]{1,0:T(8,128)(2,1)} %copy-done.14, ...), custom_call_target="tpu_custom_call" | custom-call | flops 360000000 | bytes 1200000 | tf_op jit(solution)/shard_map/grad_qkv_weight/pallas_call | solution.py:1019
  165.9 11.1 %collective-permute-done.23.got = bf16[2,4,256,384]{3,2,1,0:T(8,128)(2,1)S(1)} collective-permute-done((bf16[2,4,256,384]{3,2,1,0:T(8,128)(2,1)}, bf16[2,4,256,384]{3,2,1,0:T(8,128)(2,1)S(1)}, u32[]{:S(2)}, u32[]{:S(2)}) %collective-permute-start.23) | collective-permute-done | bytes 1572896 | tf_op jit(solution)/shard_map/ppermute | solution.py:852
  177.0 1.1 copy-done.5
  178.1 3.2 %fold.5 = (bf16[4,256,384]{2,1,0:T(8,128)(2,1)}, bf16[4,256,384]{2,1,0:T(8,128)(2,1)}) custom-call(bf16[2,4,256,384]{3,2,1,0:T(8,128)(2,1)} %get-tuple-element.139.near, bf16[2,4,256,384]{3,2,1,0:T(8,128)(2,1)} %copy-done.5), custom_call_target="tpu_custom_call" | custom-call | flops 90000000 | bytes 300000 | tf_op jit(solution)/shard_map/fold/pallas_call | solution.py:973
  182.7 2.8 fold.4
  185.5 1.4 collective-permute-start.26
  186.9 2.1 level_fold.1
  189.0 4.2 %grad_tokens.1 = bf16[4,256,768]{2,1,0:T(8,128)(2,1)} custom-call(s32[4]{0:T(128)} %pad_add_fusion.sc, bf16[1024,576]{1,0:T(8,128)(2,1)} %attend_backward.1.dqkv, bf16[4,2,96,576]{3,2,1,0:T(8,128)(2,1)} %get-tuple-element.165.weight), custom_call_target="tpu_custom_call" | custom-call | flops 360000000 | bytes 1200000 | tf_op jit(solution)/shard_map/grad_tokens/pallas_call | solution.py:973
  193.2 2.7 collective-permute-done.25.got
  196.6 1.8 fold.6
  201.1 3.0 %level_merge.1 = (bf16[2,448,384]{2,1,0:T(8,128)(2,1)}, bf16[2,448,384]{2,1,0:T(8,128)(2,1)}) custom-call(s32[4]{0:T(128)} %pad_add_fusion.sc, bf16[4,96,768]{2,1,0:T(8,128)(2,1)} %get-tuple-element.148.d_mine, bf16[4,96,768]{2,1,0:T(8,128)(2,1)} %copy-done.12, bf16[4,256,384]{2,1,0:T(8,128)(2,1)} %get-tuple-element.150.u_mine, bf16[4,256,384]{2,1,0:T(8,128)(2,1)} %copy-done.8), custom_call_target="tpu_custom_call" | custom-call | flops 180000000 | bytes 600000 | tf_op jit(solution)/shard_map/level_merge/pallas_call | solution.py:973
  204.2 3.5 %collective-permute-start.28 = (bf16[112,576]{1,0:T(8,128)(2,1)S(1)}, bf16[112,576]{1,0:T(8,128)(2,1)S(1)}, u32[]{:S(2)}, u32[]{:S(2)}) collective-permute-start(bf16[112,576]{1,0:T(8,128)(2,1)S(1)} %copy-done.33), channel_id=1, source_target_pairs={{0,4},{2,6},{4,0},{6,2},{1,5},{3,7},{5,1},{7,3},{8,12},{10,14},{12... | collective-permute-start | bytes 387080 | tf_op jit(solution)/shard_map/ppermute | solution.py:858
  207.7 12.3 %collective-permute-done.28.e1 = bf16[112,576]{1,0:T(8,128)(2,1)S(1)} collective-permute-done((bf16[112,576]{1,0:T(8,128)(2,1)S(1)}, bf16[112,576]{1,0:T(8,128)(2,1)S(1)}, u32[]{:S(2)}, u32[]{:S(2)}) %collective-permute-start.28) | collective-permute-done | bytes 129056 | tf_op jit(solution)/shard_map/ppermute | solution.py:858
  220.1 2.2 collective-permute-done.29.got
  223.1 2.2 fold.7
  225.3 1.4 collective-permute-start.30
  226.7 1.7 sum.1.b0
  228.4 1.4 collective-permute-start.33
  229.8 1.7 collective-permute-start.32
  231.9 6.8 %collective-permute-done.33.b3 = bf16[112,576]{1,0:T(8,128)(2,1)S(1)} collective-permute-done((bf16[112,576]{1,0:T(8,128)(2,1)}, bf16[112,576]{1,0:T(8,128)(2,1)S(1)}, u32[]{:S(2)}, u32[]{:S(2)}) %collective-permute-start.33) | collective-permute-done | bytes 129056 | tf_op jit(solution)/shard_map/ppermute | solution.py:852
  238.7 1.4 collective-permute-done.32.b2
  240.1 1.9 collective-permute-done.30.e1
  242.8 2.0 split_up.1
  244.8 1.5 collective-permute-done.34.got
  247.0 1.9 join.1
  248.8 1.6 collective-permute-start.37
  250.4 1.7 collective-permute-start.36
  252.3 1.4 slice_bitcast_fusion
  253.8 1.3 reduce
  255.1 2.3 finish_qkv.1
  257.4 1.8 fusion
  259.2 2.2 collective-permute-done.37.b3
  261.4 7.1 %collective-permute-done.36.b2 = bf16[240,768]{1,0:T(8,128)(2,1)S(1)} collective-permute-done((bf16[240,768]{1,0:T(8,128)(2,1)}, bf16[240,768]{1,0:T(8,128)(2,1)S(1)}, u32[]{:S(2)}, u32[]{:S(2)}) %collective-permute-start.36) | collective-permute-done | bytes 368672 | tf_op jit(solution)/shard_map/ppermute | solution.py:852
  270.0 3.0 %finish.1 = (f32[384,768]{1,0:T(8,128)}, f32[96,3072]{1,0:T(8,128)}, f32[96,768]{1,0:T(8,128)}) custom-call(s32[4]{0:T(128)} %pad_add_fusion.sc, bf16[240,768]{1,0:T(8,128)(2,1)} %get-tuple-element.177.b0, bf16[240,768]{1,0:T(8,128)(2,1)} %copy-done.19, bf16[240,768]{1,0:T(8,128)(2,1)} %copy-done.18, bf16[240,768]{1,0:T(8,128)(2,1)} %copy-done.17), custom_call_target="tpu_custom_call" | custom-call | flops 180000000 | bytes 600000 | tf_op jit(solution)/shard_map/finish/pallas_call | solution.py:973
  (126 shorter events, 22.5 us)
Async XLA Ops:
  7.2 8.2 %copy-start = (bf16[384,768]{1,0:T(8,128)(2,1)S(1)}, bf16[384,768]{1,0:T(8,128)(2,1)}, u32[]{:S(2)}) copy-start(bf16[384,768]{1,0:T(8,128)(2,1)} %param.27) | copy-start | bytes 1769476
  7.2 18.8 %copy-start.4 = (bf16[1,256,768]{2,1,0:T(8,128)(2,1)S(1)}, bf16[1,256,768]{2,1,0:T(8,128)(2,1)}, u32[]{:S(2)}) copy-start(bf16[1,256,768]{2,1,0:T(8,128)(2,1)} %param.16) | copy-start | bytes 1179652
  7.2 98.6 %all-gather.2.cloned.1.call-start = ((), (), s32[]{:S(2)}) async-start(), calls=%async_computation.1 | async-start | bytes 4866048 | tf_op jit(solution)/shard_map/all_gather | solution.py:867
  8.9 239.9 %reduce-scatter.2.cloned.1.call-start = ((), (), s32[]{:S(2)}) async-start(), calls=%async_computation.2 | async-start | bytes 1966080 | tf_op jit(solution)/shard_map/reduce_scatter | solution.py:1073
  10.2 41.1 %copy-start.11 = (bf16[96,768]{1,0:T(8,128)(2,1)S(1)}, bf16[96,768]{1,0:T(8,128)(2,1)}, u32[]{:S(2)}) copy-start(bf16[96,768]{1,0:T(8,128)(2,1)} %param.21) | copy-start | bytes 442372
  12.3 7.8 %collective-permute-start.2 = (bf16[112,576]{1,0:T(8,128)(2,1)}, bf16[112,576]{1,0:T(8,128)(2,1)S(1)}, u32[]{:S(2)}, u32[]{:S(2)}) collective-permute-start(bf16[112,576]{1,0:T(8,128)(2,1)} %pack.1), channel_id=1, source_target_pairs={{0,2},{2,0},{4,6},{6,4},{1,3},{3,1},{5,7},{7,5},{8,10},{10,8},{12,... | collective-permute-start | bytes 387080 | tf_op jit(solution)/shard_map/ppermute | solution.py:858
  15.4 8.9 %collective-permute-start = (bf16[96,768]{1,0:T(8,128)(2,1)S(1)}, bf16[96,768]{1,0:T(8,128)(2,1)S(1)}, u32[]{:S(2)}, u32[]{:S(2)}) collective-permute-start(bf16[96,768]{1,0:T(8,128)(2,1)S(1)} %constant_dynamic-slice_fusion.1), channel_id=1, source_target_pairs={{0,2},{2,0},{4,6},{6,4},{1,3},{3,1},{5,7},{7,5},{8,10},{10,8},{12,... | collective-permute-start | bytes 442376 | tf_op jit(solution)/shard_map/ppermute | solution.py:858
  21.1 25.6 %collective-permute-start.3 = (bf16[2,112,576]{2,1,0:T(8,128)(2,1)S(1)}, bf16[2,112,576]{2,1,0:T(8,128)(2,1)S(1)}, u32[]{:S(2)}, u32[]{:S(2)}) collective-permute-start(bf16[2,112,576]{2,1,0:T(8,128)(2,1)S(1)} %pad_maximum_fusion.6), channel_id=1, source_target_pairs={{0,4},{2,6},{4,0},{6,2},{1,5},{3,7},{5,1},{7,3},{8,12},{10,14},{12... | collective-permute-start | bytes 774152 | tf_op jit(solution)/shard_map/ppermute | solution.py:858
  24.3 27.0 %collective-permute-start.1 = (bf16[2,96,768]{2,1,0:T(8,128)(2,1)S(1)}, bf16[2,96,768]{2,1,0:T(8,128)(2,1)S(1)}, u32[]{:S(2)}, u32[]{:S(2)}) collective-permute-start(bf16[2,96,768]{2,1,0:T(8,128)(2,1)S(1)} %pad_maximum_fusion.4), channel_id=1, source_target_pairs={{0,4},{2,6},{4,0},{6,2},{1,5},{3,7},{5,1},{7,3},{8,12},{10,14},{12... | collective-permute-start | bytes 884744 | tf_op jit(solution)/shard_map/ppermute | solution.py:858
  26.0 25.4 %collective-permute-start.6 = (bf16[256,768]{1,0:T(8,128)(2,1)S(1)}, bf16[256,768]{1,0:T(8,128)(2,1)S(1)}, u32[]{:S(2)}, u32[]{:S(2)}) collective-permute-start(bf16[256,768]{1,0:T(8,128)(2,1)S(1)} %bitcast.49), channel_id=1, source_target_pairs={{0,24},{8,16},{16,8},{24,0},{1,25},{9,17},{17,9},{25,1},{2,26},{10... | collective-permute-start | bytes 1179656 | tf_op jit(solution)/shard_map/ppermute | solution.py:852
  28.4 22.9 %collective-permute-start.5 = (bf16[256,768]{1,0:T(8,128)(2,1)S(1)}, bf16[256,768]{1,0:T(8,128)(2,1)S(1)}, u32[]{:S(2)}, u32[]{:S(2)}) collective-permute-start(bf16[256,768]{1,0:T(8,128)(2,1)S(1)} %bitcast.50), channel_id=1, source_target_pairs={{0,16},{8,24},{16,0},{24,8},{1,17},{9,25},{17,1},{25,9},{2,18},{10... | collective-permute-start | bytes 1179656 | tf_op jit(solution)/shard_map/ppermute | solution.py:852
  28.9 22.5 %collective-permute-start.4 = (bf16[256,768]{1,0:T(8,128)(2,1)S(1)}, bf16[256,768]{1,0:T(8,128)(2,1)S(1)}, u32[]{:S(2)}, u32[]{:S(2)}) collective-permute-start(bf16[256,768]{1,0:T(8,128)(2,1)S(1)} %bitcast.51), channel_id=1, source_target_pairs={{0,8},{8,0},{16,24},{24,16},{1,9},{9,1},{17,25},{25,17},{2,10},{10... | collective-permute-start | bytes 1179656 | tf_op jit(solution)/shard_map/ppermute | solution.py:852
  47.7 33.0 %copy-start.13 = (bf16[4,112,576]{2,1,0:T(8,128)(2,1)}, bf16[4,112,576]{2,1,0:T(8,128)(2,1)S(1)}, u32[]{:S(2)}) copy-start(bf16[4,112,576]{2,1,0:T(8,128)(2,1)S(1)} %pad_maximum_fusion.3.own) | copy-start | bytes 1548292
  51.3 29.3 %copy-start.14 = (bf16[256,768]{1,0:T(8,128)(2,1)}, bf16[256,768]{1,0:T(8,128)(2,1)S(1)}, u32[]{:S(2)}) copy-start(bf16[256,768]{1,0:T(8,128)(2,1)S(1)} %collective-permute-done.6.t3) | copy-start | bytes 1179652
  51.4 29.3 %copy-start.15 = (bf16[256,768]{1,0:T(8,128)(2,1)}, bf16[256,768]{1,0:T(8,128)(2,1)S(1)}, u32[]{:S(2)}) copy-start(bf16[256,768]{1,0:T(8,128)(2,1)S(1)} %collective-permute-done.5.t2) | copy-start | bytes 1179652
  51.4 5.2 %copy-start.16 = (bf16[256,768]{1,0:T(8,128)(2,1)}, bf16[256,768]{1,0:T(8,128)(2,1)S(1)}, u32[]{:S(2)}) copy-start(bf16[256,768]{1,0:T(8,128)(2,1)S(1)} %collective-permute-done.4.t1) | copy-start | bytes 1179652
  51.4 5.2 %collective-permute-start.7 = (bf16[96,768]{1,0:T(8,128)(2,1)S(1)}, bf16[96,768]{1,0:T(8,128)(2,1)S(1)}, u32[]{:S(2)}, u32[]{:S(2)}) collective-permute-start(bf16[96,768]{1,0:T(8,128)(2,1)S(1)} %copy-done.11), channel_id=1, source_target_pairs={{0,2},{2,0},{4,6},{6,4},{1,3},{3,1},{5,7},{7,5},{8,10},{10,8},{12,... | collective-permute-start | bytes 442376 | tf_op jit(solution)/shard_map/ppermute | solution.py:858
  52.0 28.7 %collective-permute-start.9 = (bf16[4,112,576]{2,1,0:T(8,128)(2,1)S(1)}, bf16[4,112,576]{2,1,0:T(8,128)(2,1)}, u32[]{:S(2)}, u32[]{:S(2)}) collective-permute-start(bf16[4,112,576]{2,1,0:T(8,128)(2,1)S(1)} %pad_maximum_fusion.3.own), channel_id=1, source_target_pairs={{0,1},{1,0},{2,3},{3,2},{4,5},{5,4},{6,7},{7,6},{8,9},{9,8},{10,11... | collective-permute-start | bytes 1548296 | tf_op jit(solution)/shard_map/ppermute | solution.py:855
  52.0 41.7 %collective-permute-start.15 = (bf16[4,96,768]{2,1,0:T(8,128)(2,1)S(1)}, bf16[4,96,768]{2,1,0:T(8,128)(2,1)}, u32[]{:S(2)}, u32[]{:S(2)}) collective-permute-start(bf16[4,96,768]{2,1,0:T(8,128)(2,1)S(1)} %pad_maximum_fusion.1), channel_id=1, source_target_pairs={{0,24},{8,16},{16,8},{24,0},{1,25},{9,17},{17,9},{25,1},{2,26},{10... | collective-permute-start | bytes 1769480 | tf_op jit(solution)/shard_map/ppermute | solution.py:852
  54.4 39.3 %collective-permute-start.14 = (bf16[4,96,768]{2,1,0:T(8,128)(2,1)S(1)}, bf16[4,96,768]{2,1,0:T(8,128)(2,1)}, u32[]{:S(2)}, u32[]{:S(2)}) collective-permute-start(bf16[4,96,768]{2,1,0:T(8,128)(2,1)S(1)} %pad_maximum_fusion.1), channel_id=1, source_target_pairs={{0,16},{8,24},{16,0},{24,8},{1,17},{9,25},{17,1},{25,9},{2,18},{10... | collective-permute-start | bytes 1769480 | tf_op jit(solution)/shard_map/ppermute | solution.py:852
  54.9 38.7 %collective-permute-start.13 = (bf16[4,96,768]{2,1,0:T(8,128)(2,1)S(1)}, bf16[4,96,768]{2,1,0:T(8,128)(2,1)}, u32[]{:S(2)}, u32[]{:S(2)}) collective-permute-start(bf16[4,96,768]{2,1,0:T(8,128)(2,1)S(1)} %pad_maximum_fusion.1), channel_id=1, source_target_pairs={{0,8},{8,0},{16,24},{24,16},{1,9},{9,1},{17,25},{25,17},{2,10},{10... | collective-permute-start | bytes 1769480 | tf_op jit(solution)/shard_map/ppermute | solution.py:852
  56.6 22.2 %collective-permute-start.8 = (bf16[2,96,768]{2,1,0:T(8,128)(2,1)S(1)}, bf16[2,96,768]{2,1,0:T(8,128)(2,1)}, u32[]{:S(2)}, u32[]{:S(2)}) collective-permute-start(bf16[2,96,768]{2,1,0:T(8,128)(2,1)S(1)} %pad_maximum_fusion.5), channel_id=1, source_target_pairs={{0,4},{2,6},{4,0},{6,2},{1,5},{3,7},{5,1},{7,3},{8,12},{10,14},{12... | collective-permute-start | bytes 884744 | tf_op jit(solution)/shard_map/ppermute | solution.py:858
  93.7 1.9 copy-start.3
  93.7 2.4 copy-start.36
  93.7 3.2 %copy-start.35 = (bf16[256,192]{1,0:T(8,128)(2,1)S(1)}, bf16[256,192]{1,0:T(8,128)(2,1)}, u32[]{:S(2)}) copy-start(bf16[256,192]{1,0:T(8,128)(2,1)} %get-tuple-element.107) | copy-start | bytes 294916
  93.7 5.2 %copy-start.34 = (bf16[256,192]{1,0:T(8,128)(2,1)S(1)}, bf16[256,192]{1,0:T(8,128)(2,1)}, u32[]{:S(2)}) copy-start(bf16[256,192]{1,0:T(8,128)(2,1)} %get-tuple-element.108) | copy-start | bytes 294916
  95.5 10.3 %copy-start.2 = (bf16[4,4,96,768]{3,2,1,0:T(8,128)(2,1)}, bf16[4,4,96,768]{3,2,1,0:T(8,128)(2,1)S(1)}, u32[]{:S(2)}) copy-start(bf16[4,4,96,768]{3,2,1,0:T(8,128)(2,1)S(1)} %pad_maximum_fusion.own_down) | copy-start | bytes 7077892
  95.5 10.3 %collective-permute-start.16 = (bf16[4,4,96,768]{3,2,1,0:T(8,128)(2,1)S(1)}, bf16[4,4,96,768]{3,2,1,0:T(8,128)(2,1)}, u32[]{:S(2)}, u32[]{:S(2)}) collective-permute-start(bf16[4,4,96,768]{3,2,1,0:T(8,128)(2,1)S(1)} %pad_maximum_fusion.own_down), channel_id=1, source_target_pairs={{0,1},{1,0},{2,3},{3,2},{4,5},{5,4},{6,7},{7,6},{8,9},{9,8},{10,11... | collective-permute-start | bytes 7077896 | tf_op jit(solution)/shard_map/ppermute | solution.py:855
  95.6 9.6 %collective-permute-start.17 = (bf16[4,96,768]{2,1,0:T(8,128)(2,1)S(1)}, bf16[4,96,768]{2,1,0:T(8,128)(2,1)S(1)}, u32[]{:S(2)}, u32[]{:S(2)}) collective-permute-start(bf16[4,96,768]{2,1,0:T(8,128)(2,1)S(1)} %copy-done.3), channel_id=1, source_target_pairs={{0,1},{1,0},{2,3},{3,2},{4,5},{5,4},{6,7},{7,6},{8,9},{9,8},{10,11... | collective-permute-start | bytes 1769480 | tf_op jit(solution)/shard_map/ppermute | solution.py:855
  96.1 6.3 %collective-permute-start.10 = (bf16[256,192]{1,0:T(8,128)(2,1)S(1)}, bf16[256,192]{1,0:T(8,128)(2,1)S(1)}, u32[]{:S(2)}, u32[]{:S(2)}) collective-permute-start(bf16[256,192]{1,0:T(8,128)(2,1)S(1)} %copy-done.36), channel_id=1, source_target_pairs={{0,8},{8,0},{16,24},{24,16},{1,9},{9,1},{17,25},{25,17},{2,10},{10... | collective-permute-start | bytes 294920 | tf_op jit(solution)/shard_map/ppermute | solution.py:852
  96.9 7.5 %collective-permute-start.11 = (bf16[256,192]{1,0:T(8,128)(2,1)S(1)}, bf16[256,192]{1,0:T(8,128)(2,1)S(1)}, u32[]{:S(2)}, u32[]{:S(2)}) collective-permute-start(bf16[256,192]{1,0:T(8,128)(2,1)S(1)} %copy-done.35), channel_id=1, source_target_pairs={{0,16},{8,24},{16,0},{24,8},{1,17},{9,25},{17,1},{25,9},{2,18},{10... | collective-permute-start | bytes 294920 | tf_op jit(solution)/shard_map/ppermute | solution.py:852
  98.9 6.3 %collective-permute-start.12 = (bf16[256,192]{1,0:T(8,128)(2,1)S(1)}, bf16[256,192]{1,0:T(8,128)(2,1)S(1)}, u32[]{:S(2)}, u32[]{:S(2)}) collective-permute-start(bf16[256,192]{1,0:T(8,128)(2,1)S(1)} %copy-done.34), channel_id=1, source_target_pairs={{0,24},{8,16},{16,8},{24,0},{1,25},{9,17},{17,9},{25,1},{2,26},{10... | collective-permute-start | bytes 294920 | tf_op jit(solution)/shard_map/ppermute | solution.py:852
  102.4 2.8 %copy-start.26 = (bf16[256,192]{1,0:T(8,128)(2,1)}, bf16[256,192]{1,0:T(8,128)(2,1)S(1)}, u32[]{:S(2)}) copy-start(bf16[256,192]{1,0:T(8,128)(2,1)S(1)} %collective-permute-done.10.x1) | copy-start | bytes 294916
  122.3 10.2 %collective-permute-start.18 = (bf16[256,5760]{1,0:T(8,128)(2,1)}, bf16[256,5760]{1,0:T(8,128)(2,1)S(1)}, u32[]{:S(2)}, u32[]{:S(2)}) collective-permute-start(bf16[256,5760]{1,0:T(8,128)(2,1)} %get-tuple-element.118), channel_id=1, source_target_pairs={{0,1},{1,0},{2,3},{3,2},{4,5},{5,4},{6,7},{7,6},{8,9},{9,8},{10,11... | collective-permute-start | bytes 8847368 | tf_op jit(solution)/shard_map/ppermute | solution.py:855
  122.4 6.6 %collective-permute-start.19 = (bf16[256,192]{1,0:T(8,128)(2,1)}, bf16[256,192]{1,0:T(8,128)(2,1)S(1)}, u32[]{:S(2)}, u32[]{:S(2)}) collective-permute-start(bf16[256,192]{1,0:T(8,128)(2,1)} %get-tuple-element.119), channel_id=1, source_target_pairs={{0,8},{8,0},{16,24},{24,16},{1,9},{9,1},{17,25},{25,17},{2,10},{10... | collective-permute-start | bytes 294920 | tf_op jit(solution)/shard_map/ppermute | solution.py:852
  123.9 7.2 %collective-permute-start.20 = (bf16[256,192]{1,0:T(8,128)(2,1)}, bf16[256,192]{1,0:T(8,128)(2,1)S(1)}, u32[]{:S(2)}, u32[]{:S(2)}) collective-permute-start(bf16[256,192]{1,0:T(8,128)(2,1)} %get-tuple-element.120), channel_id=1, source_target_pairs={{0,16},{8,24},{16,0},{24,8},{1,17},{9,25},{17,1},{25,9},{2,18},{10... | collective-permute-start | bytes 294920 | tf_op jit(solution)/shard_map/ppermute | solution.py:852
  124.8 7.7 %collective-permute-start.21 = (bf16[256,192]{1,0:T(8,128)(2,1)}, bf16[256,192]{1,0:T(8,128)(2,1)S(1)}, u32[]{:S(2)}, u32[]{:S(2)}) collective-permute-start(bf16[256,192]{1,0:T(8,128)(2,1)} %get-tuple-element.121), channel_id=1, source_target_pairs={{0,24},{8,16},{16,8},{24,0},{1,25},{9,17},{17,9},{25,1},{2,26},{10... | collective-permute-start | bytes 294920 | tf_op jit(solution)/shard_map/ppermute | solution.py:852
  129.0 3.6 %copy-start.29 = (bf16[256,192]{1,0:T(8,128)(2,1)}, bf16[256,192]{1,0:T(8,128)(2,1)S(1)}, u32[]{:S(2)}) copy-start(bf16[256,192]{1,0:T(8,128)(2,1)S(1)} %collective-permute-done.19.g1) | copy-start | bytes 294916
  131.1 1.5 copy-start.30
  132.6 1.6 copy-start.1
  140.8 36.2 %collective-permute-start.23 = (bf16[2,4,256,384]{3,2,1,0:T(8,128)(2,1)}, bf16[2,4,256,384]{3,2,1,0:T(8,128)(2,1)S(1)}, u32[]{:S(2)}, u32[]{:S(2)}) collective-permute-start(bf16[2,4,256,384]{3,2,1,0:T(8,128)(2,1)} %get-tuple-element.140), channel_id=1, source_target_pairs={{0,16},{8,24},{16,0},{24,8},{1,17},{9,25},{17,1},{25,9},{2,18},{10... | collective-permute-start | bytes 4718600 | tf_op jit(solution)/shard_map/ppermute | solution.py:852
  147.6 34.1 %collective-permute-start.22 = (bf16[2,4,96,768]{3,2,1,0:T(8,128)(2,1)}, bf16[2,4,96,768]{3,2,1,0:T(8,128)(2,1)S(1)}, u32[]{:S(2)}, u32[]{:S(2)}) collective-permute-start(bf16[2,4,96,768]{3,2,1,0:T(8,128)(2,1)} %get-tuple-element.137), channel_id=1, source_target_pairs={{0,8},{8,0},{16,24},{24,16},{1,9},{9,1},{17,25},{25,17},{2,10},{10... | collective-permute-start | bytes 3538952 | tf_op jit(solution)/shard_map/ppermute | solution.py:852
  165.9 21.0 %collective-permute-start.24 = (bf16[4,112,576]{2,1,0:T(8,128)(2,1)}, bf16[4,112,576]{2,1,0:T(8,128)(2,1)}, u32[]{:S(2)}, u32[]{:S(2)}) collective-permute-start(bf16[4,112,576]{2,1,0:T(8,128)(2,1)} %get-tuple-element.144), channel_id=1, source_target_pairs={{0,1},{1,0},{2,3},{3,2},{4,5},{5,4},{6,7},{7,6},{8,9},{9,8},{10,11... | collective-permute-start | bytes 1548296 | tf_op jit(solution)/shard_map/ppermute | solution.py:855
  177.0 1.1 copy-start.5
  181.4 18.4 %collective-permute-start.27 = (bf16[4,256,384]{2,1,0:T(8,128)(2,1)}, bf16[4,256,384]{2,1,0:T(8,128)(2,1)S(1)}, u32[]{:S(2)}, u32[]{:S(2)}) collective-permute-start(bf16[4,256,384]{2,1,0:T(8,128)(2,1)} %get-tuple-element.151), channel_id=1, source_target_pairs={{0,8},{8,0},{16,24},{24,16},{1,9},{9,1},{17,25},{25,17},{2,10},{10... | collective-permute-start | bytes 2359304 | tf_op jit(solution)/shard_map/ppermute | solution.py:852
  185.5 13.9 %collective-permute-start.26 = (bf16[4,96,768]{2,1,0:T(8,128)(2,1)}, bf16[4,96,768]{2,1,0:T(8,128)(2,1)S(1)}, u32[]{:S(2)}, u32[]{:S(2)}) collective-permute-start(bf16[4,96,768]{2,1,0:T(8,128)(2,1)} %get-tuple-element.149), channel_id=1, source_target_pairs={{0,16},{8,24},{16,0},{24,8},{1,17},{9,25},{17,1},{25,9},{2,18},{10... | collective-permute-start | bytes 1769480 | tf_op jit(solution)/shard_map/ppermute | solution.py:852
  189.0 6.8 %collective-permute-start.25 = (bf16[2,112,576]{2,1,0:T(8,128)(2,1)}, bf16[2,112,576]{2,1,0:T(8,128)(2,1)S(1)}, u32[]{:S(2)}, u32[]{:S(2)}) collective-permute-start(bf16[2,112,576]{2,1,0:T(8,128)(2,1)} %get-tuple-element.146), channel_id=1, source_target_pairs={{0,2},{2,0},{4,6},{6,4},{1,3},{3,1},{5,7},{7,5},{8,10},{10,8},{12,... | collective-permute-start | bytes 774152 | tf_op jit(solution)/shard_map/ppermute | solution.py:858
  198.4 5.8 %copy-start.33 = (bf16[112,576]{1,0:T(8,128)(2,1)S(1)}, bf16[112,576]{1,0:T(8,128)(2,1)}, u32[]{:S(2)}) copy-start(bf16[112,576]{1,0:T(8,128)(2,1)} %get-tuple-element.153) | copy-start | bytes 387076
  204.0 53.4 %copy-start.7 = (f32[256,768]{1,0:T(8,128)S(1)}, f32[256,768]{1,0:T(8,128)}, u32[]{:S(2)}) copy-start(f32[256,768]{1,0:T(8,128)} %get-tuple-element.115) | copy-start | bytes 2359300
  204.1 18.2 %collective-permute-start.29 = (bf16[2,448,384]{2,1,0:T(8,128)(2,1)}, bf16[2,448,384]{2,1,0:T(8,128)(2,1)S(1)}, u32[]{:S(2)}, u32[]{:S(2)}) collective-permute-start(bf16[2,448,384]{2,1,0:T(8,128)(2,1)} %get-tuple-element.155), channel_id=1, source_target_pairs={{0,2},{2,0},{4,6},{6,4},{1,3},{3,1},{5,7},{7,5},{8,10},{10,8},{12,... | collective-permute-start | bytes 2064392 | tf_op jit(solution)/shard_map/ppermute | solution.py:858
  204.2 15.8 %collective-permute-start.28 = (bf16[112,576]{1,0:T(8,128)(2,1)S(1)}, bf16[112,576]{1,0:T(8,128)(2,1)S(1)}, u32[]{:S(2)}, u32[]{:S(2)}) collective-permute-start(bf16[112,576]{1,0:T(8,128)(2,1)S(1)} %copy-done.33), channel_id=1, source_target_pairs={{0,4},{2,6},{4,0},{6,2},{1,5},{3,7},{5,1},{7,3},{8,12},{10,14},{12... | collective-permute-start | bytes 387080 | tf_op jit(solution)/shard_map/ppermute | solution.py:858
  220.1 6.6 %copy-start.25 = (bf16[112,576]{1,0:T(8,128)(2,1)}, bf16[112,576]{1,0:T(8,128)(2,1)S(1)}, u32[]{:S(2)}) copy-start(bf16[112,576]{1,0:T(8,128)(2,1)S(1)} %collective-permute-done.28.e1) | copy-start | bytes 387076
  225.3 16.7 %collective-permute-start.30 = (bf16[448,384]{1,0:T(8,128)(2,1)}, bf16[448,384]{1,0:T(8,128)(2,1)S(1)}, u32[]{:S(2)}, u32[]{:S(2)}) collective-permute-start(bf16[448,384]{1,0:T(8,128)(2,1)} %get-tuple-element.157), channel_id=1, source_target_pairs={{0,4},{2,6},{4,0},{6,2},{1,5},{3,7},{5,1},{7,3},{8,12},{10,14},{12... | collective-permute-start | bytes 1032200 | tf_op jit(solution)/shard_map/ppermute | solution.py:858
  228.4 10.3 %collective-permute-start.33 = (bf16[112,576]{1,0:T(8,128)(2,1)}, bf16[112,576]{1,0:T(8,128)(2,1)S(1)}, u32[]{:S(2)}, u32[]{:S(2)}) collective-permute-start(bf16[112,576]{1,0:T(8,128)(2,1)} %sum.1.b0), channel_id=1, source_target_pairs={{0,24},{8,16},{16,8},{24,0},{1,25},{9,17},{17,9},{25,1},{2,26},{10... | collective-permute-start | bytes 387080 | tf_op jit(solution)/shard_map/ppermute | solution.py:852
  229.8 10.3 %collective-permute-start.32 = (bf16[112,576]{1,0:T(8,128)(2,1)}, bf16[112,576]{1,0:T(8,128)(2,1)S(1)}, u32[]{:S(2)}, u32[]{:S(2)}) collective-permute-start(bf16[112,576]{1,0:T(8,128)(2,1)} %sum.1.b0), channel_id=1, source_target_pairs={{0,16},{8,24},{16,0},{24,8},{1,17},{9,25},{17,1},{25,9},{2,18},{10... | collective-permute-start | bytes 387080 | tf_op jit(solution)/shard_map/ppermute | solution.py:852
  231.5 8.6 %collective-permute-start.31 = (bf16[112,576]{1,0:T(8,128)(2,1)}, bf16[112,576]{1,0:T(8,128)(2,1)S(1)}, u32[]{:S(2)}, u32[]{:S(2)}) collective-permute-start(bf16[112,576]{1,0:T(8,128)(2,1)} %sum.1.b0), channel_id=1, source_target_pairs={{0,8},{8,0},{16,24},{24,16},{1,9},{9,1},{17,25},{25,17},{2,10},{10... | collective-permute-start | bytes 387080 | tf_op jit(solution)/shard_map/ppermute | solution.py:852
  238.7 16.3 %copy-start.22 = (bf16[112,576]{1,0:T(8,128)(2,1)}, bf16[112,576]{1,0:T(8,128)(2,1)S(1)}, u32[]{:S(2)}) copy-start(bf16[112,576]{1,0:T(8,128)(2,1)S(1)} %collective-permute-done.33.b3) | copy-start | bytes 387076
  240.1 14.9 %copy-start.23 = (bf16[112,576]{1,0:T(8,128)(2,1)}, bf16[112,576]{1,0:T(8,128)(2,1)S(1)}, u32[]{:S(2)}) copy-start(bf16[112,576]{1,0:T(8,128)(2,1)S(1)} %collective-permute-done.32.b2) | copy-start | bytes 387076
  240.1 14.9 %copy-start.24 = (bf16[112,576]{1,0:T(8,128)(2,1)}, bf16[112,576]{1,0:T(8,128)(2,1)S(1)}, u32[]{:S(2)}) copy-start(bf16[112,576]{1,0:T(8,128)(2,1)S(1)} %collective-permute-done.31.b1) | copy-start | bytes 387076
  244.8 1.5 collective-permute-start.34
  248.8 12.6 %collective-permute-start.37 = (bf16[240,768]{1,0:T(8,128)(2,1)}, bf16[240,768]{1,0:T(8,128)(2,1)S(1)}, u32[]{:S(2)}, u32[]{:S(2)}) collective-permute-start(bf16[240,768]{1,0:T(8,128)(2,1)} %get-tuple-element.177.b0), channel_id=1, source_target_pairs={{0,24},{8,16},{16,8},{24,0},{1,25},{9,17},{17,9},{25,1},{2,26},{10... | collective-permute-start | bytes 1105928 | tf_op jit(solution)/shard_map/ppermute | solution.py:852
  250.4 18.1 %collective-permute-start.36 = (bf16[240,768]{1,0:T(8,128)(2,1)}, bf16[240,768]{1,0:T(8,128)(2,1)S(1)}, u32[]{:S(2)}, u32[]{:S(2)}) collective-permute-start(bf16[240,768]{1,0:T(8,128)(2,1)} %get-tuple-element.177.b0), channel_id=1, source_target_pairs={{0,16},{8,24},{16,0},{24,8},{1,17},{9,25},{17,1},{25,9},{2,18},{10... | collective-permute-start | bytes 1105928 | tf_op jit(solution)/shard_map/ppermute | solution.py:852
  252.2 16.3 %collective-permute-start.35 = (bf16[240,768]{1,0:T(8,128)(2,1)}, bf16[240,768]{1,0:T(8,128)(2,1)S(1)}, u32[]{:S(2)}, u32[]{:S(2)}) collective-permute-start(bf16[240,768]{1,0:T(8,128)(2,1)} %get-tuple-element.177.b0), channel_id=1, source_target_pairs={{0,8},{8,0},{16,24},{24,16},{1,9},{9,1},{17,25},{25,17},{2,10},{10... | collective-permute-start | bytes 1105928 | tf_op jit(solution)/shard_map/ppermute | solution.py:852
  261.4 7.1 %copy-start.17 = (bf16[240,768]{1,0:T(8,128)(2,1)}, bf16[240,768]{1,0:T(8,128)(2,1)S(1)}, u32[]{:S(2)}) copy-start(bf16[240,768]{1,0:T(8,128)(2,1)S(1)} %collective-permute-done.37.b3) | copy-start | bytes 1105924
  (13 other events, 10.0 us)
Sparse Core Ops, SparseCore 0:
  11.5 93.2 all-gather.1
  204.2 36.9 reduce-scatter.1

commit v6 on v5

--- a/solution.py
+++ b/solution.py
@@ -722,17 +722,17 @@
         out[at] = total.astype(jnp.bfloat16)
 
 
-def level_merge_kernel(sc, d_mine, d_got, u_mine, u_got, near, far):
+def level_merge_kernel(sc, d_mine, d_got, u_mine, u_got, *outs):
     level = sc[3]
     up_rows, cols = u_mine.shape[1:]
     rows = d_mine.shape[1]
-    for out, at, k in ((near, 0, 0), (near, 1, 2), (far, 0, 1), (far, 1, 3)):
+    for k, out in enumerate(outs):
         total = u_mine[level ^ k].astype(jnp.float32) + u_got[level ^ k].astype(jnp.float32)
-        out[at, :up_rows] = total.astype(jnp.bfloat16)
+        out[:up_rows] = total.astype(jnp.bfloat16)
         total = d_mine[level ^ k].astype(jnp.float32) + d_got[level ^ k].astype(jnp.float32)
         total = total.astype(jnp.bfloat16)
-        out[at, up_rows : up_rows + rows] = total[:, :cols]
-        out[at, up_rows + rows :] = total[:, cols:]
+        out[up_rows : up_rows + rows] = total[:, :cols]
+        out[up_rows + rows :] = total[:, cols:]
 
 
 def block_sum(refs):
@@ -742,12 +742,12 @@
     return total
 
 
-def split_up_kernel(sc, e0, e1, keep, send, down, held):
+def split_up_kernel(sc, e0, e1, e2, e3, keep, send, down, held):
     core = sc[2]
     shard_rows, width = down.shape
     cols = width // 2
     half_rows = keep.shape[0] - shard_rows
-    held[...] = block_sum((e0, e1)).astype(jnp.bfloat16)
+    held[...] = block_sum((e0, e1, e2, e3)).astype(jnp.bfloat16)
     for ref, side in ((keep, core), (send, 1 - core)):
         ref[:shard_rows] = held[pl.ds(pl.multiple_of(side * shard_rows, 16), shard_rows), :]
         ref[shard_rows:] = held[2 * shard_rows : 2 * shard_rows + half_rows, :]
@@ -1060,22 +1060,21 @@
 
     d_mine, u_mine, _ = lax.optimization_barrier((d_mine, u_mine, q_mine))
     merged_rows = block_rows + 2 * shard_rows
-    near, far = call(
+    blocks = call(
         level_merge_kernel,
         2,
-        [struct((2, merged_rows, quad))] * 2,
+        [struct((merged_rows, quad))] * 4,
         d_mine,
         across(d_pass, 2),
         u_mine,
         across(u_pass, 1),
     )
-    token_parts, _ = lax.optimization_barrier((token_parts, near))
+    token_parts, _ = lax.optimization_barrier((token_parts, blocks[0]))
     token_sum = lax.psum_scatter(
         token_parts.reshape(4 * rows, width), "seq", scatter_dimension=0, tiled=True
     )
     q_others = [across(q_part, j) for j in (1, 2, 3)]
-    near, _ = lax.optimization_barrier((near, q_last))
-    merged = level_sum(near, far, (merged_rows, quad))
+    merged = [blocks[0]] + [level_across(blocks[k], k) for k in (1, 2, 3)]
     merged, q_others = lax.optimization_barrier((merged, q_others))
     half_rows = shard_rows + shard_rows // 2 + 16
     u_keep, u_send, d_part = call(

time: 281 us -> 278 us (0.989)
  waiting for transfers between devices: 108 us -> 101 us
    ppermute x10 -> x11, waiting for transfers between devices: 63.8 us -> 54.5 us  [level_across(): return lax.ppermute(value, 'z', [(i, i ^ step) for i in range(4)])]
    ppermute x22, waiting for transfers between devices: 42.2 us -> 45.4 us  [across(): return lax.ppermute(value, 'seq', [(i, i ^ step) for i in range(4)])]
    pallas_call x14 -> x13, Pallas kernels: 42.8 us -> 40.8 us  [call(): pl.pallas_call(kernel, name=kernel.__name__.replace('_kernel', ''), cost_...]
    ppermute x10 -> x11, starting transfers between devices: 16.4 us -> 17.4 us  [level_across(): return lax.ppermute(value, 'z', [(i, i ^ step) for i in range(4)])]
    unnamed x74 -> x76, local copies, waits for them, and re-layouts: 11 us -> 11.5 us
  transfers between devices with their start and end apart: 40 -> 41, of which waited for: 23 -> 22; matrix products, arithmetic and copies ran while one was open for 4% -> 4% of each run, Pallas kernels for 22% -> 22%
where the time goes in v6:
time: 278 us; the launch traced here: 274 us
  waiting for transfers between devices  101 us (36%)
  Pallas kernels  88.4 us (32%)
  starting transfers between devices  43.9 us (16%)
  local copies, waits for them, and re-layouts  15.9 us (6%)
  between operations  15.1 us (5%)
  other arithmetic  9.43 us (3%)
    ppermute x11, waiting for transfers between devices, level_across(): return lax.ppermute(value, 'z', [(i, i ^ step) for i in range(4)])  54.5 us
    ppermute x22, waiting for transfers between devices, across(): return lax.ppermute(value, 'seq', [(i, i ^ step) for i in range(4)])  45.4 us
    pallas_call x13, Pallas kernels, call(): pl.pallas_call(kernel, name=kernel.__name__.replace('_kernel', ''), cost_...  40.8 us
    ppermute x22, starting transfers between devices, across(): return lax.ppermute(value, 'seq', [(i, i ^ step) for i in range(4)])  25.9 us
    ppermute x11, starting transfers between devices, level_across(): return lax.ppermute(value, 'z', [(i, i ^ step) for i in range(4)])  17.4 us
    pallas_call x1, Pallas kernels, fast_body(): pl.pallas_call(middle_kernel, name='middle', cost_estimate=work(15), out_...  15.7 us
    pallas_call x1, Pallas kernels, fast_body(): pl.pallas_call(attend_forward_kernel, name='attend_forward', cost_estimat...  13 us
    pallas_call x1, Pallas kernels, fast_body(): pl.pallas_call(attend_backward_kernel, name='attend_backward', cost_estim...  12.6 us
  transfers between devices with their start and end apart: 41, of which 22 were waited for; matrix products, arithmetic and copies ran while one was open for 4% of the time, Pallas kernels for 22%

profile of v6, /device:TPU:0, one launch (start us, length us, event | category | flops | bytes accessed | tf_op | source)
XLA Modules:
  0.0 274.2 jit_solution(4644529770553045028)
XLA Ops:
  7.3 1.7 constant_dynamic-slice_fusion
  9.0 1.2 broadcast_in_dim.42.refs_8_
  10.2 2.1 pack.1
  12.3 3.0 %collective-permute-start.2 = (bf16[112,576]{1,0:T(8,128)(2,1)}, bf16[112,576]{1,0:T(8,128)(2,1)S(1)}, u32[]{:S(2)}, u32[]{:S(2)}) collective-permute-start(bf16[112,576]{1,0:T(8,128)(2,1)} %pack.1), channel_id=1, source_target_pairs={{0,2},{2,0},{4,6},{6,4},{1,3},{3,1},{5,7},{7,5},{8,10},{10,8},{12,... | collective-permute-start | bytes 387080 | tf_op jit(solution)/shard_map/ppermute | solution.py:858
  15.5 4.7 %collective-permute-done.2 = bf16[112,576]{1,0:T(8,128)(2,1)S(1)} collective-permute-done((bf16[112,576]{1,0:T(8,128)(2,1)}, bf16[112,576]{1,0:T(8,128)(2,1)S(1)}, u32[]{:S(2)}, u32[]{:S(2)}) %collective-permute-start.2) | collective-permute-done | bytes 129056 | tf_op jit(solution)/shard_map/ppermute | solution.py:858
  21.1 3.1 %collective-permute-start.3 = (bf16[2,112,576]{2,1,0:T(8,128)(2,1)S(1)}, bf16[2,112,576]{2,1,0:T(8,128)(2,1)S(1)}, u32[]{:S(2)}, u32[]{:S(2)}) collective-permute-start(bf16[2,112,576]{2,1,0:T(8,128)(2,1)S(1)} %pad_maximum_fusion.6), channel_id=1, source_target_pairs={{0,4},{2,6},{4,0},{6,2},{1,5},{3,7},{5,1},{7,3},{8,12},{10,14},{12... | collective-permute-start | bytes 774152 | tf_op jit(solution)/shard_map/ppermute | solution.py:858
  24.3 1.7 collective-permute-start.1
  26.0 2.4 collective-permute-start.6
  29.5 17.2 %collective-permute-done.3 = bf16[2,112,576]{2,1,0:T(8,128)(2,1)S(1)} collective-permute-done((bf16[2,112,576]{2,1,0:T(8,128)(2,1)S(1)}, bf16[2,112,576]{2,1,0:T(8,128)(2,1)S(1)}, u32[]{:S(2)}, u32[]{:S(2)}) %collective-permute-start.3) | collective-permute-done | bytes 258080 | tf_op jit(solution)/shard_map/ppermute | solution.py:858
  47.7 3.6 %collective-permute-done.1 = bf16[2,96,768]{2,1,0:T(8,128)(2,1)S(1)} collective-permute-done((bf16[2,96,768]{2,1,0:T(8,128)(2,1)S(1)}, bf16[2,96,768]{2,1,0:T(8,128)(2,1)S(1)}, u32[]{:S(2)}, u32[]{:S(2)}) %collective-permute-start.1) | collective-permute-done | bytes 294944 | tf_op jit(solution)/shard_map/ppermute | solution.py:858
  52.0 2.4 collective-permute-start.15
  55.5 1.1 collective-permute-done.7
  56.6 2.8 %collective-permute-start.8 = (bf16[2,96,768]{2,1,0:T(8,128)(2,1)S(1)}, bf16[2,96,768]{2,1,0:T(8,128)(2,1)}, u32[]{:S(2)}, u32[]{:S(2)}) collective-permute-start(bf16[2,96,768]{2,1,0:T(8,128)(2,1)S(1)} %pad_maximum_fusion.5), channel_id=1, source_target_pairs={{0,4},{2,6},{4,0},{6,2},{1,5},{3,7},{5,1},{7,3},{8,12},{10,14},{12... | collective-permute-start | bytes 884744 | tf_op jit(solution)/shard_map/ppermute | solution.py:858
  60.8 18.0 %collective-permute-done.8 = bf16[2,96,768]{2,1,0:T(8,128)(2,1)} collective-permute-done((bf16[2,96,768]{2,1,0:T(8,128)(2,1)S(1)}, bf16[2,96,768]{2,1,0:T(8,128)(2,1)}, u32[]{:S(2)}, u32[]{:S(2)}) %collective-permute-start.8) | collective-permute-done | bytes 294944 | tf_op jit(solution)/shard_map/ppermute | solution.py:858
  78.8 1.8 pad_maximum_fusion.2.own_out
  80.7 13.0 %attend_forward.1 = (bf16[1024,576]{1,0:T(8,128)(2,1)}, f32[192,1024]{1,0:T(8,128)}, bf16[256,192]{1,0:T(8,128)(2,1)}, bf16[256,192]{1,0:T(8,128)(2,1)}, bf16[25...) custom-call(s32[4]{0:T(128)} %pad_add_fusion.sc, ...), custom_call_target="tpu_custom_call" | custom-call | flops 1170000000 | bytes 3900000 | tf_op jit(solution)/shard_map/attend_forward/pallas_call | solution.py:895
  93.7 1.8 pad_maximum_fusion.own_down
  96.9 2.0 collective-permute-start.11
  99.6 2.8 %collective-permute-done.10.x1 = bf16[256,192]{1,0:T(8,128)(2,1)S(1)} collective-permute-done((bf16[256,192]{1,0:T(8,128)(2,1)S(1)}, bf16[256,192]{1,0:T(8,128)(2,1)S(1)}, u32[]{:S(2)}, u32[]{:S(2)}) %collective-permute-start.10) | collective-permute-done | bytes 98336 | tf_op jit(solution)/shard_map/ppermute | solution.py:852
  102.4 2.0 collective-permute-done.11.x2
  106.6 15.7 %middle.1 = (bf16[256,768]{1,0:T(8,128)(2,1)}, f32[256,768]{1,0:T(8,128)}, bf16[256,192]{1,0:T(8,128)(2,1)}, bf16[256,192]{1,0:T(8,128)(2,1)}, bf16[256,192]{1,0...) custom-call(s32[4]{0:T(128)} %pad_add_fusion.sc, ...), custom_call_target="tpu_custom_call" | custom-call | flops 1350000000 | bytes 4500000 | tf_op jit(solution)/shard_map/middle/pallas_call | solution.py:923
  122.4 1.5 collective-permute-start.19
  124.8 1.1 collective-permute-start.21
  126.0 3.0 %collective-permute-done.19.g1 = bf16[256,192]{1,0:T(8,128)(2,1)S(1)} collective-permute-done((bf16[256,192]{1,0:T(8,128)(2,1)}, bf16[256,192]{1,0:T(8,128)(2,1)S(1)}, u32[]{:S(2)}, u32[]{:S(2)}) %collective-permute-start.19) | collective-permute-done | bytes 98336 | tf_op jit(solution)/shard_map/ppermute | solution.py:852
  129.0 2.1 collective-permute-done.20.g2
  131.1 1.5 collective-permute-done.21.g3
  133.2 1.0 copy-done.1
  134.2 6.6 %up_grad.1 = (bf16[2,4,256,384]{3,2,1,0:T(8,128)(2,1)}, bf16[2,4,256,384]{3,2,1,0:T(8,128)(2,1)}) custom-call(s32[4]{0:T(128)} %pad_add_fusion.sc, bf16[256,5760]{1,0:T(8,128)(2,1)} %get-tuple-element.118.keep, bf16[256,5760]{1,0:T(8,128)(2,1)} %copy-done.1, bf16[4,16,384]{2,1,0:T(8,128)(2,1)} %get-tuple-element.125.vectors), custom_call_target="tpu_custom_call" | custom-call | flops 360000000 | bytes 1200000 | tf_op jit(solution)/shard_map/up_grad/pallas_call | solution.py:973
  141.7 5.9 %down_grad.1 = (bf16[2,4,96,768]{3,2,1,0:T(8,128)(2,1)}, bf16[2,4,96,768]{3,2,1,0:T(8,128)(2,1)}) custom-call(s32[4]{0:T(128)} %pad_add_fusion.sc, bf16[256,5760]{1,0:T(8,128)(2,1)} %get-tuple-element.118.keep, bf16[256,5760]{1,0:T(8,128)(2,1)} %copy-done.1), custom_call_target="tpu_custom_call" | custom-call | flops 360000000 | bytes 1200000 | tf_op jit(solution)/shard_map/down_grad/pallas_call | solution.py:973
  147.7 1.4 collective-permute-start.22
  149.1 12.6 %attend_backward.1.dqkv = bf16[1024,576]{1,0:T(8,128)(2,1)} custom-call(s32[4]{0:T(128)} %pad_add_fusion.sc, bf16[1024,576]{1,0:T(8,128)(2,1)} %get-tuple-element.129.qkv, f32[192,1024]{1,0:T(8,128)} %get-tuple-element.130.ctx_t, f32[3,1024]{1,0:T(4,128)} %get-tuple-element.131.lse, bf16[256,192]{1,0:T(8,128)(2,1)} %get-tuple-element.132.g0, ...), custom_call_target="tpu_custom_call" | custom-call | flops 990000000 | bytes 3300000 | tf_op jit(solution)/shard_map/attend_backward/pallas_call | solution.py:1005
  161.7 4.2 %grad_qkv_weight.1 = (bf16[4,112,576]{2,1,0:T(8,128)(2,1)}, bf16[4,112,576]{2,1,0:T(8,128)(2,1)}) custom-call(s32[4]{0:T(128)} %pad_add_fusion.sc, bf16[256,768]{1,0:T(8,128)(2,1)} %bitcast.48, bf16[256,768]{1,0:T(8,128)(2,1)} %copy-done.15, bf16[256,768]{1,0:T(8,128)(2,1)} %copy-done.14, bf16[256,768]{1,0:T(8,128)(2,1)} %copy-done.13, ...), custom_call_target="tpu_custom_call" | custom-call | flops 360000000 | bytes 1200000 | tf_op jit(solution)/shard_map/grad_qkv_weight/pallas_call | solution.py:1019
  165.9 11.1 %collective-permute-done.23.got = bf16[2,4,256,384]{3,2,1,0:T(8,128)(2,1)S(1)} collective-permute-done((bf16[2,4,256,384]{3,2,1,0:T(8,128)(2,1)}, bf16[2,4,256,384]{3,2,1,0:T(8,128)(2,1)S(1)}, u32[]{:S(2)}, u32[]{:S(2)}) %collective-permute-start.23) | collective-permute-done | bytes 1572896 | tf_op jit(solution)/shard_map/ppermute | solution.py:852
  177.0 1.1 copy-done.5
  178.1 3.2 %fold.4 = (bf16[4,256,384]{2,1,0:T(8,128)(2,1)}, bf16[4,256,384]{2,1,0:T(8,128)(2,1)}) custom-call(bf16[2,4,256,384]{3,2,1,0:T(8,128)(2,1)} %get-tuple-element.140.near, bf16[2,4,256,384]{3,2,1,0:T(8,128)(2,1)} %copy-done.5), custom_call_target="tpu_custom_call" | custom-call | flops 90000000 | bytes 300000 | tf_op jit(solution)/shard_map/fold/pallas_call | solution.py:973
  181.7 1.0 copy-done.6
  182.8 2.8 %fold.3 = (bf16[4,96,768]{2,1,0:T(8,128)(2,1)}, bf16[4,96,768]{2,1,0:T(8,128)(2,1)}) custom-call(bf16[2,4,96,768]{3,2,1,0:T(8,128)(2,1)} %get-tuple-element.137.near, bf16[2,4,96,768]{3,2,1,0:T(8,128)(2,1)} %copy-done.6), custom_call_target="tpu_custom_call" | custom-call | flops 90000000 | bytes 300000 | tf_op jit(solution)/shard_map/fold/pallas_call | solution.py:973
  185.5 1.4 collective-permute-start.26
  186.9 2.1 level_fold.1
  189.0 4.2 %grad_tokens.1 = bf16[4,256,768]{2,1,0:T(8,128)(2,1)} custom-call(s32[4]{0:T(128)} %pad_add_fusion.sc, bf16[1024,576]{1,0:T(8,128)(2,1)} %attend_backward.1.dqkv, bf16[4,2,96,576]{3,2,1,0:T(8,128)(2,1)} %get-tuple-element.167.weight), custom_call_target="tpu_custom_call" | custom-call | flops 360000000 | bytes 1200000 | tf_op jit(solution)/shard_map/grad_tokens/pallas_call | solution.py:973
  193.2 2.7 collective-permute-done.25.got
  196.6 1.8 fold.5
  201.1 2.9 %level_merge.1 = (bf16[448,384]{1,0:T(8,128)(2,1)}, bf16[448,384]{1,0:T(8,128)(2,1)}, bf16[448,384]{1,0:T(8,128)(2,1)}, bf16[448,384]{1,0:T(8,128)(2,1)}) custom-call(s32[4]{0:T(128)} %pad_add_fusion.sc, bf16[4,96,768]{2,1,0:T(8,128)(2,1)} %get-tuple-element.149.d_mine, bf16[4,96,768]{2,1,0:T(8,128)(2,1)} %copy-done.11, ...), custom_call_target="tpu_custom_call" | custom-call | flops 180000000 | bytes 600000 | tf_op jit(solution)/shard_map/level_merge/pallas_call | solution.py:973
  204.7 3.0 %collective-permute-start.28 = (bf16[448,384]{1,0:T(8,128)(2,1)}, bf16[448,384]{1,0:T(8,128)(2,1)S(1)}, u32[]{:S(2)}, u32[]{:S(2)}) collective-permute-start(bf16[448,384]{1,0:T(8,128)(2,1)} %get-tuple-element.154), channel_id=1, source_target_pairs={{0,2},{2,0},{4,6},{6,4},{1,3},{3,1},{5,7},{7,5},{8,10},{10,8},{12,... | collective-permute-start | bytes 1032200 | tf_op jit(solution)/shard_map/ppermute | solution.py:858
  207.8 2.3 collective-permute-start.30
  210.1 3.2 %collective-permute-done.31.e1 = bf16[112,576]{1,0:T(8,128)(2,1)S(1)} collective-permute-done((bf16[112,576]{1,0:T(8,128)(2,1)S(1)}, bf16[112,576]{1,0:T(8,128)(2,1)S(1)}, u32[]{:S(2)}, u32[]{:S(2)}) %collective-permute-start.31) | collective-permute-done | bytes 129056 | tf_op jit(solution)/shard_map/ppermute | solution.py:858
  214.0 1.7 sum.1.b0
  215.6 1.6 collective-permute-start.34
  217.2 1.7 collective-permute-start.33
  218.9 7.1 %collective-permute-done.34.b3 = bf16[112,576]{1,0:T(8,128)(2,1)S(1)} collective-permute-done((bf16[112,576]{1,0:T(8,128)(2,1)}, bf16[112,576]{1,0:T(8,128)(2,1)S(1)}, u32[]{:S(2)}, u32[]{:S(2)}) %collective-permute-start.34) | collective-permute-done | bytes 129056 | tf_op jit(solution)/shard_map/ppermute | solution.py:852
  227.0 4.4 %collective-permute-done.32.b1 = bf16[112,576]{1,0:T(8,128)(2,1)S(1)} collective-permute-done((bf16[112,576]{1,0:T(8,128)(2,1)}, bf16[112,576]{1,0:T(8,128)(2,1)S(1)}, u32[]{:S(2)}, u32[]{:S(2)}) %collective-permute-start.32) | collective-permute-done | bytes 129056 | tf_op jit(solution)/shard_map/ppermute | solution.py:852
  231.4 3.9 %collective-permute-done.29.e2 = bf16[448,384]{1,0:T(8,128)(2,1)S(1)} collective-permute-done((bf16[448,384]{1,0:T(8,128)(2,1)}, bf16[448,384]{1,0:T(8,128)(2,1)S(1)}, u32[]{:S(2)}, u32[]{:S(2)}) %collective-permute-start.29) | collective-permute-done | bytes 344096 | tf_op jit(solution)/shard_map/ppermute | solution.py:858
  236.7 2.4 split_up.1
  239.1 1.5 collective-permute-done.35.got
  241.3 1.9 join.1
  243.2 1.5 collective-permute-start.38
  244.6 1.8 collective-permute-start.37
  246.7 1.4 slice_bitcast_fusion
  248.1 1.3 reduce
  249.4 2.3 finish_qkv.1
  251.7 1.8 fusion
  253.5 2.2 collective-permute-done.38.b3
  255.8 7.1 %collective-permute-done.37.b2 = bf16[240,768]{1,0:T(8,128)(2,1)S(1)} collective-permute-done((bf16[240,768]{1,0:T(8,128)(2,1)}, bf16[240,768]{1,0:T(8,128)(2,1)S(1)}, u32[]{:S(2)}, u32[]{:S(2)}) %collective-permute-start.37) | collective-permute-done | bytes 368672 | tf_op jit(solution)/shard_map/ppermute | solution.py:852
  264.3 3.0 %finish.1 = (f32[384,768]{1,0:T(8,128)}, f32[96,3072]{1,0:T(8,128)}, f32[96,768]{1,0:T(8,128)}) custom-call(s32[4]{0:T(128)} %pad_add_fusion.sc, bf16[240,768]{1,0:T(8,128)(2,1)} %get-tuple-element.179.b0, bf16[240,768]{1,0:T(8,128)(2,1)} %copy-done.18, bf16[240,768]{1,0:T(8,128)(2,1)} %copy-done.17, bf16[240,768]{1,0:T(8,128)(2,1)} %copy-done.16), custom_call_target="tpu_custom_call" | custom-call | flops 180000000 | bytes 600000 | tf_op jit(solution)/shard_map/finish/pallas_call | solution.py:973
  (129 shorter events, 22.5 us)
Async XLA Ops:
  7.2 8.2 %copy-start = (bf16[384,768]{1,0:T(8,128)(2,1)S(1)}, bf16[384,768]{1,0:T(8,128)(2,1)}, u32[]{:S(2)}) copy-start(bf16[384,768]{1,0:T(8,128)(2,1)} %param.27) | copy-start | bytes 1769476
  7.2 18.8 %copy-start.4 = (bf16[1,256,768]{2,1,0:T(8,128)(2,1)S(1)}, bf16[1,256,768]{2,1,0:T(8,128)(2,1)}, u32[]{:S(2)}) copy-start(bf16[1,256,768]{2,1,0:T(8,128)(2,1)} %param.16) | copy-start | bytes 1179652
  7.2 98.6 %all-gather.2.cloned.1.call-start = ((), (), s32[]{:S(2)}) async-start(), calls=%async_computation.1 | async-start | bytes 4866048 | tf_op jit(solution)/shard_map/all_gather | solution.py:867
  8.9 234.2 %reduce-scatter.2.cloned.1.call-start = ((), (), s32[]{:S(2)}) async-start(), calls=%async_computation.2 | async-start | bytes 1966080 | tf_op jit(solution)/shard_map/reduce_scatter | solution.py:1073
  10.2 41.1 %copy-start.10 = (bf16[96,768]{1,0:T(8,128)(2,1)S(1)}, bf16[96,768]{1,0:T(8,128)(2,1)}, u32[]{:S(2)}) copy-start(bf16[96,768]{1,0:T(8,128)(2,1)} %param.21) | copy-start | bytes 442372
  12.3 7.8 %collective-permute-start.2 = (bf16[112,576]{1,0:T(8,128)(2,1)}, bf16[112,576]{1,0:T(8,128)(2,1)S(1)}, u32[]{:S(2)}, u32[]{:S(2)}) collective-permute-start(bf16[112,576]{1,0:T(8,128)(2,1)} %pack.1), channel_id=1, source_target_pairs={{0,2},{2,0},{4,6},{6,4},{1,3},{3,1},{5,7},{7,5},{8,10},{10,8},{12,... | collective-permute-start | bytes 387080 | tf_op jit(solution)/shard_map/ppermute | solution.py:858
  15.4 8.9 %collective-permute-start = (bf16[96,768]{1,0:T(8,128)(2,1)S(1)}, bf16[96,768]{1,0:T(8,128)(2,1)S(1)}, u32[]{:S(2)}, u32[]{:S(2)}) collective-permute-start(bf16[96,768]{1,0:T(8,128)(2,1)S(1)} %constant_dynamic-slice_fusion.1), channel_id=1, source_target_pairs={{0,2},{2,0},{4,6},{6,4},{1,3},{3,1},{5,7},{7,5},{8,10},{10,8},{12,... | collective-permute-start | bytes 442376 | tf_op jit(solution)/shard_map/ppermute | solution.py:858
  21.1 25.6 %collective-permute-start.3 = (bf16[2,112,576]{2,1,0:T(8,128)(2,1)S(1)}, bf16[2,112,576]{2,1,0:T(8,128)(2,1)S(1)}, u32[]{:S(2)}, u32[]{:S(2)}) collective-permute-start(bf16[2,112,576]{2,1,0:T(8,128)(2,1)S(1)} %pad_maximum_fusion.6), channel_id=1, source_target_pairs={{0,4},{2,6},{4,0},{6,2},{1,5},{3,7},{5,1},{7,3},{8,12},{10,14},{12... | collective-permute-start | bytes 774152 | tf_op jit(solution)/shard_map/ppermute | solution.py:858
  24.3 27.0 %collective-permute-start.1 = (bf16[2,96,768]{2,1,0:T(8,128)(2,1)S(1)}, bf16[2,96,768]{2,1,0:T(8,128)(2,1)S(1)}, u32[]{:S(2)}, u32[]{:S(2)}) collective-permute-start(bf16[2,96,768]{2,1,0:T(8,128)(2,1)S(1)} %pad_maximum_fusion.4), channel_id=1, source_target_pairs={{0,4},{2,6},{4,0},{6,2},{1,5},{3,7},{5,1},{7,3},{8,12},{10,14},{12... | collective-permute-start | bytes 884744 | tf_op jit(solution)/shard_map/ppermute | solution.py:858
  26.0 25.4 %collective-permute-start.6 = (bf16[256,768]{1,0:T(8,128)(2,1)S(1)}, bf16[256,768]{1,0:T(8,128)(2,1)S(1)}, u32[]{:S(2)}, u32[]{:S(2)}) collective-permute-start(bf16[256,768]{1,0:T(8,128)(2,1)S(1)} %bitcast.49), channel_id=1, source_target_pairs={{0,24},{8,16},{16,8},{24,0},{1,25},{9,17},{17,9},{25,1},{2,26},{10... | collective-permute-start | bytes 1179656 | tf_op jit(solution)/shard_map/ppermute | solution.py:852
  28.4 22.9 %collective-permute-start.5 = (bf16[256,768]{1,0:T(8,128)(2,1)S(1)}, bf16[256,768]{1,0:T(8,128)(2,1)S(1)}, u32[]{:S(2)}, u32[]{:S(2)}) collective-permute-start(bf16[256,768]{1,0:T(8,128)(2,1)S(1)} %bitcast.50), channel_id=1, source_target_pairs={{0,16},{8,24},{16,0},{24,8},{1,17},{9,25},{17,1},{25,9},{2,18},{10... | collective-permute-start | bytes 1179656 | tf_op jit(solution)/shard_map/ppermute | solution.py:852
  28.9 22.5 %collective-permute-start.4 = (bf16[256,768]{1,0:T(8,128)(2,1)S(1)}, bf16[256,768]{1,0:T(8,128)(2,1)S(1)}, u32[]{:S(2)}, u32[]{:S(2)}) collective-permute-start(bf16[256,768]{1,0:T(8,128)(2,1)S(1)} %bitcast.51), channel_id=1, source_target_pairs={{0,8},{8,0},{16,24},{24,16},{1,9},{9,1},{17,25},{25,17},{2,10},{10... | collective-permute-start | bytes 1179656 | tf_op jit(solution)/shard_map/ppermute | solution.py:852
  47.7 33.0 %copy-start.12 = (bf16[4,112,576]{2,1,0:T(8,128)(2,1)}, bf16[4,112,576]{2,1,0:T(8,128)(2,1)S(1)}, u32[]{:S(2)}) copy-start(bf16[4,112,576]{2,1,0:T(8,128)(2,1)S(1)} %pad_maximum_fusion.3.own) | copy-start | bytes 1548292
  51.3 29.3 %copy-start.13 = (bf16[256,768]{1,0:T(8,128)(2,1)}, bf16[256,768]{1,0:T(8,128)(2,1)S(1)}, u32[]{:S(2)}) copy-start(bf16[256,768]{1,0:T(8,128)(2,1)S(1)} %collective-permute-done.6.t3) | copy-start | bytes 1179652
  51.4 29.3 %copy-start.14 = (bf16[256,768]{1,0:T(8,128)(2,1)}, bf16[256,768]{1,0:T(8,128)(2,1)S(1)}, u32[]{:S(2)}) copy-start(bf16[256,768]{1,0:T(8,128)(2,1)S(1)} %collective-permute-done.5.t2) | copy-start | bytes 1179652
  51.4 5.2 %copy-start.15 = (bf16[256,768]{1,0:T(8,128)(2,1)}, bf16[256,768]{1,0:T(8,128)(2,1)S(1)}, u32[]{:S(2)}) copy-start(bf16[256,768]{1,0:T(8,128)(2,1)S(1)} %collective-permute-done.4.t1) | copy-start | bytes 1179652
  51.4 5.2 %collective-permute-start.7 = (bf16[96,768]{1,0:T(8,128)(2,1)S(1)}, bf16[96,768]{1,0:T(8,128)(2,1)S(1)}, u32[]{:S(2)}, u32[]{:S(2)}) collective-permute-start(bf16[96,768]{1,0:T(8,128)(2,1)S(1)} %copy-done.10), channel_id=1, source_target_pairs={{0,2},{2,0},{4,6},{6,4},{1,3},{3,1},{5,7},{7,5},{8,10},{10,8},{12,... | collective-permute-start | bytes 442376 | tf_op jit(solution)/shard_map/ppermute | solution.py:858
  52.0 28.7 %collective-permute-start.9 = (bf16[4,112,576]{2,1,0:T(8,128)(2,1)S(1)}, bf16[4,112,576]{2,1,0:T(8,128)(2,1)}, u32[]{:S(2)}, u32[]{:S(2)}) collective-permute-start(bf16[4,112,576]{2,1,0:T(8,128)(2,1)S(1)} %pad_maximum_fusion.3.own), channel_id=1, source_target_pairs={{0,1},{1,0},{2,3},{3,2},{4,5},{5,4},{6,7},{7,6},{8,9},{9,8},{10,11... | collective-permute-start | bytes 1548296 | tf_op jit(solution)/shard_map/ppermute | solution.py:855
  52.0 41.7 %collective-permute-start.15 = (bf16[4,96,768]{2,1,0:T(8,128)(2,1)S(1)}, bf16[4,96,768]{2,1,0:T(8,128)(2,1)}, u32[]{:S(2)}, u32[]{:S(2)}) collective-permute-start(bf16[4,96,768]{2,1,0:T(8,128)(2,1)S(1)} %pad_maximum_fusion.1), channel_id=1, source_target_pairs={{0,24},{8,16},{16,8},{24,0},{1,25},{9,17},{17,9},{25,1},{2,26},{10... | collective-permute-start | bytes 1769480 | tf_op jit(solution)/shard_map/ppermute | solution.py:852
  54.4 39.3 %collective-permute-start.14 = (bf16[4,96,768]{2,1,0:T(8,128)(2,1)S(1)}, bf16[4,96,768]{2,1,0:T(8,128)(2,1)}, u32[]{:S(2)}, u32[]{:S(2)}) collective-permute-start(bf16[4,96,768]{2,1,0:T(8,128)(2,1)S(1)} %pad_maximum_fusion.1), channel_id=1, source_target_pairs={{0,16},{8,24},{16,0},{24,8},{1,17},{9,25},{17,1},{25,9},{2,18},{10... | collective-permute-start | bytes 1769480 | tf_op jit(solution)/shard_map/ppermute | solution.py:852
  54.9 38.7 %collective-permute-start.13 = (bf16[4,96,768]{2,1,0:T(8,128)(2,1)S(1)}, bf16[4,96,768]{2,1,0:T(8,128)(2,1)}, u32[]{:S(2)}, u32[]{:S(2)}) collective-permute-start(bf16[4,96,768]{2,1,0:T(8,128)(2,1)S(1)} %pad_maximum_fusion.1), channel_id=1, source_target_pairs={{0,8},{8,0},{16,24},{24,16},{1,9},{9,1},{17,25},{25,17},{2,10},{10... | collective-permute-start | bytes 1769480 | tf_op jit(solution)/shard_map/ppermute | solution.py:852
  56.6 22.2 %collective-permute-start.8 = (bf16[2,96,768]{2,1,0:T(8,128)(2,1)S(1)}, bf16[2,96,768]{2,1,0:T(8,128)(2,1)}, u32[]{:S(2)}, u32[]{:S(2)}) collective-permute-start(bf16[2,96,768]{2,1,0:T(8,128)(2,1)S(1)} %pad_maximum_fusion.5), channel_id=1, source_target_pairs={{0,4},{2,6},{4,0},{6,2},{1,5},{3,7},{5,1},{7,3},{8,12},{10,14},{12... | collective-permute-start | bytes 884744 | tf_op jit(solution)/shard_map/ppermute | solution.py:858
  93.7 1.9 copy-start.3
  93.7 2.4 copy-start.37
  93.7 3.2 %copy-start.36 = (bf16[256,192]{1,0:T(8,128)(2,1)S(1)}, bf16[256,192]{1,0:T(8,128)(2,1)}, u32[]{:S(2)}) copy-start(bf16[256,192]{1,0:T(8,128)(2,1)} %get-tuple-element.108) | copy-start | bytes 294916
  93.7 5.2 %copy-start.35 = (bf16[256,192]{1,0:T(8,128)(2,1)S(1)}, bf16[256,192]{1,0:T(8,128)(2,1)}, u32[]{:S(2)}) copy-start(bf16[256,192]{1,0:T(8,128)(2,1)} %get-tuple-element.109) | copy-start | bytes 294916
  95.5 10.3 %copy-start.2 = (bf16[4,4,96,768]{3,2,1,0:T(8,128)(2,1)}, bf16[4,4,96,768]{3,2,1,0:T(8,128)(2,1)S(1)}, u32[]{:S(2)}) copy-start(bf16[4,4,96,768]{3,2,1,0:T(8,128)(2,1)S(1)} %pad_maximum_fusion.own_down) | copy-start | bytes 7077892
  95.5 10.3 %collective-permute-start.16 = (bf16[4,4,96,768]{3,2,1,0:T(8,128)(2,1)S(1)}, bf16[4,4,96,768]{3,2,1,0:T(8,128)(2,1)}, u32[]{:S(2)}, u32[]{:S(2)}) collective-permute-start(bf16[4,4,96,768]{3,2,1,0:T(8,128)(2,1)S(1)} %pad_maximum_fusion.own_down), channel_id=1, source_target_pairs={{0,1},{1,0},{2,3},{3,2},{4,5},{5,4},{6,7},{7,6},{8,9},{9,8},{10,11... | collective-permute-start | bytes 7077896 | tf_op jit(solution)/shard_map/ppermute | solution.py:855
  95.6 9.6 %collective-permute-start.17 = (bf16[4,96,768]{2,1,0:T(8,128)(2,1)S(1)}, bf16[4,96,768]{2,1,0:T(8,128)(2,1)S(1)}, u32[]{:S(2)}, u32[]{:S(2)}) collective-permute-start(bf16[4,96,768]{2,1,0:T(8,128)(2,1)S(1)} %copy-done.3), channel_id=1, source_target_pairs={{0,1},{1,0},{2,3},{3,2},{4,5},{5,4},{6,7},{7,6},{8,9},{9,8},{10,11... | collective-permute-start | bytes 1769480 | tf_op jit(solution)/shard_map/ppermute | solution.py:855
  96.1 6.3 %collective-permute-start.10 = (bf16[256,192]{1,0:T(8,128)(2,1)S(1)}, bf16[256,192]{1,0:T(8,128)(2,1)S(1)}, u32[]{:S(2)}, u32[]{:S(2)}) collective-permute-start(bf16[256,192]{1,0:T(8,128)(2,1)S(1)} %copy-done.37), channel_id=1, source_target_pairs={{0,8},{8,0},{16,24},{24,16},{1,9},{9,1},{17,25},{25,17},{2,10},{10... | collective-permute-start | bytes 294920 | tf_op jit(solution)/shard_map/ppermute | solution.py:852
  96.9 7.5 %collective-permute-start.11 = (bf16[256,192]{1,0:T(8,128)(2,1)S(1)}, bf16[256,192]{1,0:T(8,128)(2,1)S(1)}, u32[]{:S(2)}, u32[]{:S(2)}) collective-permute-start(bf16[256,192]{1,0:T(8,128)(2,1)S(1)} %copy-done.36), channel_id=1, source_target_pairs={{0,16},{8,24},{16,0},{24,8},{1,17},{9,25},{17,1},{25,9},{2,18},{10... | collective-permute-start | bytes 294920 | tf_op jit(solution)/shard_map/ppermute | solution.py:852
  98.9 6.3 %collective-permute-start.12 = (bf16[256,192]{1,0:T(8,128)(2,1)S(1)}, bf16[256,192]{1,0:T(8,128)(2,1)S(1)}, u32[]{:S(2)}, u32[]{:S(2)}) collective-permute-start(bf16[256,192]{1,0:T(8,128)(2,1)S(1)} %copy-done.35), channel_id=1, source_target_pairs={{0,24},{8,16},{16,8},{24,0},{1,25},{9,17},{17,9},{25,1},{2,26},{10... | collective-permute-start | bytes 294920 | tf_op jit(solution)/shard_map/ppermute | solution.py:852
  102.4 2.8 %copy-start.27 = (bf16[256,192]{1,0:T(8,128)(2,1)}, bf16[256,192]{1,0:T(8,128)(2,1)S(1)}, u32[]{:S(2)}) copy-start(bf16[256,192]{1,0:T(8,128)(2,1)S(1)} %collective-permute-done.10.x1) | copy-start | bytes 294916
  122.3 10.2 %collective-permute-start.18 = (bf16[256,5760]{1,0:T(8,128)(2,1)}, bf16[256,5760]{1,0:T(8,128)(2,1)S(1)}, u32[]{:S(2)}, u32[]{:S(2)}) collective-permute-start(bf16[256,5760]{1,0:T(8,128)(2,1)} %get-tuple-element.119), channel_id=1, source_target_pairs={{0,1},{1,0},{2,3},{3,2},{4,5},{5,4},{6,7},{7,6},{8,9},{9,8},{10,11... | collective-permute-start | bytes 8847368 | tf_op jit(solution)/shard_map/ppermute | solution.py:855
  122.4 6.6 %collective-permute-start.19 = (bf16[256,192]{1,0:T(8,128)(2,1)}, bf16[256,192]{1,0:T(8,128)(2,1)S(1)}, u32[]{:S(2)}, u32[]{:S(2)}) collective-permute-start(bf16[256,192]{1,0:T(8,128)(2,1)} %get-tuple-element.120), channel_id=1, source_target_pairs={{0,8},{8,0},{16,24},{24,16},{1,9},{9,1},{17,25},{25,17},{2,10},{10... | collective-permute-start | bytes 294920 | tf_op jit(solution)/shard_map/ppermute | solution.py:852
  123.9 7.2 %collective-permute-start.20 = (bf16[256,192]{1,0:T(8,128)(2,1)}, bf16[256,192]{1,0:T(8,128)(2,1)S(1)}, u32[]{:S(2)}, u32[]{:S(2)}) collective-permute-start(bf16[256,192]{1,0:T(8,128)(2,1)} %get-tuple-element.121), channel_id=1, source_target_pairs={{0,16},{8,24},{16,0},{24,8},{1,17},{9,25},{17,1},{25,9},{2,18},{10... | collective-permute-start | bytes 294920 | tf_op jit(solution)/shard_map/ppermute | solution.py:852
  124.8 7.7 %collective-permute-start.21 = (bf16[256,192]{1,0:T(8,128)(2,1)}, bf16[256,192]{1,0:T(8,128)(2,1)S(1)}, u32[]{:S(2)}, u32[]{:S(2)}) collective-permute-start(bf16[256,192]{1,0:T(8,128)(2,1)} %get-tuple-element.122), channel_id=1, source_target_pairs={{0,24},{8,16},{16,8},{24,0},{1,25},{9,17},{17,9},{25,1},{2,26},{10... | collective-permute-start | bytes 294920 | tf_op jit(solution)/shard_map/ppermute | solution.py:852
  129.0 3.6 %copy-start.30 = (bf16[256,192]{1,0:T(8,128)(2,1)}, bf16[256,192]{1,0:T(8,128)(2,1)S(1)}, u32[]{:S(2)}) copy-start(bf16[256,192]{1,0:T(8,128)(2,1)S(1)} %collective-permute-done.19.g1) | copy-start | bytes 294916
  131.1 1.5 copy-start.31
  132.6 1.6 copy-start.1
  140.8 36.2 %collective-permute-start.23 = (bf16[2,4,256,384]{3,2,1,0:T(8,128)(2,1)}, bf16[2,4,256,384]{3,2,1,0:T(8,128)(2,1)S(1)}, u32[]{:S(2)}, u32[]{:S(2)}) collective-permute-start(bf16[2,4,256,384]{3,2,1,0:T(8,128)(2,1)} %get-tuple-element.141), channel_id=1, source_target_pairs={{0,16},{8,24},{16,0},{24,8},{1,17},{9,25},{17,1},{25,9},{2,18},{10... | collective-permute-start | bytes 4718600 | tf_op jit(solution)/shard_map/ppermute | solution.py:852
  147.7 34.1 %collective-permute-start.22 = (bf16[2,4,96,768]{3,2,1,0:T(8,128)(2,1)}, bf16[2,4,96,768]{3,2,1,0:T(8,128)(2,1)S(1)}, u32[]{:S(2)}, u32[]{:S(2)}) collective-permute-start(bf16[2,4,96,768]{3,2,1,0:T(8,128)(2,1)} %get-tuple-element.138), channel_id=1, source_target_pairs={{0,8},{8,0},{16,24},{24,16},{1,9},{9,1},{17,25},{25,17},{2,10},{10... | collective-permute-start | bytes 3538952 | tf_op jit(solution)/shard_map/ppermute | solution.py:852
  165.9 21.0 %collective-permute-start.24 = (bf16[4,112,576]{2,1,0:T(8,128)(2,1)}, bf16[4,112,576]{2,1,0:T(8,128)(2,1)}, u32[]{:S(2)}, u32[]{:S(2)}) collective-permute-start(bf16[4,112,576]{2,1,0:T(8,128)(2,1)} %get-tuple-element.145), channel_id=1, source_target_pairs={{0,1},{1,0},{2,3},{3,2},{4,5},{5,4},{6,7},{7,6},{8,9},{9,8},{10,11... | collective-permute-start | bytes 1548296 | tf_op jit(solution)/shard_map/ppermute | solution.py:855
  181.4 18.4 %collective-permute-start.27 = (bf16[4,256,384]{2,1,0:T(8,128)(2,1)}, bf16[4,256,384]{2,1,0:T(8,128)(2,1)S(1)}, u32[]{:S(2)}, u32[]{:S(2)}) collective-permute-start(bf16[4,256,384]{2,1,0:T(8,128)(2,1)} %get-tuple-element.152), channel_id=1, source_target_pairs={{0,8},{8,0},{16,24},{24,16},{1,9},{9,1},{17,25},{25,17},{2,10},{10... | collective-permute-start | bytes 2359304 | tf_op jit(solution)/shard_map/ppermute | solution.py:852
  185.5 13.8 %collective-permute-start.26 = (bf16[4,96,768]{2,1,0:T(8,128)(2,1)}, bf16[4,96,768]{2,1,0:T(8,128)(2,1)S(1)}, u32[]{:S(2)}, u32[]{:S(2)}) collective-permute-start(bf16[4,96,768]{2,1,0:T(8,128)(2,1)} %get-tuple-element.150), channel_id=1, source_target_pairs={{0,16},{8,24},{16,0},{24,8},{1,17},{9,25},{17,1},{25,9},{2,18},{10... | collective-permute-start | bytes 1769480 | tf_op jit(solution)/shard_map/ppermute | solution.py:852
  189.0 6.8 %collective-permute-start.25 = (bf16[2,112,576]{2,1,0:T(8,128)(2,1)}, bf16[2,112,576]{2,1,0:T(8,128)(2,1)S(1)}, u32[]{:S(2)}, u32[]{:S(2)}) collective-permute-start(bf16[2,112,576]{2,1,0:T(8,128)(2,1)} %get-tuple-element.147), channel_id=1, source_target_pairs={{0,2},{2,0},{4,6},{6,4},{1,3},{3,1},{5,7},{7,5},{8,10},{10,8},{12,... | collective-permute-start | bytes 774152 | tf_op jit(solution)/shard_map/ppermute | solution.py:858
  198.4 5.6 %copy-start.34 = (bf16[112,576]{1,0:T(8,128)(2,1)S(1)}, bf16[112,576]{1,0:T(8,128)(2,1)}, u32[]{:S(2)}) copy-start(bf16[112,576]{1,0:T(8,128)(2,1)} %get-tuple-element.157) | copy-start | bytes 387076
  204.0 47.8 %copy-start.7 = (f32[256,768]{1,0:T(8,128)S(1)}, f32[256,768]{1,0:T(8,128)}, u32[]{:S(2)}) copy-start(f32[256,768]{1,0:T(8,128)} %get-tuple-element.116) | copy-start | bytes 2359300
  204.0 9.3 %collective-permute-start.31 = (bf16[112,576]{1,0:T(8,128)(2,1)S(1)}, bf16[112,576]{1,0:T(8,128)(2,1)S(1)}, u32[]{:S(2)}, u32[]{:S(2)}) collective-permute-start(bf16[112,576]{1,0:T(8,128)(2,1)S(1)} %copy-done.34), channel_id=1, source_target_pairs={{0,4},{2,6},{4,0},{6,2},{1,5},{3,7},{5,1},{7,3},{8,12},{10,14},{12... | collective-permute-start | bytes 387080 | tf_op jit(solution)/shard_map/ppermute | solution.py:858
  204.7 26.7 %collective-permute-start.28 = (bf16[448,384]{1,0:T(8,128)(2,1)}, bf16[448,384]{1,0:T(8,128)(2,1)S(1)}, u32[]{:S(2)}, u32[]{:S(2)}) collective-permute-start(bf16[448,384]{1,0:T(8,128)(2,1)} %get-tuple-element.154), channel_id=1, source_target_pairs={{0,2},{2,0},{4,6},{6,4},{1,3},{3,1},{5,7},{7,5},{8,10},{10,8},{12,... | collective-permute-start | bytes 1032200 | tf_op jit(solution)/shard_map/ppermute | solution.py:858
  207.7 27.6 %collective-permute-start.29 = (bf16[448,384]{1,0:T(8,128)(2,1)}, bf16[448,384]{1,0:T(8,128)(2,1)S(1)}, u32[]{:S(2)}, u32[]{:S(2)}) collective-permute-start(bf16[448,384]{1,0:T(8,128)(2,1)} %get-tuple-element.155), channel_id=1, source_target_pairs={{0,4},{2,6},{4,0},{6,2},{1,5},{3,7},{5,1},{7,3},{8,12},{10,14},{12... | collective-permute-start | bytes 1032200 | tf_op jit(solution)/shard_map/ppermute | solution.py:858
  207.8 27.5 %collective-permute-start.30 = (bf16[448,384]{1,0:T(8,128)(2,1)}, bf16[448,384]{1,0:T(8,128)(2,1)S(1)}, u32[]{:S(2)}, u32[]{:S(2)}) collective-permute-start(bf16[448,384]{1,0:T(8,128)(2,1)} %get-tuple-element.156), channel_id=1, source_target_pairs={{0,6},{2,4},{4,2},{6,0},{1,7},{3,5},{5,3},{7,1},{8,14},{10,12},{12... | collective-permute-start | bytes 1032200 | tf_op jit(solution)/shard_map/ppermute | solution.py:858
  215.6 10.4 %collective-permute-start.34 = (bf16[112,576]{1,0:T(8,128)(2,1)}, bf16[112,576]{1,0:T(8,128)(2,1)S(1)}, u32[]{:S(2)}, u32[]{:S(2)}) collective-permute-start(bf16[112,576]{1,0:T(8,128)(2,1)} %sum.1.b0), channel_id=1, source_target_pairs={{0,24},{8,16},{16,8},{24,0},{1,25},{9,17},{17,9},{25,1},{2,26},{10... | collective-permute-start | bytes 387080 | tf_op jit(solution)/shard_map/ppermute | solution.py:852
  217.2 9.8 %collective-permute-start.33 = (bf16[112,576]{1,0:T(8,128)(2,1)}, bf16[112,576]{1,0:T(8,128)(2,1)S(1)}, u32[]{:S(2)}, u32[]{:S(2)}) collective-permute-start(bf16[112,576]{1,0:T(8,128)(2,1)} %sum.1.b0), channel_id=1, source_target_pairs={{0,16},{8,24},{16,0},{24,8},{1,17},{9,25},{17,1},{25,9},{2,18},{10... | collective-permute-start | bytes 387080 | tf_op jit(solution)/shard_map/ppermute | solution.py:852
  226.1 23.3 %copy-start.23 = (bf16[112,576]{1,0:T(8,128)(2,1)}, bf16[112,576]{1,0:T(8,128)(2,1)S(1)}, u32[]{:S(2)}) copy-start(bf16[112,576]{1,0:T(8,128)(2,1)S(1)} %collective-permute-done.34.b3) | copy-start | bytes 387076
  226.1 5.3 %collective-permute-start.32 = (bf16[112,576]{1,0:T(8,128)(2,1)}, bf16[112,576]{1,0:T(8,128)(2,1)S(1)}, u32[]{:S(2)}, u32[]{:S(2)}) collective-permute-start(bf16[112,576]{1,0:T(8,128)(2,1)} %sum.1.b0), channel_id=1, source_target_pairs={{0,8},{8,0},{16,24},{24,16},{1,9},{9,1},{17,25},{25,17},{2,10},{10... | collective-permute-start | bytes 387080 | tf_op jit(solution)/shard_map/ppermute | solution.py:852
  227.0 22.4 %copy-start.24 = (bf16[112,576]{1,0:T(8,128)(2,1)}, bf16[112,576]{1,0:T(8,128)(2,1)S(1)}, u32[]{:S(2)}) copy-start(bf16[112,576]{1,0:T(8,128)(2,1)S(1)} %collective-permute-done.33.b2) | copy-start | bytes 387076
  231.4 18.0 %copy-start.25 = (bf16[112,576]{1,0:T(8,128)(2,1)}, bf16[112,576]{1,0:T(8,128)(2,1)S(1)}, u32[]{:S(2)}) copy-start(bf16[112,576]{1,0:T(8,128)(2,1)S(1)} %collective-permute-done.32.b1) | copy-start | bytes 387076
  231.4 3.9 %copy-start.19 = (bf16[448,384]{1,0:T(8,128)(2,1)}, bf16[448,384]{1,0:T(8,128)(2,1)S(1)}, u32[]{:S(2)}) copy-start(bf16[448,384]{1,0:T(8,128)(2,1)S(1)} %collective-permute-done.28.e1) | copy-start | bytes 1032196
  239.1 1.5 collective-permute-start.35
  243.2 12.6 %collective-permute-start.38 = (bf16[240,768]{1,0:T(8,128)(2,1)}, bf16[240,768]{1,0:T(8,128)(2,1)S(1)}, u32[]{:S(2)}, u32[]{:S(2)}) collective-permute-start(bf16[240,768]{1,0:T(8,128)(2,1)} %get-tuple-element.179.b0), channel_id=1, source_target_pairs={{0,24},{8,16},{16,8},{24,0},{1,25},{9,17},{17,9},{25,1},{2,26},{10... | collective-permute-start | bytes 1105928 | tf_op jit(solution)/shard_map/ppermute | solution.py:852
  244.6 18.2 %collective-permute-start.37 = (bf16[240,768]{1,0:T(8,128)(2,1)}, bf16[240,768]{1,0:T(8,128)(2,1)S(1)}, u32[]{:S(2)}, u32[]{:S(2)}) collective-permute-start(bf16[240,768]{1,0:T(8,128)(2,1)} %get-tuple-element.179.b0), channel_id=1, source_target_pairs={{0,16},{8,24},{16,0},{24,8},{1,17},{9,25},{17,1},{25,9},{2,18},{10... | collective-permute-start | bytes 1105928 | tf_op jit(solution)/shard_map/ppermute | solution.py:852
  246.4 16.4 %collective-permute-start.36 = (bf16[240,768]{1,0:T(8,128)(2,1)}, bf16[240,768]{1,0:T(8,128)(2,1)S(1)}, u32[]{:S(2)}, u32[]{:S(2)}) collective-permute-start(bf16[240,768]{1,0:T(8,128)(2,1)} %get-tuple-element.179.b0), channel_id=1, source_target_pairs={{0,8},{8,0},{16,24},{24,16},{1,9},{9,1},{17,25},{25,17},{2,10},{10... | collective-permute-start | bytes 1105928 | tf_op jit(solution)/shard_map/ppermute | solution.py:852
  255.8 7.1 %copy-start.16 = (bf16[240,768]{1,0:T(8,128)(2,1)}, bf16[240,768]{1,0:T(8,128)(2,1)S(1)}, u32[]{:S(2)}) copy-start(bf16[240,768]{1,0:T(8,128)(2,1)S(1)} %collective-permute-done.38.b3) | copy-start | bytes 1105924
  (15 other events, 11.7 us)
Sparse Core Ops, SparseCore 0:
  11.5 93.2 all-gather.1
  204.1 36.8 reduce-scatter.1
